TPU v7x, 32 devices: a whole 2x2x4 slice. The times are simulated.
32 devices in a mesh: fsdp: 4 (over z), ctx: 2 (over y), tp: 4 (over x, core).
Axes of the slice: x: 2, y: 2, z: 4, core: 2. Of those that a mesh axis runs over, the one named last changes fastest.
Arguments:
- inputs: bfloat16 [12288, 768], P(('fsdp', 'ctx')), may hold values from -6 to 6
- segments: int32 [4, 3072], P('fsdp', 'ctx'), may hold values from 0 to 11, never falling along the last dimension, each value on 1 to 512 neighbouring positions
- w_query: bfloat16 [768, 768], P('fsdp', 'tp'), may hold values from -0.21875 to 0.21875
- b_query: bfloat16 [768], P('tp'), may hold values from -4 to 4
- w_key: bfloat16 [768, 768], P('fsdp', 'tp'), may hold values from -0.21875 to 0.21875
- w_value: bfloat16 [768, 768], P('fsdp', 'tp'), may hold values from -0.21875 to 0.21875
- b_value: bfloat16 [768], P('tp'), may hold values from -4 to 4
- w_out: bfloat16 [768, 768], P('tp', 'fsdp'), may hold values from -3 to 3
- b_out: bfloat16 [768], replicated, may hold values from -4 to 4
- gain_one: bfloat16 [768], replicated, may hold values from 0.099609375 to 1.8984375
- shift_one: bfloat16 [768], replicated, may hold values from -4 to 4
- w_inner: bfloat16 [768, 3072], P('fsdp', 'tp'), may hold values from -0.21875 to 0.21875
- b_inner: bfloat16 [3072], P('tp'), may hold values from -4 to 4
- w_outer: bfloat16 [3072, 768], P('tp', 'fsdp'), may hold values from -0.109375 to 0.109375
- b_outer: bfloat16 [768], replicated, may hold values from -4 to 4
- gain_two: bfloat16 [768], replicated, may hold values from 0.099609375 to 1.8984375
- shift_two: bfloat16 [768], replicated, may hold values from -4 to 4
- grad_output: bfloat16 [12288, 768], P(('fsdp', 'ctx')), may hold values from -6 to 6
Outputs:
- output: bfloat16 [12288, 768], P(('fsdp', 'ctx'))
- grad_inputs: float32 [12288, 768], P(('fsdp', 'ctx'))
- grad_w_query: float32 [768, 768], P('fsdp', 'tp')
- grad_b_query: float32 [768], P('tp')
- grad_w_key: float32 [768, 768], P('fsdp', 'tp')
- grad_w_value: float32 [768, 768], P('fsdp', 'tp')
- grad_b_value: float32 [768], P('tp')
- grad_w_out: float32 [768, 768], P('tp', 'fsdp')
- grad_b_out: float32 [768], replicated
- grad_gain_one: float32 [768], replicated
- grad_shift_one: float32 [768], replicated
- grad_w_inner: float32 [768, 3072], P('fsdp', 'tp')
- grad_b_inner: float32 [3072], P('tp')
- grad_w_outer: float32 [3072, 768], P('tp', 'fsdp')
- grad_b_outer: float32 [768], replicated
- grad_gain_two: float32 [768], replicated
- grad_shift_two: float32 [768], replicated
Inputs may be any that keep to these rules, and one draw needn't show every extreme that they name: `segments`: along each sequence the ids never fall and every id of 0 to 11 occurs; a document has 1 to 512 tokens, and one has exactly 512.
All inputs are finite; a program needn't handle non-finite values.
Results may differ from a plain program's by a relative error of at most 0.023.
Values may be sent and summed in bfloat16 or wider, within the bound.
No kernel may reach another device: no remote copies, remote signals or barrier semaphores. Data moves between devices by JAX's collectives and lax.ppermute only.
A program may use at most 128 MiB of HBM per device.

v0:
```python
import math

import jax
import jax.numpy as jnp
from jax import lax
from jax.experimental import pallas as pl
from jax.experimental.pallas import tpu as pltpu
from jax.sharding import PartitionSpec as P

HEAD_DIM = 64
MOST = 512
IDS = 64
NO_ID = 63
LSE_LANE = 60
FAR = -1e30

layer_eps = 1e-12
low = jnp.bfloat16
high = jnp.float32


def nn(left, right):
    return jnp.dot(left, right, preferred_element_type=high)


def nt(left, right):
    return lax.dot_general(left, right, (((1,), (1,)), ((), ())), preferred_element_type=high)


def tn(left, right):
    return lax.dot_general(left, right, (((0,), (0,)), ((), ())), preferred_element_type=high)


def swap(value, axis, bit):
    count = lax.axis_size(axis)
    return lax.ppermute(value, axis, [(i, i ^ bit) for i in range(count)])


def shift(value, axis, step):
    count = lax.axis_size(axis)
    return lax.ppermute(value, axis, [(i, (i + step) % count) for i in range(count)])


def place(whole, part, first):
    return lax.dynamic_update_slice_in_dim(whole, part, first, 0)


def take(whole, first, count):
    return lax.dynamic_slice_in_dim(whole, first, count, 0)


def norm_parts(hidden):
    average = jnp.mean(hidden, axis=-1, keepdims=True)
    centred = hidden - average
    variance = jnp.mean(centred * centred, axis=-1, keepdims=True)
    inverse = lax.rsqrt(variance + layer_eps)
    return centred * inverse, inverse


def norm_back(grad, hat, inverse, gain):
    scaled = grad * gain
    first = jnp.mean(scaled, axis=-1, keepdims=True)
    second = jnp.mean(scaled * hat, axis=-1, keepdims=True)
    return inverse * (scaled - first - hat * second)


def gelu_parts(inner):
    half = 0.5 * (1.0 + lax.erf(inner * 0.7071067811865476))
    slope = half + inner * (jnp.exp(-0.5 * inner * inner) * 0.3989422804014327)
    return inner * half, slope


def three(value):
    first = value.astype(low)
    rest = value - first.astype(high)
    second = rest.astype(low)
    third = (rest - second.astype(high)).astype(low)
    return first, second, third


def meets(seg_q, first_q, size_q, seg_k, first_k, size_k):
    return (seg_q[first_q + size_q - 1] >= seg_k[first_k]) & (
        seg_q[first_q] <= seg_k[first_k + size_k - 1]
    )


def score_part(r, q_ref, q_row, first_q, seg_q, seg_k, ka_ref, vt_ref, acc_ref, top_ref, width):
    heads, keys = ka_ref.shape[0], ka_ref.shape[1]
    block = acc_ref.shape[2]
    acc_ref[...] = jnp.zeros_like(acc_ref)
    top_ref[...] = jnp.full_like(top_ref, 2 * FAR)

    def one_block(b, carry):
        first_k = b * width

        @pl.when(meets(seg_q, first_q, block, seg_k, first_k, width))
        def _():
            for h in range(heads):
                scores = nt(ka_ref[h, pl.ds(first_k, width), :], q_ref[h, q_row])
                top = top_ref[h]
                peak = jnp.maximum(top, jnp.max(scores, axis=0, keepdims=True))
                weights = jnp.exp(scores - peak).astype(low)
                acc_ref[h] = acc_ref[h] * jnp.exp(top - peak) + nn(
                    vt_ref[h, :, pl.ds(first_k, width)], weights
                )
                top_ref[h] = peak

        return carry

    lax.fori_loop(0, keys // width, one_block, 0)
    outs = []
    lane = lax.broadcasted_iota(jnp.int32, (block, HEAD_DIM), 1)
    for h in range(heads):
        acc = acc_ref[h]
        total = acc[HEAD_DIM : HEAD_DIM + 1]
        lse = top_ref[h] + jnp.log(total)
        joined = jnp.concatenate(
            [acc[:HEAD_DIM] / total, jnp.broadcast_to(lse, (HEAD_DIM, block))], axis=0
        )
        turned = joined.T
        outs.append(turned[:, :HEAD_DIM])
        minus = three(-turned[:, HEAD_DIM:])
        mask = q_ref[h, q_row, :, HEAD_DIM:].astype(high)
        for i in range(3):
            mask = jnp.where(lane == LSE_LANE + i, minus[i].astype(high), mask)
        q_ref[h, q_row, :, HEAD_DIM:] = mask.astype(low)
    return jnp.concatenate(outs, axis=1)


def attend_far_kernel(*refs, block, width, heads, marks):
    pieces = len(marks)
    here, seg_q, seg_k, x_ref, halo_ref, bias_ref, mq_ref, mk_ref = refs[:8]
    w_refs = refs[8 : 8 + pieces]
    (out_2, out_3, full_ref, q_near, q_far, ka_ref, v_ref, vt_ref, w_ref) = refs[8 + pieces : 17 + pieces]
    acc_ref, top_ref, sems = refs[17 + pieces :]
    keys = v_ref.shape[0]
    rows = x_ref.shape[0]
    local = heads * HEAD_DIM
    scale = 1.0 / math.sqrt(HEAD_DIM)
    mine, f, c = here[0], here[1], here[2]
    copies = []
    for i, mark in enumerate(marks):
        first, count = mark(f, c)
        copies.append(
            pltpu.make_async_copy(w_refs[i], w_ref.at[pl.ds(first, count)], sems.at[i])
        )
        copies[-1].start()
    vt_ref[:, HEAD_DIM:, :] = jnp.ones((heads, vt_ref.shape[1] - HEAD_DIM, keys), low)
    for copy in copies:
        copy.wait()
    weights_all = w_ref[...].reshape(-1, w_ref.shape[2])

    def keep(first, count, mask, kv):
        span = pl.ds(first, count)
        for h in range(heads):
            cols = slice(h * HEAD_DIM, (h + 1) * HEAD_DIM)
            tail = slice(local + h * HEAD_DIM, local + (h + 1) * HEAD_DIM)
            ka_ref[h, span, :] = jnp.concatenate([kv[:, cols], mask], axis=1)
            vt_ref[h, :HEAD_DIM, span] = kv[:, tail].T
        v_ref[span, :] = kv[:, local:]

    for q_ref, base in ((q_near, 0), (q_far, 2)):

        def project(i, carry, q_ref=q_ref, base=base):
            first = pl.multiple_of((mine ^ (base + i)) * block, block)
            span = pl.ds(first, block)
            both = (nn(x_ref[span, :], weights_all) + bias_ref[...]).astype(low)
            for h in range(heads):
                cols = slice(h * HEAD_DIM, (h + 1) * HEAD_DIM)
                q_ref[h, i] = jnp.concatenate(
                    [both[:, cols] * jnp.array(scale, low), mq_ref[span, :]], axis=1
                )
            keep(first, block, mk_ref[span, :], both[:, local:])
            return carry

        lax.fori_loop(0, 2, project, 0)
    step = min(512, keys - rows)
    for first in range(rows, keys, step):
        span = slice(first - rows, first - rows + step)
        kv = (nn(halo_ref[span, :], weights_all[:, local:]) + bias_ref[:, local:]).astype(low)
        keep(first, step, mk_ref[first : first + step, :], kv)
    for i, out_ref in enumerate((out_2, out_3)):
        joined = score_part(
            2 + i, q_far, i, (mine ^ (2 + i)) * block, seg_q, seg_k, ka_ref, vt_ref, acc_ref, top_ref, width
        )
        full_ref[i] = joined
        out_ref[...] = joined.astype(low)


def attend_near_kernel(
    here, seg_q, seg_k, q_in, ka_ref, vt_ref, out_0, out_1, full_ref, q_ref, acc_ref, top_ref, *, block, width
):
    mine = here[0]
    q_ref[...] = q_in[...]
    for i, out_ref in enumerate((out_0, out_1)):
        joined = score_part(
            i, q_ref, i, (mine ^ i) * block, seg_q, seg_k, ka_ref, vt_ref, acc_ref, top_ref, width
        )
        full_ref[i] = joined
        out_ref[...] = joined.astype(low)


VMEM = pl.BlockSpec(memory_space=pltpu.VMEM)
SMEM = pl.BlockSpec(memory_space=pltpu.SMEM)
ANY = pl.BlockSpec(memory_space=pl.ANY)
HBM = pl.BlockSpec(memory_space=pltpu.HBM)


def shape(*dims, kind=low):
    return jax.ShapeDtypeStruct(dims, kind)


def cost(flops, size, transcendentals=0):
    return pl.CostEstimate(flops=flops, transcendentals=transcendentals, bytes_accessed=size)


def attend_far(here, seg_q, seg_k, x, halo, bias, mask_q, mask_k, pieces, marks, blocks, block):
    rows = x.shape[0]
    local = bias.shape[1] // 3
    count = rows + halo.shape[0]
    heads = local // HEAD_DIM
    wide = 2 * HEAD_DIM
    return pl.pallas_call(
        lambda *refs: attend_far_kernel(*refs, block=block, width=256, heads=heads, marks=marks),
        name="attend_far",
        out_shape=(
            shape(block, local),
            shape(block, local),
            shape(2, block, local, kind=high),
            shape(heads, 2, block, wide),
            shape(heads, 2, block, wide),
            shape(heads, count, wide),
            shape(count, local),
            shape(heads, HEAD_DIM + 16, count),
            shape(*blocks, 3 * local),
        ),
        in_specs=[SMEM] * 3 + [VMEM] * 5 + [ANY] * len(pieces),
        out_specs=(VMEM,) * 9,
        scratch_shapes=[
            pltpu.VMEM((heads, HEAD_DIM + 16, block), high),
            pltpu.VMEM((heads, 1, block), high),
            pltpu.SemaphoreType.DMA((len(pieces),)),
        ],
        cost_estimate=cost(FAR_COST, 8 << 20),
    )(here, seg_q, seg_k, x, halo, bias, mask_q, mask_k, *pieces)


def attend_near(here, seg_q, seg_k, q_near, keys_wide, values_t):
    heads, _, block, wide = q_near.shape
    local = heads * HEAD_DIM
    return pl.pallas_call(
        lambda *refs: attend_near_kernel(*refs, block=block, width=256),
        name="attend_near",
        out_shape=(
            shape(block, local),
            shape(block, local),
            shape(2, block, local, kind=high),
            shape(heads, 2, block, wide),
        ),
        in_specs=[SMEM] * 3 + [VMEM] * 3,
        out_specs=(VMEM,) * 4,
        scratch_shapes=[
            pltpu.VMEM((heads, HEAD_DIM + 16, block), high),
            pltpu.VMEM((heads, 1, block), high),
        ],
        cost_estimate=cost(NEAR_COST, 8 << 20),
    )(here, seg_q, seg_k, q_near, keys_wide, values_t)


FAR_COST = 20 * 10**9
NEAR_COST = 12 * 10**9
FEED_COST = 26 * 10**9
UNIT_COST = 12 * 10**9
BACK_COST = 24 * 10**9
LAST_COST = 9 * 10**9
SMALL_COST = 3 * 10**9


def feed_kernel(*refs, plan, count, hidden, local):
    here, x_all, g_all, att_0, att_1, att_2, att_3, vec_ref = refs[:8]
    w_refs = refs[8 : 8 + count]
    (out_ref, one_ref, stat_ref, ga_0, ga_1, ga_2, ga_3, rows_hbm, keep_hbm, send_hbm) = refs[8 + count : 18 + count]
    (w_ref, b_ref, x_ref, g_ref, att_ref, hat_ref, inv_ref, norm_ref, acc_ref, slope_ref, gl_ref,
     rows_ref, keep_ref, send_ref, sems, out_sems) = refs[18 + count :]
    puts = []

    def put(src, dst):
        puts.append(pltpu.make_async_copy(src, dst, out_sems.at[len(puts)]))
        puts[-1].start()

    tokens, width = x_ref.shape
    mine, f, c = here[0], here[1], here[2]
    wide = 2 * hidden + local
    copies = []

    def begin(src, dst):
        copies.append(pltpu.make_async_copy(src, dst, sems.at[len(copies)]))
        copies[-1].start()

    first = pl.multiple_of(mine * tokens, tokens)
    begin(x_all.at[pl.ds(first, tokens)], x_ref)
    begin(g_all.at[pl.ds(first, tokens)], g_ref)
    for r, att in enumerate((att_0, att_1, att_2, att_3)):
        begin(att, att_ref.at[r])
    for i, offset, r, mark in plan:
        if mark is None:
            begin(w_refs[i].at[pl.ds(offset, 8)], b_ref.at[r])
        else:
            start, size = mark(f, c)
            begin(w_refs[i].at[pl.ds(offset, size)], w_ref.at[r, pl.ds(start, size)])
    for copy in copies:
        copy.wait()
    b_out, gain_one, shift_one, b_outer, gain_two, shift_two = (
        vec_ref[i : i + 1, :].astype(high) for i in range(6)
    )

    def weights(r, first, last):
        return w_ref[r, :, first:last]

    acc_ref[...] = nt(att_ref[0], weights(0, 2 * hidden, 2 * hidden + local))
    for r in range(1, 4):
        acc_ref[...] += nt(att_ref[r], weights(r, 2 * hidden, 2 * hidden + local))
    step = 64
    chunks = tokens // step

    def first_norm(i, carry):
        span = pl.ds(pl.multiple_of(i * step, step), step)
        hat, inverse = norm_parts(x_ref[span, :].astype(high) + (acc_ref[span, :] + b_out))
        hat_ref[span, :] = hat
        inv_ref[span, :] = inverse
        normed = hat * gain_one + shift_one
        norm_ref[span, :] = normed.astype(low)
        acc_ref[span, :] = normed + b_outer
        return carry

    lax.fori_loop(0, chunks, first_norm, 0)
    part = 256
    for k, side in enumerate((keep_ref, send_ref)):
        for x in range(2):
            side[x, :, 2 * hidden : wide] = att_ref[2 * x + k]
            side[x, :, wide:] = jnp.zeros((tokens, side.shape[2] - wide), low)

        def up(x, carry, k=k, side=side):
            r = 2 * x + k
            for j in range(0, hidden, part):
                inner = nn(norm_ref[...], weights(r, j, j + part))
                inner = inner + b_ref[r, 0:1, j : j + part].astype(high)
                act, slope = gelu_parts(inner)
                side[x, :, hidden + j : hidden + j + part] = act.astype(low)
                slope_ref[r, :, j : j + part] = slope
            acc_ref[...] += nt(side[x, :, hidden : 2 * hidden], weights(r, hidden, 2 * hidden))
            return carry

        lax.fori_loop(0, 2, up, 0)

    zero = jnp.zeros((1, width), high)

    def second_norm(i, sums):
        span = pl.ds(pl.multiple_of(i * step, step), step)
        hat, inverse = norm_parts(acc_ref[span, :])
        out_ref[span, :] = (hat * gain_two + shift_two).astype(low)
        grad = g_ref[span, :].astype(high)
        two = norm_back(grad, hat, inverse, gain_two)
        acc_ref[span, :] = two
        two_low = two.astype(low)
        gl_ref[span, :] = two_low
        terms = (two_low.astype(high), grad * hat, grad)
        return tuple(s + jnp.sum(v, axis=0, keepdims=True) for s, v in zip(sums, terms))

    sums_two = lax.fori_loop(0, chunks, second_norm, (zero,) * 3)
    rows_ref[0] = norm_ref[...].T
    rows_ref[1] = gl_ref[...].T
    put(rows_ref.at[pl.ds(0, 2)], rows_hbm.at[pl.ds(0, 2)])
    for k, side in ((1, send_ref), (0, keep_ref)):

        def down(x, carry, k=k, side=side):
            r = 2 * x + k
            for j in range(0, hidden, part):
                grad = nn(gl_ref[...], weights(r, hidden + j, hidden + j + part))
                grad = (grad * slope_ref[r, :, j : j + part]).astype(low)
                side[x, :, j : j + part] = grad
                stat_ref[8 + r, 0:1, j : j + part] = jnp.sum(grad.astype(high), axis=0, keepdims=True)
            acc_ref[...] += nt(side[x, :, :hidden], weights(r, 0, hidden))
            return carry

        lax.fori_loop(0, 2, down, 0)
        put(side, send_hbm if k else keep_hbm)

    def first_back(i, sums):
        span = pl.ds(pl.multiple_of(i * step, step), step)
        grad = acc_ref[span, :]
        hat = hat_ref[span, :]
        one = norm_back(grad, hat, inv_ref[span, :], gain_one)
        one_ref[span, :] = one
        one_low = one.astype(low)
        gl_ref[span, :] = one_low
        terms = (one_low.astype(high), grad * hat, grad)
        return tuple(s + jnp.sum(v, axis=0, keepdims=True) for s, v in zip(sums, terms))

    sums_one = lax.fori_loop(0, chunks, first_back, (zero,) * 3)
    for i, value in enumerate(sums_one + sums_two):
        stat_ref[i, 0:1, :] = value
    rows_ref[2] = gl_ref[...].T
    put(rows_ref.at[2], rows_hbm.at[2])
    for r, ga in enumerate((ga_0, ga_1, ga_2, ga_3)):
        ga[...] = nn(gl_ref[...], weights(r, 2 * hidden, 2 * hidden + local)).astype(low)
    for copy in puts:
        copy.wait()


def feed(here, x, grad, att, vectors, pieces, plan, tokens, hidden, local):
    width = x.shape[1]
    wide = 2 * hidden + local
    padded = (wide + 127) // 128 * 128
    copies = 6 + len(plan)
    return pl.pallas_call(
        lambda *refs: feed_kernel(*refs, plan=plan, count=len(pieces), hidden=hidden, local=local),
        name="feed",
        out_shape=(
            shape(tokens, width),
            shape(tokens, width, kind=high),
            shape(12, 1, width, kind=high),
            shape(tokens, local),
            shape(tokens, local),
            shape(tokens, local),
            shape(tokens, local),
            shape(3, width, tokens),
            shape(2, tokens, padded),
            shape(2, tokens, padded),
        ),
        in_specs=[SMEM] + [ANY] * 6 + [VMEM] + [ANY] * len(pieces),
        out_specs=(VMEM,) * 7 + (HBM,) * 3,
        scratch_shapes=[
            pltpu.VMEM((4, width, wide), low),
            pltpu.VMEM((4, 8, wide), low),
            pltpu.VMEM((tokens, width), low),
            pltpu.VMEM((tokens, width), low),
            pltpu.VMEM((4, tokens, local), low),
            pltpu.VMEM((tokens, width), high),
            pltpu.VMEM((tokens, 1), high),
            pltpu.VMEM((tokens, width), low),
            pltpu.VMEM((tokens, width), high),
            pltpu.VMEM((4, tokens, hidden), high),
            pltpu.VMEM((tokens, width), low),
            pltpu.VMEM((3, width, tokens), low),
            pltpu.VMEM((2, tokens, padded), low),
            pltpu.VMEM((2, tokens, padded), low),
            pltpu.SemaphoreType.DMA((copies,)),
            pltpu.SemaphoreType.DMA((4,)),
        ],
        cost_estimate=cost(FEED_COST, 24 << 20),
    )(here, x, grad, *att, vectors, *pieces)


def unit_kernel(here, rows_own, rows_mate, wide_own, wide_mate, *refs, hidden):
    ak_ref, as_ref, bk_ref, bs_ref, rows_ref, wide_ref, sems = refs
    c = here[2]
    tokens = rows_own.shape[2]
    wide = ak_ref.shape[2]
    half = ak_ref.shape[1]
    mid = rows_own.shape[1] // 2
    copies = [
        pltpu.make_async_copy(rows_own, rows_ref.at[:, :, pl.ds(0, tokens)], sems.at[0]),
        pltpu.make_async_copy(wide_own, wide_ref.at[:, pl.ds(0, tokens)], sems.at[1]),
        pltpu.make_async_copy(rows_mate, rows_ref.at[:, :, pl.ds(tokens, tokens)], sems.at[2]),
        pltpu.make_async_copy(wide_mate, wide_ref.at[:, pl.ds(tokens, tokens)], sems.at[3]),
    ]
    for copy in copies:
        copy.start()
    for copy in copies:
        copy.wait()
    spans = ((0, 0, hidden), (1, hidden, 2 * hidden), (2, 2 * hidden, wide))
    for x in range(2):
        for i, first, last in spans:
            for top in range(2):
                part = slice(top * mid, (top + 1) * mid)
                got = nn(rows_ref[i, part, :], wide_ref[x, :, first:last]).astype(low)
                if top == 0:
                    side = ak_ref if x == 0 else as_ref
                    side[:, :, first:last] = got.reshape(-1, half, last - first)
                else:
                    got = got.reshape(-1, 2, half, last - first)
                    for z in range(got.shape[0]):

                        @pl.when(c == 0)
                        def _():
                            bk_ref[x, z, :, first:last] = got[z, 0]
                            bs_ref[x, z, :, first:last] = got[z, 1]

                        @pl.when(c != 0)
                        def _():
                            bk_ref[x, z, :, first:last] = got[z, 1]
                            bs_ref[x, z, :, first:last] = got[z, 0]


def unit_grads(here, rows, mate_rows, keep, mate, half, hidden, local):
    wide = 2 * hidden + local
    tokens = rows.shape[2]
    width = rows.shape[1]
    quarters = width // 4 // half
    return pl.pallas_call(
        lambda *refs: unit_kernel(*refs, hidden=hidden),
        name="unit_grads",
        out_shape=(
            shape(2 * quarters, half, wide),
            shape(2 * quarters, half, wide),
            shape(2, quarters, half, wide),
            shape(2, quarters, half, wide),
        ),
        in_specs=[SMEM] + [ANY] * 4,
        out_specs=(VMEM,) * 4,
        scratch_shapes=[
            pltpu.VMEM((3, width, 2 * tokens), low),
            pltpu.VMEM((2, 2 * tokens, keep.shape[2]), low),
            pltpu.SemaphoreType.DMA((4,)),
        ],
        cost_estimate=cost(UNIT_COST, 14 << 20),
    )(here, rows, mate_rows, keep, mate)


def merge_one_kernel(here, ak, ga, bk, gb, a_keep, a_send, b_keep, b_send):
    c = here[2]
    for z in range(2):
        for side in range(2):
            i = 2 * z + side
            got = ak[i] + ga[i]

            @pl.when(c == side)
            def _():
                a_keep[z] = got

            @pl.when(c != side)
            def _():
                a_send[z] = got

    b_keep[...] = bk[0] + gb[0]
    b_send[...] = bk[1] + gb[1]


def merge_one(here, ak, ga, bk, gb):
    out = shape(*bk.shape[1:])
    return pl.pallas_call(
        merge_one_kernel,
        name="merge_one",
        out_shape=(out,) * 4,
        in_specs=[SMEM] + [VMEM] * 4,
        out_specs=(VMEM,) * 4,
        cost_estimate=cost(SMALL_COST, 8 << 20),
    )(here, ak, ga, bk, gb)


def merge_two_kernel(here, a_keep, a_got, b_keep, b_got, d_keep, d_got, *refs, start):
    outs, all_ref = refs[:4], refs[4]
    f = here[1]
    wide = a_keep.shape[2]
    for z in range(2):
        all_ref[z, :, :wide] = a_keep[z] + a_got[z]
        all_ref[2 + z, :, :wide] = b_keep[z] + b_got[z]
    all_ref[:, :, start:] = d_keep[...] + d_got[...]
    for s, out in enumerate(outs):
        out[...] = all_ref[(f + s) % 4]


def merge_two(here, a_keep, a_got, b_keep, b_got, d_keep, d_got, start):
    half = a_keep.shape[1]
    full = start + d_keep.shape[2]
    return pl.pallas_call(
        lambda *refs: merge_two_kernel(*refs, start=start),
        name="merge_two",
        out_shape=(shape(half, full),) * 4,
        in_specs=[SMEM] + [VMEM] * 6,
        out_specs=(VMEM,) * 4,
        scratch_shapes=[pltpu.VMEM((4, half, full), low)],
        cost_estimate=cost(SMALL_COST, 8 << 20),
    )(here, a_keep, a_got, b_keep, b_got, d_keep, d_got)


def merge_three_kernel(here, own, got_1, got_2, got_3, out, all_ref):
    f = here[1]
    for s, piece in enumerate((own, got_1, got_2, got_3)):
        all_ref[(f - s + 4) % 4] = piece[...]
    total = all_ref[0].astype(high)
    for z in range(1, 4):
        total = total + all_ref[z].astype(high)
    out[...] = total.astype(low)


def merge_three(here, pieces):
    return pl.pallas_call(
        merge_three_kernel,
        name="merge_three",
        out_shape=shape(*pieces[0].shape),
        in_specs=[SMEM] + [VMEM] * 4,
        out_specs=VMEM,
        scratch_shapes=[pltpu.VMEM((4,) + pieces[0].shape, low)],
        cost_estimate=cost(SMALL_COST, 4 << 20),
    )(here, *pieces)


def finish_kernel(here, own, got, inner, outer, out, query, key, value, bias, all_ref, *, start):
    c = here[2]
    hidden = inner.shape[1]
    local = query.shape[1]
    all_ref[c] = own[...]
    all_ref[1 - c] = got[...]
    half, full = own.shape

    def cols(first, last):
        return all_ref[:, :, first:last].reshape(2 * half, last - first).astype(high)

    inner[...] = cols(0, hidden)
    outer[...] = cols(hidden, 2 * hidden)
    out[...] = cols(2 * hidden, 2 * hidden + local).T
    rest = cols(start, full)
    query[...] = rest[:, :local]
    key[...] = rest[:, local : 2 * local]
    value[...] = rest[:, 2 * local : 3 * local]
    bias[...] = own[:16, start + 3 * local :].astype(high)


def finish(here, own, got, start, hidden, local):
    half, full = own.shape
    piece = 2 * half
    return pl.pallas_call(
        lambda *refs: finish_kernel(*refs, start=start),
        name="finish",
        out_shape=(
            shape(piece, hidden, kind=high),
            shape(piece, hidden, kind=high),
            shape(local, piece, kind=high),
            shape(piece, local, kind=high),
            shape(piece, local, kind=high),
            shape(piece, local, kind=high),
            shape(16, full - start - 3 * local, kind=high),
        ),
        in_specs=[SMEM] + [VMEM] * 2,
        out_specs=(VMEM,) * 7,
        scratch_shapes=[pltpu.VMEM((2, half, full), low)],
        cost_estimate=cost(SMALL_COST, 4 << 20),
    )(here, own, got)


def spread_kernel(here, p_0, p_1, p_2, p_3, out):
    tokens = p_0.shape[0]
    for r, piece in enumerate((p_0, p_1, p_2, p_3)):
        first = pl.multiple_of((here[0] ^ r) * tokens, tokens)
        out[pl.ds(first, tokens), :] = piece[...].astype(out.dtype)


def spread(here, pieces, kind):
    tokens, width = pieces[0].shape
    return pl.pallas_call(
        spread_kernel,
        name="spread",
        out_shape=shape(4 * tokens, width, kind=kind),
        in_specs=[SMEM] + [VMEM] * 4,
        out_specs=VMEM,
        cost_estimate=cost(SMALL_COST, 8 << 20),
    )(here, *pieces)


def project_back_kernel(here, g_ref, edge_ref, x_ref, w_ref, keep, send, d_keep, d_send, all_ref, *, local):
    mine, c = here[0], here[2]
    rows = g_ref.shape[0]
    rim = edge_ref.shape[0]
    tokens = keep.shape[1]
    half = d_keep.shape[1]
    pad = d_keep.shape[2] - 3 * local
    all_ref[...] = g_ref[...]
    edge = pl.ds(pl.multiple_of((1 - c) * (rows - rim), rim), rim)
    all_ref[edge, local:] = (
        g_ref[edge, local:].astype(high) + edge_ref[...].astype(high)
    ).astype(low)
    for k, side in ((1, send), (0, keep)):
        for x in range(2):
            first = pl.multiple_of((mine ^ (2 * x + k)) * tokens, tokens)
            side[x] = nt(all_ref[pl.ds(first, tokens), :], w_ref[...]).astype(low)
    sums = jnp.zeros((1, 3 * local), high)
    for i in range(rows // tokens):
        part = all_ref[i * tokens : (i + 1) * tokens, :].astype(high)
        sums = sums + jnp.sum(part, axis=0, keepdims=True)
    row = lax.broadcasted_iota(jnp.int32, (half, pad), 0)
    extra = jnp.zeros((half, pad), high)
    for j in range(3 * local // pad):
        extra = jnp.where(row == j, sums[:, j * pad : (j + 1) * pad], extra)
    extra = extra.astype(low)
    got = tn(x_ref[...], all_ref[...]).astype(low).reshape(-1, 2, half, 3 * local)
    for z in range(got.shape[0]):
        d_keep[z, :, 3 * local :] = extra
        d_send[z, :, 3 * local :] = extra
        for side in range(2):

            @pl.when(c == side)
            def _():
                d_keep[z, :, : 3 * local] = got[z, side]

            @pl.when(c != side)
            def _():
                d_send[z, :, : 3 * local] = got[z, side]


def project_back(here, grads, edge, x, weights, tokens, half):
    rows, width = x.shape
    local = grads.shape[1] // 3
    pad = HEAD_DIM
    return pl.pallas_call(
        lambda *refs: project_back_kernel(*refs, local=local),
        name="project_back",
        out_shape=(
            shape(2, tokens, width),
            shape(2, tokens, width),
            shape(width // half // 2, half, 3 * local + pad),
            shape(width // half // 2, half, 3 * local + pad),
        ),
        in_specs=[SMEM] + [VMEM] * 4,
        out_specs=(VMEM,) * 4,
        scratch_shapes=[pltpu.VMEM(grads.shape, low)],
        cost_estimate=cost(LAST_COST, 8 << 20),
    )(here, grads, edge, x, weights)


def attend_back_kernel(
    here, seg_q, seg_k, g_0, g_1, g_2, g_3, full_near, full_far, q_near, q_far, ka_ref, v_ref, own_ref, rim_ref,
    g_ref, full_ref, q_ref, kt_ref, va_ref, ga_ref, dka_ref, dva_ref, dqa_ref, sems, *, block, width, heads
):
    copies = [
        pltpu.make_async_copy(g, g_ref.at[r], sems.at[r]) for r, g in enumerate((g_0, g_1, g_2, g_3))
    ]
    for i, (q_part, full_part) in enumerate(((q_near, full_near), (q_far, full_far))):
        span = pl.ds(2 * i, 2)
        copies.append(pltpu.make_async_copy(q_part, q_ref.at[:, span], sems.at[4 + 2 * i]))
        copies.append(pltpu.make_async_copy(full_part, full_ref.at[span], sems.at[5 + 2 * i]))
    for copy in copies:
        copy.start()
    keys = v_ref.shape[0]
    rows = own_ref.shape[0]
    local = heads * HEAD_DIM
    scale = 1.0 / math.sqrt(HEAD_DIM)
    mine = here[0]
    for h in range(heads):
        cols = slice(h * HEAD_DIM, (h + 1) * HEAD_DIM)
        kt_ref[h] = ka_ref[h, :, :HEAD_DIM].T
        va_ref[h] = jnp.concatenate([v_ref[:, cols], jnp.ones((keys, HEAD_DIM), low)], axis=1)
    dka_ref[...] = jnp.zeros_like(dka_ref)
    dva_ref[...] = jnp.zeros_like(dva_ref)
    for copy in copies:
        copy.wait()

    def one_part(i, carry):
        first_q = pl.multiple_of((mine ^ i) * block, block)
        for h in range(heads):
            cols = slice(h * HEAD_DIM, (h + 1) * HEAD_DIM)
            grad = g_ref[i, :, cols]
            delta = jnp.sum(grad.astype(high) * full_ref[i, :, cols], axis=1, keepdims=True)
            lane = lax.broadcasted_iota(jnp.int32, (block, HEAD_DIM), 1)
            extra = jnp.zeros((block, HEAD_DIM), high)
            for j, piece in enumerate(three(-delta)):
                extra = jnp.where(lane == j, piece.astype(high), extra)
            ga_ref[h] = jnp.concatenate([grad, extra.astype(low)], axis=1)
        dqa_ref[...] = jnp.zeros_like(dqa_ref)

        def one_block(b, carry):
            first_k = b * width

            @pl.when(meets(seg_q, first_q, block, seg_k, first_k, width))
            def _():
                for h in range(heads):
                    span = pl.ds(first_k, width)
                    asks = q_ref[h, i]
                    probs = jnp.exp(nt(ka_ref[h, span, :], asks))
                    slopes = (probs * nt(va_ref[h, span, :], ga_ref[h])).astype(low)
                    dva_ref[h, span, :] += nn(probs.astype(low), ga_ref[h, :, :HEAD_DIM])
                    dka_ref[h, span, :] += nn(slopes, asks[:, :HEAD_DIM])
                    dqa_ref[h] += nn(kt_ref[h, :, span], slopes)

            return carry

        lax.fori_loop(0, keys // width, one_block, 0)
        own_ref[pl.ds(first_q, block), :local] = jnp.concatenate(
            [(dqa_ref[h] * scale).T for h in range(heads)], axis=1
        ).astype(low)
        return carry

    lax.fori_loop(0, 4, one_part, 0)
    for j, part in enumerate((dka_ref, dva_ref)):
        wide = jnp.concatenate([part[h] for h in range(heads)], axis=1).astype(low)
        own_ref[:, (1 + j) * local : (2 + j) * local] = wide[:rows]
        rim_ref[:, j * local : (j + 1) * local] = wide[rows:]


def attend_back(here, seg_q, seg_k, grads, full_near, full_far, q_near, q_far, keys, values):
    parts = len(grads)
    block, local = grads[0].shape
    rows = parts * block
    count = values.shape[0]
    heads = local // HEAD_DIM
    return pl.pallas_call(
        lambda *refs: attend_back_kernel(*refs, block=block, width=256, heads=heads),
        name="attend_back",
        out_shape=(shape(rows, 3 * local), shape(count - rows, 2 * local)),
        in_specs=[SMEM] * 3 + [ANY] * 8 + [VMEM] * 2,
        out_specs=(VMEM,) * 2,
        scratch_shapes=[
            pltpu.VMEM((parts, block, local), low),
            pltpu.VMEM((parts, block, local), high),
            pltpu.VMEM((heads, parts, block, 2 * HEAD_DIM), low),
            pltpu.VMEM((heads, HEAD_DIM, count), low),
            pltpu.VMEM((heads, count, 2 * HEAD_DIM), low),
            pltpu.VMEM((heads, block, 2 * HEAD_DIM), low),
            pltpu.VMEM((heads, count, HEAD_DIM), high),
            pltpu.VMEM((heads, count, HEAD_DIM), high),
            pltpu.VMEM((heads, HEAD_DIM, block), high),
            pltpu.SemaphoreType.DMA((parts + 4,)),
        ],
        cost_estimate=cost(BACK_COST, 8 << 20),
    )(here, seg_q, seg_k, *grads, full_near, full_far, q_near, q_far, keys, values)


def after(values, gate):
    return lax.optimization_barrier((tuple(values), gate))[0]


def halo_of(value, c, span):
    rows = value.shape[0]
    return take(value, (1 - c) * (rows - span), span)


def shards(
    inputs, segments, w_query, b_query, w_key, w_value, b_value, w_out, b_out, gain_one, shift_one,
    w_inner, b_inner, w_outer, b_outer, gain_two, shift_two, grad_output,
):
    rows, width = inputs.shape
    local = w_query.shape[1]
    hidden = w_inner.shape[1]
    n_f, n_c, n_t = (lax.axis_size(a) for a in ("fsdp", "ctx", "tp"))
    f, c, t = (lax.axis_index(a) for a in ("fsdp", "ctx", "tp"))
    tokens = rows // n_t
    rim = MOST
    quick = n_f == 4 and n_c == 2 and n_t == 4
    piece = width // n_f
    flip = [t ^ r for r in range(n_t)]

    half = piece // 2
    blocks = (2 * n_f, half)
    here = jnp.stack([t, f, c]).astype(jnp.int32)
    bundle_a = jnp.concatenate([w_query, w_key, w_value], axis=1)

    def spot(s, side):
        def mark(f, c):
            return (f - s + n_f) % n_f * 2 + (c if side == 0 else 1 - c), 1

        return mark

    def spot_from(s):
        return lambda f, c: ((f - s + n_f) % n_f * 2, 2)

    def spot_all(f, c):
        return 0, 2 * n_f

    def in_rows(mark):
        def rows_mark(f, c):
            first, count = mark(f, c)
            return (first if isinstance(first, int) else pl.multiple_of(first * half, half)), count * half

        return rows_mark

    seg_own = segments.reshape(rows)
    if quick:
        halves_a = bundle_a.reshape(2, half, -1)
        pieces_a = [halves_a] + [shift(halves_a, "fsdp", s) for s in range(1, n_f)]
        marks_a = [spot_from(s) for s in range(n_f)]
    else:
        whole_a = lax.all_gather(bundle_a, "fsdp", axis=0, tiled=True)
        pieces_a, marks_a = [whole_a.reshape(blocks + (-1,))], [spot_all]

    if n_c == 2:
        sent = halo_of(inputs, c, rim)
        if quick:
            part = rim // 2
            ids = halo_of(seg_own, c, rim).astype(low).reshape(2, part)
            ids = jnp.pad(ids, ((0, 14), (0, width - part)))
            got = swap(jnp.concatenate([take(sent, (t & 1) * part, part), ids], axis=0), "ctx", 1)
            halo_seg = got[part : part + 2, :part].astype(jnp.int32).reshape(rim)
            got = got[:part]
            mate = swap(got, "tp", 1)
            even = (t & 1) == 0
            halo_in = jnp.concatenate([jnp.where(even, got, mate), jnp.where(even, mate, got)], axis=0)
        else:
            halo_in = swap(sent, "ctx", 1)
            halo_seg = swap(halo_of(seg_own, c, rim), "ctx", 1)
    else:
        ahead = [(i, i + 1) for i in range(n_c - 1)]
        behind = [(i + 1, i) for i in range(n_c - 1)]

        def both(value):
            return jnp.concatenate(
                [
                    lax.ppermute(value[rows - rim :], "ctx", ahead),
                    lax.ppermute(value[:rim], "ctx", behind),
                ],
                axis=0,
            )

        halo_in = both(inputs)
        halo_seg = both(seg_own + 1) - 1
        halo_seg = jnp.where(halo_seg < 0, NO_ID, halo_seg)

    bias_row = jnp.pad(b_inner[None], ((0, 7), (0, hidden + local)))
    bundle_f = jnp.concatenate([w_inner, w_outer.T, w_out.T], axis=1)
    own_rows = jnp.concatenate([bundle_f, bias_row], axis=0)
    if quick:
        far_rows = swap(own_rows, "tp", 2)
        own_f = take(bundle_f, c * half, half)
        (own_1,) = after([own_f], (pieces_a[1], pieces_a[3]))
        gots = {s: shift(own_1, "fsdp", s) for s in (1, 3)}
        halo_in, far_rows = lax.optimization_barrier((halo_in, far_rows))
        far_f = take(far_rows, (1 - c) * half, half)
        corners = {s: shift(far_f, "fsdp", s) for s in (1, 3)}

    bias = jnp.concatenate([b_query, jnp.zeros_like(b_query), b_value]).astype(high)[None]
    seg_all = jnp.concatenate([seg_own, halo_seg])
    lane = jnp.arange(IDS)
    near_id = seg_all[:, None] == lane
    mask_k = (near_id | ((lane >= LSE_LANE) & (lane < LSE_LANE + 3))).astype(low)
    mask_q = jnp.where(near_id[:rows] | ((lane >= LSE_LANE) & (lane < LSE_LANE + 3)), 0.0, FAR).astype(low)
    att_2, att_3, full_far, q_near, q_far, keys_wide, values, values_t, w_qkv = attend_far(
        here, seg_own, seg_all, inputs, halo_in, bias, mask_q, mask_k, pieces_a, marks_a, blocks, tokens
    )
    w_qkv = w_qkv.reshape(width, 3 * local)

    if quick:
        (own_2,) = after([own_f], att_2)
        gots[2] = shift(own_2, "fsdp", 2)
        *near, corners[1], corners[3] = after([gots[1], gots[3], corners[1], corners[3]], att_2)
        (q_near,) = after([q_near], (*near, corners[1], corners[3]))
    att_0, att_1, full_near, q_near = attend_near(here, seg_own, seg_all, q_near, keys_wide, values_t)
    if quick:
        pieces_f, plan = [], []

        def add(r, value, marks, gate=None, bias=False):
            twin = value
            if gate is not None:
                (twin,) = after([value], gate)
            for r, piece in ((r, value), (r + 1, swap(twin, "tp", 1))):
                offset = 0
                for mark in marks:
                    plan.append((len(pieces_f), offset, r, in_rows(mark)))
                    offset += half
                if bias:
                    plan.append((len(pieces_f), piece_rows, r, None))
                pieces_f.append(piece)

        piece_rows = piece
        add(0, own_rows, [spot_from(0)], att_0, bias=True)
        add(2, far_rows, [spot_from(0)], att_0, bias=True)
        for s, got in zip((1, 3), near):
            add(0, got, [spot(s, 0)], att_0)
            add(2, corners[s], [spot(s, 1)], att_0)
        near = jnp.concatenate(near, axis=0)
        near_x, near_y = swap(near, "tp", 2), swap(near, "ctx", 1)
        last, near_x, near_y, *att = lax.optimization_barrier((gots[2], near_x, near_y, att_0, att_1, att_2, att_3))
        att_0, att_1, att_2, att_3 = att
        att = [att_0, swap(att_1, "tp", 1), swap(att_2, "tp", 2), swap(att_3, "tp", 3)]
        add(2, near_x, [spot(1, 0), spot(3, 0)])
        add(0, near_y, [spot(1, 1), spot(3, 1)])
        add(0, last, [spot(2, 0)])
        add(2, swap(last, "tp", 2), [spot(2, 0)])
        add(0, swap(last, "ctx", 1), [spot(2, 1)])
        corner = lax.ppermute(last, ("ctx", "tp"), [(i, i ^ (n_t + 2)) for i in range(n_c * n_t)])
        add(2, corner, [spot(2, 1)])
    else:
        gathered = lax.all_gather(bundle_f, "fsdp", axis=0, tiled=True)
        gathered = jnp.concatenate([gathered, bias_row], axis=0)
        gathered = lax.all_gather(gathered, "tp", axis=0)
        pieces_f = [lax.dynamic_index_in_dim(gathered, i, 0, keepdims=False) for i in flip]
        plan = [(r, 0, r, in_rows(spot_all)) for r in range(n_t)]
        plan += [(r, width, r, None) for r in range(n_t)]

    if not quick:
        att = [att_0, swap(att_1, "tp", 1), swap(att_2, "tp", 2), swap(att_3, "tp", 3)]

    vectors = jnp.stack([b_out, gain_one, shift_one, b_outer, gain_two, shift_two, b_out, b_out])
    output, g_one, stats, ga_0, ga_1, ga_2, ga_3, rows_t, keep, send = feed(
        here, inputs, grad_output, att, vectors, pieces_f, plan, tokens, hidden, local
    )
    g_att = [ga_0, swap(ga_1, "tp", 1), swap(ga_2, "tp", 2), swap(ga_3, "tp", 3)]
    stats = stats[:, 0]

    if quick:
        mate_rows = swap(rows_t, "tp", 1)
        mate = swap(send, "tp", 1)
        near_sums = jnp.concatenate([stats[:6], stats[8:9], stats[10:11]], axis=0)
        away = jnp.concatenate([stats[:6], stats[9:10], stats[11:12]], axis=0)
        keep_a, send_a, keep_b, send_b = unit_grads(here, rows_t, mate_rows, keep, mate, half, hidden, local)
        got_a = swap(send_a, "tp", 2)
        got_b = swap(send_b, "ctx", 1)
        *g_att, keep_a, keep_b = lax.optimization_barrier((*g_att, keep_a, keep_b))
    else:
        ordered = []
        for r in range(n_t):
            wide = (keep, send)[r % 2][r // 2]
            ordered.append(
                jnp.concatenate(
                    [
                        nn(rows_t[0], wide[:, :hidden]),
                        nn(rows_t[1], wide[:, hidden : 2 * hidden]),
                        nn(rows_t[2], wide[:, 2 * hidden : 2 * hidden + local]),
                    ],
                    axis=1,
                )
            )
        stacked = jnp.stack(ordered)
        ordered = jnp.stack([lax.dynamic_index_in_dim(stacked, i, 0, keepdims=False) for i in flip])
        mine = lax.psum_scatter(ordered, "tp", scatter_dimension=0, tiled=False)
        mine = lax.psum(mine, ("fsdp", "ctx"))
        shard_f = take(mine, f * piece, piece)

    g_own, g_rim = attend_back(
        here, seg_own, seg_all, g_att, full_near, full_far, q_near, q_far, keys_wide, values
    )
    if quick:
        got_a, got_b = after([got_a, got_b], g_own)
        (rim_out,) = after([g_rim], (got_a, got_b))
        (away,) = after([away], g_own)
        pair = near_sums + swap(away, "tp", 1)
        edge = swap(rim_out, "ctx", 1)
        keep_a, send_a, keep_b, send_b = merge_one(here, keep_a, got_a, keep_b, got_b)
        got_a = swap(send_a, "ctx", 1)
        got_b = swap(send_b, "tp", 2)
        (edge,) = after([edge], (send_a, send_b, pair))
        away = jnp.concatenate([pair[:6], pair[7:8], pair[7:8]], axis=0)
        pair = pair + swap(away, "tp", 2)
        dx_keep, dx_send, d_keep, d_send = project_back(here, g_own, edge, inputs, w_qkv, tokens, half)
        (dx_send,) = after([dx_send], (got_a, got_b))
        dx_got = swap(dx_send, "tp", 1)
        d_got = swap(d_send, "ctx", 1)
        near_dx = dx_keep[0] + dx_got[0]
        far_dx = dx_keep[1] + dx_got[1]
        far_got = swap(far_dx, "tp", 2)
        start = (2 * hidden + local + 127) // 128 * 128
        pair = pair + swap(pair, "ctx", 1)
        keep_a, pair = lax.optimization_barrier((keep_a, pair))
        outs = merge_two(here, keep_a, got_a, keep_b, got_b, d_keep, d_got, start)
        (output,) = after([output], outs[0])
        pair = pair + swap(pair, "fsdp", 1)
        totals = [outs[0]] + [shift(outs[s], "fsdp", s) for s in range(1, n_f)]
        mine = (near_dx.astype(high) + far_got.astype(high) + g_one).astype(low)

        def everyone(value, kind):
            far_value = swap(value, "tp", 2)
            return spread(here, [value, swap(value, "tp", 1), far_value, swap(far_value, "tp", 1)], kind)

        output = everyone(output, low)
        grad_inputs = everyone(mine, high)
        totals[1], pair = lax.optimization_barrier((totals[1], pair))
        total = merge_three(here, totals)
        pair = pair + swap(pair, "fsdp", 2)
        got = swap(total, "ctx", 1)
        got, output, grad_inputs = lax.optimization_barrier((got, output, grad_inputs))
        s_inner, s_outer, s_out, s_query, s_key, s_value, s_bias = finish(
            here, total, got, start, hidden, local
        )
        s_outer = s_outer.T
        s_qkv = s_bias.reshape(-1)[: 3 * local]
        shared, s_b_inner = pair[:6], pair[6]
    else:
        edge_got = []
        if n_c == 2:
            edge_got.append(((1 - c) * (rows - rim), swap(g_rim, "ctx", 1)))
        else:
            edge_got.append((0, lax.ppermute(g_rim[rim:], "ctx", ahead)))
            edge_got.append((rows - rim, lax.ppermute(g_rim[:rim], "ctx", behind)))
        g_all = g_own.astype(high)
        for first, got in edge_got:
            got = jnp.pad(got.astype(high), ((0, 0), (local, 0)))
            g_all = place(g_all, take(g_all, first, rim) + got, first)
        g_all = g_all.astype(low)
        part = nt(g_all, w_qkv).reshape(n_t, tokens, width)
        mine = lax.psum_scatter(part, "tp", scatter_dimension=0, tiled=False)
        grad_inputs = lax.all_gather((mine + g_one).astype(low), "tp", axis=0, tiled=True).astype(high)
        output = lax.all_gather(output, "tp", axis=0, tiled=True)
        shard_a = take(lax.psum(tn(inputs, g_all), ("fsdp", "ctx")), f * piece, piece)
        s_query, s_key, s_value = (shard_a[:, i * local : (i + 1) * local] for i in range(3))
        s_qkv = lax.psum(jnp.sum(g_all.astype(high), axis=0), ("fsdp", "ctx"))
        s_inner, s_outer, s_out = shard_f[:, :hidden], shard_f[:, hidden : 2 * hidden].T, shard_f[:, 2 * hidden :].T
        ordered = jnp.stack([lax.dynamic_index_in_dim(stats[8:], i, 0, keepdims=False) for i in flip])
        s_b_inner = lax.psum(
            lax.psum_scatter(ordered, "tp", scatter_dimension=0, tiled=False), ("fsdp", "ctx")
        )
        shared = lax.psum(stats[:6], ("fsdp", "ctx", "tp"))
    return (
        output,
        grad_inputs,
        s_query,
        s_qkv[:local],
        s_key,
        s_value,
        s_qkv[2 * local :],
        s_out,
        shared[0],
        shared[1],
        shared[2],
        s_inner,
        s_b_inner,
        s_outer,
        shared[3],
        shared[4],
        shared[5],
    )


def solution(mesh):
    rows = P(("fsdp", "ctx"), None)
    down, flat, across = P("fsdp", "tp"), P("tp"), P("tp", "fsdp")
    return jax.shard_map(
        shards,
        mesh=mesh,
        in_specs=(
            rows, P("fsdp", "ctx"), down, flat, down, down, flat, across, P(), P(), P(), down, flat,
            across, P(), P(), P(), rows,
        ),
        out_specs=(
            rows, rows, down, flat, down, down, flat, across, P(), P(), P(), down, flat, across,
            P(), P(), P(),
        ),
        check_vma=False,
    )
```

profile of v0, /device:TPU:10, one launch (start us, length us, event | category | flops | bytes accessed | tf_op | source)
XLA Modules:
  0.0 322.1 jit_solution(6455812661568555581)
XLA Ops:
  0.7 1.2 pad_maximum_fusion.1
  2.4 2.6 collective-permute-start.4
  5.0 2.5 collective-permute-start.3
  8.2 1.1 constant_dynamic-slice_fusion.1
  9.3 1.6 collective-permute-start
  13.2 8.1 %collective-permute-done.5.refs_11_ = bf16[2,96,576]{2,1,0:T(8,128)(2,1)S(1)} collective-permute-done((bf16[2,96,576]{2,1,0:T(8,128)(2,1)S(1)}, bf16[2,96,576]{2,1,0:T(8,128)(2,1)S(1)}, u32[]{:S(2)}, u32[]{:S(2)}) %collective-permute-start.5) | collective-permute-done | bytes 221216 | tf_op jit(solution)/shard_map/ppermute | solution.py:41
  21.3 11.8 %collective-permute-done.3.refs_9_ = bf16[2,96,576]{2,1,0:T(8,128)(2,1)} collective-permute-done((bf16[2,96,576]{2,1,0:T(8,128)(2,1)S(1)}, bf16[2,96,576]{2,1,0:T(8,128)(2,1)}, u32[]{:S(2)}, u32[]{:S(2)}) %collective-permute-start.3) | collective-permute-done | bytes 221216 | tf_op jit(solution)/shard_map/ppermute | solution.py:41
  33.1 2.6 collective-permute-start.7
  35.9 1.1 or_convert_fusion
  37.0 0.9 select_convert_fusion.refs_6_
  38.0 0.9 pad_maximum_fusion.refs_4_
  38.9 1.0 constant_dynamic-slice_fusion
  40.0 2.1 collective-permute-start.9
  42.1 18.0 %attend_far.1 = (bf16[384,192]{1,0:T(8,128)(2,1)}, bf16[384,192]{1,0:T(8,128)(2,1)}, f32[2,384,192]{2,1,0:T(8,128)}, bf16[3,2,384,128]{3,2,1,0:T(8,128)(2,1)}, b...) custom-call(s32[3]{0:T(128)} %pad_add_fusion.1.refs_0_.here, ...), custom_call_target="tpu_custom_call" | custom-call | flops 20000000000 | bytes 8388608 | tf_op jit(solution)/shard_map/attend_far/pallas_call | solution.py:223
  60.1 3.3 %collective-permute-start.6 = (bf16[96,1728]{1,0:T(8,128)(2,1)S(1)}, bf16[96,1728]{1,0:T(8,128)(2,1)}, u32[]{:S(2)}, u32[]{:S(2)}) collective-permute-start(bf16[96,1728]{1,0:T(8,128)(2,1)S(1)} %fusion.9), channel_id=1, source_target_pairs={{0,16},{8,24},{16,0},{24,8},{1,17},{9,25},{17,1},{25,9},{2,18},{10... | collective-permute-start | bytes 995336 | tf_op jit(solution)/shard_map/ppermute | solution.py:41
  63.4 0.8 copy-done.41
  64.3 5.8 %collective-permute-start.12 = (bf16[192,1728]{1,0:T(8,128)(2,1)S(1)}, bf16[192,1728]{1,0:T(8,128)(2,1)}, u32[]{:S(2)}, u32[]{:S(2)}) collective-permute-start(bf16[192,1728]{1,0:T(8,128)(2,1)S(1)} %constant_dynamic-update-slice_fusion), channel_id=1, source_target_pairs={{0,4},{4,0},{1,5},{5,1},{2,6},{6,2},{3,7},{7,3},{8,12},{12,8},{9,1... | collective-permute-start | bytes 1990664 | tf_op jit(solution)/shard_map/ppermute | solution.py:36
  70.1 13.5 %attend_near.1 = (bf16[384,192]{1,0:T(8,128)(2,1)}, bf16[384,192]{1,0:T(8,128)(2,1)}, f32[2,384,192]{2,1,0:T(8,128)}, bf16[3,2,384,128]{3,2,1,0:T(8,128)(2,1)}) custom-call(s32[3]{0:T(128)} %pad_add_fusion.1.refs_0_.here, s32[1536]{0:T(1024)} %copy-done.11, s32[2048]{0:T(1024)} %copy-done.10, bf16[3,2,384,128]{3,2,1,0:T(8,128)(2,1)} %get-tuple-element.117.refs_3_, ...), custom_call_target="tpu_custom_call" | custom-call | flops 12000000000 | bytes 8388608 | tf_op jit(solution)/shard_map/attend_near/pallas_call | solution.py:251
  84.2 1.1 collective-permute-done.18.refs_13_
  85.8 1.1 collective-permute-done.11.refs_20_
  86.9 0.9 collective-permute-done.19.refs_15_
  87.8 1.5 collective-permute-start.29
  89.4 1.7 collective-permute-start.15
  91.5 1.7 collective-permute-start.25
  93.2 9.4 %collective-permute-done.14.refs_5_ = bf16[384,192]{1,0:T(8,128)(2,1)S(1)} collective-permute-done((bf16[384,192]{1,0:T(8,128)(2,1)}, bf16[384,192]{1,0:T(8,128)(2,1)S(1)}, u32[]{:S(2)}, u32[]{:S(2)}) %collective-permute-start.14) | collective-permute-done | bytes 147488 | tf_op jit(solution)/shard_map/ppermute | solution.py:36
  102.5 4.0 %collective-permute-done.15.refs_6_ = bf16[384,192]{1,0:T(8,128)(2,1)S(1)} collective-permute-done((bf16[384,192]{1,0:T(8,128)(2,1)}, bf16[384,192]{1,0:T(8,128)(2,1)S(1)}, u32[]{:S(2)}, u32[]{:S(2)}) %collective-permute-start.15) | collective-permute-done | bytes 147488 | tf_op jit(solution)/shard_map/ppermute | solution.py:36
  107.3 6.1 %collective-permute-done.25.refs_26_ = bf16[96,1728]{1,0:T(8,128)(2,1)} collective-permute-done((bf16[96,1728]{1,0:T(8,128)(2,1)}, bf16[96,1728]{1,0:T(8,128)(2,1)}, u32[]{:S(2)}, u32[]{:S(2)}) %collective-permute-start.25) | collective-permute-done | bytes 331808 | tf_op jit(solution)/shard_map/ppermute | solution.py:36
  115.4 0.8 collective-permute-done.26.refs_27_
  117.1 0.9 copy-done.26
  118.0 25.4 %feed.1 = (bf16[384,768]{1,0:T(8,128)(2,1)}, f32[384,768]{1,0:T(8,128)}, f32[12,1,768]{2,1,0:T(1,128)}, bf16[384,192]{1,0:T(8,128)(2,1)}, bf16[384,192]{1,0:T(8,...) custom-call(s32[3]{0:T(128)} %pad_add_fusion.1.refs_0_.here, ...), custom_call_target="tpu_custom_call" | custom-call | flops 25999998976 | bytes 25165824 | tf_op jit(solution)/shard_map/feed/pallas_call | solution.py:416
  145.2 2.3 collective-permute-start.32
  148.2 3.2 collective-permute-done.34.refs_2_
  151.3 1.2 copy-done.21
  152.6 1.5 copy-done.20
  154.1 12.3 %unit_grads.1 = (bf16[4,96,1728]{2,1,0:T(8,128)(2,1)}, bf16[4,96,1728]{2,1,0:T(8,128)(2,1)}, bf16[2,2,96,1728]{3,2,1,0:T(8,128)(2,1)}, bf16[2,2,96,1728]{3,2,1,0:T(8,128)(2,1)}) custom-call(s32[3]{0:T(128)} %pad_add_fusion.1.refs_0_.here, bf16[3,768,384]{2,1,0:T(8,128)(2,1)} %get-tuple-element.140.refs_1_, bf16[3,768,384]{2,1,0:T(8,128)(2,1)} %copy-done.21, ...), custom_call_target="tpu_custom_call" | custom-call | flops 12000000000 | bytes 14680064 | tf_op jit(solution)/shard_map/unit_grads/pallas_call | solution.py:501
  166.4 2.3 collective-permute-start.36
  168.8 23.4 %attend_back.1 = (bf16[1536,576]{1,0:T(8,128)(2,1)}, bf16[512,384]{1,0:T(8,128)(2,1)}) custom-call(s32[3]{0:T(128)} %pad_add_fusion.1.refs_0_.here, s32[1536]{0:T(1024)} %copy-done.11, s32[2048]{0:T(1024)} %copy-done.10, bf16[384,192]{1,0:T(8,128)(2,1)} %get-tuple-element.148.refs_3_, bf16[384,192]{1,0:T(8,128)(2,1)} %copy-done.53, ...), custom_call_target="tpu_custom_call" | custom-call | flops 24000000000 | bytes 8388608 | tf_op jit(solution)/shard_map/attend_back/pallas_call | solution.py:797
  192.4 7.3 %collective-permute-done.36.ga = bf16[4,96,1728]{2,1,0:T(8,128)(2,1)S(1)} collective-permute-done((bf16[4,96,1728]{2,1,0:T(8,128)(2,1)}, bf16[4,96,1728]{2,1,0:T(8,128)(2,1)S(1)}, u32[]{:S(2)}, u32[]{:S(2)}) %collective-permute-start.36) | collective-permute-done | bytes 1327136 | tf_op jit(solution)/shard_map/ppermute | solution.py:36
  199.7 1.6 collective-permute-done.37.gb
  201.6 4.4 %merge_one.1 = (bf16[2,96,1728]{2,1,0:T(8,128)(2,1)}, bf16[2,96,1728]{2,1,0:T(8,128)(2,1)}, bf16[2,96,1728]{2,1,0:T(8,128)(2,1)}, bf16[2,96,1728]{2,1,0:T(8,128)(2,1)}) custom-call(s32[3]{0:T(128)} %pad_add_fusion.1.refs_0_.here, bf16[4,96,1728]{2,1,0:T(8,128)(2,1)} %get-tuple-element.145.ak, bf16[4,96,1728]{2,1,0:T(8,128)(2,1)} %copy-done.22, ...), custom_call_target="tpu_custom_call" | custom-call | flops 3000000000 | bytes 8388608 | tf_op jit(solution)/shard_map/merge_one/pallas_call | solution.py:542
  205.9 1.7 collective-permute-start.41
  208.0 5.4 %collective-permute-done.43.refs_2_ = bf16[512,384]{1,0:T(8,128)(2,1)S(1)} collective-permute-done((bf16[512,384]{1,0:T(8,128)(2,1)}, bf16[512,384]{1,0:T(8,128)(2,1)S(1)}, u32[]{:S(2)}, u32[]{:S(2)}) %collective-permute-start.43) | collective-permute-done | bytes 393248 | tf_op jit(solution)/shard_map/ppermute | solution.py:36
  214.2 8.7 %project_back.1 = (bf16[2,384,768]{2,1,0:T(8,128)(2,1)}, bf16[2,384,768]{2,1,0:T(8,128)(2,1)}, bf16[4,96,640]{2,1,0:T(8,128)(2,1)}, bf16[4,96,640]{2,1,0:T(8,128)(2,1)}) custom-call(s32[3]{0:T(128)} %pad_add_fusion.1.refs_0_.here, bf16[1536,576]{1,0:T(8,128)(2,1)} %get-tuple-element.157.refs_1_, bf16[512,384]{1,0:T(8,128)(2,1)} %copy-done.40, ...), custom_call_target="tpu_custom_call" | custom-call | flops 8999999488 | bytes 8388608 | tf_op jit(solution)/shard_map/project_back/pallas_call | solution.py:706
  222.9 3.6 %collective-permute-done.41.refs_2_ = bf16[2,96,1728]{2,1,0:T(8,128)(2,1)S(1)} collective-permute-done((bf16[2,96,1728]{2,1,0:T(8,128)(2,1)}, bf16[2,96,1728]{2,1,0:T(8,128)(2,1)S(1)}, u32[]{:S(2)}, u32[]{:S(2)}) %collective-permute-start.41) | collective-permute-done | bytes 663584 | tf_op jit(solution)/shard_map/ppermute | solution.py:36
  226.5 0.8 copy-done.27
  227.9 2.5 collective-permute-done.53
  230.4 1.9 fusion.5
  233.0 1.5 collective-permute-start.39
  234.4 14.0 %collective-permute-done.39 = f32[8,768]{1,0:T(8,128)S(1)} collective-permute-done((f32[8,768]{1,0:T(8,128)S(1)}, f32[8,768]{1,0:T(8,128)S(1)}, u32[]{:S(2)}, u32[]{:S(2)}) %collective-permute-start.39) | collective-permute-done | bytes 24608 | tf_op jit(solution)/shard_map/ppermute | solution.py:36
  249.0 3.3 %collective-permute-done.40 = f32[8,768]{1,0:T(8,128)S(1)} collective-permute-done((f32[8,768]{1,0:T(8,128)S(1)}, f32[8,768]{1,0:T(8,128)S(1)}, u32[]{:S(2)}, u32[]{:S(2)}) %collective-permute-start.40) | collective-permute-done | bytes 24608 | tf_op jit(solution)/shard_map/ppermute | solution.py:36
  253.7 3.7 %merge_two.1 = (bf16[96,2432]{1,0:T(8,128)(2,1)}, bf16[96,2432]{1,0:T(8,128)(2,1)}, bf16[96,2432]{1,0:T(8,128)(2,1)}, bf16[96,2432]{1,0:T(8,128)(2,1)}) custom-call(s32[3]{0:T(128)} %pad_add_fusion.1.refs_0_.here, bf16[2,96,1728]{2,1,0:T(8,128)(2,1)} %get-tuple-element.164.refs_1_, bf16[2,96,1728]{2,1,0:T(8,128)(2,1)} %copy-done.27, ...), custom_call_target="tpu_custom_call" | custom-call | flops 3000000000 | bytes 8388608 | tf_op jit(solution)/shard_map/merge_two/pallas_call | solution.py:567
  258.1 2.2 fusion.2.p_0
  260.3 1.4 collective-permute-start.56
  261.7 2.0 collective-permute-start.46
  263.7 2.1 collective-permute-start.47
  265.8 5.8 %collective-permute-done.46 = f32[8,768]{1,0:T(8,128)S(1)} collective-permute-done((f32[8,768]{1,0:T(8,128)S(1)}, f32[8,768]{1,0:T(8,128)S(1)}, u32[]{:S(2)}, u32[]{:S(2)}) %collective-permute-start.46) | collective-permute-done | bytes 24608 | tf_op jit(solution)/shard_map/ppermute | solution.py:36
  271.7 17.0 %collective-permute-done.45.got_1 = bf16[96,2432]{1,0:T(8,128)(2,1)S(1)} collective-permute-done((bf16[96,2432]{1,0:T(8,128)(2,1)}, bf16[96,2432]{1,0:T(8,128)(2,1)S(1)}, u32[]{:S(2)}, u32[]{:S(2)}) %collective-permute-start.45) | collective-permute-done | bytes 466976 | tf_op jit(solution)/shard_map/ppermute | solution.py:41
  289.2 7.6 %collective-permute-done.47.got_2 = bf16[96,2432]{1,0:T(8,128)(2,1)S(1)} collective-permute-done((bf16[96,2432]{1,0:T(8,128)(2,1)S(1)}, bf16[96,2432]{1,0:T(8,128)(2,1)S(1)}, u32[]{:S(2)}, u32[]{:S(2)}) %collective-permute-start.47) | collective-permute-done | bytes 466976 | tf_op jit(solution)/shard_map/ppermute | solution.py:41
  296.8 3.4 %collective-permute-start.58 = (f32[8,768]{1,0:T(8,128)S(1)}, f32[8,768]{1,0:T(8,128)S(1)}, u32[]{:S(2)}, u32[]{:S(2)}) collective-permute-start(f32[8,768]{1,0:T(8,128)S(1)} %add.57), channel_id=1, source_target_pairs={{0,16},{8,24},{16,0},{24,8},{1,17},{9,25},{17,1},{25,9},{2,18},{10... | collective-permute-start | bytes 73736 | tf_op jit(solution)/shard_map/ppermute | solution.py:36
  300.8 2.9 merge_three.1.refs_1_
  306.5 3.2 spread.2
  311.3 4.1 %spread.3 = f32[1536,768]{1,0:T(8,128)} custom-call(s32[3]{0:T(128)} %pad_add_fusion.1.refs_0_.here, bf16[384,768]{1,0:T(8,128)(2,1)} %fusion.2.p_0, bf16[384,768]{1,0:T(8,128)(2,1)} %copy-done.32, bf16[384,768]{1,0:T(8,128)(2,1)} %copy-done.29, bf16[384,768]{1,0:T(8,128)(2,1)} %copy-done.33), custom_call_target="tpu_custom_call" | custom-call | flops 3000000000 | bytes 8388608 | tf_op jit(solution)/shard_map/spread/pallas_call | solution.py:652
  315.4 1.3 collective-permute-done.49.refs_2_
  317.5 2.6 finish.1
  (234 shorter events, 25.2 us)
Async XLA Ops:
  1.9 19.4 %collective-permute-start.5 = (bf16[2,96,576]{2,1,0:T(8,128)(2,1)S(1)}, bf16[2,96,576]{2,1,0:T(8,128)(2,1)S(1)}, u32[]{:S(2)}, u32[]{:S(2)}) collective-permute-start(bf16[2,96,576]{2,1,0:T(8,128)(2,1)S(1)} %bitcast.34), channel_id=1, source_target_pairs={{0,24},{8,0},{16,8},{24,16},{1,25},{9,1},{17,9},{25,17},{2,26},{10... | collective-permute-start | bytes 663560 | tf_op jit(solution)/shard_map/ppermute | solution.py:41
  2.4 39.7 %collective-permute-start.4 = (bf16[2,96,576]{2,1,0:T(8,128)(2,1)S(1)}, bf16[2,96,576]{2,1,0:T(8,128)(2,1)}, u32[]{:S(2)}, u32[]{:S(2)}) collective-permute-start(bf16[2,96,576]{2,1,0:T(8,128)(2,1)S(1)} %bitcast.35), channel_id=1, source_target_pairs={{0,16},{8,24},{16,0},{24,8},{1,17},{9,25},{17,1},{25,9},{2,18},{10... | collective-permute-start | bytes 663560 | tf_op jit(solution)/shard_map/ppermute | solution.py:41
  5.0 28.1 %collective-permute-start.3 = (bf16[2,96,576]{2,1,0:T(8,128)(2,1)S(1)}, bf16[2,96,576]{2,1,0:T(8,128)(2,1)}, u32[]{:S(2)}, u32[]{:S(2)}) collective-permute-start(bf16[2,96,576]{2,1,0:T(8,128)(2,1)S(1)} %bitcast.36), channel_id=1, source_target_pairs={{0,8},{8,16},{16,24},{24,0},{1,9},{9,17},{17,25},{25,1},{2,10},{10... | collective-permute-start | bytes 663560 | tf_op jit(solution)/shard_map/ppermute | solution.py:41
  9.3 26.4 %collective-permute-start = (bf16[272,768]{1,0:T(8,128)(2,1)S(1)}, bf16[272,768]{1,0:T(8,128)(2,1)S(1)}, u32[]{:S(2)}, u32[]{:S(2)}) collective-permute-start(bf16[272,768]{1,0:T(8,128)(2,1)S(1)} %fusion.7), channel_id=1, source_target_pairs={{0,4},{4,0},{1,5},{5,1},{2,6},{6,2},{3,7},{7,3},{8,12},{12,8},{9,1... | collective-permute-start | bytes 1253384 | tf_op jit(solution)/shard_map/ppermute | solution.py:36
  11.1 72.4 %copy-start.4 = (bf16[200,1728]{1,0:T(8,128)(2,1)}, bf16[200,1728]{1,0:T(8,128)(2,1)S(1)}, u32[]{:S(2)}) copy-start(bf16[200,1728]{1,0:T(8,128)(2,1)S(1)} %fusion.4.refs_8_) | copy-start | bytes 2073604
  11.2 27.8 %collective-permute-start.2 = (bf16[200,1728]{1,0:T(8,128)(2,1)S(1)}, bf16[200,1728]{1,0:T(8,128)(2,1)}, u32[]{:S(2)}, u32[]{:S(2)}) collective-permute-start(bf16[200,1728]{1,0:T(8,128)(2,1)S(1)} %fusion.4.refs_8_), channel_id=1, source_target_pairs={{0,2},{1,3},{2,0},{3,1},{4,6},{5,7},{6,4},{7,5},{8,10},{9,11},{10,... | collective-permute-start | bytes 2073608 | tf_op jit(solution)/shard_map/ppermute | solution.py:36
  33.1 30.2 %collective-permute-start.8 = (bf16[96,1728]{1,0:T(8,128)(2,1)S(1)}, bf16[96,1728]{1,0:T(8,128)(2,1)S(1)}, u32[]{:S(2)}, u32[]{:S(2)}) collective-permute-start(bf16[96,1728]{1,0:T(8,128)(2,1)S(1)} %fusion.9), channel_id=1, source_target_pairs={{0,24},{8,0},{16,8},{24,16},{1,25},{9,1},{17,9},{25,17},{2,26},{10... | collective-permute-start | bytes 995336 | tf_op jit(solution)/shard_map/ppermute | solution.py:41
  33.1 30.2 %collective-permute-start.7 = (bf16[96,1728]{1,0:T(8,128)(2,1)S(1)}, bf16[96,1728]{1,0:T(8,128)(2,1)S(1)}, u32[]{:S(2)}, u32[]{:S(2)}) collective-permute-start(bf16[96,1728]{1,0:T(8,128)(2,1)S(1)} %fusion.9), channel_id=1, source_target_pairs={{0,8},{8,16},{16,24},{24,0},{1,9},{9,17},{17,25},{25,1},{2,10},{10... | collective-permute-start | bytes 995336 | tf_op jit(solution)/shard_map/ppermute | solution.py:41
  35.8 2.1 collective-permute-start.1
  39.9 23.4 %collective-permute-start.10 = (bf16[96,1728]{1,0:T(8,128)(2,1)S(1)}, bf16[96,1728]{1,0:T(8,128)(2,1)S(1)}, u32[]{:S(2)}, u32[]{:S(2)}) collective-permute-start(bf16[96,1728]{1,0:T(8,128)(2,1)S(1)} %constant_dynamic-slice_fusion), channel_id=1, source_target_pairs={{0,24},{8,0},{16,8},{24,16},{1,25},{9,1},{17,9},{25,17},{2,26},{10... | collective-permute-start | bytes 995336 | tf_op jit(solution)/shard_map/ppermute | solution.py:41
  40.0 24.2 %collective-permute-start.9 = (bf16[96,1728]{1,0:T(8,128)(2,1)S(1)}, bf16[96,1728]{1,0:T(8,128)(2,1)}, u32[]{:S(2)}, u32[]{:S(2)}) collective-permute-start(bf16[96,1728]{1,0:T(8,128)(2,1)S(1)} %constant_dynamic-slice_fusion), channel_id=1, source_target_pairs={{0,8},{8,16},{16,24},{24,0},{1,9},{9,17},{17,25},{25,1},{2,10},{10... | collective-permute-start | bytes 995336 | tf_op jit(solution)/shard_map/ppermute | solution.py:41
  60.1 24.0 %collective-permute-start.6 = (bf16[96,1728]{1,0:T(8,128)(2,1)S(1)}, bf16[96,1728]{1,0:T(8,128)(2,1)}, u32[]{:S(2)}, u32[]{:S(2)}) collective-permute-start(bf16[96,1728]{1,0:T(8,128)(2,1)S(1)} %fusion.9), channel_id=1, source_target_pairs={{0,16},{8,24},{16,0},{24,8},{1,17},{9,25},{17,1},{25,9},{2,18},{10... | collective-permute-start | bytes 995336 | tf_op jit(solution)/shard_map/ppermute | solution.py:41
  64.3 21.1 %collective-permute-start.12 = (bf16[192,1728]{1,0:T(8,128)(2,1)S(1)}, bf16[192,1728]{1,0:T(8,128)(2,1)}, u32[]{:S(2)}, u32[]{:S(2)}) collective-permute-start(bf16[192,1728]{1,0:T(8,128)(2,1)S(1)} %constant_dynamic-update-slice_fusion), channel_id=1, source_target_pairs={{0,4},{4,0},{1,5},{5,1},{2,6},{6,2},{3,7},{7,3},{8,12},{12,8},{9,1... | collective-permute-start | bytes 1990664 | tf_op jit(solution)/shard_map/ppermute | solution.py:36
  70.0 16.8 %collective-permute-start.11 = (bf16[192,1728]{1,0:T(8,128)(2,1)S(1)}, bf16[192,1728]{1,0:T(8,128)(2,1)}, u32[]{:S(2)}, u32[]{:S(2)}) collective-permute-start(bf16[192,1728]{1,0:T(8,128)(2,1)S(1)} %constant_dynamic-update-slice_fusion), channel_id=1, source_target_pairs={{0,2},{1,3},{2,0},{3,1},{4,6},{5,7},{6,4},{7,5},{8,10},{9,11},{10,... | collective-permute-start | bytes 1990664 | tf_op jit(solution)/shard_map/ppermute | solution.py:36
  70.0 44.6 %copy-start.16 = (bf16[768]{0:T(1024)(128)(2,1)S(1)}, bf16[768]{0:T(1024)(128)(2,1)}, u32[]{:S(2)}) copy-start(bf16[768]{0:T(1024)(128)(2,1)} %param.28) | copy-start | bytes 4612
  70.1 44.6 %copy-start.17 = (bf16[768]{0:T(1024)(128)(2,1)S(1)}, bf16[768]{0:T(1024)(128)(2,1)}, u32[]{:S(2)}) copy-start(bf16[768]{0:T(1024)(128)(2,1)} %param.32) | copy-start | bytes 4612
  70.1 44.6 %copy-start.18 = (bf16[768]{0:T(1024)(128)(2,1)S(1)}, bf16[768]{0:T(1024)(128)(2,1)}, u32[]{:S(2)}) copy-start(bf16[768]{0:T(1024)(128)(2,1)} %param.33) | copy-start | bytes 4612
  70.1 44.6 %copy-start.19 = (bf16[768]{0:T(1024)(128)(2,1)S(1)}, bf16[768]{0:T(1024)(128)(2,1)}, u32[]{:S(2)}) copy-start(bf16[768]{0:T(1024)(128)(2,1)} %param.34) | copy-start | bytes 4612
  83.6 1.7 collective-permute-start.18
  83.6 5.8 %collective-permute-start.16 = (bf16[200,1728]{1,0:T(8,128)(2,1)S(1)}, bf16[200,1728]{1,0:T(8,128)(2,1)S(1)}, u32[]{:S(2)}, u32[]{:S(2)}) collective-permute-start(bf16[200,1728]{1,0:T(8,128)(2,1)S(1)} %fusion.4.refs_8_), channel_id=1, source_target_pairs={{0,1},{1,0},{2,3},{3,2},{4,5},{5,4},{6,7},{7,6},{8,9},{9,8},{10,11... | collective-permute-start | bytes 2073608 | tf_op jit(solution)/shard_map/ppermute | solution.py:36
  84.1 7.1 %collective-permute-start.17 = (bf16[200,1728]{1,0:T(8,128)(2,1)}, bf16[200,1728]{1,0:T(8,128)(2,1)S(1)}, u32[]{:S(2)}, u32[]{:S(2)}) collective-permute-start(bf16[200,1728]{1,0:T(8,128)(2,1)} %collective-permute-done.2.refs_10_), channel_id=1, source_target_pairs={{0,1},{1,0},{2,3},{3,2},{4,5},{5,4},{6,7},{7,6},{8,9},{9,8},{10,11... | collective-permute-start | bytes 2073608 | tf_op jit(solution)/shard_map/ppermute | solution.py:36
  85.2 2.5 collective-permute-start.19
  85.4 3.9 %collective-permute-start.20 = (bf16[96,1728]{1,0:T(8,128)(2,1)S(1)}, bf16[96,1728]{1,0:T(8,128)(2,1)S(1)}, u32[]{:S(2)}, u32[]{:S(2)}) collective-permute-start(bf16[96,1728]{1,0:T(8,128)(2,1)S(1)} %collective-permute-done.8.refs_16_), channel_id=1, source_target_pairs={{0,1},{1,0},{2,3},{3,2},{4,5},{5,4},{6,7},{7,6},{8,9},{9,8},{10,11... | collective-permute-start | bytes 995336 | tf_op jit(solution)/shard_map/ppermute | solution.py:36
  86.9 2.5 collective-permute-start.21
  87.8 18.8 %collective-permute-start.29 = (bf16[96,1728]{1,0:T(8,128)(2,1)}, bf16[96,1728]{1,0:T(8,128)(2,1)S(1)}, u32[]{:S(2)}, u32[]{:S(2)}) collective-permute-start(bf16[96,1728]{1,0:T(8,128)(2,1)} %collective-permute-done.6.refs_24_), channel_id=1, source_target_pairs={{0,6},{1,7},{2,4},{3,5},{4,2},{5,3},{6,0},{7,1},{8,14},{9,15},{10,... | collective-permute-start | bytes 995336 | tf_op jit(solution)/shard_map/ppermute | solution.py:969
  89.3 2.2 collective-permute-start.13
  89.3 13.2 %collective-permute-start.14 = (bf16[384,192]{1,0:T(8,128)(2,1)}, bf16[384,192]{1,0:T(8,128)(2,1)S(1)}, u32[]{:S(2)}, u32[]{:S(2)}) collective-permute-start(bf16[384,192]{1,0:T(8,128)(2,1)} %get-tuple-element.125), channel_id=1, source_target_pairs={{0,2},{1,3},{2,0},{3,1},{4,6},{5,7},{6,4},{7,5},{8,10},{9,11},{10,... | collective-permute-start | bytes 442376 | tf_op jit(solution)/shard_map/ppermute | solution.py:36
  89.4 17.1 %collective-permute-start.15 = (bf16[384,192]{1,0:T(8,128)(2,1)}, bf16[384,192]{1,0:T(8,128)(2,1)S(1)}, u32[]{:S(2)}, u32[]{:S(2)}) collective-permute-start(bf16[384,192]{1,0:T(8,128)(2,1)} %get-tuple-element.126), channel_id=1, source_target_pairs={{0,3},{1,2},{2,1},{3,0},{4,7},{5,6},{6,5},{7,4},{8,11},{9,10},{10,... | collective-permute-start | bytes 442376 | tf_op jit(solution)/shard_map/ppermute | solution.py:36
  91.2 16.0 %collective-permute-start.27 = (bf16[96,1728]{1,0:T(8,128)(2,1)}, bf16[96,1728]{1,0:T(8,128)(2,1)S(1)}, u32[]{:S(2)}, u32[]{:S(2)}) collective-permute-start(bf16[96,1728]{1,0:T(8,128)(2,1)} %collective-permute-done.6.refs_24_), channel_id=1, source_target_pairs={{0,4},{4,0},{1,5},{5,1},{2,6},{6,2},{3,7},{7,3},{8,12},{12,8},{9,1... | collective-permute-start | bytes 995336 | tf_op jit(solution)/shard_map/ppermute | solution.py:36
  91.5 21.8 %collective-permute-start.25 = (bf16[96,1728]{1,0:T(8,128)(2,1)}, bf16[96,1728]{1,0:T(8,128)(2,1)}, u32[]{:S(2)}, u32[]{:S(2)}) collective-permute-start(bf16[96,1728]{1,0:T(8,128)(2,1)} %collective-permute-done.6.refs_24_), channel_id=1, source_target_pairs={{0,2},{1,3},{2,0},{3,1},{4,6},{5,7},{6,4},{7,5},{8,10},{9,11},{10,... | collective-permute-start | bytes 995336 | tf_op jit(solution)/shard_map/ppermute | solution.py:36
  102.5 10.8 %collective-permute-start.24 = (bf16[96,1728]{1,0:T(8,128)(2,1)}, bf16[96,1728]{1,0:T(8,128)(2,1)S(1)}, u32[]{:S(2)}, u32[]{:S(2)}) collective-permute-start(bf16[96,1728]{1,0:T(8,128)(2,1)} %collective-permute-done.6.refs_24_), channel_id=1, source_target_pairs={{0,1},{1,0},{2,3},{3,2},{4,5},{5,4},{6,7},{7,6},{8,9},{9,8},{10,11... | collective-permute-start | bytes 995336 | tf_op jit(solution)/shard_map/ppermute | solution.py:36
  106.6 9.7 %collective-permute-start.22 = (bf16[192,1728]{1,0:T(8,128)(2,1)}, bf16[192,1728]{1,0:T(8,128)(2,1)S(1)}, u32[]{:S(2)}, u32[]{:S(2)}) collective-permute-start(bf16[192,1728]{1,0:T(8,128)(2,1)} %collective-permute-done.11.refs_20_), channel_id=1, source_target_pairs={{0,1},{1,0},{2,3},{3,2},{4,5},{5,4},{6,7},{7,6},{8,9},{9,8},{10,11... | collective-permute-start | bytes 1990664 | tf_op jit(solution)/shard_map/ppermute | solution.py:36
  106.6 9.6 %collective-permute-start.23 = (bf16[192,1728]{1,0:T(8,128)(2,1)}, bf16[192,1728]{1,0:T(8,128)(2,1)S(1)}, u32[]{:S(2)}, u32[]{:S(2)}) collective-permute-start(bf16[192,1728]{1,0:T(8,128)(2,1)} %collective-permute-done.12.refs_22_), channel_id=1, source_target_pairs={{0,1},{1,0},{2,3},{3,2},{4,5},{5,4},{6,7},{7,6},{8,9},{9,8},{10,11... | collective-permute-start | bytes 1990664 | tf_op jit(solution)/shard_map/ppermute | solution.py:36
  107.2 8.2 %collective-permute-start.30 = (bf16[96,1728]{1,0:T(8,128)(2,1)S(1)}, bf16[96,1728]{1,0:T(8,128)(2,1)}, u32[]{:S(2)}, u32[]{:S(2)}) collective-permute-start(bf16[96,1728]{1,0:T(8,128)(2,1)S(1)} %collective-permute-done.29.refs_30_), channel_id=1, source_target_pairs={{0,1},{1,0},{2,3},{3,2},{4,5},{5,4},{6,7},{7,6},{8,9},{9,8},{10,11... | collective-permute-start | bytes 995336 | tf_op jit(solution)/shard_map/ppermute | solution.py:36
  113.3 2.0 collective-permute-start.28
  114.1 2.1 collective-permute-start.26
  143.4 7.9 %collective-permute-start.35 = (bf16[2,384,1792]{2,1,0:T(8,128)(2,1)}, bf16[2,384,1792]{2,1,0:T(8,128)(2,1)S(1)}, u32[]{:S(2)}, u32[]{:S(2)}) collective-permute-start(bf16[2,384,1792]{2,1,0:T(8,128)(2,1)} %get-tuple-element.142), channel_id=1, source_target_pairs={{0,1},{1,0},{2,3},{3,2},{4,5},{5,4},{6,7},{7,6},{8,9},{9,8},{10,11... | collective-permute-start | bytes 8257544 | tf_op jit(solution)/shard_map/ppermute | solution.py:36
  143.9 7.5 %collective-permute-start.34 = (bf16[3,768,384]{2,1,0:T(8,128)(2,1)}, bf16[3,768,384]{2,1,0:T(8,128)(2,1)S(1)}, u32[]{:S(2)}, u32[]{:S(2)}) collective-permute-start(bf16[3,768,384]{2,1,0:T(8,128)(2,1)} %get-tuple-element.140.refs_1_), channel_id=1, source_target_pairs={{0,1},{1,0},{2,3},{3,2},{4,5},{5,4},{6,7},{7,6},{8,9},{9,8},{10,11... | collective-permute-start | bytes 5308424 | tf_op jit(solution)/shard_map/ppermute | solution.py:36
  144.7 21.6 %collective-permute-start.31 = (bf16[384,192]{1,0:T(8,128)(2,1)}, bf16[384,192]{1,0:T(8,128)(2,1)S(1)}, u32[]{:S(2)}, u32[]{:S(2)}) collective-permute-start(bf16[384,192]{1,0:T(8,128)(2,1)} %get-tuple-element.137), channel_id=1, source_target_pairs={{0,1},{1,0},{2,3},{3,2},{4,5},{5,4},{6,7},{7,6},{8,9},{9,8},{10,11... | collective-permute-start | bytes 442376 | tf_op jit(solution)/shard_map/ppermute | solution.py:36
  145.2 21.2 %collective-permute-start.32 = (bf16[384,192]{1,0:T(8,128)(2,1)}, bf16[384,192]{1,0:T(8,128)(2,1)S(1)}, u32[]{:S(2)}, u32[]{:S(2)}) collective-permute-start(bf16[384,192]{1,0:T(8,128)(2,1)} %get-tuple-element.138), channel_id=1, source_target_pairs={{0,2},{1,3},{2,0},{3,1},{4,6},{5,7},{6,4},{7,5},{8,10},{9,11},{10,... | collective-permute-start | bytes 442376 | tf_op jit(solution)/shard_map/ppermute | solution.py:36
  147.4 19.0 %collective-permute-start.33 = (bf16[384,192]{1,0:T(8,128)(2,1)}, bf16[384,192]{1,0:T(8,128)(2,1)S(1)}, u32[]{:S(2)}, u32[]{:S(2)}) collective-permute-start(bf16[384,192]{1,0:T(8,128)(2,1)} %get-tuple-element.139), channel_id=1, source_target_pairs={{0,3},{1,2},{2,1},{3,0},{4,7},{5,6},{6,5},{7,4},{8,11},{9,10},{10,... | collective-permute-start | bytes 442376 | tf_op jit(solution)/shard_map/ppermute | solution.py:36
  166.4 33.3 %collective-permute-start.36 = (bf16[4,96,1728]{2,1,0:T(8,128)(2,1)}, bf16[4,96,1728]{2,1,0:T(8,128)(2,1)S(1)}, u32[]{:S(2)}, u32[]{:S(2)}) collective-permute-start(bf16[4,96,1728]{2,1,0:T(8,128)(2,1)} %get-tuple-element.146), channel_id=1, source_target_pairs={{0,2},{1,3},{2,0},{3,1},{4,6},{5,7},{6,4},{7,5},{8,10},{9,11},{10,... | collective-permute-start | bytes 3981320 | tf_op jit(solution)/shard_map/ppermute | solution.py:36
  168.8 32.5 %collective-permute-start.37 = (bf16[2,2,96,1728]{3,2,1,0:T(8,128)(2,1)}, bf16[2,2,96,1728]{3,2,1,0:T(8,128)(2,1)}, u32[]{:S(2)}, u32[]{:S(2)}) collective-permute-start(bf16[2,2,96,1728]{3,2,1,0:T(8,128)(2,1)} %get-tuple-element.147), channel_id=1, source_target_pairs={{0,4},{4,0},{1,5},{5,1},{2,6},{6,2},{3,7},{7,3},{8,12},{12,8},{9,1... | collective-permute-start | bytes 3981320 | tf_op jit(solution)/shard_map/ppermute | solution.py:36
  192.2 9.3 %collective-permute-start.38 = (f32[8,768]{1,0:T(8,128)S(1)}, f32[8,768]{1,0:T(8,128)S(1)}, u32[]{:S(2)}, u32[]{:S(2)}) collective-permute-start(f32[8,768]{1,0:T(8,128)S(1)} %pad_maximum_fusion.2), channel_id=1, source_target_pairs={{0,1},{1,0},{2,3},{3,2},{4,5},{5,4},{6,7},{7,6},{8,9},{9,8},{10,11... | collective-permute-start | bytes 73736 | tf_op jit(solution)/shard_map/ppermute | solution.py:36
  201.3 12.2 %collective-permute-start.43 = (bf16[512,384]{1,0:T(8,128)(2,1)}, bf16[512,384]{1,0:T(8,128)(2,1)S(1)}, u32[]{:S(2)}, u32[]{:S(2)}) collective-permute-start(bf16[512,384]{1,0:T(8,128)(2,1)} %get-tuple-element.169), channel_id=1, source_target_pairs={{0,4},{4,0},{1,5},{5,1},{2,6},{6,2},{3,7},{7,3},{8,12},{12,8},{9,1... | collective-permute-start | bytes 1179656 | tf_op jit(solution)/shard_map/ppermute | solution.py:36
  205.9 20.5 %collective-permute-start.41 = (bf16[2,96,1728]{2,1,0:T(8,128)(2,1)}, bf16[2,96,1728]{2,1,0:T(8,128)(2,1)S(1)}, u32[]{:S(2)}, u32[]{:S(2)}) collective-permute-start(bf16[2,96,1728]{2,1,0:T(8,128)(2,1)} %get-tuple-element.165), channel_id=1, source_target_pairs={{0,4},{4,0},{1,5},{5,1},{2,6},{6,2},{3,7},{7,3},{8,12},{12,8},{9,1... | collective-permute-start | bytes 1990664 | tf_op jit(solution)/shard_map/ppermute | solution.py:36
  207.7 18.8 %collective-permute-start.42 = (bf16[2,96,1728]{2,1,0:T(8,128)(2,1)}, bf16[2,96,1728]{2,1,0:T(8,128)(2,1)S(1)}, u32[]{:S(2)}, u32[]{:S(2)}) collective-permute-start(bf16[2,96,1728]{2,1,0:T(8,128)(2,1)} %get-tuple-element.167), channel_id=1, source_target_pairs={{0,2},{1,3},{2,0},{3,1},{4,6},{5,7},{6,4},{7,5},{8,10},{9,11},{10,... | collective-permute-start | bytes 1990664 | tf_op jit(solution)/shard_map/ppermute | solution.py:36
  227.3 3.1 collective-permute-start.53
  227.3 25.6 %collective-permute-start.44 = (bf16[4,96,640]{2,1,0:T(8,128)(2,1)}, bf16[4,96,640]{2,1,0:T(8,128)(2,1)S(1)}, u32[]{:S(2)}, u32[]{:S(2)}) collective-permute-start(bf16[4,96,640]{2,1,0:T(8,128)(2,1)} %get-tuple-element.173), channel_id=1, source_target_pairs={{0,4},{4,0},{1,5},{5,1},{2,6},{6,2},{3,7},{7,3},{8,12},{12,8},{9,1... | collective-permute-start | bytes 1474568 | tf_op jit(solution)/shard_map/ppermute | solution.py:36
  232.3 25.7 %collective-permute-start.54 = (bf16[384,768]{1,0:T(8,128)(2,1)}, bf16[384,768]{1,0:T(8,128)(2,1)}, u32[]{:S(2)}, u32[]{:S(2)}) collective-permute-start(bf16[384,768]{1,0:T(8,128)(2,1)} %fusion.5), channel_id=1, source_target_pairs={{0,2},{1,3},{2,0},{3,1},{4,6},{5,7},{6,4},{7,5},{8,10},{9,11},{10,... | collective-permute-start | bytes 1769480 | tf_op jit(solution)/shard_map/ppermute | solution.py:36
  233.0 15.4 %collective-permute-start.39 = (f32[8,768]{1,0:T(8,128)S(1)}, f32[8,768]{1,0:T(8,128)S(1)}, u32[]{:S(2)}, u32[]{:S(2)}) collective-permute-start(f32[8,768]{1,0:T(8,128)S(1)} %pad_maximum_fusion.3), channel_id=1, source_target_pairs={{0,2},{1,3},{2,0},{3,1},{4,6},{5,7},{6,4},{7,5},{8,10},{9,11},{10,... | collective-permute-start | bytes 73736 | tf_op jit(solution)/shard_map/ppermute | solution.py:36
  248.4 3.8 %collective-permute-start.40 = (f32[8,768]{1,0:T(8,128)S(1)}, f32[8,768]{1,0:T(8,128)S(1)}, u32[]{:S(2)}, u32[]{:S(2)}) collective-permute-start(f32[8,768]{1,0:T(8,128)S(1)} %add.55), channel_id=1, source_target_pairs={{0,4},{4,0},{1,5},{5,1},{2,6},{6,2},{3,7},{7,3},{8,12},{12,8},{9,1... | collective-permute-start | bytes 73736 | tf_op jit(solution)/shard_map/ppermute | solution.py:36
  257.4 31.3 %collective-permute-start.45 = (bf16[96,2432]{1,0:T(8,128)(2,1)}, bf16[96,2432]{1,0:T(8,128)(2,1)S(1)}, u32[]{:S(2)}, u32[]{:S(2)}) collective-permute-start(bf16[96,2432]{1,0:T(8,128)(2,1)} %get-tuple-element.175), channel_id=1, source_target_pairs={{0,8},{8,16},{16,24},{24,0},{1,9},{9,17},{17,25},{25,1},{2,10},{10... | collective-permute-start | bytes 1400840 | tf_op jit(solution)/shard_map/ppermute | solution.py:41
  257.4 31.3 %collective-permute-start.51 = (bf16[384,768]{1,0:T(8,128)(2,1)}, bf16[384,768]{1,0:T(8,128)(2,1)}, u32[]{:S(2)}, u32[]{:S(2)}) collective-permute-start(bf16[384,768]{1,0:T(8,128)(2,1)} %get-tuple-element.181.p_0), channel_id=1, source_target_pairs={{0,2},{1,3},{2,0},{3,1},{4,6},{5,7},{6,4},{7,5},{8,10},{9,11},{10,... | collective-permute-start | bytes 1769480 | tf_op jit(solution)/shard_map/ppermute | solution.py:36
  260.3 39.9 %collective-permute-start.56 = (bf16[384,768]{1,0:T(8,128)(2,1)}, bf16[384,768]{1,0:T(8,128)(2,1)S(1)}, u32[]{:S(2)}, u32[]{:S(2)}) collective-permute-start(bf16[384,768]{1,0:T(8,128)(2,1)} %fusion.2.p_0), channel_id=1, source_target_pairs={{0,2},{1,3},{2,0},{3,1},{4,6},{5,7},{6,4},{7,5},{8,10},{9,11},{10,... | collective-permute-start | bytes 1769480 | tf_op jit(solution)/shard_map/ppermute | solution.py:36
  261.7 10.0 %collective-permute-start.46 = (f32[8,768]{1,0:T(8,128)S(1)}, f32[8,768]{1,0:T(8,128)S(1)}, u32[]{:S(2)}, u32[]{:S(2)}) collective-permute-start(f32[8,768]{1,0:T(8,128)S(1)} %copy-done.9), channel_id=1, source_target_pairs={{0,8},{8,0},{16,24},{24,16},{1,9},{9,1},{17,25},{25,17},{2,10},{10... | collective-permute-start | bytes 73736 | tf_op jit(solution)/shard_map/ppermute | solution.py:36
  263.7 33.1 %collective-permute-start.47 = (bf16[96,2432]{1,0:T(8,128)(2,1)S(1)}, bf16[96,2432]{1,0:T(8,128)(2,1)S(1)}, u32[]{:S(2)}, u32[]{:S(2)}) collective-permute-start(bf16[96,2432]{1,0:T(8,128)(2,1)S(1)} %copy-done.37), channel_id=1, source_target_pairs={{0,16},{8,24},{16,0},{24,8},{1,17},{9,25},{17,1},{25,9},{2,18},{10... | collective-permute-start | bytes 1400840 | tf_op jit(solution)/shard_map/ppermute | solution.py:41
  271.7 28.5 %collective-permute-start.48 = (bf16[96,2432]{1,0:T(8,128)(2,1)S(1)}, bf16[96,2432]{1,0:T(8,128)(2,1)}, u32[]{:S(2)}, u32[]{:S(2)}) collective-permute-start(bf16[96,2432]{1,0:T(8,128)(2,1)S(1)} %copy-done.36), channel_id=1, source_target_pairs={{0,24},{8,0},{16,8},{24,16},{1,25},{9,1},{17,9},{25,17},{2,26},{10... | collective-permute-start | bytes 1400840 | tf_op jit(solution)/shard_map/ppermute | solution.py:41
  288.7 16.2 %collective-permute-start.50 = (bf16[384,768]{1,0:T(8,128)(2,1)}, bf16[384,768]{1,0:T(8,128)(2,1)S(1)}, u32[]{:S(2)}, u32[]{:S(2)}) collective-permute-start(bf16[384,768]{1,0:T(8,128)(2,1)} %get-tuple-element.181.p_0), channel_id=1, source_target_pairs={{0,1},{1,0},{2,3},{3,2},{4,5},{5,4},{6,7},{7,6},{8,9},{9,8},{10,11... | collective-permute-start | bytes 1769480 | tf_op jit(solution)/shard_map/ppermute | solution.py:36
  288.7 16.2 %collective-permute-start.52 = (bf16[384,768]{1,0:T(8,128)(2,1)}, bf16[384,768]{1,0:T(8,128)(2,1)S(1)}, u32[]{:S(2)}, u32[]{:S(2)}) collective-permute-start(bf16[384,768]{1,0:T(8,128)(2,1)} %collective-permute-done.51.p_2), channel_id=1, source_target_pairs={{0,1},{1,0},{2,3},{3,2},{4,5},{5,4},{6,7},{7,6},{8,9},{9,8},{10,11... | collective-permute-start | bytes 1769480 | tf_op jit(solution)/shard_map/ppermute | solution.py:36
  296.8 6.9 %collective-permute-start.58 = (f32[8,768]{1,0:T(8,128)S(1)}, f32[8,768]{1,0:T(8,128)S(1)}, u32[]{:S(2)}, u32[]{:S(2)}) collective-permute-start(f32[8,768]{1,0:T(8,128)S(1)} %add.57), channel_id=1, source_target_pairs={{0,16},{8,24},{16,0},{24,8},{1,17},{9,25},{17,1},{25,9},{2,18},{10... | collective-permute-start | bytes 73736 | tf_op jit(solution)/shard_map/ppermute | solution.py:36
  300.2 9.5 %collective-permute-start.55 = (bf16[384,768]{1,0:T(8,128)(2,1)}, bf16[384,768]{1,0:T(8,128)(2,1)S(1)}, u32[]{:S(2)}, u32[]{:S(2)}) collective-permute-start(bf16[384,768]{1,0:T(8,128)(2,1)} %fusion.2.p_0), channel_id=1, source_target_pairs={{0,1},{1,0},{2,3},{3,2},{4,5},{5,4},{6,7},{7,6},{8,9},{9,8},{10,11... | collective-permute-start | bytes 1769480 | tf_op jit(solution)/shard_map/ppermute | solution.py:36
  300.2 9.5 %collective-permute-start.57 = (bf16[384,768]{1,0:T(8,128)(2,1)S(1)}, bf16[384,768]{1,0:T(8,128)(2,1)S(1)}, u32[]{:S(2)}, u32[]{:S(2)}) collective-permute-start(bf16[384,768]{1,0:T(8,128)(2,1)S(1)} %collective-permute-done.56.p_2), channel_id=1, source_target_pairs={{0,1},{1,0},{2,3},{3,2},{4,5},{5,4},{6,7},{7,6},{8,9},{9,8},{10,11... | collective-permute-start | bytes 1769480 | tf_op jit(solution)/shard_map/ppermute | solution.py:36
  303.7 13.0 %collective-permute-start.49 = (bf16[96,2432]{1,0:T(8,128)(2,1)}, bf16[96,2432]{1,0:T(8,128)(2,1)S(1)}, u32[]{:S(2)}, u32[]{:S(2)}) collective-permute-start(bf16[96,2432]{1,0:T(8,128)(2,1)} %merge_three.1.refs_1_), channel_id=1, source_target_pairs={{0,4},{4,0},{1,5},{5,1},{2,6},{6,2},{3,7},{7,3},{8,12},{12,8},{9,1... | collective-permute-start | bytes 1400840 | tf_op jit(solution)/shard_map/ppermute | solution.py:36
  (53 other events, 536.5 us)
where the time goes:
time: 323 us; the launch traced here: 322 us
  Pallas kernels  122 us (38%)
  waiting for transfers between devices  116 us (36%)
  starting transfers between devices  51.7 us (16%)
  local copies, waits for them, and re-layouts  19.8 us (6%)
  other arithmetic  11.1 us (3%)
    ppermute x47, waiting for transfers between devices, swap(): return lax.ppermute(value, axis, [(i, i ^ bit) for i in range(count)])  71.4 us
    ppermute x11, waiting for transfers between devices, shift(): lax.ppermute(value, axis, [(i, (i + step) % count) for i in range(count)])  44.6 us
    ppermute x47, starting transfers between devices, swap(): return lax.ppermute(value, axis, [(i, i ^ bit) for i in range(count)])  34.4 us
    pallas_call x1, Pallas kernels, feed(): pl.pallas_call(lambda *refs: feed_kernel(*refs, plan=plan, count=len(piec...  25.4 us
    pallas_call x1, Pallas kernels, attend_back(): pl.pallas_call(lambda *refs: attend_back_kernel(*refs, block=block, width...  23.4 us
    pallas_call x1, Pallas kernels, attend_far(): pl.pallas_call(lambda *refs: attend_far_kernel(*refs, block=block, width=...  18 us
    ppermute x11, starting transfers between devices, shift(): lax.ppermute(value, axis, [(i, (i + step) % count) for i in range(count)])  15.7 us
    pallas_call x1, Pallas kernels, attend_near(): pl.pallas_call(lambda *refs: attend_near_kernel(*refs, block=block, width...  13.5 us
  transfers between devices with their start and end apart: 59, of which 22 were waited for; matrix products, arithmetic and copies ran while one was open for 5% of the time, Pallas kernels for 29%

commit v1 on v0

--- a/solution.py
+++ b/solution.py
@@ -139,12 +139,16 @@
     scale = 1.0 / math.sqrt(HEAD_DIM)
     mine, f, c = here[0], here[1], here[2]
     copies = []
-    for i, mark in enumerate(marks):
-        first, count = mark(f, c)
-        copies.append(
-            pltpu.make_async_copy(w_refs[i], w_ref.at[pl.ds(first, count)], sems.at[i])
-        )
-        copies[-1].start()
+    for i, spots in enumerate(marks):
+        offset = 0
+        for mark in spots:
+            first, count = mark(f, c)
+            src = w_refs[i].at[pl.ds(offset, count)]
+            copies.append(
+                pltpu.make_async_copy(src, w_ref.at[pl.ds(first, count)], sems.at[len(copies)])
+            )
+            copies[-1].start()
+            offset += count
     vt_ref[:, HEAD_DIM:, :] = jnp.ones((heads, vt_ref.shape[1] - HEAD_DIM, keys), low)
     for copy in copies:
         copy.wait()
@@ -239,7 +243,7 @@
         scratch_shapes=[
             pltpu.VMEM((heads, HEAD_DIM + 16, block), high),
             pltpu.VMEM((heads, 1, block), high),
-            pltpu.SemaphoreType.DMA((len(pieces),)),
+            pltpu.SemaphoreType.DMA((sum(map(len, marks)),)),
         ],
         cost_estimate=cost(FAR_COST, 8 << 20),
     )(here, seg_q, seg_k, x, halo, bias, mask_q, mask_k, *pieces)
@@ -307,8 +311,19 @@
             begin(w_refs[i].at[pl.ds(offset, 8)], b_ref.at[r])
         else:
             start, size = mark(f, c)
-            begin(w_refs[i].at[pl.ds(offset, size)], w_ref.at[r, pl.ds(start, size)])
-    for copy in copies:
+            begin(
+                w_refs[i].at[pl.ds(offset, size), pl.ds(2 * hidden, local)],
+                w_ref.at[r, pl.ds(start, size), pl.ds(2 * hidden, local)],
+            )
+    first_copies = len(copies)
+    for i, offset, r, mark in plan:
+        if mark is not None:
+            start, size = mark(f, c)
+            begin(
+                w_refs[i].at[pl.ds(offset, size), pl.ds(0, 2 * hidden)],
+                w_ref.at[r, pl.ds(start, size), pl.ds(0, 2 * hidden)],
+            )
+    for copy in copies[:first_copies]:
         copy.wait()
     b_out, gain_one, shift_one, b_outer, gain_two, shift_two = (
         vec_ref[i : i + 1, :].astype(high) for i in range(6)
@@ -334,6 +349,8 @@
         return carry
 
     lax.fori_loop(0, chunks, first_norm, 0)
+    for copy in copies[first_copies:]:
+        copy.wait()
     part = 256
     for k, side in enumerate((keep_ref, send_ref)):
         for x in range(2):
@@ -412,7 +429,7 @@
     width = x.shape[1]
     wide = 2 * hidden + local
     padded = (wide + 127) // 128 * 128
-    copies = 6 + len(plan)
+    copies = 6 + len(plan) + sum(mark is not None for _, _, _, mark in plan)
     return pl.pallas_call(
         lambda *refs: feed_kernel(*refs, plan=plan, count=len(pieces), hidden=hidden, local=local),
         name="feed",
@@ -867,11 +884,16 @@
     seg_own = segments.reshape(rows)
     if quick:
         halves_a = bundle_a.reshape(2, half, -1)
-        pieces_a = [halves_a] + [shift(halves_a, "fsdp", s) for s in range(1, n_f)]
-        marks_a = [spot_from(s) for s in range(n_f)]
+        own_a = lax.dynamic_index_in_dim(halves_a, c, 0)
+        gots_a = [shift(own_a, "fsdp", s) for s in range(1, n_f)]
+        joined = jnp.concatenate(gots_a, axis=0)
+        mates_a = swap(joined, "ctx", 1)
+        pieces_a = [halves_a, joined, mates_a]
+        marks_a = [[spot_from(0)]]
+        marks_a += [[spot(s, side) for s in range(1, n_f)] for side in range(2)]
     else:
         whole_a = lax.all_gather(bundle_a, "fsdp", axis=0, tiled=True)
-        pieces_a, marks_a = [whole_a.reshape(blocks + (-1,))], [spot_all]
+        pieces_a, marks_a = [whole_a.reshape(blocks + (-1,))], [[spot_all]]
 
     if n_c == 2:
         sent = halo_of(inputs, c, rim)
@@ -911,7 +933,7 @@
     if quick:
         far_rows = swap(own_rows, "tp", 2)
         own_f = take(bundle_f, c * half, half)
-        (own_1,) = after([own_f], (pieces_a[1], pieces_a[3]))
+        (own_1,) = after([own_f], joined)
         gots = {s: shift(own_1, "fsdp", s) for s in (1, 3)}
         halo_in, far_rows = lax.optimization_barrier((halo_in, far_rows))
         far_f = take(far_rows, (1 - c) * half, half)
@@ -931,6 +953,8 @@
     if quick:
         (own_2,) = after([own_f], att_2)
         gots[2] = shift(own_2, "fsdp", 2)
+        (far_2,) = after([far_f], att_2)
+        corners[2] = shift(far_2, "fsdp", 2)
         *near, corners[1], corners[3] = after([gots[1], gots[3], corners[1], corners[3]], att_2)
         (q_near,) = after([q_near], (*near, corners[1], corners[3]))
     att_0, att_1, full_near, q_near = attend_near(here, seg_own, seg_all, q_near, keys_wide, values_t)
@@ -953,12 +977,14 @@
         piece_rows = piece
         add(0, own_rows, [spot_from(0)], att_0, bias=True)
         add(2, far_rows, [spot_from(0)], att_0, bias=True)
-        for s, got in zip((1, 3), near):
-            add(0, got, [spot(s, 0)], att_0)
+        near = jnp.concatenate(near, axis=0)
+        add(0, near, [spot(1, 0), spot(3, 0)], att_0)
+        for s in (1, 3):
             add(2, corners[s], [spot(s, 1)], att_0)
-        near = jnp.concatenate(near, axis=0)
         near_x, near_y = swap(near, "tp", 2), swap(near, "ctx", 1)
-        last, near_x, near_y, *att = lax.optimization_barrier((gots[2], near_x, near_y, att_0, att_1, att_2, att_3))
+        last, corner, near_x, near_y, *att = lax.optimization_barrier(
+            (gots[2], corners[2], near_x, near_y, att_0, att_1, att_2, att_3)
+        )
         att_0, att_1, att_2, att_3 = att
         att = [att_0, swap(att_1, "tp", 1), swap(att_2, "tp", 2), swap(att_3, "tp", 3)]
         add(2, near_x, [spot(1, 0), spot(3, 0)])
@@ -966,7 +992,6 @@
         add(0, last, [spot(2, 0)])
         add(2, swap(last, "tp", 2), [spot(2, 0)])
         add(0, swap(last, "ctx", 1), [spot(2, 1)])
-        corner = lax.ppermute(last, ("ctx", "tp"), [(i, i ^ (n_t + 2)) for i in range(n_c * n_t)])
         add(2, corner, [spot(2, 1)])
     else:
         gathered = lax.all_gather(bundle_f, "fsdp", axis=0, tiled=True)
@@ -994,6 +1019,8 @@
         keep_a, send_a, keep_b, send_b = unit_grads(here, rows_t, mate_rows, keep, mate, half, hidden, local)
         got_a = swap(send_a, "tp", 2)
         got_b = swap(send_b, "ctx", 1)
+        (away,) = after([away], keep_a)
+        away = swap(away, "tp", 1)
         *g_att, keep_a, keep_b = lax.optimization_barrier((*g_att, keep_a, keep_b))
     else:
         ordered = []
@@ -1020,29 +1047,31 @@
     )
     if quick:
         got_a, got_b = after([got_a, got_b], g_own)
-        (rim_out,) = after([g_rim], (got_a, got_b))
         (away,) = after([away], g_own)
-        pair = near_sums + swap(away, "tp", 1)
+        pair = near_sums + away
+        (rim_out,) = after([g_rim], (got_a, got_b, pair))
+        away = jnp.concatenate([pair[:6], pair[7:8], pair[7:8]], axis=0)
+        away = swap(away, "tp", 2)
         edge = swap(rim_out, "ctx", 1)
         keep_a, send_a, keep_b, send_b = merge_one(here, keep_a, got_a, keep_b, got_b)
         got_a = swap(send_a, "ctx", 1)
         got_b = swap(send_b, "tp", 2)
-        (edge,) = after([edge], (send_a, send_b, pair))
-        away = jnp.concatenate([pair[:6], pair[7:8], pair[7:8]], axis=0)
-        pair = pair + swap(away, "tp", 2)
+        edge, away = after([edge, away], (send_a, send_b))
+        pair = pair + away
+        pair = pair + swap(pair, "ctx", 1)
         dx_keep, dx_send, d_keep, d_send = project_back(here, g_own, edge, inputs, w_qkv, tokens, half)
-        (dx_send,) = after([dx_send], (got_a, got_b))
+        (dx_send,) = after([dx_send], (got_a, got_b, pair))
+        pair = pair + swap(pair, "fsdp", 1)
         dx_got = swap(dx_send, "tp", 1)
         d_got = swap(d_send, "ctx", 1)
         near_dx = dx_keep[0] + dx_got[0]
         far_dx = dx_keep[1] + dx_got[1]
         far_got = swap(far_dx, "tp", 2)
         start = (2 * hidden + local + 127) // 128 * 128
-        pair = pair + swap(pair, "ctx", 1)
         keep_a, pair = lax.optimization_barrier((keep_a, pair))
         outs = merge_two(here, keep_a, got_a, keep_b, got_b, d_keep, d_got, start)
         (output,) = after([output], outs[0])
-        pair = pair + swap(pair, "fsdp", 1)
+        pair = pair + swap(pair, "fsdp", 2)
         totals = [outs[0]] + [shift(outs[s], "fsdp", s) for s in range(1, n_f)]
         mine = (near_dx.astype(high) + far_got.astype(high) + g_one).astype(low)
 
@@ -1054,7 +1083,6 @@
         grad_inputs = everyone(mine, high)
         totals[1], pair = lax.optimization_barrier((totals[1], pair))
         total = merge_three(here, totals)
-        pair = pair + swap(pair, "fsdp", 2)
         got = swap(total, "ctx", 1)
         got, output, grad_inputs = lax.optimization_barrier((got, output, grad_inputs))
         s_inner, s_outer, s_out, s_query, s_key, s_value, s_bias = finish(

time: 323 us -> 305 us (0.944); the launches traced: 322 us -> 300 us
  waiting for transfers between devices: 116 us -> 79.7 us
  starting transfers between devices: 51.7 us -> 67.9 us
    ppermute x11 -> x12, waiting for transfers between devices: 44.6 us -> 26.3 us  [shift(): lax.ppermute(value, axis, [(i, (i + step) % count) for i in range(count)])]
    ppermute x47, waiting for transfers between devices: 71.4 us -> 53.5 us  [swap(): return lax.ppermute(value, axis, [(i, i ^ bit) for i in range(count)])]
    ppermute x11 -> x12, starting transfers between devices: 15.7 us -> 25.7 us  [shift(): lax.ppermute(value, axis, [(i, (i + step) % count) for i in range(count)])]
    ppermute x47, starting transfers between devices: 34.4 us -> 42.2 us  [swap(): return lax.ppermute(value, axis, [(i, i ^ bit) for i in range(count)])]
  transfers between devices with their start and end apart: 59 -> 59, of which waited for: 22 -> 22; matrix products, arithmetic and copies ran while one was open for 5% -> 5% of each run, Pallas kernels for 29% -> 31%
where the time goes in v1:
time: 305 us; the launch traced here: 300 us
  Pallas kernels  120 us (39%)
  waiting for transfers between devices  79.7 us (26%)
  starting transfers between devices  67.9 us (22%)
  local copies, waits for them, and re-layouts  19.9 us (7%)
  other arithmetic  11.1 us (4%)
    ppermute x47, waiting for transfers between devices, swap(): return lax.ppermute(value, axis, [(i, i ^ bit) for i in range(count)])  53.5 us
    ppermute x47, starting transfers between devices, swap(): return lax.ppermute(value, axis, [(i, i ^ bit) for i in range(count)])  42.2 us
    ppermute x12, waiting for transfers between devices, shift(): lax.ppermute(value, axis, [(i, (i + step) % count) for i in range(count)])  26.3 us
    ppermute x12, starting transfers between devices, shift(): lax.ppermute(value, axis, [(i, (i + step) % count) for i in range(count)])  25.7 us
    pallas_call x1, Pallas kernels, feed(): pl.pallas_call(lambda *refs: feed_kernel(*refs, plan=plan, count=len(piec...  23.6 us
    pallas_call x1, Pallas kernels, attend_back(): pl.pallas_call(lambda *refs: attend_back_kernel(*refs, block=block, width...  23.4 us
    pallas_call x1, Pallas kernels, attend_far(): pl.pallas_call(lambda *refs: attend_far_kernel(*refs, block=block, width=...  18.1 us
    pallas_call x1, Pallas kernels, attend_near(): pl.pallas_call(lambda *refs: attend_near_kernel(*refs, block=block, width...  13.5 us
  transfers between devices with their start and end apart: 59, of which 22 were waited for; matrix products, arithmetic and copies ran while one was open for 5% of the time, Pallas kernels for 31%

profile of v1, /device:TPU:10, one launch (start us, length us, event | category | flops | bytes accessed | tf_op | source)
XLA Modules:
  0.0 300.4 jit_solution(4096354543266706292)
XLA Ops:
  0.7 1.2 pad_maximum_fusion.1
  2.4 2.6 collective-permute-start.4
  5.0 2.5 collective-permute-start.3
  8.2 1.1 constant_dynamic-slice_fusion.2
  9.4 1.6 collective-permute-start
  13.2 2.0 collective-permute-done.3
  15.3 1.4 collective-permute-start.10
  16.7 1.2 collective-permute-start.9
  17.9 1.5 collective-permute-start.6
  20.5 1.1 or_convert_fusion
  23.6 4.4 %collective-permute-done.2.refs_10_ = bf16[200,1728]{1,0:T(8,128)(2,1)} collective-permute-done((bf16[200,1728]{1,0:T(8,128)(2,1)S(1)}, bf16[200,1728]{1,0:T(8,128)(2,1)}, u32[]{:S(2)}, u32[]{:S(2)}) %collective-permute-start.2) | collective-permute-done | bytes 691232 | tf_op jit(solution)/shard_map/ppermute | solution.py:36
  29.1 2.0 collective-permute-start.11
  31.8 18.1 %attend_far.1 = (bf16[384,192]{1,0:T(8,128)(2,1)}, bf16[384,192]{1,0:T(8,128)(2,1)}, f32[2,384,192]{2,1,0:T(8,128)}, bf16[3,2,384,128]{3,2,1,0:T(8,128)(2,1)}, b...) custom-call(s32[3]{0:T(128)} %pad_add_fusion.1.refs_0_.here, ...), custom_call_target="tpu_custom_call" | custom-call | flops 20000000000 | bytes 8388608 | tf_op jit(solution)/shard_map/attend_far/pallas_call | solution.py:227
  49.9 4.1 %collective-permute-start.7 = (bf16[96,1728]{1,0:T(8,128)(2,1)S(1)}, bf16[96,1728]{1,0:T(8,128)(2,1)}, u32[]{:S(2)}, u32[]{:S(2)}) collective-permute-start(bf16[96,1728]{1,0:T(8,128)(2,1)S(1)} %fusion.9), channel_id=1, source_target_pairs={{0,16},{8,24},{16,0},{24,8},{1,17},{9,25},{17,1},{25,9},{2,18},{10... | collective-permute-start | bytes 995336 | tf_op jit(solution)/shard_map/ppermute | solution.py:41
  55.0 2.6 collective-permute-start.14
  57.7 13.5 %attend_near.1 = (bf16[384,192]{1,0:T(8,128)(2,1)}, bf16[384,192]{1,0:T(8,128)(2,1)}, f32[2,384,192]{2,1,0:T(8,128)}, bf16[3,2,384,128]{3,2,1,0:T(8,128)(2,1)}) custom-call(s32[3]{0:T(128)} %pad_add_fusion.1.refs_0_.here, s32[1536]{0:T(1024)} %copy-done.11, s32[2048]{0:T(1024)} %copy-done.10, bf16[3,2,384,128]{3,2,1,0:T(8,128)(2,1)} %get-tuple-element.121.refs_3_, ...), custom_call_target="tpu_custom_call" | custom-call | flops 12000000000 | bytes 8388608 | tf_op jit(solution)/shard_map/attend_near/pallas_call | solution.py:255
  71.7 6.1 %collective-permute-done.8.refs_28_ = bf16[96,1728]{1,0:T(8,128)(2,1)} collective-permute-done((bf16[96,1728]{1,0:T(8,128)(2,1)S(1)}, bf16[96,1728]{1,0:T(8,128)(2,1)}, u32[]{:S(2)}, u32[]{:S(2)}) %collective-permute-start.8) | collective-permute-done | bytes 331808 | tf_op jit(solution)/shard_map/ppermute | solution.py:41
  78.4 2.3 collective-permute-done.21.refs_15_
  81.2 3.2 %collective-permute-start.16 = (bf16[384,192]{1,0:T(8,128)(2,1)}, bf16[384,192]{1,0:T(8,128)(2,1)S(1)}, u32[]{:S(2)}, u32[]{:S(2)}) collective-permute-start(bf16[384,192]{1,0:T(8,128)(2,1)} %get-tuple-element.129), channel_id=1, source_target_pairs={{0,2},{1,3},{2,0},{3,1},{4,6},{5,7},{6,4},{7,5},{8,10},{9,11},{10,... | collective-permute-start | bytes 442376 | tf_op jit(solution)/shard_map/ppermute | solution.py:36
  84.5 3.0 %collective-permute-start.28 = (bf16[96,1728]{1,0:T(8,128)(2,1)}, bf16[96,1728]{1,0:T(8,128)(2,1)S(1)}, u32[]{:S(2)}, u32[]{:S(2)}) collective-permute-start(bf16[96,1728]{1,0:T(8,128)(2,1)} %collective-permute-done.7.refs_22_), channel_id=1, source_target_pairs={{0,4},{4,0},{1,5},{5,1},{2,6},{6,2},{3,7},{7,3},{8,12},{12,8},{9,1... | collective-permute-start | bytes 995336 | tf_op jit(solution)/shard_map/ppermute | solution.py:36
  87.6 2.6 collective-permute-done.16.refs_5_
  90.3 3.9 %collective-permute-done.17.refs_6_ = bf16[384,192]{1,0:T(8,128)(2,1)} collective-permute-done((bf16[384,192]{1,0:T(8,128)(2,1)}, bf16[384,192]{1,0:T(8,128)(2,1)}, u32[]{:S(2)}, u32[]{:S(2)}) %collective-permute-start.17) | collective-permute-done | bytes 147488 | tf_op jit(solution)/shard_map/ppermute | solution.py:36
  94.7 1.4 collective-permute-done.28.refs_26_
  96.1 5.3 %collective-permute-done.26.refs_24_ = bf16[96,1728]{1,0:T(8,128)(2,1)} collective-permute-done((bf16[96,1728]{1,0:T(8,128)(2,1)}, bf16[96,1728]{1,0:T(8,128)(2,1)}, u32[]{:S(2)}, u32[]{:S(2)}) %collective-permute-start.26) | collective-permute-done | bytes 331808 | tf_op jit(solution)/shard_map/ppermute | solution.py:36
  102.3 1.2 collective-permute-done.27.refs_25_
  105.2 23.6 %feed.1 = (bf16[384,768]{1,0:T(8,128)(2,1)}, f32[384,768]{1,0:T(8,128)}, f32[12,1,768]{2,1,0:T(1,128)}, bf16[384,192]{1,0:T(8,128)(2,1)}, bf16[384,192]{1,0:T(8,...) custom-call(s32[3]{0:T(128)} %pad_add_fusion.1.refs_0_.here, ...), custom_call_target="tpu_custom_call" | custom-call | flops 25999998976 | bytes 25165824 | tf_op jit(solution)/shard_map/feed/pallas_call | solution.py:433
  130.4 1.7 collective-permute-start.32
  132.8 3.9 %collective-permute-done.34.refs_2_ = bf16[3,768,384]{2,1,0:T(8,128)(2,1)S(1)} collective-permute-done((bf16[3,768,384]{2,1,0:T(8,128)(2,1)}, bf16[3,768,384]{2,1,0:T(8,128)(2,1)S(1)}, u32[]{:S(2)}, u32[]{:S(2)}) %collective-permute-start.34) | collective-permute-done | bytes 1769504 | tf_op jit(solution)/shard_map/ppermute | solution.py:36
  136.8 1.2 copy-done.21
  138.0 1.5 copy-done.20
  139.5 12.2 %unit_grads.1 = (bf16[4,96,1728]{2,1,0:T(8,128)(2,1)}, bf16[4,96,1728]{2,1,0:T(8,128)(2,1)}, bf16[2,2,96,1728]{3,2,1,0:T(8,128)(2,1)}, bf16[2,2,96,1728]{3,2,1,0:T(8,128)(2,1)}) custom-call(s32[3]{0:T(128)} %pad_add_fusion.1.refs_0_.here, bf16[3,768,384]{2,1,0:T(8,128)(2,1)} %get-tuple-element.144.refs_1_, bf16[3,768,384]{2,1,0:T(8,128)(2,1)} %copy-done.21, ...), custom_call_target="tpu_custom_call" | custom-call | flops 12000000000 | bytes 14680064 | tf_op jit(solution)/shard_map/unit_grads/pallas_call | solution.py:518
  152.0 1.7 collective-permute-start.36
  153.8 1.4 collective-permute-start.37
  155.2 23.4 %attend_back.1 = (bf16[1536,576]{1,0:T(8,128)(2,1)}, bf16[512,384]{1,0:T(8,128)(2,1)}) custom-call(s32[3]{0:T(128)} %pad_add_fusion.1.refs_0_.here, s32[1536]{0:T(1024)} %copy-done.11, s32[2048]{0:T(1024)} %copy-done.10, bf16[384,192]{1,0:T(8,128)(2,1)} %get-tuple-element.152.refs_3_, bf16[384,192]{1,0:T(8,128)(2,1)} %copy-done.52, ...), custom_call_target="tpu_custom_call" | custom-call | flops 24000000000 | bytes 8388608 | tf_op jit(solution)/shard_map/attend_back/pallas_call | solution.py:814
  178.6 6.1 %collective-permute-done.36.ga = bf16[4,96,1728]{2,1,0:T(8,128)(2,1)S(1)} collective-permute-done((bf16[4,96,1728]{2,1,0:T(8,128)(2,1)}, bf16[4,96,1728]{2,1,0:T(8,128)(2,1)S(1)}, u32[]{:S(2)}, u32[]{:S(2)}) %collective-permute-start.36) | collective-permute-done | bytes 1327136 | tf_op jit(solution)/shard_map/ppermute | solution.py:36
  184.7 1.5 collective-permute-done.37.gb
  186.2 1.4 collective-permute-start.39
  187.6 1.7 collective-permute-start.40
  189.4 4.4 %merge_one.1 = (bf16[2,96,1728]{2,1,0:T(8,128)(2,1)}, bf16[2,96,1728]{2,1,0:T(8,128)(2,1)}, bf16[2,96,1728]{2,1,0:T(8,128)(2,1)}, bf16[2,96,1728]{2,1,0:T(8,128)(2,1)}) custom-call(s32[3]{0:T(128)} %pad_add_fusion.1.refs_0_.here, bf16[4,96,1728]{2,1,0:T(8,128)(2,1)} %get-tuple-element.149.ak, bf16[4,96,1728]{2,1,0:T(8,128)(2,1)} %copy-done.22, ...), custom_call_target="tpu_custom_call" | custom-call | flops 3000000000 | bytes 8388608 | tf_op jit(solution)/shard_map/merge_one/pallas_call | solution.py:559
  194.8 3.3 %collective-permute-done.39.refs_2_ = bf16[512,384]{1,0:T(8,128)(2,1)S(1)} collective-permute-done((bf16[512,384]{1,0:T(8,128)(2,1)}, bf16[512,384]{1,0:T(8,128)(2,1)S(1)}, u32[]{:S(2)}, u32[]{:S(2)}) %collective-permute-start.39) | collective-permute-done | bytes 393248 | tf_op jit(solution)/shard_map/ppermute | solution.py:36
  198.1 1.8 collective-permute-start.41
  199.9 8.7 %project_back.1 = (bf16[2,384,768]{2,1,0:T(8,128)(2,1)}, bf16[2,384,768]{2,1,0:T(8,128)(2,1)}, bf16[4,96,640]{2,1,0:T(8,128)(2,1)}, bf16[4,96,640]{2,1,0:T(8,128)(2,1)}) custom-call(s32[3]{0:T(128)} %pad_add_fusion.1.refs_0_.here, bf16[1536,576]{1,0:T(8,128)(2,1)} %get-tuple-element.161.refs_1_, bf16[512,384]{1,0:T(8,128)(2,1)} %copy-done.42, ...), custom_call_target="tpu_custom_call" | custom-call | flops 8999999488 | bytes 8388608 | tf_op jit(solution)/shard_map/project_back/pallas_call | solution.py:723
  208.5 3.4 %collective-permute-done.41 = f32[8,768]{1,0:T(8,128)S(1)} collective-permute-done((f32[8,768]{1,0:T(8,128)S(1)}, f32[8,768]{1,0:T(8,128)S(1)}, u32[]{:S(2)}, u32[]{:S(2)}) %collective-permute-start.41) | collective-permute-done | bytes 24608 | tf_op jit(solution)/shard_map/ppermute | solution.py:36
  213.6 1.7 collective-permute-start.45
  215.3 1.4 collective-permute-done.54
  216.7 1.9 fusion.5
  218.6 1.6 collective-permute-start.55
  220.3 3.2 %collective-permute-start.42 = (f32[8,768]{1,0:T(8,128)S(1)}, f32[8,768]{1,0:T(8,128)S(1)}, u32[]{:S(2)}, u32[]{:S(2)}) collective-permute-start(f32[8,768]{1,0:T(8,128)S(1)} %add.61), channel_id=1, source_target_pairs={{0,8},{8,0},{16,24},{24,16},{1,9},{9,1},{17,25},{25,17},{2,10},{10... | collective-permute-start | bytes 73736 | tf_op jit(solution)/shard_map/ppermute | solution.py:36
  223.4 1.8 collective-permute-done.42
  225.8 1.6 collective-permute-done.45.refs_6_
  228.3 3.6 %merge_two.1 = (bf16[96,2432]{1,0:T(8,128)(2,1)}, bf16[96,2432]{1,0:T(8,128)(2,1)}, bf16[96,2432]{1,0:T(8,128)(2,1)}, bf16[96,2432]{1,0:T(8,128)(2,1)}) custom-call(s32[3]{0:T(128)} %pad_add_fusion.1.refs_0_.here, bf16[2,96,1728]{2,1,0:T(8,128)(2,1)} %get-tuple-element.174.refs_1_, bf16[2,96,1728]{2,1,0:T(8,128)(2,1)} %copy-done.29, ...), custom_call_target="tpu_custom_call" | custom-call | flops 3000000000 | bytes 8388608 | tf_op jit(solution)/shard_map/merge_two/pallas_call | solution.py:584
  233.1 1.7 collective-permute-start.52
  234.8 2.2 fusion.2.p_0
  237.0 1.2 collective-permute-start.57
  238.2 3.5 %collective-permute-start.47 = (f32[8,768]{1,0:T(8,128)S(1)}, f32[8,768]{1,0:T(8,128)S(1)}, u32[]{:S(2)}, u32[]{:S(2)}) collective-permute-start(f32[8,768]{1,0:T(8,128)S(1)} %copy-done.8), channel_id=1, source_target_pairs={{0,16},{8,24},{16,0},{24,8},{1,17},{9,25},{17,1},{25,9},{2,18},{10... | collective-permute-start | bytes 73736 | tf_op jit(solution)/shard_map/ppermute | solution.py:36
  241.8 8.0 %collective-permute-done.47 = f32[8,768]{1,0:T(8,128)S(1)} collective-permute-done((f32[8,768]{1,0:T(8,128)S(1)}, f32[8,768]{1,0:T(8,128)S(1)}, u32[]{:S(2)}, u32[]{:S(2)}) %collective-permute-start.47) | collective-permute-done | bytes 24608 | tf_op jit(solution)/shard_map/ppermute | solution.py:36
  249.8 10.1 %collective-permute-start.49 = (bf16[96,2432]{1,0:T(8,128)(2,1)S(1)}, bf16[96,2432]{1,0:T(8,128)(2,1)}, u32[]{:S(2)}, u32[]{:S(2)}) collective-permute-start(bf16[96,2432]{1,0:T(8,128)(2,1)S(1)} %copy-done.37), channel_id=1, source_target_pairs={{0,24},{8,0},{16,8},{24,16},{1,25},{9,1},{17,9},{25,17},{2,26},{10... | collective-permute-start | bytes 1400840 | tf_op jit(solution)/shard_map/ppermute | solution.py:41
  260.5 13.7 %collective-permute-done.48.got_2 = bf16[96,2432]{1,0:T(8,128)(2,1)S(1)} collective-permute-done((bf16[96,2432]{1,0:T(8,128)(2,1)S(1)}, bf16[96,2432]{1,0:T(8,128)(2,1)S(1)}, u32[]{:S(2)}, u32[]{:S(2)}) %collective-permute-start.48) | collective-permute-done | bytes 466976 | tf_op jit(solution)/shard_map/ppermute | solution.py:41
  274.8 4.4 %collective-permute-done.49.got_3 = bf16[96,2432]{1,0:T(8,128)(2,1)} collective-permute-done((bf16[96,2432]{1,0:T(8,128)(2,1)S(1)}, bf16[96,2432]{1,0:T(8,128)(2,1)}, u32[]{:S(2)}, u32[]{:S(2)}) %collective-permute-start.49) | collective-permute-done | bytes 466976 | tf_op jit(solution)/shard_map/ppermute | solution.py:41
  279.2 2.9 merge_three.1.refs_1_
  282.1 1.7 collective-permute-start.50
  286.1 3.2 %spread.2 = bf16[1536,768]{1,0:T(8,128)(2,1)} custom-call(s32[3]{0:T(128)} %pad_add_fusion.1.refs_0_.here, bf16[384,768]{1,0:T(8,128)(2,1)} %get-tuple-element.187.p_0, bf16[384,768]{1,0:T(8,128)(2,1)} %copy-done.32, bf16[384,768]{1,0:T(8,128)(2,1)} %collective-permute-done.52.p_2, bf16[384,768]{1,0:T(8,128)(2,1)} %copy-done.33), custom_call_target="tpu_custom_call" | custom-call | flops 3000000000 | bytes 8388608 | tf_op jit(solution)/shard_map/spread/pallas_call | solution.py:669
  290.9 4.1 %spread.3 = f32[1536,768]{1,0:T(8,128)} custom-call(s32[3]{0:T(128)} %pad_add_fusion.1.refs_0_.here, bf16[384,768]{1,0:T(8,128)(2,1)} %fusion.2.p_0, bf16[384,768]{1,0:T(8,128)(2,1)} %copy-done.34, bf16[384,768]{1,0:T(8,128)(2,1)} %copy-done.31, bf16[384,768]{1,0:T(8,128)(2,1)} %copy-done.35), custom_call_target="tpu_custom_call" | custom-call | flops 3000000000 | bytes 8388608 | tf_op jit(solution)/shard_map/spread/pallas_call | solution.py:669
  295.8 2.6 finish.1
  (236 shorter events, 29.7 us)
Async XLA Ops:
  1.9 13.3 %collective-permute-start.5 = (bf16[1,96,576]{2,1,0:T(8,128)(2,1)S(1)}, bf16[1,96,576]{2,1,0:T(8,128)(2,1)S(1)}, u32[]{:S(2)}, u32[]{:S(2)}) collective-permute-start(bf16[1,96,576]{2,1,0:T(8,128)(2,1)S(1)} %constant_dynamic-slice_fusion.1), channel_id=1, source_target_pairs={{0,24},{8,0},{16,8},{24,16},{1,25},{9,1},{17,9},{25,17},{2,26},{10... | collective-permute-start | bytes 331784 | tf_op jit(solution)/shard_map/ppermute | solution.py:41
  2.4 12.8 %collective-permute-start.4 = (bf16[1,96,576]{2,1,0:T(8,128)(2,1)S(1)}, bf16[1,96,576]{2,1,0:T(8,128)(2,1)S(1)}, u32[]{:S(2)}, u32[]{:S(2)}) collective-permute-start(bf16[1,96,576]{2,1,0:T(8,128)(2,1)S(1)} %constant_dynamic-slice_fusion.1), channel_id=1, source_target_pairs={{0,16},{8,24},{16,0},{24,8},{1,17},{9,25},{17,1},{25,9},{2,18},{10... | collective-permute-start | bytes 331784 | tf_op jit(solution)/shard_map/ppermute | solution.py:41
  5.0 10.2 %collective-permute-start.3 = (bf16[1,96,576]{2,1,0:T(8,128)(2,1)S(1)}, bf16[1,96,576]{2,1,0:T(8,128)(2,1)S(1)}, u32[]{:S(2)}, u32[]{:S(2)}) collective-permute-start(bf16[1,96,576]{2,1,0:T(8,128)(2,1)S(1)} %constant_dynamic-slice_fusion.1), channel_id=1, source_target_pairs={{0,8},{8,16},{16,24},{24,0},{1,9},{9,17},{17,25},{25,1},{2,10},{10... | collective-permute-start | bytes 331784 | tf_op jit(solution)/shard_map/ppermute | solution.py:41
  9.4 11.0 %collective-permute-start = (bf16[272,768]{1,0:T(8,128)(2,1)S(1)}, bf16[272,768]{1,0:T(8,128)(2,1)S(1)}, u32[]{:S(2)}, u32[]{:S(2)}) collective-permute-start(bf16[272,768]{1,0:T(8,128)(2,1)S(1)} %fusion.7), channel_id=1, source_target_pairs={{0,4},{4,0},{1,5},{5,1},{2,6},{6,2},{3,7},{7,3},{8,12},{12,8},{9,1... | collective-permute-start | bytes 1253384 | tf_op jit(solution)/shard_map/ppermute | solution.py:36
  11.2 60.0 %copy-start.4 = (bf16[200,1728]{1,0:T(8,128)(2,1)}, bf16[200,1728]{1,0:T(8,128)(2,1)S(1)}, u32[]{:S(2)}) copy-start(bf16[200,1728]{1,0:T(8,128)(2,1)S(1)} %fusion.4.refs_8_) | copy-start | bytes 2073604
  11.2 16.8 %collective-permute-start.2 = (bf16[200,1728]{1,0:T(8,128)(2,1)S(1)}, bf16[200,1728]{1,0:T(8,128)(2,1)}, u32[]{:S(2)}, u32[]{:S(2)}) collective-permute-start(bf16[200,1728]{1,0:T(8,128)(2,1)S(1)} %fusion.4.refs_8_), channel_id=1, source_target_pairs={{0,2},{1,3},{2,0},{3,1},{4,6},{5,7},{6,4},{7,5},{8,10},{9,11},{10,... | collective-permute-start | bytes 2073608 | tf_op jit(solution)/shard_map/ppermute | solution.py:36
  15.3 38.7 %collective-permute-start.10 = (bf16[96,1728]{1,0:T(8,128)(2,1)S(1)}, bf16[96,1728]{1,0:T(8,128)(2,1)S(1)}, u32[]{:S(2)}, u32[]{:S(2)}) collective-permute-start(bf16[96,1728]{1,0:T(8,128)(2,1)S(1)} %fusion.9), channel_id=1, source_target_pairs={{0,24},{8,0},{16,8},{24,16},{1,25},{9,1},{17,9},{25,17},{2,26},{10... | collective-permute-start | bytes 995336 | tf_op jit(solution)/shard_map/ppermute | solution.py:41
  16.7 37.4 %collective-permute-start.9 = (bf16[96,1728]{1,0:T(8,128)(2,1)S(1)}, bf16[96,1728]{1,0:T(8,128)(2,1)S(1)}, u32[]{:S(2)}, u32[]{:S(2)}) collective-permute-start(bf16[96,1728]{1,0:T(8,128)(2,1)S(1)} %fusion.9), channel_id=1, source_target_pairs={{0,8},{8,16},{16,24},{24,0},{1,9},{9,17},{17,25},{25,1},{2,10},{10... | collective-permute-start | bytes 995336 | tf_op jit(solution)/shard_map/ppermute | solution.py:41
  17.9 13.2 %collective-permute-start.6 = (bf16[3,96,576]{2,1,0:T(8,128)(2,1)S(1)}, bf16[3,96,576]{2,1,0:T(8,128)(2,1)S(1)}, u32[]{:S(2)}, u32[]{:S(2)}) collective-permute-start(bf16[3,96,576]{2,1,0:T(8,128)(2,1)S(1)} %constant_dynamic-update-slice_fusion.refs_9_), channel_id=1, source_target_pairs={{0,4},{4,0},{1,5},{5,1},{2,6},{6,2},{3,7},{7,3},{8,12},{12,8},{9,1... | collective-permute-start | bytes 995336 | tf_op jit(solution)/shard_map/ppermute | solution.py:36
  20.4 2.1 collective-permute-start.1
  29.0 25.1 %collective-permute-start.12 = (bf16[96,1728]{1,0:T(8,128)(2,1)S(1)}, bf16[96,1728]{1,0:T(8,128)(2,1)S(1)}, u32[]{:S(2)}, u32[]{:S(2)}) collective-permute-start(bf16[96,1728]{1,0:T(8,128)(2,1)S(1)} %constant_dynamic-slice_fusion), channel_id=1, source_target_pairs={{0,24},{8,0},{16,8},{24,16},{1,25},{9,1},{17,9},{25,17},{2,26},{10... | collective-permute-start | bytes 995336 | tf_op jit(solution)/shard_map/ppermute | solution.py:41
  29.1 25.8 %collective-permute-start.11 = (bf16[96,1728]{1,0:T(8,128)(2,1)S(1)}, bf16[96,1728]{1,0:T(8,128)(2,1)}, u32[]{:S(2)}, u32[]{:S(2)}) collective-permute-start(bf16[96,1728]{1,0:T(8,128)(2,1)S(1)} %constant_dynamic-slice_fusion), channel_id=1, source_target_pairs={{0,8},{8,16},{16,24},{24,0},{1,9},{9,17},{17,25},{25,1},{2,10},{10... | collective-permute-start | bytes 995336 | tf_op jit(solution)/shard_map/ppermute | solution.py:41
  49.9 21.2 %collective-permute-start.7 = (bf16[96,1728]{1,0:T(8,128)(2,1)S(1)}, bf16[96,1728]{1,0:T(8,128)(2,1)}, u32[]{:S(2)}, u32[]{:S(2)}) collective-permute-start(bf16[96,1728]{1,0:T(8,128)(2,1)S(1)} %fusion.9), channel_id=1, source_target_pairs={{0,16},{8,24},{16,0},{24,8},{1,17},{9,25},{17,1},{25,9},{2,18},{10... | collective-permute-start | bytes 995336 | tf_op jit(solution)/shard_map/ppermute | solution.py:41
  54.0 23.8 %collective-permute-start.8 = (bf16[96,1728]{1,0:T(8,128)(2,1)S(1)}, bf16[96,1728]{1,0:T(8,128)(2,1)}, u32[]{:S(2)}, u32[]{:S(2)}) collective-permute-start(bf16[96,1728]{1,0:T(8,128)(2,1)S(1)} %constant_dynamic-slice_fusion), channel_id=1, source_target_pairs={{0,16},{8,24},{16,0},{24,8},{1,17},{9,25},{17,1},{25,9},{2,18},{10... | collective-permute-start | bytes 995336 | tf_op jit(solution)/shard_map/ppermute | solution.py:41
  55.0 22.8 %collective-permute-start.14 = (bf16[192,1728]{1,0:T(8,128)(2,1)S(1)}, bf16[192,1728]{1,0:T(8,128)(2,1)}, u32[]{:S(2)}, u32[]{:S(2)}) collective-permute-start(bf16[192,1728]{1,0:T(8,128)(2,1)S(1)} %constant_dynamic-update-slice_fusion.3.refs_12_), channel_id=1, source_target_pairs={{0,4},{4,0},{1,5},{5,1},{2,6},{6,2},{3,7},{7,3},{8,12},{12,8},{9,1... | collective-permute-start | bytes 1990664 | tf_op jit(solution)/shard_map/ppermute | solution.py:36
  57.6 20.7 %collective-permute-start.13 = (bf16[192,1728]{1,0:T(8,128)(2,1)S(1)}, bf16[192,1728]{1,0:T(8,128)(2,1)}, u32[]{:S(2)}, u32[]{:S(2)}) collective-permute-start(bf16[192,1728]{1,0:T(8,128)(2,1)S(1)} %constant_dynamic-update-slice_fusion.3.refs_12_), channel_id=1, source_target_pairs={{0,2},{1,3},{2,0},{3,1},{4,6},{5,7},{6,4},{7,5},{8,10},{9,11},{10,... | collective-permute-start | bytes 1990664 | tf_op jit(solution)/shard_map/ppermute | solution.py:36
  57.6 43.9 %copy-start.16 = (bf16[768]{0:T(1024)(128)(2,1)S(1)}, bf16[768]{0:T(1024)(128)(2,1)}, u32[]{:S(2)}) copy-start(bf16[768]{0:T(1024)(128)(2,1)} %param.28) | copy-start | bytes 4612
  57.7 44.0 %copy-start.17 = (bf16[768]{0:T(1024)(128)(2,1)S(1)}, bf16[768]{0:T(1024)(128)(2,1)}, u32[]{:S(2)}) copy-start(bf16[768]{0:T(1024)(128)(2,1)} %param.32) | copy-start | bytes 4612
  57.7 44.0 %copy-start.18 = (bf16[768]{0:T(1024)(128)(2,1)S(1)}, bf16[768]{0:T(1024)(128)(2,1)}, u32[]{:S(2)}) copy-start(bf16[768]{0:T(1024)(128)(2,1)} %param.33) | copy-start | bytes 4612
  57.7 44.0 %copy-start.19 = (bf16[768]{0:T(1024)(128)(2,1)S(1)}, bf16[768]{0:T(1024)(128)(2,1)}, u32[]{:S(2)}) copy-start(bf16[768]{0:T(1024)(128)(2,1)} %param.34) | copy-start | bytes 4612
  71.2 13.2 %collective-permute-start.20 = (bf16[192,1728]{1,0:T(8,128)(2,1)S(1)}, bf16[192,1728]{1,0:T(8,128)(2,1)S(1)}, u32[]{:S(2)}, u32[]{:S(2)}) collective-permute-start(bf16[192,1728]{1,0:T(8,128)(2,1)S(1)} %constant_dynamic-update-slice_fusion.3.refs_12_), channel_id=1, source_target_pairs={{0,1},{1,0},{2,3},{3,2},{4,5},{5,4},{6,7},{7,6},{8,9},{9,8},{10,11... | collective-permute-start | bytes 1990664 | tf_op jit(solution)/shard_map/ppermute | solution.py:36
  71.2 13.1 %collective-permute-start.18 = (bf16[200,1728]{1,0:T(8,128)(2,1)S(1)}, bf16[200,1728]{1,0:T(8,128)(2,1)S(1)}, u32[]{:S(2)}, u32[]{:S(2)}) collective-permute-start(bf16[200,1728]{1,0:T(8,128)(2,1)S(1)} %fusion.4.refs_8_), channel_id=1, source_target_pairs={{0,1},{1,0},{2,3},{3,2},{4,5},{5,4},{6,7},{7,6},{8,9},{9,8},{10,11... | collective-permute-start | bytes 2073608 | tf_op jit(solution)/shard_map/ppermute | solution.py:36
  77.8 6.7 %collective-permute-start.19 = (bf16[200,1728]{1,0:T(8,128)(2,1)}, bf16[200,1728]{1,0:T(8,128)(2,1)S(1)}, u32[]{:S(2)}, u32[]{:S(2)}) collective-permute-start(bf16[200,1728]{1,0:T(8,128)(2,1)} %collective-permute-done.2.refs_10_), channel_id=1, source_target_pairs={{0,1},{1,0},{2,3},{3,2},{4,5},{5,4},{6,7},{7,6},{8,9},{9,8},{10,11... | collective-permute-start | bytes 2073608 | tf_op jit(solution)/shard_map/ppermute | solution.py:36
  77.8 2.9 collective-permute-start.21
  78.3 2.9 collective-permute-start.22
  80.7 6.9 %collective-permute-start.15 = (bf16[384,192]{1,0:T(8,128)(2,1)}, bf16[384,192]{1,0:T(8,128)(2,1)S(1)}, u32[]{:S(2)}, u32[]{:S(2)}) collective-permute-start(bf16[384,192]{1,0:T(8,128)(2,1)} %get-tuple-element.128), channel_id=1, source_target_pairs={{0,1},{1,0},{2,3},{3,2},{4,5},{5,4},{6,7},{7,6},{8,9},{9,8},{10,11... | collective-permute-start | bytes 442376 | tf_op jit(solution)/shard_map/ppermute | solution.py:36
  81.2 9.1 %collective-permute-start.16 = (bf16[384,192]{1,0:T(8,128)(2,1)}, bf16[384,192]{1,0:T(8,128)(2,1)S(1)}, u32[]{:S(2)}, u32[]{:S(2)}) collective-permute-start(bf16[384,192]{1,0:T(8,128)(2,1)} %get-tuple-element.129), channel_id=1, source_target_pairs={{0,2},{1,3},{2,0},{3,1},{4,6},{5,7},{6,4},{7,5},{8,10},{9,11},{10,... | collective-permute-start | bytes 442376 | tf_op jit(solution)/shard_map/ppermute | solution.py:36
  84.3 9.8 %collective-permute-start.17 = (bf16[384,192]{1,0:T(8,128)(2,1)}, bf16[384,192]{1,0:T(8,128)(2,1)}, u32[]{:S(2)}, u32[]{:S(2)}) collective-permute-start(bf16[384,192]{1,0:T(8,128)(2,1)} %get-tuple-element.130), channel_id=1, source_target_pairs={{0,3},{1,2},{2,1},{3,0},{4,7},{5,6},{6,5},{7,4},{8,11},{9,10},{10,... | collective-permute-start | bytes 442376 | tf_op jit(solution)/shard_map/ppermute | solution.py:36
  84.4 10.3 %collective-permute-start.30 = (bf16[96,1728]{1,0:T(8,128)(2,1)}, bf16[96,1728]{1,0:T(8,128)(2,1)S(1)}, u32[]{:S(2)}, u32[]{:S(2)}) collective-permute-start(bf16[96,1728]{1,0:T(8,128)(2,1)} %collective-permute-done.8.refs_28_), channel_id=1, source_target_pairs={{0,1},{1,0},{2,3},{3,2},{4,5},{5,4},{6,7},{7,6},{8,9},{9,8},{10,11... | collective-permute-start | bytes 995336 | tf_op jit(solution)/shard_map/ppermute | solution.py:36
  84.5 11.5 %collective-permute-start.28 = (bf16[96,1728]{1,0:T(8,128)(2,1)}, bf16[96,1728]{1,0:T(8,128)(2,1)S(1)}, u32[]{:S(2)}, u32[]{:S(2)}) collective-permute-start(bf16[96,1728]{1,0:T(8,128)(2,1)} %collective-permute-done.7.refs_22_), channel_id=1, source_target_pairs={{0,4},{4,0},{1,5},{5,1},{2,6},{6,2},{3,7},{7,3},{8,12},{12,8},{9,1... | collective-permute-start | bytes 995336 | tf_op jit(solution)/shard_map/ppermute | solution.py:36
  87.6 13.9 %collective-permute-start.26 = (bf16[96,1728]{1,0:T(8,128)(2,1)}, bf16[96,1728]{1,0:T(8,128)(2,1)}, u32[]{:S(2)}, u32[]{:S(2)}) collective-permute-start(bf16[96,1728]{1,0:T(8,128)(2,1)} %collective-permute-done.7.refs_22_), channel_id=1, source_target_pairs={{0,2},{1,3},{2,0},{3,1},{4,6},{5,7},{6,4},{7,5},{8,10},{9,11},{10,... | collective-permute-start | bytes 995336 | tf_op jit(solution)/shard_map/ppermute | solution.py:36
  90.3 13.2 %collective-permute-start.23 = (bf16[192,1728]{1,0:T(8,128)(2,1)}, bf16[192,1728]{1,0:T(8,128)(2,1)S(1)}, u32[]{:S(2)}, u32[]{:S(2)}) collective-permute-start(bf16[192,1728]{1,0:T(8,128)(2,1)} %collective-permute-done.13.refs_18_), channel_id=1, source_target_pairs={{0,1},{1,0},{2,3},{3,2},{4,5},{5,4},{6,7},{7,6},{8,9},{9,8},{10,11... | collective-permute-start | bytes 1990664 | tf_op jit(solution)/shard_map/ppermute | solution.py:36
  94.1 9.4 %collective-permute-start.24 = (bf16[192,1728]{1,0:T(8,128)(2,1)}, bf16[192,1728]{1,0:T(8,128)(2,1)S(1)}, u32[]{:S(2)}, u32[]{:S(2)}) collective-permute-start(bf16[192,1728]{1,0:T(8,128)(2,1)} %collective-permute-done.14.refs_20_), channel_id=1, source_target_pairs={{0,1},{1,0},{2,3},{3,2},{4,5},{5,4},{6,7},{7,6},{8,9},{9,8},{10,11... | collective-permute-start | bytes 1990664 | tf_op jit(solution)/shard_map/ppermute | solution.py:36
  94.6 7.7 %collective-permute-start.25 = (bf16[96,1728]{1,0:T(8,128)(2,1)}, bf16[96,1728]{1,0:T(8,128)(2,1)}, u32[]{:S(2)}, u32[]{:S(2)}) collective-permute-start(bf16[96,1728]{1,0:T(8,128)(2,1)} %collective-permute-done.7.refs_22_), channel_id=1, source_target_pairs={{0,1},{1,0},{2,3},{3,2},{4,5},{5,4},{6,7},{7,6},{8,9},{9,8},{10,11... | collective-permute-start | bytes 995336 | tf_op jit(solution)/shard_map/ppermute | solution.py:36
  96.1 6.2 %collective-permute-start.29 = (bf16[96,1728]{1,0:T(8,128)(2,1)S(1)}, bf16[96,1728]{1,0:T(8,128)(2,1)}, u32[]{:S(2)}, u32[]{:S(2)}) collective-permute-start(bf16[96,1728]{1,0:T(8,128)(2,1)S(1)} %collective-permute-done.28.refs_26_), channel_id=1, source_target_pairs={{0,1},{1,0},{2,3},{3,2},{4,5},{5,4},{6,7},{7,6},{8,9},{9,8},{10,11... | collective-permute-start | bytes 995336 | tf_op jit(solution)/shard_map/ppermute | solution.py:36
  101.5 2.1 collective-permute-start.27
  128.9 7.9 %collective-permute-start.35 = (bf16[2,384,1792]{2,1,0:T(8,128)(2,1)}, bf16[2,384,1792]{2,1,0:T(8,128)(2,1)S(1)}, u32[]{:S(2)}, u32[]{:S(2)}) collective-permute-start(bf16[2,384,1792]{2,1,0:T(8,128)(2,1)} %get-tuple-element.146), channel_id=1, source_target_pairs={{0,1},{1,0},{2,3},{3,2},{4,5},{5,4},{6,7},{7,6},{8,9},{9,8},{10,11... | collective-permute-start | bytes 8257544 | tf_op jit(solution)/shard_map/ppermute | solution.py:36
  129.1 7.7 %collective-permute-start.34 = (bf16[3,768,384]{2,1,0:T(8,128)(2,1)}, bf16[3,768,384]{2,1,0:T(8,128)(2,1)S(1)}, u32[]{:S(2)}, u32[]{:S(2)}) collective-permute-start(bf16[3,768,384]{2,1,0:T(8,128)(2,1)} %get-tuple-element.144.refs_1_), channel_id=1, source_target_pairs={{0,1},{1,0},{2,3},{3,2},{4,5},{5,4},{6,7},{7,6},{8,9},{9,8},{10,11... | collective-permute-start | bytes 5308424 | tf_op jit(solution)/shard_map/ppermute | solution.py:36
  130.2 21.6 %collective-permute-start.31 = (bf16[384,192]{1,0:T(8,128)(2,1)}, bf16[384,192]{1,0:T(8,128)(2,1)S(1)}, u32[]{:S(2)}, u32[]{:S(2)}) collective-permute-start(bf16[384,192]{1,0:T(8,128)(2,1)} %get-tuple-element.141), channel_id=1, source_target_pairs={{0,1},{1,0},{2,3},{3,2},{4,5},{5,4},{6,7},{7,6},{8,9},{9,8},{10,11... | collective-permute-start | bytes 442376 | tf_op jit(solution)/shard_map/ppermute | solution.py:36
  130.4 21.4 %collective-permute-start.32 = (bf16[384,192]{1,0:T(8,128)(2,1)}, bf16[384,192]{1,0:T(8,128)(2,1)S(1)}, u32[]{:S(2)}, u32[]{:S(2)}) collective-permute-start(bf16[384,192]{1,0:T(8,128)(2,1)} %get-tuple-element.142), channel_id=1, source_target_pairs={{0,2},{1,3},{2,0},{3,1},{4,6},{5,7},{6,4},{7,5},{8,10},{9,11},{10,... | collective-permute-start | bytes 442376 | tf_op jit(solution)/shard_map/ppermute | solution.py:36
  132.1 19.7 %collective-permute-start.33 = (bf16[384,192]{1,0:T(8,128)(2,1)}, bf16[384,192]{1,0:T(8,128)(2,1)S(1)}, u32[]{:S(2)}, u32[]{:S(2)}) collective-permute-start(bf16[384,192]{1,0:T(8,128)(2,1)} %get-tuple-element.143), channel_id=1, source_target_pairs={{0,3},{1,2},{2,1},{3,0},{4,7},{5,6},{6,5},{7,4},{8,11},{9,10},{10,... | collective-permute-start | bytes 442376 | tf_op jit(solution)/shard_map/ppermute | solution.py:36
  151.8 26.7 %collective-permute-start.38 = (f32[8,768]{1,0:T(8,128)S(1)}, f32[8,768]{1,0:T(8,128)S(1)}, u32[]{:S(2)}, u32[]{:S(2)}) collective-permute-start(f32[8,768]{1,0:T(8,128)S(1)} %pad_maximum_fusion.2), channel_id=1, source_target_pairs={{0,1},{1,0},{2,3},{3,2},{4,5},{5,4},{6,7},{7,6},{8,9},{9,8},{10,11... | collective-permute-start | bytes 73736 | tf_op jit(solution)/shard_map/ppermute | solution.py:36
  152.0 32.7 %collective-permute-start.36 = (bf16[4,96,1728]{2,1,0:T(8,128)(2,1)}, bf16[4,96,1728]{2,1,0:T(8,128)(2,1)S(1)}, u32[]{:S(2)}, u32[]{:S(2)}) collective-permute-start(bf16[4,96,1728]{2,1,0:T(8,128)(2,1)} %get-tuple-element.150), channel_id=1, source_target_pairs={{0,2},{1,3},{2,0},{3,1},{4,6},{5,7},{6,4},{7,5},{8,10},{9,11},{10,... | collective-permute-start | bytes 3981320 | tf_op jit(solution)/shard_map/ppermute | solution.py:36
  153.8 32.4 %collective-permute-start.37 = (bf16[2,2,96,1728]{3,2,1,0:T(8,128)(2,1)}, bf16[2,2,96,1728]{3,2,1,0:T(8,128)(2,1)S(1)}, u32[]{:S(2)}, u32[]{:S(2)}) collective-permute-start(bf16[2,2,96,1728]{3,2,1,0:T(8,128)(2,1)} %get-tuple-element.151), channel_id=1, source_target_pairs={{0,4},{4,0},{1,5},{5,1},{2,6},{6,2},{3,7},{7,3},{8,12},{12,8},{9,1... | collective-permute-start | bytes 3981320 | tf_op jit(solution)/shard_map/ppermute | solution.py:36
  186.2 11.9 %collective-permute-start.39 = (bf16[512,384]{1,0:T(8,128)(2,1)}, bf16[512,384]{1,0:T(8,128)(2,1)S(1)}, u32[]{:S(2)}, u32[]{:S(2)}) collective-permute-start(bf16[512,384]{1,0:T(8,128)(2,1)} %get-tuple-element.170), channel_id=1, source_target_pairs={{0,4},{4,0},{1,5},{5,1},{2,6},{6,2},{3,7},{7,3},{8,12},{12,8},{9,1... | collective-permute-start | bytes 1179656 | tf_op jit(solution)/shard_map/ppermute | solution.py:36
  187.6 7.1 %collective-permute-start.40 = (f32[8,768]{1,0:T(8,128)S(1)}, f32[8,768]{1,0:T(8,128)S(1)}, u32[]{:S(2)}, u32[]{:S(2)}) collective-permute-start(f32[8,768]{1,0:T(8,128)S(1)} %pad_maximum_fusion.3), channel_id=1, source_target_pairs={{0,2},{1,3},{2,0},{3,1},{4,6},{5,7},{6,4},{7,5},{8,10},{9,11},{10,... | collective-permute-start | bytes 73736 | tf_op jit(solution)/shard_map/ppermute | solution.py:36
  193.7 18.2 %collective-permute-start.43 = (bf16[2,96,1728]{2,1,0:T(8,128)(2,1)}, bf16[2,96,1728]{2,1,0:T(8,128)(2,1)S(1)}, u32[]{:S(2)}, u32[]{:S(2)}) collective-permute-start(bf16[2,96,1728]{2,1,0:T(8,128)(2,1)} %get-tuple-element.171), channel_id=1, source_target_pairs={{0,4},{4,0},{1,5},{5,1},{2,6},{6,2},{3,7},{7,3},{8,12},{12,8},{9,1... | collective-permute-start | bytes 1990664 | tf_op jit(solution)/shard_map/ppermute | solution.py:36
  194.0 17.9 %collective-permute-start.44 = (bf16[2,96,1728]{2,1,0:T(8,128)(2,1)}, bf16[2,96,1728]{2,1,0:T(8,128)(2,1)S(1)}, u32[]{:S(2)}, u32[]{:S(2)}) collective-permute-start(bf16[2,96,1728]{2,1,0:T(8,128)(2,1)} %get-tuple-element.172), channel_id=1, source_target_pairs={{0,2},{1,3},{2,0},{3,1},{4,6},{5,7},{6,4},{7,5},{8,10},{9,11},{10,... | collective-permute-start | bytes 1990664 | tf_op jit(solution)/shard_map/ppermute | solution.py:36
  198.1 13.8 %collective-permute-start.41 = (f32[8,768]{1,0:T(8,128)S(1)}, f32[8,768]{1,0:T(8,128)S(1)}, u32[]{:S(2)}, u32[]{:S(2)}) collective-permute-start(f32[8,768]{1,0:T(8,128)S(1)} %add.60), channel_id=1, source_target_pairs={{0,4},{4,0},{1,5},{5,1},{2,6},{6,2},{3,7},{7,3},{8,12},{12,8},{9,1... | collective-permute-start | bytes 73736 | tf_op jit(solution)/shard_map/ppermute | solution.py:36
  213.6 3.1 %collective-permute-start.54 = (bf16[2,384,768]{2,1,0:T(8,128)(2,1)}, bf16[2,384,768]{2,1,0:T(8,128)(2,1)S(1)}, u32[]{:S(2)}, u32[]{:S(2)}) collective-permute-start(bf16[2,384,768]{2,1,0:T(8,128)(2,1)} %get-tuple-element.190), channel_id=1, source_target_pairs={{0,1},{1,0},{2,3},{3,2},{4,5},{5,4},{6,7},{7,6},{8,9},{9,8},{10,11... | collective-permute-start | bytes 3538952 | tf_op jit(solution)/shard_map/ppermute | solution.py:36
  213.6 13.8 %collective-permute-start.45 = (bf16[4,96,640]{2,1,0:T(8,128)(2,1)}, bf16[4,96,640]{2,1,0:T(8,128)(2,1)S(1)}, u32[]{:S(2)}, u32[]{:S(2)}) collective-permute-start(bf16[4,96,640]{2,1,0:T(8,128)(2,1)} %get-tuple-element.179), channel_id=1, source_target_pairs={{0,4},{4,0},{1,5},{5,1},{2,6},{6,2},{3,7},{7,3},{8,12},{12,8},{9,1... | collective-permute-start | bytes 1474568 | tf_op jit(solution)/shard_map/ppermute | solution.py:36
  218.6 16.1 %collective-permute-start.55 = (bf16[384,768]{1,0:T(8,128)(2,1)}, bf16[384,768]{1,0:T(8,128)(2,1)}, u32[]{:S(2)}, u32[]{:S(2)}) collective-permute-start(bf16[384,768]{1,0:T(8,128)(2,1)} %fusion.5), channel_id=1, source_target_pairs={{0,2},{1,3},{2,0},{3,1},{4,6},{5,7},{6,4},{7,5},{8,10},{9,11},{10,... | collective-permute-start | bytes 1769480 | tf_op jit(solution)/shard_map/ppermute | solution.py:36
  220.3 5.0 %collective-permute-start.42 = (f32[8,768]{1,0:T(8,128)S(1)}, f32[8,768]{1,0:T(8,128)S(1)}, u32[]{:S(2)}, u32[]{:S(2)}) collective-permute-start(f32[8,768]{1,0:T(8,128)S(1)} %add.61), channel_id=1, source_target_pairs={{0,8},{8,0},{16,24},{24,16},{1,9},{9,1},{17,25},{25,17},{2,10},{10... | collective-permute-start | bytes 73736 | tf_op jit(solution)/shard_map/ppermute | solution.py:36
  232.0 28.0 %collective-permute-start.46 = (bf16[96,2432]{1,0:T(8,128)(2,1)}, bf16[96,2432]{1,0:T(8,128)(2,1)S(1)}, u32[]{:S(2)}, u32[]{:S(2)}) collective-permute-start(bf16[96,2432]{1,0:T(8,128)(2,1)} %get-tuple-element.181), channel_id=1, source_target_pairs={{0,8},{8,16},{16,24},{24,0},{1,9},{9,17},{17,25},{25,1},{2,10},{10... | collective-permute-start | bytes 1400840 | tf_op jit(solution)/shard_map/ppermute | solution.py:41
  233.1 26.9 %collective-permute-start.52 = (bf16[384,768]{1,0:T(8,128)(2,1)}, bf16[384,768]{1,0:T(8,128)(2,1)}, u32[]{:S(2)}, u32[]{:S(2)}) collective-permute-start(bf16[384,768]{1,0:T(8,128)(2,1)} %get-tuple-element.187.p_0), channel_id=1, source_target_pairs={{0,2},{1,3},{2,0},{3,1},{4,6},{5,7},{6,4},{7,5},{8,10},{9,11},{10,... | collective-permute-start | bytes 1769480 | tf_op jit(solution)/shard_map/ppermute | solution.py:36
  237.0 37.2 %collective-permute-start.57 = (bf16[384,768]{1,0:T(8,128)(2,1)}, bf16[384,768]{1,0:T(8,128)(2,1)S(1)}, u32[]{:S(2)}, u32[]{:S(2)}) collective-permute-start(bf16[384,768]{1,0:T(8,128)(2,1)} %fusion.2.p_0), channel_id=1, source_target_pairs={{0,2},{1,3},{2,0},{3,1},{4,6},{5,7},{6,4},{7,5},{8,10},{9,11},{10,... | collective-permute-start | bytes 1769480 | tf_op jit(solution)/shard_map/ppermute | solution.py:36
  238.2 11.6 %collective-permute-start.47 = (f32[8,768]{1,0:T(8,128)S(1)}, f32[8,768]{1,0:T(8,128)S(1)}, u32[]{:S(2)}, u32[]{:S(2)}) collective-permute-start(f32[8,768]{1,0:T(8,128)S(1)} %copy-done.8), channel_id=1, source_target_pairs={{0,16},{8,24},{16,0},{24,8},{1,17},{9,25},{17,1},{25,9},{2,18},{10... | collective-permute-start | bytes 73736 | tf_op jit(solution)/shard_map/ppermute | solution.py:36
  241.7 32.5 %collective-permute-start.48 = (bf16[96,2432]{1,0:T(8,128)(2,1)S(1)}, bf16[96,2432]{1,0:T(8,128)(2,1)S(1)}, u32[]{:S(2)}, u32[]{:S(2)}) collective-permute-start(bf16[96,2432]{1,0:T(8,128)(2,1)S(1)} %copy-done.39), channel_id=1, source_target_pairs={{0,16},{8,24},{16,0},{24,8},{1,17},{9,25},{17,1},{25,9},{2,18},{10... | collective-permute-start | bytes 1400840 | tf_op jit(solution)/shard_map/ppermute | solution.py:41
  249.8 29.4 %collective-permute-start.49 = (bf16[96,2432]{1,0:T(8,128)(2,1)S(1)}, bf16[96,2432]{1,0:T(8,128)(2,1)}, u32[]{:S(2)}, u32[]{:S(2)}) collective-permute-start(bf16[96,2432]{1,0:T(8,128)(2,1)S(1)} %copy-done.37), channel_id=1, source_target_pairs={{0,24},{8,0},{16,8},{24,16},{1,25},{9,1},{17,9},{25,17},{2,26},{10... | collective-permute-start | bytes 1400840 | tf_op jit(solution)/shard_map/ppermute | solution.py:41
  260.0 24.5 %collective-permute-start.51 = (bf16[384,768]{1,0:T(8,128)(2,1)}, bf16[384,768]{1,0:T(8,128)(2,1)S(1)}, u32[]{:S(2)}, u32[]{:S(2)}) collective-permute-start(bf16[384,768]{1,0:T(8,128)(2,1)} %get-tuple-element.187.p_0), channel_id=1, source_target_pairs={{0,1},{1,0},{2,3},{3,2},{4,5},{5,4},{6,7},{7,6},{8,9},{9,8},{10,11... | collective-permute-start | bytes 1769480 | tf_op jit(solution)/shard_map/ppermute | solution.py:36
  260.0 24.5 %collective-permute-start.53 = (bf16[384,768]{1,0:T(8,128)(2,1)}, bf16[384,768]{1,0:T(8,128)(2,1)S(1)}, u32[]{:S(2)}, u32[]{:S(2)}) collective-permute-start(bf16[384,768]{1,0:T(8,128)(2,1)} %collective-permute-done.52.p_2), channel_id=1, source_target_pairs={{0,1},{1,0},{2,3},{3,2},{4,5},{5,4},{6,7},{7,6},{8,9},{9,8},{10,11... | collective-permute-start | bytes 1769480 | tf_op jit(solution)/shard_map/ppermute | solution.py:36
  274.2 15.1 %collective-permute-start.56 = (bf16[384,768]{1,0:T(8,128)(2,1)}, bf16[384,768]{1,0:T(8,128)(2,1)S(1)}, u32[]{:S(2)}, u32[]{:S(2)}) collective-permute-start(bf16[384,768]{1,0:T(8,128)(2,1)} %fusion.2.p_0), channel_id=1, source_target_pairs={{0,1},{1,0},{2,3},{3,2},{4,5},{5,4},{6,7},{7,6},{8,9},{9,8},{10,11... | collective-permute-start | bytes 1769480 | tf_op jit(solution)/shard_map/ppermute | solution.py:36
  274.2 15.1 %collective-permute-start.58 = (bf16[384,768]{1,0:T(8,128)(2,1)S(1)}, bf16[384,768]{1,0:T(8,128)(2,1)S(1)}, u32[]{:S(2)}, u32[]{:S(2)}) collective-permute-start(bf16[384,768]{1,0:T(8,128)(2,1)S(1)} %collective-permute-done.57.p_2), channel_id=1, source_target_pairs={{0,1},{1,0},{2,3},{3,2},{4,5},{5,4},{6,7},{7,6},{8,9},{9,8},{10,11... | collective-permute-start | bytes 1769480 | tf_op jit(solution)/shard_map/ppermute | solution.py:36
  282.1 12.9 %collective-permute-start.50 = (bf16[96,2432]{1,0:T(8,128)(2,1)}, bf16[96,2432]{1,0:T(8,128)(2,1)S(1)}, u32[]{:S(2)}, u32[]{:S(2)}) collective-permute-start(bf16[96,2432]{1,0:T(8,128)(2,1)} %merge_three.1.refs_1_), channel_id=1, source_target_pairs={{0,4},{4,0},{1,5},{5,1},{2,6},{6,2},{3,7},{7,3},{8,12},{12,8},{9,1... | collective-permute-start | bytes 1400840 | tf_op jit(solution)/shard_map/ppermute | solution.py:36
  (52 other events, 441.0 us)

commit v2 on v1

--- a/solution.py
+++ b/solution.py
@@ -487,27 +487,29 @@
     for copy in copies:
         copy.wait()
     spans = ((0, 0, hidden), (1, hidden, 2 * hidden), (2, 2 * hidden, wide))
-    for x in range(2):
-        for i, first, last in spans:
-            for top in range(2):
-                part = slice(top * mid, (top + 1) * mid)
-                got = nn(rows_ref[i, part, :], wide_ref[x, :, first:last]).astype(low)
-                if top == 0:
-                    side = ak_ref if x == 0 else as_ref
-                    side[:, :, first:last] = got.reshape(-1, half, last - first)
-                else:
-                    got = got.reshape(-1, 2, half, last - first)
-                    for z in range(got.shape[0]):
-
-                        @pl.when(c == 0)
-                        def _():
-                            bk_ref[x, z, :, first:last] = got[z, 0]
-                            bs_ref[x, z, :, first:last] = got[z, 1]
-
-                        @pl.when(c != 0)
-                        def _():
-                            bk_ref[x, z, :, first:last] = got[z, 1]
-                            bs_ref[x, z, :, first:last] = got[z, 0]
+    for i, first, last in spans:
+        for x, side in enumerate((ak_ref, as_ref)):
+            got = nn(rows_ref[i, :mid, :], wide_ref[x, :, first:last]).astype(low)
+            side[:, :, first:last] = got.reshape(-1, half, last - first)
+
+        def lower(x, carry, i=i, first=first, last=last):
+            got = nn(rows_ref[i, mid:, :], wide_ref[x, :, first:last]).astype(low)
+            got = got.reshape(-1, 2, half, last - first)
+            for z in range(got.shape[0]):
+
+                @pl.when(c == 0)
+                def _():
+                    bk_ref[x, z, :, first:last] = got[z, 0]
+                    bs_ref[x, z, :, first:last] = got[z, 1]
+
+                @pl.when(c != 0)
+                def _():
+                    bk_ref[x, z, :, first:last] = got[z, 1]
+                    bs_ref[x, z, :, first:last] = got[z, 0]
+
+            return carry
+
+        lax.fori_loop(0, 2, lower, 0)
 
 
 def unit_grads(here, rows, mate_rows, keep, mate, half, hidden, local):
@@ -566,30 +568,27 @@
     )(here, ak, ga, bk, gb)
 
 
-def merge_two_kernel(here, a_keep, a_got, b_keep, b_got, d_keep, d_got, *refs, start):
-    outs, all_ref = refs[:4], refs[4]
+def merge_two_kernel(here, *refs, pairs):
+    ins, outs, all_ref = refs[: 2 * pairs], refs[2 * pairs : -1], refs[-1]
     f = here[1]
-    wide = a_keep.shape[2]
-    for z in range(2):
-        all_ref[z, :, :wide] = a_keep[z] + a_got[z]
-        all_ref[2 + z, :, :wide] = b_keep[z] + b_got[z]
-    all_ref[:, :, start:] = d_keep[...] + d_got[...]
+    count = 4 // pairs
+    for i in range(pairs):
+        all_ref[i * count : (i + 1) * count] = ins[2 * i][...] + ins[2 * i + 1][...]
     for s, out in enumerate(outs):
         out[...] = all_ref[(f + s) % 4]
 
 
-def merge_two(here, a_keep, a_got, b_keep, b_got, d_keep, d_got, start):
-    half = a_keep.shape[1]
-    full = start + d_keep.shape[2]
+def merge_two(here, *parts):
+    piece = parts[0].shape[1:]
     return pl.pallas_call(
-        lambda *refs: merge_two_kernel(*refs, start=start),
+        lambda *refs: merge_two_kernel(*refs, pairs=len(parts) // 2),
         name="merge_two",
-        out_shape=(shape(half, full),) * 4,
-        in_specs=[SMEM] + [VMEM] * 6,
+        out_shape=(shape(*piece),) * 4,
+        in_specs=[SMEM] + [VMEM] * len(parts),
         out_specs=(VMEM,) * 4,
-        scratch_shapes=[pltpu.VMEM((4, half, full), low)],
+        scratch_shapes=[pltpu.VMEM((4,) + piece, low)],
         cost_estimate=cost(SMALL_COST, 8 << 20),
-    )(here, a_keep, a_got, b_keep, b_got, d_keep, d_got)
+    )(here, *parts)
 
 
 def merge_three_kernel(here, own, got_1, got_2, got_3, out, all_ref):
@@ -614,32 +613,35 @@
     )(here, *pieces)
 
 
-def finish_kernel(here, own, got, inner, outer, out, query, key, value, bias, all_ref, *, start):
+def finish_kernel(here, own, got, d_own, d_got, inner, outer, out, query, key, value, bias, all_ref, d_ref):
     c = here[2]
     hidden = inner.shape[1]
     local = query.shape[1]
     all_ref[c] = own[...]
     all_ref[1 - c] = got[...]
-    half, full = own.shape
-
-    def cols(first, last):
-        return all_ref[:, :, first:last].reshape(2 * half, last - first).astype(high)
-
-    inner[...] = cols(0, hidden)
-    outer[...] = cols(hidden, 2 * hidden)
-    out[...] = cols(2 * hidden, 2 * hidden + local).T
-    rest = cols(start, full)
+    d_ref[c] = d_own[...]
+    d_ref[1 - c] = d_got[...]
+    half = own.shape[0]
+
+    def cols(ref, first, last):
+        return ref[:, :, first:last].reshape(2 * half, last - first).astype(high)
+
+    inner[...] = cols(all_ref, 0, hidden)
+    outer[...] = cols(all_ref, hidden, 2 * hidden)
+    out[...] = cols(all_ref, 2 * hidden, 2 * hidden + local).T
+    rest = cols(d_ref, 0, 3 * local)
     query[...] = rest[:, :local]
     key[...] = rest[:, local : 2 * local]
     value[...] = rest[:, 2 * local : 3 * local]
-    bias[...] = own[:16, start + 3 * local :].astype(high)
-
-
-def finish(here, own, got, start, hidden, local):
-    half, full = own.shape
+    bias[...] = d_own[:16, 3 * local :].astype(high)
+
+
+def finish(here, own, got, d_own, d_got, hidden, local):
+    half, wide = own.shape
+    full = d_own.shape[1]
     piece = 2 * half
     return pl.pallas_call(
-        lambda *refs: finish_kernel(*refs, start=start),
+        finish_kernel,
         name="finish",
         out_shape=(
             shape(piece, hidden, kind=high),
@@ -648,13 +650,13 @@
             shape(piece, local, kind=high),
             shape(piece, local, kind=high),
             shape(piece, local, kind=high),
-            shape(16, full - start - 3 * local, kind=high),
+            shape(16, full - 3 * local, kind=high),
         ),
-        in_specs=[SMEM] + [VMEM] * 2,
+        in_specs=[SMEM] + [VMEM] * 4,
         out_specs=(VMEM,) * 7,
-        scratch_shapes=[pltpu.VMEM((2, half, full), low)],
+        scratch_shapes=[pltpu.VMEM((2, half, wide), low), pltpu.VMEM((2, half, full), low)],
         cost_estimate=cost(SMALL_COST, 4 << 20),
-    )(here, own, got)
+    )(here, own, got, d_own, d_got)
 
 
 def spread_kernel(here, p_0, p_1, p_2, p_3, out):
@@ -689,9 +691,13 @@
         g_ref[edge, local:].astype(high) + edge_ref[...].astype(high)
     ).astype(low)
     for k, side in ((1, send), (0, keep)):
-        for x in range(2):
+
+        def back(x, carry, k=k, side=side):
             first = pl.multiple_of((mine ^ (2 * x + k)) * tokens, tokens)
             side[x] = nt(all_ref[pl.ds(first, tokens), :], w_ref[...]).astype(low)
+            return carry
+
+        lax.fori_loop(0, 2, back, 0)
     sums = jnp.zeros((1, 3 * local), high)
     for i in range(rows // tokens):
         part = all_ref[i * tokens : (i + 1) * tokens, :].astype(high)
@@ -837,6 +843,15 @@
     return lax.optimization_barrier((tuple(values), gate))[0]
 
 
+def add_many(pieces, plan, value, spots, in_rows):
+    offset = 0
+    for r, mark in spots:
+        mark = None if mark is None else in_rows(mark)
+        plan.append((len(pieces), offset, r, mark))
+        offset += 8 if mark is None else mark(0, 0)[1]
+    pieces.append(value)
+
+
 def halo_of(value, c, span):
     rows = value.shape[0]
     return take(value, (1 - c) * (rows - span), span)
@@ -936,6 +951,7 @@
         (own_1,) = after([own_f], joined)
         gots = {s: shift(own_1, "fsdp", s) for s in (1, 3)}
         halo_in, far_rows = lax.optimization_barrier((halo_in, far_rows))
+        home_mate = swap(jnp.concatenate([own_rows, far_rows], axis=0), "tp", 1)
         far_f = take(far_rows, (1 - c) * half, half)
         corners = {s: shift(far_f, "fsdp", s) for s in (1, 3)}
 
@@ -956,43 +972,49 @@
         (far_2,) = after([far_f], att_2)
         corners[2] = shift(far_2, "fsdp", 2)
         *near, corners[1], corners[3] = after([gots[1], gots[3], corners[1], corners[3]], att_2)
-        (q_near,) = after([q_near], (*near, corners[1], corners[3]))
+        near = jnp.concatenate(near, axis=0)
+        home_mate, q_near = lax.optimization_barrier((home_mate, q_near))
+        (q_near,) = after([q_near], (near, corners[1], corners[3]))
     att_0, att_1, full_near, q_near = attend_near(here, seg_own, seg_all, q_near, keys_wide, values_t)
     if quick:
         pieces_f, plan = [], []
 
-        def add(r, value, marks, gate=None, bias=False):
-            twin = value
-            if gate is not None:
-                (twin,) = after([value], gate)
-            for r, piece in ((r, value), (r + 1, swap(twin, "tp", 1))):
-                offset = 0
-                for mark in marks:
-                    plan.append((len(pieces_f), offset, r, in_rows(mark)))
-                    offset += half
-                if bias:
-                    plan.append((len(pieces_f), piece_rows, r, None))
-                pieces_f.append(piece)
-
-        piece_rows = piece
-        add(0, own_rows, [spot_from(0)], att_0, bias=True)
-        add(2, far_rows, [spot_from(0)], att_0, bias=True)
-        near = jnp.concatenate(near, axis=0)
-        add(0, near, [spot(1, 0), spot(3, 0)], att_0)
-        for s in (1, 3):
-            add(2, corners[s], [spot(s, 1)], att_0)
+        def add(r, value, marks):
+            offset = 0
+            for mark in marks:
+                if mark is None:
+                    plan.append((len(pieces_f), offset, r, None))
+                    offset += 8
+                else:
+                    mark = in_rows(mark)
+                    plan.append((len(pieces_f), offset, r, mark))
+                    offset += mark(0, 0)[1]
+            pieces_f.append(value)
+
+        def add_both(r, value, marks):
+            add(r, value, marks)
+            add(r + 1, swap(value, "tp", 1), marks)
+
+        for r, value in ((0, own_rows), (2, far_rows)):
+            add(r, value, [spot_from(0), None])
+        add_many(pieces_f, plan, home_mate, ((1, spot_from(0)), (1, None), (3, spot_from(0)), (3, None)), in_rows)
         near_x, near_y = swap(near, "tp", 2), swap(near, "ctx", 1)
-        last, corner, near_x, near_y, *att = lax.optimization_barrier(
-            (gots[2], corners[2], near_x, near_y, att_0, att_1, att_2, att_3)
+        last, near_x, near_y, *att = lax.optimization_barrier(
+            (gots[2], near_x, near_y, att_0, att_1, att_2, att_3)
         )
         att_0, att_1, att_2, att_3 = att
         att = [att_0, swap(att_1, "tp", 1), swap(att_2, "tp", 2), swap(att_3, "tp", 3)]
-        add(2, near_x, [spot(1, 0), spot(3, 0)])
-        add(0, near_y, [spot(1, 1), spot(3, 1)])
-        add(0, last, [spot(2, 0)])
-        add(2, swap(last, "tp", 2), [spot(2, 0)])
-        add(0, swap(last, "ctx", 1), [spot(2, 1)])
-        add(2, corner, [spot(2, 1)])
+        near, corners[1], corners[3] = after([near, corners[1], corners[3]], att_0)
+        add_both(0, near, [spot(1, 0), spot(3, 0)])
+        add_both(2, corners[1], [spot(1, 1)])
+        add_both(2, corners[3], [spot(3, 1)])
+        add_both(2, near_x, [spot(1, 0), spot(3, 0)])
+        add_both(0, near_y, [spot(1, 1), spot(3, 1)])
+        add_both(0, last, [spot(2, 0)])
+        add_both(2, swap(last, "tp", 2), [spot(2, 0)])
+        add_both(0, swap(last, "ctx", 1), [spot(2, 1)])
+        (corner,) = after([corners[2]], att_0)
+        add_both(2, corner, [spot(2, 1)])
     else:
         gathered = lax.all_gather(bundle_f, "fsdp", axis=0, tiled=True)
         gathered = jnp.concatenate([gathered, bias_row], axis=0)
@@ -1016,12 +1038,21 @@
         mate = swap(send, "tp", 1)
         near_sums = jnp.concatenate([stats[:6], stats[8:9], stats[10:11]], axis=0)
         away = jnp.concatenate([stats[:6], stats[9:10], stats[11:12]], axis=0)
+        (away,) = after([away], mate)
+        away = swap(away, "tp", 1)
         keep_a, send_a, keep_b, send_b = unit_grads(here, rows_t, mate_rows, keep, mate, half, hidden, local)
+        send_a, send_b, away, *g_att = lax.optimization_barrier((send_a, send_b, away, *g_att))
         got_a = swap(send_a, "tp", 2)
         got_b = swap(send_b, "ctx", 1)
         (away,) = after([away], keep_a)
-        away = swap(away, "tp", 1)
+        pair = near_sums + away
+        away = jnp.concatenate([pair[:6], pair[7:8], pair[7:8]], axis=0)
+        away = swap(away, "tp", 2)
         *g_att, keep_a, keep_b = lax.optimization_barrier((*g_att, keep_a, keep_b))
+
+        def everyone(value, far_value, kind):
+            return spread(here, [value, swap(value, "tp", 1), far_value, swap(far_value, "tp", 1)], kind)
+
     else:
         ordered = []
         for r in range(n_t):
@@ -1048,45 +1079,42 @@
     if quick:
         got_a, got_b = after([got_a, got_b], g_own)
         (away,) = after([away], g_own)
-        pair = near_sums + away
+        pair = pair + away
         (rim_out,) = after([g_rim], (got_a, got_b, pair))
-        away = jnp.concatenate([pair[:6], pair[7:8], pair[7:8]], axis=0)
-        away = swap(away, "tp", 2)
+        away = swap(pair, "ctx", 1)
         edge = swap(rim_out, "ctx", 1)
         keep_a, send_a, keep_b, send_b = merge_one(here, keep_a, got_a, keep_b, got_b)
         got_a = swap(send_a, "ctx", 1)
         got_b = swap(send_b, "tp", 2)
         edge, away = after([edge, away], (send_a, send_b))
         pair = pair + away
-        pair = pair + swap(pair, "ctx", 1)
+        pair = pair + swap(pair, "fsdp", 1)
         dx_keep, dx_send, d_keep, d_send = project_back(here, g_own, edge, inputs, w_qkv, tokens, half)
         (dx_send,) = after([dx_send], (got_a, got_b, pair))
-        pair = pair + swap(pair, "fsdp", 1)
+        pair = pair + swap(pair, "fsdp", 2)
         dx_got = swap(dx_send, "tp", 1)
         d_got = swap(d_send, "ctx", 1)
+        outs = merge_two(here, keep_a, got_a, keep_b, got_b)
+        totals = [outs[0]] + [shift(outs[s], "fsdp", s) for s in range(1, n_f)]
         near_dx = dx_keep[0] + dx_got[0]
         far_dx = dx_keep[1] + dx_got[1]
         far_got = swap(far_dx, "tp", 2)
-        start = (2 * hidden + local + 127) // 128 * 128
-        keep_a, pair = lax.optimization_barrier((keep_a, pair))
-        outs = merge_two(here, keep_a, got_a, keep_b, got_b, d_keep, d_got, start)
-        (output,) = after([output], outs[0])
-        pair = pair + swap(pair, "fsdp", 2)
-        totals = [outs[0]] + [shift(outs[s], "fsdp", s) for s in range(1, n_f)]
+        (d_got,) = after([d_got], outs[0])
+        outs = merge_two(here, d_keep, d_got)
+        d_totals = [outs[0]] + [shift(outs[s], "fsdp", s) for s in range(1, n_f)]
+        (output,) = after([output], d_totals[0])
+        output = everyone(output, swap(output, "tp", 2), low)
+        (far_got,) = after([far_got], (*totals, d_totals[0]))
         mine = (near_dx.astype(high) + far_got.astype(high) + g_one).astype(low)
-
-        def everyone(value, kind):
-            far_value = swap(value, "tp", 2)
-            return spread(here, [value, swap(value, "tp", 1), far_value, swap(far_value, "tp", 1)], kind)
-
-        output = everyone(output, low)
-        grad_inputs = everyone(mine, high)
-        totals[1], pair = lax.optimization_barrier((totals[1], pair))
+        (far_mine,) = after([swap(mine, "tp", 2)], d_totals)
+        grad_inputs = everyone(mine, far_mine, high)
         total = merge_three(here, totals)
         got = swap(total, "ctx", 1)
-        got, output, grad_inputs = lax.optimization_barrier((got, output, grad_inputs))
+        d_total = merge_three(here, d_totals)
+        d_got = swap(d_total, "ctx", 1)
+        d_got, grad_inputs, output, pair = lax.optimization_barrier((d_got, grad_inputs, output, pair))
         s_inner, s_outer, s_out, s_query, s_key, s_value, s_bias = finish(
-            here, total, got, start, hidden, local
+            here, total, got, d_total, d_got, hidden, local
         )
         s_outer = s_outer.T
         s_qkv = s_bias.reshape(-1)[: 3 * local]

time: 305 us -> 302 us (level)
  starting transfers between devices: 67.9 us -> 58.4 us
  waiting for transfers between devices: 79.7 us -> 87.2 us
    ppermute x47, starting transfers between devices: 42.2 us -> 32.5 us  [swap(): return lax.ppermute(value, axis, [(i, i ^ bit) for i in range(count)])]
    ppermute x12 -> x15, waiting for transfers between devices: 26.3 us -> 33.4 us  [shift(): lax.ppermute(value, axis, [(i, (i + step) % count) for i in range(count)])]
    unnamed x120 -> x128, local copies, waits for them, and re-layouts: 12.8 us -> 10.6 us
    pallas_call x2 -> x3, Pallas kernels: 6.21 us -> 7.7 us  [the longest x2 5.17 us: merge_two(): pl.pallas_call(lambda *refs: merge_two_kernel(*refs, pairs=len(parts) //...]
    ppermute x12 -> x15, starting transfers between devices: 25.7 us -> 25.8 us  [shift(): lax.ppermute(value, axis, [(i, (i + step) % count) for i in range(count)])]
  transfers between devices with their start and end apart: 59 -> 62, of which waited for: 22 -> 25; matrix products, arithmetic and copies ran while one was open for 5% -> 6% of each run, Pallas kernels for 31% -> 32%
where the time goes in v2:
time: 302 us; the launch traced here: 300 us
  Pallas kernels  123 us (41%)
  waiting for transfers between devices  87.2 us (29%)
  starting transfers between devices  58.4 us (19%)
  local copies, waits for them, and re-layouts  17.7 us (6%)
  other arithmetic  12 us (4%)
    ppermute x47, waiting for transfers between devices, swap(): return lax.ppermute(value, axis, [(i, i ^ bit) for i in range(count)])  53.8 us
    ppermute x15, waiting for transfers between devices, shift(): lax.ppermute(value, axis, [(i, (i + step) % count) for i in range(count)])  33.4 us
    ppermute x47, starting transfers between devices, swap(): return lax.ppermute(value, axis, [(i, i ^ bit) for i in range(count)])  32.5 us
    ppermute x15, starting transfers between devices, shift(): lax.ppermute(value, axis, [(i, (i + step) % count) for i in range(count)])  25.8 us
    pallas_call x1, Pallas kernels, feed(): pl.pallas_call(lambda *refs: feed_kernel(*refs, plan=plan, count=len(piec...  23.7 us
    pallas_call x1, Pallas kernels, attend_back(): pl.pallas_call(lambda *refs: attend_back_kernel(*refs, block=block, width...  22.7 us
    pallas_call x1, Pallas kernels, attend_far(): pl.pallas_call(lambda *refs: attend_far_kernel(*refs, block=block, width=...  17.2 us
    pallas_call x1, Pallas kernels, attend_near(): pl.pallas_call(lambda *refs: attend_near_kernel(*refs, block=block, width...  13.6 us
  transfers between devices with their start and end apart: 62, of which 25 were waited for; matrix products, arithmetic and copies ran while one was open for 6% of the time, Pallas kernels for 32%

profile of v2, /device:TPU:10, one launch (start us, length us, event | category | flops | bytes accessed | tf_op | source)
XLA Modules:
  0.0 300.2 jit_solution(6580786717727613684)
XLA Ops:
  0.7 1.2 pad_maximum_fusion.3
  3.1 2.6 collective-permute-start.4
  5.7 2.5 collective-permute-start.3
  8.9 1.1 constant_dynamic-slice_fusion.2
  10.0 1.6 collective-permute-start
  14.6 1.3 collective-permute-done.3
  16.0 1.4 collective-permute-start.9
  17.4 1.2 collective-permute-start.8
  18.6 1.5 collective-permute-start.6
  20.1 1.0 collective-permute-done
  21.2 1.1 or_convert_fusion
  22.4 0.9 select_convert_fusion.refs_6_
  23.4 0.9 pad_maximum_fusion.1.refs_4_
  24.4 4.2 %collective-permute-done.2.refs_9_ = bf16[200,1728]{1,0:T(8,128)(2,1)S(1)} collective-permute-done((bf16[200,1728]{1,0:T(8,128)(2,1)S(1)}, bf16[200,1728]{1,0:T(8,128)(2,1)S(1)}, u32[]{:S(2)}, u32[]{:S(2)}) %collective-permute-start.2) | collective-permute-done | bytes 691232 | tf_op jit(solution)/shard_map/ppermute | solution.py:36
  28.7 2.0 collective-permute-start.10
  31.6 17.2 %attend_far.1 = (bf16[384,192]{1,0:T(8,128)(2,1)}, bf16[384,192]{1,0:T(8,128)(2,1)}, f32[2,384,192]{2,1,0:T(8,128)}, bf16[3,2,384,128]{3,2,1,0:T(8,128)(2,1)}, b...) custom-call(s32[3]{0:T(128)} %pad_add_fusion.1.refs_0_.here, ...), custom_call_target="tpu_custom_call" | custom-call | flops 20000000000 | bytes 8388608 | tf_op jit(solution)/shard_map/attend_far/pallas_call | solution.py:227
  48.8 4.1 %collective-permute-start.7 = (bf16[96,1728]{1,0:T(8,128)(2,1)}, bf16[96,1728]{1,0:T(8,128)(2,1)}, u32[]{:S(2)}, u32[]{:S(2)}) collective-permute-start(bf16[96,1728]{1,0:T(8,128)(2,1)} %fusion.7), channel_id=1, source_target_pairs={{0,16},{8,24},{16,0},{24,8},{1,17},{9,25},{17,1},{25,9},{2,18},{10... | collective-permute-start | bytes 995336 | tf_op jit(solution)/shard_map/ppermute | solution.py:41
  53.0 1.0 constant_dynamic-update-slice_fusion.4
  54.0 1.0 constant_dynamic-update-slice_fusion.3.refs_11_
  55.0 4.6 %collective-permute-start.13 = (bf16[192,1728]{1,0:T(8,128)(2,1)S(1)}, bf16[192,1728]{1,0:T(8,128)(2,1)S(1)}, u32[]{:S(2)}, u32[]{:S(2)}) collective-permute-start(bf16[192,1728]{1,0:T(8,128)(2,1)S(1)} %constant_dynamic-update-slice_fusion.3.refs_11_), channel_id=1, source_target_pairs={{0,4},{4,0},{1,5},{5,1},{2,6},{6,2},{3,7},{7,3},{8,12},{12,8},{9,1... | collective-permute-start | bytes 1990664 | tf_op jit(solution)/shard_map/ppermute | solution.py:36
  59.7 13.6 %attend_near.1 = (bf16[384,192]{1,0:T(8,128)(2,1)}, bf16[384,192]{1,0:T(8,128)(2,1)}, f32[2,384,192]{2,1,0:T(8,128)}, bf16[3,2,384,128]{3,2,1,0:T(8,128)(2,1)}) custom-call(s32[3]{0:T(128)} %pad_add_fusion.1.refs_0_.here, s32[1536]{0:T(1024)} %copy-done.14, s32[2048]{0:T(1024)} %copy-done.13, bf16[3,2,384,128]{3,2,1,0:T(8,128)(2,1)} %get-tuple-element.133.refs_3_, ...), custom_call_target="tpu_custom_call" | custom-call | flops 12000000000 | bytes 8388608 | tf_op jit(solution)/shard_map/attend_near/pallas_call | solution.py:255
  73.6 0.9 collective-permute-done.13.refs_19_
  74.5 1.6 collective-permute-done.12.refs_17_
  76.6 4.2 %collective-permute-done.28.refs_27_ = bf16[96,1728]{1,0:T(8,128)(2,1)} collective-permute-done((bf16[96,1728]{1,0:T(8,128)(2,1)S(1)}, bf16[96,1728]{1,0:T(8,128)(2,1)}, u32[]{:S(2)}, u32[]{:S(2)}) %collective-permute-start.28) | collective-permute-done | bytes 331808 | tf_op jit(solution)/shard_map/ppermute | solution.py:41
  80.8 3.6 %collective-permute-start.26 = (bf16[96,1728]{1,0:T(8,128)(2,1)}, bf16[96,1728]{1,0:T(8,128)(2,1)}, u32[]{:S(2)}, u32[]{:S(2)}) collective-permute-start(bf16[96,1728]{1,0:T(8,128)(2,1)} %collective-permute-done.7.refs_21_), channel_id=1, source_target_pairs={{0,4},{4,0},{1,5},{5,1},{2,6},{6,2},{3,7},{7,3},{8,12},{12,8},{9,1... | collective-permute-start | bytes 995336 | tf_op jit(solution)/shard_map/ppermute | solution.py:36
  84.5 7.0 %collective-permute-done.16.refs_5_ = bf16[384,192]{1,0:T(8,128)(2,1)S(1)} collective-permute-done((bf16[384,192]{1,0:T(8,128)(2,1)S(1)}, bf16[384,192]{1,0:T(8,128)(2,1)S(1)}, u32[]{:S(2)}, u32[]{:S(2)}) %collective-permute-start.16) | collective-permute-done | bytes 147488 | tf_op jit(solution)/shard_map/ppermute | solution.py:36
  91.5 6.8 %collective-permute-done.17.refs_6_ = bf16[384,192]{1,0:T(8,128)(2,1)S(1)} collective-permute-done((bf16[384,192]{1,0:T(8,128)(2,1)S(1)}, bf16[384,192]{1,0:T(8,128)(2,1)S(1)}, u32[]{:S(2)}, u32[]{:S(2)}) %collective-permute-start.17) | collective-permute-done | bytes 147488 | tf_op jit(solution)/shard_map/ppermute | solution.py:36
  100.1 8.3 %collective-permute-done.24.refs_23_ = bf16[96,1728]{1,0:T(8,128)(2,1)} collective-permute-done((bf16[96,1728]{1,0:T(8,128)(2,1)}, bf16[96,1728]{1,0:T(8,128)(2,1)}, u32[]{:S(2)}, u32[]{:S(2)}) %collective-permute-start.24) | collective-permute-done | bytes 331808 | tf_op jit(solution)/shard_map/ppermute | solution.py:36
  113.2 23.7 %feed.1 = (bf16[384,768]{1,0:T(8,128)(2,1)}, f32[384,768]{1,0:T(8,128)}, f32[12,1,768]{2,1,0:T(1,128)}, bf16[384,192]{1,0:T(8,128)(2,1)}, bf16[384,192]{1,0:T(8,...) custom-call(s32[3]{0:T(128)} %pad_add_fusion.1.refs_0_.here, ...), custom_call_target="tpu_custom_call" | custom-call | flops 25999998976 | bytes 25165824 | tf_op jit(solution)/shard_map/feed/pallas_call | solution.py:433
  140.8 1.4 collective-permute-done.31.refs_4_
  142.7 2.3 collective-permute-done.30.refs_2_
  144.9 12.8 %unit_grads.1 = (bf16[4,96,1728]{2,1,0:T(8,128)(2,1)}, bf16[4,96,1728]{2,1,0:T(8,128)(2,1)}, bf16[2,2,96,1728]{3,2,1,0:T(8,128)(2,1)}, bf16[2,2,96,1728]{3,2,1,0:T(8,128)(2,1)}) custom-call(s32[3]{0:T(128)} %pad_add_fusion.1.refs_0_.here, bf16[3,768,384]{2,1,0:T(8,128)(2,1)} %get-tuple-element.152.refs_1_, ...), custom_call_target="tpu_custom_call" | custom-call | flops 12000000000 | bytes 14680064 | tf_op jit(solution)/shard_map/unit_grads/pallas_call | solution.py:520
  158.7 1.3 collective-permute-start.36
  160.8 22.7 %attend_back.1 = (bf16[1536,576]{1,0:T(8,128)(2,1)}, bf16[512,384]{1,0:T(8,128)(2,1)}) custom-call(s32[3]{0:T(128)} %pad_add_fusion.1.refs_0_.here, s32[1536]{0:T(1024)} %copy-done.14, s32[2048]{0:T(1024)} %copy-done.13, bf16[384,192]{1,0:T(8,128)(2,1)} %get-tuple-element.169.refs_3_, bf16[384,192]{1,0:T(8,128)(2,1)} %copy-done.50, ...), custom_call_target="tpu_custom_call" | custom-call | flops 24000000000 | bytes 8388608 | tf_op jit(solution)/shard_map/attend_back/pallas_call | solution.py:820
  183.6 7.7 %collective-permute-done.36.ga = bf16[4,96,1728]{2,1,0:T(8,128)(2,1)S(1)} collective-permute-done((bf16[4,96,1728]{2,1,0:T(8,128)(2,1)}, bf16[4,96,1728]{2,1,0:T(8,128)(2,1)S(1)}, u32[]{:S(2)}, u32[]{:S(2)}) %collective-permute-start.36) | collective-permute-done | bytes 1327136 | tf_op jit(solution)/shard_map/ppermute | solution.py:36
  193.0 1.2 collective-permute-start.40
  194.1 4.3 %merge_one.1 = (bf16[2,96,1728]{2,1,0:T(8,128)(2,1)}, bf16[2,96,1728]{2,1,0:T(8,128)(2,1)}, bf16[2,96,1728]{2,1,0:T(8,128)(2,1)}, bf16[2,96,1728]{2,1,0:T(8,128)(2,1)}) custom-call(s32[3]{0:T(128)} %pad_add_fusion.1.refs_0_.here, bf16[4,96,1728]{2,1,0:T(8,128)(2,1)} %get-tuple-element.188.ak, bf16[4,96,1728]{2,1,0:T(8,128)(2,1)} %copy-done.24, ...), custom_call_target="tpu_custom_call" | custom-call | flops 3000000000 | bytes 8388608 | tf_op jit(solution)/shard_map/merge_one/pallas_call | solution.py:561
  199.7 5.1 %collective-permute-done.40 = f32[8,768]{1,0:T(8,128)S(1)} collective-permute-done((f32[8,768]{1,0:T(8,128)S(1)}, f32[8,768]{1,0:T(8,128)S(1)}, u32[]{:S(2)}, u32[]{:S(2)}) %collective-permute-start.40) | collective-permute-done | bytes 24608 | tf_op jit(solution)/shard_map/ppermute | solution.py:36
  204.8 2.0 collective-permute-start.48
  206.8 9.5 %project_back.1 = (bf16[2,384,768]{2,1,0:T(8,128)(2,1)}, bf16[2,384,768]{2,1,0:T(8,128)(2,1)}, bf16[4,96,640]{2,1,0:T(8,128)(2,1)}, bf16[4,96,640]{2,1,0:T(8,128)(2,1)}) custom-call(s32[3]{0:T(128)} %pad_add_fusion.1.refs_0_.here, bf16[1536,576]{1,0:T(8,128)(2,1)} %get-tuple-element.178.refs_1_, bf16[512,384]{1,0:T(8,128)(2,1)} %copy-done.38, ...), custom_call_target="tpu_custom_call" | custom-call | flops 8999999488 | bytes 8388608 | tf_op jit(solution)/shard_map/project_back/pallas_call | solution.py:729
  217.6 0.9 collective-permute-start.41
  218.6 2.1 collective-permute-done.49
  220.7 1.9 fusion.3
  223.3 3.0 merge_two.2
  226.3 1.5 collective-permute-start.51
  227.8 3.1 %collective-permute-start.52 = (bf16[96,1728]{1,0:T(8,128)(2,1)}, bf16[96,1728]{1,0:T(8,128)(2,1)}, u32[]{:S(2)}, u32[]{:S(2)}) collective-permute-start(bf16[96,1728]{1,0:T(8,128)(2,1)} %get-tuple-element.209), channel_id=1, source_target_pairs={{0,16},{8,24},{16,0},{24,8},{1,17},{9,25},{17,1},{25,9},{2,18},{10... | collective-permute-start | bytes 995336 | tf_op jit(solution)/shard_map/ppermute | solution.py:41
  232.6 2.2 merge_two.3
  234.8 1.3 collective-permute-start.58
  236.1 15.1 %collective-permute-done.51.got_1 = bf16[96,1728]{1,0:T(8,128)(2,1)} collective-permute-done((bf16[96,1728]{1,0:T(8,128)(2,1)}, bf16[96,1728]{1,0:T(8,128)(2,1)}, u32[]{:S(2)}, u32[]{:S(2)}) %collective-permute-start.51) | collective-permute-done | bytes 331808 | tf_op jit(solution)/shard_map/ppermute | solution.py:41
  251.2 6.4 %collective-permute-done.52.got_2 = bf16[96,1728]{1,0:T(8,128)(2,1)} collective-permute-done((bf16[96,1728]{1,0:T(8,128)(2,1)}, bf16[96,1728]{1,0:T(8,128)(2,1)}, u32[]{:S(2)}, u32[]{:S(2)}) %collective-permute-start.52) | collective-permute-done | bytes 331808 | tf_op jit(solution)/shard_map/ppermute | solution.py:41
  257.6 3.0 %collective-permute-done.53.got_3 = bf16[96,1728]{1,0:T(8,128)(2,1)} collective-permute-done((bf16[96,1728]{1,0:T(8,128)(2,1)}, bf16[96,1728]{1,0:T(8,128)(2,1)}, u32[]{:S(2)}, u32[]{:S(2)}) %collective-permute-start.53) | collective-permute-done | bytes 331808 | tf_op jit(solution)/shard_map/ppermute | solution.py:41
  260.7 2.2 fusion.1.p_0
  262.9 1.3 collective-permute-start.55
  264.7 2.6 collective-permute-start.45
  267.2 2.2 collective-permute-done.60
  269.4 3.3 %collective-permute-start.46 = (bf16[96,640]{1,0:T(8,128)(2,1)S(1)}, bf16[96,640]{1,0:T(8,128)(2,1)S(1)}, u32[]{:S(2)}, u32[]{:S(2)}) collective-permute-start(bf16[96,640]{1,0:T(8,128)(2,1)S(1)} %copy-done.53), channel_id=1, source_target_pairs={{0,24},{8,0},{16,8},{24,16},{1,25},{9,1},{17,9},{25,17},{2,26},{10... | collective-permute-start | bytes 368648 | tf_op jit(solution)/shard_map/ppermute | solution.py:41
  273.2 2.5 collective-permute-done.45.got_2
  277.8 2.7 merge_three.3.own
  280.6 1.1 collective-permute-start.61
  281.6 1.9 merge_three.2.d_own
  283.5 0.9 collective-permute-start.47
  285.3 3.2 %spread.3 = bf16[1536,768]{1,0:T(8,128)(2,1)} custom-call(s32[3]{0:T(128)} %pad_add_fusion.1.refs_0_.here, bf16[384,768]{1,0:T(8,128)(2,1)} %get-tuple-element.215.p_0, bf16[384,768]{1,0:T(8,128)(2,1)} %copy-done.33, bf16[384,768]{1,0:T(8,128)(2,1)} %collective-permute-done.58.p_2, bf16[384,768]{1,0:T(8,128)(2,1)} %copy-done.34), custom_call_target="tpu_custom_call" | custom-call | flops 3000000000 | bytes 8388608 | tf_op jit(solution)/shard_map/spread/pallas_call | solution.py:671
  290.1 4.1 %spread.2 = f32[1536,768]{1,0:T(8,128)} custom-call(s32[3]{0:T(128)} %pad_add_fusion.1.refs_0_.here, bf16[384,768]{1,0:T(8,128)(2,1)} %fusion.1.p_0, bf16[384,768]{1,0:T(8,128)(2,1)} %copy-done.35, bf16[384,768]{1,0:T(8,128)(2,1)} %copy-done.32, bf16[384,768]{1,0:T(8,128)(2,1)} %copy-done.36), custom_call_target="tpu_custom_call" | custom-call | flops 3000000000 | bytes 8388608 | tf_op jit(solution)/shard_map/spread/pallas_call | solution.py:671
  295.6 2.5 finish.1
  (254 shorter events, 35.1 us)
Async XLA Ops:
  2.6 13.4 %collective-permute-start.5 = (bf16[1,96,576]{2,1,0:T(8,128)(2,1)S(1)}, bf16[1,96,576]{2,1,0:T(8,128)(2,1)S(1)}, u32[]{:S(2)}, u32[]{:S(2)}) collective-permute-start(bf16[1,96,576]{2,1,0:T(8,128)(2,1)S(1)} %constant_dynamic-slice_fusion.1), channel_id=1, source_target_pairs={{0,24},{8,0},{16,8},{24,16},{1,25},{9,1},{17,9},{25,17},{2,26},{10... | collective-permute-start | bytes 331784 | tf_op jit(solution)/shard_map/ppermute | solution.py:41
  3.1 12.8 %collective-permute-start.4 = (bf16[1,96,576]{2,1,0:T(8,128)(2,1)S(1)}, bf16[1,96,576]{2,1,0:T(8,128)(2,1)S(1)}, u32[]{:S(2)}, u32[]{:S(2)}) collective-permute-start(bf16[1,96,576]{2,1,0:T(8,128)(2,1)S(1)} %constant_dynamic-slice_fusion.1), channel_id=1, source_target_pairs={{0,16},{8,24},{16,0},{24,8},{1,17},{9,25},{17,1},{25,9},{2,18},{10... | collective-permute-start | bytes 331784 | tf_op jit(solution)/shard_map/ppermute | solution.py:41
  5.7 10.2 %collective-permute-start.3 = (bf16[1,96,576]{2,1,0:T(8,128)(2,1)S(1)}, bf16[1,96,576]{2,1,0:T(8,128)(2,1)S(1)}, u32[]{:S(2)}, u32[]{:S(2)}) collective-permute-start(bf16[1,96,576]{2,1,0:T(8,128)(2,1)S(1)} %constant_dynamic-slice_fusion.1), channel_id=1, source_target_pairs={{0,8},{8,16},{16,24},{24,0},{1,9},{9,17},{17,25},{25,1},{2,10},{10... | collective-permute-start | bytes 331784 | tf_op jit(solution)/shard_map/ppermute | solution.py:41
  10.0 11.1 %collective-permute-start = (bf16[272,768]{1,0:T(8,128)(2,1)S(1)}, bf16[272,768]{1,0:T(8,128)(2,1)S(1)}, u32[]{:S(2)}, u32[]{:S(2)}) collective-permute-start(bf16[272,768]{1,0:T(8,128)(2,1)S(1)} %fusion.5), channel_id=1, source_target_pairs={{0,4},{4,0},{1,5},{5,1},{2,6},{6,2},{3,7},{7,3},{8,12},{12,8},{9,1... | collective-permute-start | bytes 1253384 | tf_op jit(solution)/shard_map/ppermute | solution.py:36
  11.9 16.7 %collective-permute-start.2 = (bf16[200,1728]{1,0:T(8,128)(2,1)S(1)}, bf16[200,1728]{1,0:T(8,128)(2,1)S(1)}, u32[]{:S(2)}, u32[]{:S(2)}) collective-permute-start(bf16[200,1728]{1,0:T(8,128)(2,1)S(1)} %pad_maximum_fusion.2.refs_8_), channel_id=1, source_target_pairs={{0,2},{1,3},{2,0},{3,1},{4,6},{5,7},{6,4},{7,5},{8,10},{9,11},{10,... | collective-permute-start | bytes 2073608 | tf_op jit(solution)/shard_map/ppermute | solution.py:36
  16.0 32.8 %collective-permute-start.9 = (bf16[96,1728]{1,0:T(8,128)(2,1)}, bf16[96,1728]{1,0:T(8,128)(2,1)}, u32[]{:S(2)}, u32[]{:S(2)}) collective-permute-start(bf16[96,1728]{1,0:T(8,128)(2,1)} %fusion.7), channel_id=1, source_target_pairs={{0,24},{8,0},{16,8},{24,16},{1,25},{9,1},{17,9},{25,17},{2,26},{10... | collective-permute-start | bytes 995336 | tf_op jit(solution)/shard_map/ppermute | solution.py:41
  17.4 35.5 %collective-permute-start.8 = (bf16[96,1728]{1,0:T(8,128)(2,1)}, bf16[96,1728]{1,0:T(8,128)(2,1)}, u32[]{:S(2)}, u32[]{:S(2)}) collective-permute-start(bf16[96,1728]{1,0:T(8,128)(2,1)} %fusion.7), channel_id=1, source_target_pairs={{0,8},{8,16},{16,24},{24,0},{1,9},{9,17},{17,25},{25,1},{2,10},{10... | collective-permute-start | bytes 995336 | tf_op jit(solution)/shard_map/ppermute | solution.py:41
  18.6 12.3 %collective-permute-start.6 = (bf16[3,96,576]{2,1,0:T(8,128)(2,1)S(1)}, bf16[3,96,576]{2,1,0:T(8,128)(2,1)S(1)}, u32[]{:S(2)}, u32[]{:S(2)}) collective-permute-start(bf16[3,96,576]{2,1,0:T(8,128)(2,1)S(1)} %constant_dynamic-update-slice_fusion.refs_9_), channel_id=1, source_target_pairs={{0,4},{4,0},{1,5},{5,1},{2,6},{6,2},{3,7},{7,3},{8,12},{12,8},{9,1... | collective-permute-start | bytes 995336 | tf_op jit(solution)/shard_map/ppermute | solution.py:36
  21.1 2.2 collective-permute-start.1
  28.6 24.4 %collective-permute-start.11 = (bf16[96,1728]{1,0:T(8,128)(2,1)S(1)}, bf16[96,1728]{1,0:T(8,128)(2,1)}, u32[]{:S(2)}, u32[]{:S(2)}) collective-permute-start(bf16[96,1728]{1,0:T(8,128)(2,1)S(1)} %constant_dynamic-slice_fusion), channel_id=1, source_target_pairs={{0,24},{8,0},{16,8},{24,16},{1,25},{9,1},{17,9},{25,17},{2,26},{10... | collective-permute-start | bytes 995336 | tf_op jit(solution)/shard_map/ppermute | solution.py:41
  28.7 24.3 %collective-permute-start.10 = (bf16[96,1728]{1,0:T(8,128)(2,1)S(1)}, bf16[96,1728]{1,0:T(8,128)(2,1)}, u32[]{:S(2)}, u32[]{:S(2)}) collective-permute-start(bf16[96,1728]{1,0:T(8,128)(2,1)S(1)} %constant_dynamic-slice_fusion), channel_id=1, source_target_pairs={{0,8},{8,16},{16,24},{24,0},{1,9},{9,17},{17,25},{25,1},{2,10},{10... | collective-permute-start | bytes 995336 | tf_op jit(solution)/shard_map/ppermute | solution.py:41
  30.9 28.8 %collective-permute-start.14 = (bf16[400,1728]{1,0:T(8,128)(2,1)S(1)}, bf16[400,1728]{1,0:T(8,128)(2,1)}, u32[]{:S(2)}, u32[]{:S(2)}) collective-permute-start(bf16[400,1728]{1,0:T(8,128)(2,1)S(1)} %pad_maximum_fusion), channel_id=1, source_target_pairs={{0,1},{1,0},{2,3},{3,2},{4,5},{5,4},{6,7},{7,6},{8,9},{9,8},{10,11... | collective-permute-start | bytes 4147208 | tf_op jit(solution)/shard_map/ppermute | solution.py:36
  48.8 24.8 %collective-permute-start.7 = (bf16[96,1728]{1,0:T(8,128)(2,1)}, bf16[96,1728]{1,0:T(8,128)(2,1)}, u32[]{:S(2)}, u32[]{:S(2)}) collective-permute-start(bf16[96,1728]{1,0:T(8,128)(2,1)} %fusion.7), channel_id=1, source_target_pairs={{0,16},{8,24},{16,0},{24,8},{1,17},{9,25},{17,1},{25,9},{2,18},{10... | collective-permute-start | bytes 995336 | tf_op jit(solution)/shard_map/ppermute | solution.py:41
  52.9 27.8 %collective-permute-start.28 = (bf16[96,1728]{1,0:T(8,128)(2,1)S(1)}, bf16[96,1728]{1,0:T(8,128)(2,1)}, u32[]{:S(2)}, u32[]{:S(2)}) collective-permute-start(bf16[96,1728]{1,0:T(8,128)(2,1)S(1)} %constant_dynamic-slice_fusion), channel_id=1, source_target_pairs={{0,16},{8,24},{16,0},{24,8},{1,17},{9,25},{17,1},{25,9},{2,18},{10... | collective-permute-start | bytes 995336 | tf_op jit(solution)/shard_map/ppermute | solution.py:41
  55.0 19.5 %collective-permute-start.13 = (bf16[192,1728]{1,0:T(8,128)(2,1)S(1)}, bf16[192,1728]{1,0:T(8,128)(2,1)S(1)}, u32[]{:S(2)}, u32[]{:S(2)}) collective-permute-start(bf16[192,1728]{1,0:T(8,128)(2,1)S(1)} %constant_dynamic-update-slice_fusion.3.refs_11_), channel_id=1, source_target_pairs={{0,4},{4,0},{1,5},{5,1},{2,6},{6,2},{3,7},{7,3},{8,12},{12,8},{9,1... | collective-permute-start | bytes 1990664 | tf_op jit(solution)/shard_map/ppermute | solution.py:36
  59.7 16.4 %collective-permute-start.12 = (bf16[192,1728]{1,0:T(8,128)(2,1)S(1)}, bf16[192,1728]{1,0:T(8,128)(2,1)}, u32[]{:S(2)}, u32[]{:S(2)}) collective-permute-start(bf16[192,1728]{1,0:T(8,128)(2,1)S(1)} %constant_dynamic-update-slice_fusion.3.refs_11_), channel_id=1, source_target_pairs={{0,2},{1,3},{2,0},{3,1},{4,6},{5,7},{6,4},{7,5},{8,10},{9,11},{10,... | collective-permute-start | bytes 1990664 | tf_op jit(solution)/shard_map/ppermute | solution.py:36
  59.7 50.0 %copy-start.21 = (bf16[768]{0:T(1024)(128)(2,1)S(1)}, bf16[768]{0:T(1024)(128)(2,1)}, u32[]{:S(2)}) copy-start(bf16[768]{0:T(1024)(128)(2,1)} %param.33) | copy-start | bytes 4612
  59.7 50.0 %copy-start.22 = (bf16[768]{0:T(1024)(128)(2,1)S(1)}, bf16[768]{0:T(1024)(128)(2,1)}, u32[]{:S(2)}) copy-start(bf16[768]{0:T(1024)(128)(2,1)} %param.34) | copy-start | bytes 4612
  76.1 8.3 %collective-permute-start.15 = (bf16[384,192]{1,0:T(8,128)(2,1)}, bf16[384,192]{1,0:T(8,128)(2,1)S(1)}, u32[]{:S(2)}, u32[]{:S(2)}) collective-permute-start(bf16[384,192]{1,0:T(8,128)(2,1)} %get-tuple-element.140), channel_id=1, source_target_pairs={{0,1},{1,0},{2,3},{3,2},{4,5},{5,4},{6,7},{7,6},{8,9},{9,8},{10,11... | collective-permute-start | bytes 442376 | tf_op jit(solution)/shard_map/ppermute | solution.py:36
  76.1 22.6 %collective-permute-start.19 = (bf16[96,1728]{1,0:T(8,128)(2,1)}, bf16[96,1728]{1,0:T(8,128)(2,1)S(1)}, u32[]{:S(2)}, u32[]{:S(2)}) collective-permute-start(bf16[96,1728]{1,0:T(8,128)(2,1)} %collective-permute-done.10.refs_13_), channel_id=1, source_target_pairs={{0,1},{1,0},{2,3},{3,2},{4,5},{5,4},{6,7},{7,6},{8,9},{9,8},{10,11... | collective-permute-start | bytes 995336 | tf_op jit(solution)/shard_map/ppermute | solution.py:36
  76.6 22.9 %collective-permute-start.20 = (bf16[96,1728]{1,0:T(8,128)(2,1)}, bf16[96,1728]{1,0:T(8,128)(2,1)S(1)}, u32[]{:S(2)}, u32[]{:S(2)}) collective-permute-start(bf16[96,1728]{1,0:T(8,128)(2,1)} %collective-permute-done.11.refs_15_), channel_id=1, source_target_pairs={{0,1},{1,0},{2,3},{3,2},{4,5},{5,4},{6,7},{7,6},{8,9},{9,8},{10,11... | collective-permute-start | bytes 995336 | tf_op jit(solution)/shard_map/ppermute | solution.py:36
  80.8 18.8 %collective-permute-start.29 = (bf16[96,1728]{1,0:T(8,128)(2,1)}, bf16[96,1728]{1,0:T(8,128)(2,1)S(1)}, u32[]{:S(2)}, u32[]{:S(2)}) collective-permute-start(bf16[96,1728]{1,0:T(8,128)(2,1)} %collective-permute-done.28.refs_27_), channel_id=1, source_target_pairs={{0,1},{1,0},{2,3},{3,2},{4,5},{5,4},{6,7},{7,6},{8,9},{9,8},{10,11... | collective-permute-start | bytes 995336 | tf_op jit(solution)/shard_map/ppermute | solution.py:36
  80.8 19.3 %collective-permute-start.26 = (bf16[96,1728]{1,0:T(8,128)(2,1)}, bf16[96,1728]{1,0:T(8,128)(2,1)}, u32[]{:S(2)}, u32[]{:S(2)}) collective-permute-start(bf16[96,1728]{1,0:T(8,128)(2,1)} %collective-permute-done.7.refs_21_), channel_id=1, source_target_pairs={{0,4},{4,0},{1,5},{5,1},{2,6},{6,2},{3,7},{7,3},{8,12},{12,8},{9,1... | collective-permute-start | bytes 995336 | tf_op jit(solution)/shard_map/ppermute | solution.py:36
  84.4 7.1 %collective-permute-start.16 = (bf16[384,192]{1,0:T(8,128)(2,1)S(1)}, bf16[384,192]{1,0:T(8,128)(2,1)S(1)}, u32[]{:S(2)}, u32[]{:S(2)}) collective-permute-start(bf16[384,192]{1,0:T(8,128)(2,1)S(1)} %copy-done.49), channel_id=1, source_target_pairs={{0,2},{1,3},{2,0},{3,1},{4,6},{5,7},{6,4},{7,5},{8,10},{9,11},{10,... | collective-permute-start | bytes 442376 | tf_op jit(solution)/shard_map/ppermute | solution.py:36
  91.5 6.8 %collective-permute-start.17 = (bf16[384,192]{1,0:T(8,128)(2,1)S(1)}, bf16[384,192]{1,0:T(8,128)(2,1)S(1)}, u32[]{:S(2)}, u32[]{:S(2)}) collective-permute-start(bf16[384,192]{1,0:T(8,128)(2,1)S(1)} %copy-done.47), channel_id=1, source_target_pairs={{0,3},{1,2},{2,1},{3,0},{4,7},{5,6},{6,5},{7,4},{8,11},{9,10},{10,... | collective-permute-start | bytes 442376 | tf_op jit(solution)/shard_map/ppermute | solution.py:36
  98.4 10.0 %collective-permute-start.24 = (bf16[96,1728]{1,0:T(8,128)(2,1)}, bf16[96,1728]{1,0:T(8,128)(2,1)}, u32[]{:S(2)}, u32[]{:S(2)}) collective-permute-start(bf16[96,1728]{1,0:T(8,128)(2,1)} %collective-permute-done.7.refs_21_), channel_id=1, source_target_pairs={{0,2},{1,3},{2,0},{3,1},{4,6},{5,7},{6,4},{7,5},{8,10},{9,11},{10,... | collective-permute-start | bytes 995336 | tf_op jit(solution)/shard_map/ppermute | solution.py:36
  98.7 9.7 %collective-permute-start.23 = (bf16[96,1728]{1,0:T(8,128)(2,1)}, bf16[96,1728]{1,0:T(8,128)(2,1)S(1)}, u32[]{:S(2)}, u32[]{:S(2)}) collective-permute-start(bf16[96,1728]{1,0:T(8,128)(2,1)} %collective-permute-done.7.refs_21_), channel_id=1, source_target_pairs={{0,1},{1,0},{2,3},{3,2},{4,5},{5,4},{6,7},{7,6},{8,9},{9,8},{10,11... | collective-permute-start | bytes 995336 | tf_op jit(solution)/shard_map/ppermute | solution.py:36
  99.4 11.8 %collective-permute-start.18 = (bf16[192,1728]{1,0:T(8,128)(2,1)S(1)}, bf16[192,1728]{1,0:T(8,128)(2,1)S(1)}, u32[]{:S(2)}, u32[]{:S(2)}) collective-permute-start(bf16[192,1728]{1,0:T(8,128)(2,1)S(1)} %constant_dynamic-update-slice_fusion.3.refs_11_), channel_id=1, source_target_pairs={{0,1},{1,0},{2,3},{3,2},{4,5},{5,4},{6,7},{7,6},{8,9},{9,8},{10,11... | collective-permute-start | bytes 1990664 | tf_op jit(solution)/shard_map/ppermute | solution.py:36
  99.5 11.7 %collective-permute-start.21 = (bf16[192,1728]{1,0:T(8,128)(2,1)}, bf16[192,1728]{1,0:T(8,128)(2,1)S(1)}, u32[]{:S(2)}, u32[]{:S(2)}) collective-permute-start(bf16[192,1728]{1,0:T(8,128)(2,1)} %collective-permute-done.12.refs_17_), channel_id=1, source_target_pairs={{0,1},{1,0},{2,3},{3,2},{4,5},{5,4},{6,7},{7,6},{8,9},{9,8},{10,11... | collective-permute-start | bytes 1990664 | tf_op jit(solution)/shard_map/ppermute | solution.py:36
  100.0 11.3 %collective-permute-start.22 = (bf16[192,1728]{1,0:T(8,128)(2,1)S(1)}, bf16[192,1728]{1,0:T(8,128)(2,1)S(1)}, u32[]{:S(2)}, u32[]{:S(2)}) collective-permute-start(bf16[192,1728]{1,0:T(8,128)(2,1)S(1)} %collective-permute-done.13.refs_19_), channel_id=1, source_target_pairs={{0,1},{1,0},{2,3},{3,2},{4,5},{5,4},{6,7},{7,6},{8,9},{9,8},{10,11... | collective-permute-start | bytes 1990664 | tf_op jit(solution)/shard_map/ppermute | solution.py:36
  108.4 2.0 collective-permute-start.27
  109.2 2.1 collective-permute-start.25
  136.9 5.4 %collective-permute-start.31 = (bf16[2,384,1792]{2,1,0:T(8,128)(2,1)}, bf16[2,384,1792]{2,1,0:T(8,128)(2,1)S(1)}, u32[]{:S(2)}, u32[]{:S(2)}) collective-permute-start(bf16[2,384,1792]{2,1,0:T(8,128)(2,1)} %get-tuple-element.154), channel_id=1, source_target_pairs={{0,1},{1,0},{2,3},{3,2},{4,5},{5,4},{6,7},{7,6},{8,9},{9,8},{10,11... | collective-permute-start | bytes 8257544 | tf_op jit(solution)/shard_map/ppermute | solution.py:36
  137.3 7.6 %collective-permute-start.30 = (bf16[3,768,384]{2,1,0:T(8,128)(2,1)}, bf16[3,768,384]{2,1,0:T(8,128)(2,1)}, u32[]{:S(2)}, u32[]{:S(2)}) collective-permute-start(bf16[3,768,384]{2,1,0:T(8,128)(2,1)} %get-tuple-element.152.refs_1_), channel_id=1, source_target_pairs={{0,1},{1,0},{2,3},{3,2},{4,5},{5,4},{6,7},{7,6},{8,9},{9,8},{10,11... | collective-permute-start | bytes 5308424 | tf_op jit(solution)/shard_map/ppermute | solution.py:36
  138.2 19.5 %collective-permute-start.33 = (bf16[384,192]{1,0:T(8,128)(2,1)}, bf16[384,192]{1,0:T(8,128)(2,1)S(1)}, u32[]{:S(2)}, u32[]{:S(2)}) collective-permute-start(bf16[384,192]{1,0:T(8,128)(2,1)} %get-tuple-element.160), channel_id=1, source_target_pairs={{0,1},{1,0},{2,3},{3,2},{4,5},{5,4},{6,7},{7,6},{8,9},{9,8},{10,11... | collective-permute-start | bytes 442376 | tf_op jit(solution)/shard_map/ppermute | solution.py:36
  138.7 19.1 %collective-permute-start.34 = (bf16[384,192]{1,0:T(8,128)(2,1)}, bf16[384,192]{1,0:T(8,128)(2,1)S(1)}, u32[]{:S(2)}, u32[]{:S(2)}) collective-permute-start(bf16[384,192]{1,0:T(8,128)(2,1)} %get-tuple-element.161), channel_id=1, source_target_pairs={{0,2},{1,3},{2,0},{3,1},{4,6},{5,7},{6,4},{7,5},{8,10},{9,11},{10,... | collective-permute-start | bytes 442376 | tf_op jit(solution)/shard_map/ppermute | solution.py:36
  139.4 18.4 %collective-permute-start.35 = (bf16[384,192]{1,0:T(8,128)(2,1)}, bf16[384,192]{1,0:T(8,128)(2,1)S(1)}, u32[]{:S(2)}, u32[]{:S(2)}) collective-permute-start(bf16[384,192]{1,0:T(8,128)(2,1)} %get-tuple-element.162), channel_id=1, source_target_pairs={{0,3},{1,2},{2,1},{3,0},{4,7},{5,6},{6,5},{7,4},{8,11},{9,10},{10,... | collective-permute-start | bytes 442376 | tf_op jit(solution)/shard_map/ppermute | solution.py:36
  142.3 15.5 %collective-permute-start.32 = (f32[8,768]{1,0:T(8,128)S(1)}, f32[8,768]{1,0:T(8,128)S(1)}, u32[]{:S(2)}, u32[]{:S(2)}) collective-permute-start(f32[8,768]{1,0:T(8,128)S(1)} %pad_maximum_fusion.4), channel_id=1, source_target_pairs={{0,1},{1,0},{2,3},{3,2},{4,5},{5,4},{6,7},{7,6},{8,9},{9,8},{10,11... | collective-permute-start | bytes 73736 | tf_op jit(solution)/shard_map/ppermute | solution.py:36
  157.9 25.7 %collective-permute-start.38 = (f32[8,768]{1,0:T(8,128)S(1)}, f32[8,768]{1,0:T(8,128)S(1)}, u32[]{:S(2)}, u32[]{:S(2)}) collective-permute-start(f32[8,768]{1,0:T(8,128)S(1)} %pad_maximum_fusion.5), channel_id=1, source_target_pairs={{0,2},{1,3},{2,0},{3,1},{4,6},{5,7},{6,4},{7,5},{8,10},{9,11},{10,... | collective-permute-start | bytes 73736 | tf_op jit(solution)/shard_map/ppermute | solution.py:36
  158.7 32.6 %collective-permute-start.36 = (bf16[4,96,1728]{2,1,0:T(8,128)(2,1)}, bf16[4,96,1728]{2,1,0:T(8,128)(2,1)S(1)}, u32[]{:S(2)}, u32[]{:S(2)}) collective-permute-start(bf16[4,96,1728]{2,1,0:T(8,128)(2,1)} %get-tuple-element.180), channel_id=1, source_target_pairs={{0,2},{1,3},{2,0},{3,1},{4,6},{5,7},{6,4},{7,5},{8,10},{9,11},{10,... | collective-permute-start | bytes 3981320 | tf_op jit(solution)/shard_map/ppermute | solution.py:36
  160.0 32.1 %collective-permute-start.37 = (bf16[2,2,96,1728]{3,2,1,0:T(8,128)(2,1)}, bf16[2,2,96,1728]{3,2,1,0:T(8,128)(2,1)S(1)}, u32[]{:S(2)}, u32[]{:S(2)}) collective-permute-start(bf16[2,2,96,1728]{3,2,1,0:T(8,128)(2,1)} %get-tuple-element.181), channel_id=1, source_target_pairs={{0,4},{4,0},{1,5},{5,1},{2,6},{6,2},{3,7},{7,3},{8,12},{12,8},{9,1... | collective-permute-start | bytes 3981320 | tf_op jit(solution)/shard_map/ppermute | solution.py:36
  192.1 12.7 %collective-permute-start.39 = (bf16[512,384]{1,0:T(8,128)(2,1)}, bf16[512,384]{1,0:T(8,128)(2,1)S(1)}, u32[]{:S(2)}, u32[]{:S(2)}) collective-permute-start(bf16[512,384]{1,0:T(8,128)(2,1)} %get-tuple-element.187), channel_id=1, source_target_pairs={{0,4},{4,0},{1,5},{5,1},{2,6},{6,2},{3,7},{7,3},{8,12},{12,8},{9,1... | collective-permute-start | bytes 1179656 | tf_op jit(solution)/shard_map/ppermute | solution.py:36
  193.0 11.9 %collective-permute-start.40 = (f32[8,768]{1,0:T(8,128)S(1)}, f32[8,768]{1,0:T(8,128)S(1)}, u32[]{:S(2)}, u32[]{:S(2)}) collective-permute-start(f32[8,768]{1,0:T(8,128)S(1)} %add.60), channel_id=1, source_target_pairs={{0,4},{4,0},{1,5},{5,1},{2,6},{6,2},{3,7},{7,3},{8,12},{12,8},{9,1... | collective-permute-start | bytes 73736 | tf_op jit(solution)/shard_map/ppermute | solution.py:36
  198.5 19.1 %collective-permute-start.42 = (bf16[2,96,1728]{2,1,0:T(8,128)(2,1)}, bf16[2,96,1728]{2,1,0:T(8,128)(2,1)S(1)}, u32[]{:S(2)}, u32[]{:S(2)}) collective-permute-start(bf16[2,96,1728]{2,1,0:T(8,128)(2,1)} %get-tuple-element.190), channel_id=1, source_target_pairs={{0,4},{4,0},{1,5},{5,1},{2,6},{6,2},{3,7},{7,3},{8,12},{12,8},{9,1... | collective-permute-start | bytes 1990664 | tf_op jit(solution)/shard_map/ppermute | solution.py:36
  199.3 18.2 %collective-permute-start.43 = (bf16[2,96,1728]{2,1,0:T(8,128)(2,1)}, bf16[2,96,1728]{2,1,0:T(8,128)(2,1)S(1)}, u32[]{:S(2)}, u32[]{:S(2)}) collective-permute-start(bf16[2,96,1728]{2,1,0:T(8,128)(2,1)} %get-tuple-element.191), channel_id=1, source_target_pairs={{0,2},{1,3},{2,0},{3,1},{4,6},{5,7},{6,4},{7,5},{8,10},{9,11},{10,... | collective-permute-start | bytes 1990664 | tf_op jit(solution)/shard_map/ppermute | solution.py:36
  204.8 11.5 %collective-permute-start.48 = (f32[8,768]{1,0:T(8,128)S(1)}, f32[8,768]{1,0:T(8,128)S(1)}, u32[]{:S(2)}, u32[]{:S(2)}) collective-permute-start(f32[8,768]{1,0:T(8,128)S(1)} %add.61), channel_id=1, source_target_pairs={{0,8},{8,0},{16,24},{24,16},{1,9},{9,1},{17,25},{25,17},{2,10},{10... | collective-permute-start | bytes 73736 | tf_op jit(solution)/shard_map/ppermute | solution.py:36
  217.6 3.1 %collective-permute-start.49 = (bf16[2,384,768]{2,1,0:T(8,128)(2,1)}, bf16[2,384,768]{2,1,0:T(8,128)(2,1)S(1)}, u32[]{:S(2)}, u32[]{:S(2)}) collective-permute-start(bf16[2,384,768]{2,1,0:T(8,128)(2,1)} %get-tuple-element.207), channel_id=1, source_target_pairs={{0,1},{1,0},{2,3},{3,2},{4,5},{5,4},{6,7},{7,6},{8,9},{9,8},{10,11... | collective-permute-start | bytes 3538952 | tf_op jit(solution)/shard_map/ppermute | solution.py:36
  217.6 14.2 %collective-permute-start.41 = (bf16[4,96,640]{2,1,0:T(8,128)(2,1)}, bf16[4,96,640]{2,1,0:T(8,128)(2,1)S(1)}, u32[]{:S(2)}, u32[]{:S(2)}) collective-permute-start(bf16[4,96,640]{2,1,0:T(8,128)(2,1)} %get-tuple-element.195), channel_id=1, source_target_pairs={{0,4},{4,0},{1,5},{5,1},{2,6},{6,2},{3,7},{7,3},{8,12},{12,8},{9,1... | collective-permute-start | bytes 1474568 | tf_op jit(solution)/shard_map/ppermute | solution.py:36
  222.6 38.1 %collective-permute-start.50 = (bf16[384,768]{1,0:T(8,128)(2,1)}, bf16[384,768]{1,0:T(8,128)(2,1)}, u32[]{:S(2)}, u32[]{:S(2)}) collective-permute-start(bf16[384,768]{1,0:T(8,128)(2,1)} %fusion.3), channel_id=1, source_target_pairs={{0,2},{1,3},{2,0},{3,1},{4,6},{5,7},{6,4},{7,5},{8,10},{9,11},{10,... | collective-permute-start | bytes 1769480 | tf_op jit(solution)/shard_map/ppermute | solution.py:36
  226.3 24.9 %collective-permute-start.51 = (bf16[96,1728]{1,0:T(8,128)(2,1)}, bf16[96,1728]{1,0:T(8,128)(2,1)}, u32[]{:S(2)}, u32[]{:S(2)}) collective-permute-start(bf16[96,1728]{1,0:T(8,128)(2,1)} %get-tuple-element.208), channel_id=1, source_target_pairs={{0,8},{8,16},{16,24},{24,0},{1,9},{9,17},{17,25},{25,1},{2,10},{10... | collective-permute-start | bytes 995336 | tf_op jit(solution)/shard_map/ppermute | solution.py:41
  227.8 29.8 %collective-permute-start.52 = (bf16[96,1728]{1,0:T(8,128)(2,1)}, bf16[96,1728]{1,0:T(8,128)(2,1)}, u32[]{:S(2)}, u32[]{:S(2)}) collective-permute-start(bf16[96,1728]{1,0:T(8,128)(2,1)} %get-tuple-element.209), channel_id=1, source_target_pairs={{0,16},{8,24},{16,0},{24,8},{1,17},{9,25},{17,1},{25,9},{2,18},{10... | collective-permute-start | bytes 995336 | tf_op jit(solution)/shard_map/ppermute | solution.py:41
  231.0 29.7 %collective-permute-start.53 = (bf16[96,1728]{1,0:T(8,128)(2,1)}, bf16[96,1728]{1,0:T(8,128)(2,1)}, u32[]{:S(2)}, u32[]{:S(2)}) collective-permute-start(bf16[96,1728]{1,0:T(8,128)(2,1)} %get-tuple-element.210), channel_id=1, source_target_pairs={{0,24},{8,0},{16,8},{24,16},{1,25},{9,1},{17,9},{25,17},{2,26},{10... | collective-permute-start | bytes 995336 | tf_op jit(solution)/shard_map/ppermute | solution.py:41
  234.8 37.9 %collective-permute-start.58 = (bf16[384,768]{1,0:T(8,128)(2,1)}, bf16[384,768]{1,0:T(8,128)(2,1)}, u32[]{:S(2)}, u32[]{:S(2)}) collective-permute-start(bf16[384,768]{1,0:T(8,128)(2,1)} %get-tuple-element.215.p_0), channel_id=1, source_target_pairs={{0,2},{1,3},{2,0},{3,1},{4,6},{5,7},{6,4},{7,5},{8,10},{9,11},{10,... | collective-permute-start | bytes 1769480 | tf_op jit(solution)/shard_map/ppermute | solution.py:36
  262.9 14.9 %collective-permute-start.55 = (bf16[384,768]{1,0:T(8,128)(2,1)}, bf16[384,768]{1,0:T(8,128)(2,1)S(1)}, u32[]{:S(2)}, u32[]{:S(2)}) collective-permute-start(bf16[384,768]{1,0:T(8,128)(2,1)} %fusion.1.p_0), channel_id=1, source_target_pairs={{0,2},{1,3},{2,0},{3,1},{4,6},{5,7},{6,4},{7,5},{8,10},{9,11},{10,... | collective-permute-start | bytes 1769480 | tf_op jit(solution)/shard_map/ppermute | solution.py:36
  264.2 8.5 %collective-permute-start.44 = (bf16[96,640]{1,0:T(8,128)(2,1)S(1)}, bf16[96,640]{1,0:T(8,128)(2,1)S(1)}, u32[]{:S(2)}, u32[]{:S(2)}) collective-permute-start(bf16[96,640]{1,0:T(8,128)(2,1)S(1)} %copy-done.56), channel_id=1, source_target_pairs={{0,8},{8,16},{16,24},{24,0},{1,9},{9,17},{17,25},{25,1},{2,10},{10... | collective-permute-start | bytes 368648 | tf_op jit(solution)/shard_map/ppermute | solution.py:41
  264.2 5.2 %collective-permute-start.60 = (f32[8,768]{1,0:T(8,128)S(1)}, f32[8,768]{1,0:T(8,128)S(1)}, u32[]{:S(2)}, u32[]{:S(2)}) collective-permute-start(f32[8,768]{1,0:T(8,128)S(1)} %copy-done.11), channel_id=1, source_target_pairs={{0,16},{8,24},{16,0},{24,8},{1,17},{9,25},{17,1},{25,9},{2,18},{10... | collective-permute-start | bytes 73736 | tf_op jit(solution)/shard_map/ppermute | solution.py:36
  264.7 11.1 %collective-permute-start.45 = (bf16[96,640]{1,0:T(8,128)(2,1)S(1)}, bf16[96,640]{1,0:T(8,128)(2,1)}, u32[]{:S(2)}, u32[]{:S(2)}) collective-permute-start(bf16[96,640]{1,0:T(8,128)(2,1)S(1)} %copy-done.54), channel_id=1, source_target_pairs={{0,16},{8,24},{16,0},{24,8},{1,17},{9,25},{17,1},{25,9},{2,18},{10... | collective-permute-start | bytes 368648 | tf_op jit(solution)/shard_map/ppermute | solution.py:41
  269.4 7.0 %collective-permute-start.46 = (bf16[96,640]{1,0:T(8,128)(2,1)S(1)}, bf16[96,640]{1,0:T(8,128)(2,1)S(1)}, u32[]{:S(2)}, u32[]{:S(2)}) collective-permute-start(bf16[96,640]{1,0:T(8,128)(2,1)S(1)} %copy-done.53), channel_id=1, source_target_pairs={{0,24},{8,0},{16,8},{24,16},{1,25},{9,1},{17,9},{25,17},{2,26},{10... | collective-permute-start | bytes 368648 | tf_op jit(solution)/shard_map/ppermute | solution.py:41
  272.7 10.8 %collective-permute-start.57 = (bf16[384,768]{1,0:T(8,128)(2,1)}, bf16[384,768]{1,0:T(8,128)(2,1)S(1)}, u32[]{:S(2)}, u32[]{:S(2)}) collective-permute-start(bf16[384,768]{1,0:T(8,128)(2,1)} %get-tuple-element.215.p_0), channel_id=1, source_target_pairs={{0,1},{1,0},{2,3},{3,2},{4,5},{5,4},{6,7},{7,6},{8,9},{9,8},{10,11... | collective-permute-start | bytes 1769480 | tf_op jit(solution)/shard_map/ppermute | solution.py:36
  272.7 11.7 %collective-permute-start.59 = (bf16[384,768]{1,0:T(8,128)(2,1)}, bf16[384,768]{1,0:T(8,128)(2,1)S(1)}, u32[]{:S(2)}, u32[]{:S(2)}) collective-permute-start(bf16[384,768]{1,0:T(8,128)(2,1)} %collective-permute-done.58.p_2), channel_id=1, source_target_pairs={{0,1},{1,0},{2,3},{3,2},{4,5},{5,4},{6,7},{7,6},{8,9},{9,8},{10,11... | collective-permute-start | bytes 1769480 | tf_op jit(solution)/shard_map/ppermute | solution.py:36
  275.8 12.7 %collective-permute-start.54 = (bf16[384,768]{1,0:T(8,128)(2,1)}, bf16[384,768]{1,0:T(8,128)(2,1)S(1)}, u32[]{:S(2)}, u32[]{:S(2)}) collective-permute-start(bf16[384,768]{1,0:T(8,128)(2,1)} %fusion.1.p_0), channel_id=1, source_target_pairs={{0,1},{1,0},{2,3},{3,2},{4,5},{5,4},{6,7},{7,6},{8,9},{9,8},{10,11... | collective-permute-start | bytes 1769480 | tf_op jit(solution)/shard_map/ppermute | solution.py:36
  277.8 10.6 %collective-permute-start.56 = (bf16[384,768]{1,0:T(8,128)(2,1)S(1)}, bf16[384,768]{1,0:T(8,128)(2,1)S(1)}, u32[]{:S(2)}, u32[]{:S(2)}) collective-permute-start(bf16[384,768]{1,0:T(8,128)(2,1)S(1)} %collective-permute-done.55.p_2), channel_id=1, source_target_pairs={{0,1},{1,0},{2,3},{3,2},{4,5},{5,4},{6,7},{7,6},{8,9},{9,8},{10,11... | collective-permute-start | bytes 1769480 | tf_op jit(solution)/shard_map/ppermute | solution.py:36
  280.6 14.3 %collective-permute-start.61 = (bf16[96,1728]{1,0:T(8,128)(2,1)}, bf16[96,1728]{1,0:T(8,128)(2,1)S(1)}, u32[]{:S(2)}, u32[]{:S(2)}) collective-permute-start(bf16[96,1728]{1,0:T(8,128)(2,1)} %merge_three.3.own), channel_id=1, source_target_pairs={{0,4},{4,0},{1,5},{5,1},{2,6},{6,2},{3,7},{7,3},{8,12},{12,8},{9,1... | collective-permute-start | bytes 995336 | tf_op jit(solution)/shard_map/ppermute | solution.py:36
  283.5 10.7 %collective-permute-start.47 = (bf16[96,640]{1,0:T(8,128)(2,1)}, bf16[96,640]{1,0:T(8,128)(2,1)S(1)}, u32[]{:S(2)}, u32[]{:S(2)}) collective-permute-start(bf16[96,640]{1,0:T(8,128)(2,1)} %merge_three.2.d_own), channel_id=1, source_target_pairs={{0,4},{4,0},{1,5},{5,1},{2,6},{6,2},{3,7},{7,3},{8,12},{12,8},{9,1... | collective-permute-start | bytes 368648 | tf_op jit(solution)/shard_map/ppermute | solution.py:36
  (59 other events, 601.8 us)

commit v3 on v2

--- a/solution.py
+++ b/solution.py
@@ -999,21 +999,26 @@
             add(r, value, [spot_from(0), None])
         add_many(pieces_f, plan, home_mate, ((1, spot_from(0)), (1, None), (3, spot_from(0)), (3, None)), in_rows)
         near_x, near_y = swap(near, "tp", 2), swap(near, "ctx", 1)
-        last, near_x, near_y, *att = lax.optimization_barrier(
-            (gots[2], near_x, near_y, att_0, att_1, att_2, att_3)
+        near_mate = swap(near, "tp", 1)
+        near_mate, near_x, near_y, *att = lax.optimization_barrier(
+            (near_mate, near_x, near_y, att_0, att_1, att_2, att_3)
         )
         att_0, att_1, att_2, att_3 = att
         att = [att_0, swap(att_1, "tp", 1), swap(att_2, "tp", 2), swap(att_3, "tp", 3)]
-        near, corners[1], corners[3] = after([near, corners[1], corners[3]], att_0)
-        add_both(0, near, [spot(1, 0), spot(3, 0)])
+        (last,) = after([gots[2]], (near_x, near_y, att_0))
+        last_x, last_y = swap(last, "tp", 2), swap(last, "ctx", 1)
+        for r, value in ((0, near), (1, near_mate)):
+            add(r, value, [spot(1, 0), spot(3, 0)])
+        late = [corners[1], corners[3], near_x, near_y, last]
+        corners[1], corners[3], near_x, near_y, last = after(late, tuple(att[1:]))
         add_both(2, corners[1], [spot(1, 1)])
         add_both(2, corners[3], [spot(3, 1)])
         add_both(2, near_x, [spot(1, 0), spot(3, 0)])
         add_both(0, near_y, [spot(1, 1), spot(3, 1)])
         add_both(0, last, [spot(2, 0)])
-        add_both(2, swap(last, "tp", 2), [spot(2, 0)])
-        add_both(0, swap(last, "ctx", 1), [spot(2, 1)])
-        (corner,) = after([corners[2]], att_0)
+        add_both(2, last_x, [spot(2, 0)])
+        add_both(0, last_y, [spot(2, 1)])
+        (corner,) = after([corners[2]], tuple(att[1:]))
         add_both(2, corner, [spot(2, 1)])
     else:
         gathered = lax.all_gather(bundle_f, "fsdp", axis=0, tiled=True)

time: 302 us -> 292 us (0.967)
  waiting for transfers between devices: 87.2 us -> 72.2 us
  Pallas kernels: 123 us -> 127 us
    ppermute x47, waiting for transfers between devices: 53.8 us -> 43.1 us  [swap(): return lax.ppermute(value, axis, [(i, i ^ bit) for i in range(count)])]
    ppermute x15, waiting for transfers between devices: 33.4 us -> 29.1 us  [shift(): lax.ppermute(value, axis, [(i, (i + step) % count) for i in range(count)])]
  transfers between devices with their start and end apart: 62 -> 62, of which waited for: 25 -> 27; matrix products, arithmetic and copies ran while one was open for 6% -> 6% of each run, Pallas kernels for 32% -> 35%
where the time goes in v3:
time: 292 us; the launch traced here: 288 us
  Pallas kernels  127 us (43%)
  waiting for transfers between devices  72.2 us (25%)
  starting transfers between devices  56.7 us (19%)
  local copies, waits for them, and re-layouts  18.1 us (6%)
  other arithmetic  12 us (4%)
    ppermute x47, waiting for transfers between devices, swap(): return lax.ppermute(value, axis, [(i, i ^ bit) for i in range(count)])  43.1 us
    ppermute x47, starting transfers between devices, swap(): return lax.ppermute(value, axis, [(i, i ^ bit) for i in range(count)])  32 us
    ppermute x15, waiting for transfers between devices, shift(): lax.ppermute(value, axis, [(i, (i + step) % count) for i in range(count)])  29.1 us
    ppermute x15, starting transfers between devices, shift(): lax.ppermute(value, axis, [(i, (i + step) % count) for i in range(count)])  24.7 us
    pallas_call x1, Pallas kernels, attend_back(): pl.pallas_call(lambda *refs: attend_back_kernel(*refs, block=block, width...  24.7 us
    pallas_call x1, Pallas kernels, feed(): pl.pallas_call(lambda *refs: feed_kernel(*refs, plan=plan, count=len(piec...  23.7 us
    pallas_call x1, Pallas kernels, attend_far(): pl.pallas_call(lambda *refs: attend_far_kernel(*refs, block=block, width=...  19.3 us
    pallas_call x1, Pallas kernels, attend_near(): pl.pallas_call(lambda *refs: attend_near_kernel(*refs, block=block, width...  13.6 us
  transfers between devices with their start and end apart: 62, of which 27 were waited for; matrix products, arithmetic and copies ran while one was open for 6% of the time, Pallas kernels for 35%

profile of v3, /device:TPU:10, one launch (start us, length us, event | category | flops | bytes accessed | tf_op | source)
XLA Modules:
  0.0 288.0 jit_solution(12048139153681493259)
XLA Ops:
  0.7 1.2 pad_maximum_fusion.3
  3.1 2.6 collective-permute-start.2
  5.7 2.5 collective-permute-start.1
  8.9 1.1 constant_dynamic-slice_fusion.2
  10.0 1.6 collective-permute-start
  14.6 1.3 collective-permute-done.1
  16.0 1.4 collective-permute-start.5
  17.4 1.2 collective-permute-start.4
  18.6 1.5 collective-permute-start.10
  20.1 1.0 collective-permute-done
  21.2 1.1 or_convert_fusion
  22.4 0.9 select_convert_fusion.refs_6_
  23.4 0.9 pad_maximum_fusion.1.refs_4_
  24.4 4.2 %collective-permute-done.7.refs_9_ = bf16[200,1728]{1,0:T(8,128)(2,1)S(1)} collective-permute-done((bf16[200,1728]{1,0:T(8,128)(2,1)S(1)}, bf16[200,1728]{1,0:T(8,128)(2,1)S(1)}, u32[]{:S(2)}, u32[]{:S(2)}) %collective-permute-start.7) | collective-permute-done | bytes 691232 | tf_op jit(solution)/shard_map/ppermute | solution.py:36
  28.7 2.0 collective-permute-start.8
  31.6 19.3 %attend_far.1 = (bf16[384,192]{1,0:T(8,128)(2,1)}, bf16[384,192]{1,0:T(8,128)(2,1)}, f32[2,384,192]{2,1,0:T(8,128)}, bf16[3,2,384,128]{3,2,1,0:T(8,128)(2,1)}, b...) custom-call(s32[3]{0:T(128)} %pad_add_fusion.1.refs_0_.here, ...), custom_call_target="tpu_custom_call" | custom-call | flops 20000000000 | bytes 8388608 | tf_op jit(solution)/shard_map/attend_far/pallas_call | solution.py:227
  50.9 3.0 %collective-permute-start.18 = (bf16[96,1728]{1,0:T(8,128)(2,1)}, bf16[96,1728]{1,0:T(8,128)(2,1)}, u32[]{:S(2)}, u32[]{:S(2)}) collective-permute-start(bf16[96,1728]{1,0:T(8,128)(2,1)} %fusion.7), channel_id=1, source_target_pairs={{0,16},{8,24},{16,0},{24,8},{1,17},{9,25},{17,1},{25,9},{2,18},{10... | collective-permute-start | bytes 995336 | tf_op jit(solution)/shard_map/ppermute | solution.py:41
  54.1 1.0 constant_dynamic-update-slice_fusion.4
  55.1 1.0 constant_dynamic-update-slice_fusion.3.refs_11_
  56.1 2.5 collective-permute-start.13
  58.7 13.6 %attend_near.1 = (bf16[384,192]{1,0:T(8,128)(2,1)}, bf16[384,192]{1,0:T(8,128)(2,1)}, f32[2,384,192]{2,1,0:T(8,128)}, bf16[3,2,384,128]{3,2,1,0:T(8,128)(2,1)}) custom-call(s32[3]{0:T(128)} %pad_add_fusion.1.refs_0_.here, s32[1536]{0:T(1024)} %copy-done.14, s32[2048]{0:T(1024)} %copy-done.13, bf16[3,2,384,128]{3,2,1,0:T(8,128)(2,1)} %get-tuple-element.135.refs_3_, ...), custom_call_target="tpu_custom_call" | custom-call | flops 12000000000 | bytes 8388608 | tf_op jit(solution)/shard_map/attend_near/pallas_call | solution.py:255
  72.3 1.1 collective-permute-done.13.refs_19_
  73.5 1.6 collective-permute-done.12.refs_17_
  75.5 1.1 collective-permute-start.24
  76.5 1.0 collective-permute-start.16
  78.9 11.9 %collective-permute-done.16.refs_5_ = bf16[384,192]{1,0:T(8,128)(2,1)S(1)} collective-permute-done((bf16[384,192]{1,0:T(8,128)(2,1)S(1)}, bf16[384,192]{1,0:T(8,128)(2,1)S(1)}, u32[]{:S(2)}, u32[]{:S(2)}) %collective-permute-start.16) | collective-permute-done | bytes 147488 | tf_op jit(solution)/shard_map/ppermute | solution.py:36
  92.3 1.3 collective-permute-start.19
  100.4 0.8 copy-done.29
  101.3 23.7 %feed.1 = (bf16[384,768]{1,0:T(8,128)(2,1)}, f32[384,768]{1,0:T(8,128)}, f32[12,1,768]{2,1,0:T(1,128)}, bf16[384,192]{1,0:T(8,128)(2,1)}, bf16[384,192]{1,0:T(8,...) custom-call(s32[3]{0:T(128)} %pad_add_fusion.1.refs_0_.here, ...), custom_call_target="tpu_custom_call" | custom-call | flops 25999998976 | bytes 25165824 | tf_op jit(solution)/shard_map/feed/pallas_call | solution.py:433
  128.9 1.4 collective-permute-done.31.refs_4_
  130.7 2.3 collective-permute-done.30.refs_2_
  133.0 12.8 %unit_grads.1 = (bf16[4,96,1728]{2,1,0:T(8,128)(2,1)}, bf16[4,96,1728]{2,1,0:T(8,128)(2,1)}, bf16[2,2,96,1728]{3,2,1,0:T(8,128)(2,1)}, bf16[2,2,96,1728]{3,2,1,0:T(8,128)(2,1)}) custom-call(s32[3]{0:T(128)} %pad_add_fusion.1.refs_0_.here, bf16[3,768,384]{2,1,0:T(8,128)(2,1)} %get-tuple-element.158.refs_1_, ...), custom_call_target="tpu_custom_call" | custom-call | flops 12000000000 | bytes 14680064 | tf_op jit(solution)/shard_map/unit_grads/pallas_call | solution.py:520
  146.7 1.3 collective-permute-start.36
  148.5 24.7 %attend_back.1 = (bf16[1536,576]{1,0:T(8,128)(2,1)}, bf16[512,384]{1,0:T(8,128)(2,1)}) custom-call(s32[3]{0:T(128)} %pad_add_fusion.1.refs_0_.here, s32[1536]{0:T(1024)} %copy-done.14, s32[2048]{0:T(1024)} %copy-done.13, bf16[384,192]{1,0:T(8,128)(2,1)} %get-tuple-element.175.refs_3_, bf16[384,192]{1,0:T(8,128)(2,1)} %copy-done.50, ...), custom_call_target="tpu_custom_call" | custom-call | flops 24000000000 | bytes 8388608 | tf_op jit(solution)/shard_map/attend_back/pallas_call | solution.py:820
  173.2 6.1 %collective-permute-done.36.ga = bf16[4,96,1728]{2,1,0:T(8,128)(2,1)S(1)} collective-permute-done((bf16[4,96,1728]{2,1,0:T(8,128)(2,1)}, bf16[4,96,1728]{2,1,0:T(8,128)(2,1)S(1)}, u32[]{:S(2)}, u32[]{:S(2)}) %collective-permute-start.36) | collective-permute-done | bytes 1327136 | tf_op jit(solution)/shard_map/ppermute | solution.py:36
  180.6 1.6 collective-permute-start.40
  182.2 4.3 %merge_one.1 = (bf16[2,96,1728]{2,1,0:T(8,128)(2,1)}, bf16[2,96,1728]{2,1,0:T(8,128)(2,1)}, bf16[2,96,1728]{2,1,0:T(8,128)(2,1)}, bf16[2,96,1728]{2,1,0:T(8,128)(2,1)}) custom-call(s32[3]{0:T(128)} %pad_add_fusion.1.refs_0_.here, bf16[4,96,1728]{2,1,0:T(8,128)(2,1)} %get-tuple-element.194.ak, bf16[4,96,1728]{2,1,0:T(8,128)(2,1)} %copy-done.24, ...), custom_call_target="tpu_custom_call" | custom-call | flops 3000000000 | bytes 8388608 | tf_op jit(solution)/shard_map/merge_one/pallas_call | solution.py:561
  187.0 1.5 collective-permute-start.43
  188.5 4.3 %collective-permute-done.40 = f32[8,768]{1,0:T(8,128)S(1)} collective-permute-done((f32[8,768]{1,0:T(8,128)S(1)}, f32[8,768]{1,0:T(8,128)S(1)}, u32[]{:S(2)}, u32[]{:S(2)}) %collective-permute-start.40) | collective-permute-done | bytes 24608 | tf_op jit(solution)/shard_map/ppermute | solution.py:36
  192.9 2.7 collective-permute-start.48
  195.6 9.5 %project_back.1 = (bf16[2,384,768]{2,1,0:T(8,128)(2,1)}, bf16[2,384,768]{2,1,0:T(8,128)(2,1)}, bf16[4,96,640]{2,1,0:T(8,128)(2,1)}, bf16[4,96,640]{2,1,0:T(8,128)(2,1)}) custom-call(s32[3]{0:T(128)} %pad_add_fusion.1.refs_0_.here, bf16[1536,576]{1,0:T(8,128)(2,1)} %get-tuple-element.184.refs_1_, bf16[512,384]{1,0:T(8,128)(2,1)} %copy-done.38, ...), custom_call_target="tpu_custom_call" | custom-call | flops 8999999488 | bytes 8388608 | tf_op jit(solution)/shard_map/project_back/pallas_call | solution.py:729
  206.4 2.4 collective-permute-done.49
  208.8 1.9 fusion.3
  211.4 3.0 %merge_two.2 = (bf16[96,1728]{1,0:T(8,128)(2,1)}, bf16[96,1728]{1,0:T(8,128)(2,1)}, bf16[96,1728]{1,0:T(8,128)(2,1)}, bf16[96,1728]{1,0:T(8,128)(2,1)}) custom-call(s32[3]{0:T(128)} %pad_add_fusion.1.refs_0_.here, bf16[2,96,1728]{2,1,0:T(8,128)(2,1)} %get-tuple-element.202.refs_1_, bf16[2,96,1728]{2,1,0:T(8,128)(2,1)} %copy-done.30, ...), custom_call_target="tpu_custom_call" | custom-call | flops 3000000000 | bytes 8388608 | tf_op jit(solution)/shard_map/merge_two/pallas_call | solution.py:583
  214.4 1.0 collective-permute-start.51
  215.4 3.9 %collective-permute-start.52 = (bf16[96,1728]{1,0:T(8,128)(2,1)}, bf16[96,1728]{1,0:T(8,128)(2,1)}, u32[]{:S(2)}, u32[]{:S(2)}) collective-permute-start(bf16[96,1728]{1,0:T(8,128)(2,1)} %get-tuple-element.215), channel_id=1, source_target_pairs={{0,16},{8,24},{16,0},{24,8},{1,17},{9,25},{17,1},{25,9},{2,18},{10... | collective-permute-start | bytes 995336 | tf_op jit(solution)/shard_map/ppermute | solution.py:41
  220.5 2.2 merge_two.3
  222.6 1.4 collective-permute-start.58
  224.0 2.1 collective-permute-done.51.got_1
  226.1 19.1 %collective-permute-done.52.got_2 = bf16[96,1728]{1,0:T(8,128)(2,1)} collective-permute-done((bf16[96,1728]{1,0:T(8,128)(2,1)}, bf16[96,1728]{1,0:T(8,128)(2,1)}, u32[]{:S(2)}, u32[]{:S(2)}) %collective-permute-start.52) | collective-permute-done | bytes 331808 | tf_op jit(solution)/shard_map/ppermute | solution.py:41
  245.2 3.5 %collective-permute-done.53.got_3 = bf16[96,1728]{1,0:T(8,128)(2,1)} collective-permute-done((bf16[96,1728]{1,0:T(8,128)(2,1)}, bf16[96,1728]{1,0:T(8,128)(2,1)}, u32[]{:S(2)}, u32[]{:S(2)}) %collective-permute-start.53) | collective-permute-done | bytes 331808 | tf_op jit(solution)/shard_map/ppermute | solution.py:41
  248.7 2.2 fusion.1.p_0
  250.9 1.4 collective-permute-start.55
  252.6 2.7 collective-permute-start.45
  255.3 2.0 collective-permute-done.60
  257.3 3.3 %collective-permute-start.46 = (bf16[96,640]{1,0:T(8,128)(2,1)S(1)}, bf16[96,640]{1,0:T(8,128)(2,1)S(1)}, u32[]{:S(2)}, u32[]{:S(2)}) collective-permute-start(bf16[96,640]{1,0:T(8,128)(2,1)S(1)} %copy-done.53), channel_id=1, source_target_pairs={{0,24},{8,0},{16,8},{24,16},{1,25},{9,1},{17,9},{25,17},{2,26},{10... | collective-permute-start | bytes 368648 | tf_op jit(solution)/shard_map/ppermute | solution.py:41
  261.2 1.0 collective-permute-done.45.got_2
  262.2 2.2 collective-permute-done.46.got_3
  265.5 2.7 merge_three.3.own
  268.2 1.4 collective-permute-start.61
  269.6 1.9 merge_three.2.d_own
  273.1 3.2 %spread.3 = bf16[1536,768]{1,0:T(8,128)(2,1)} custom-call(s32[3]{0:T(128)} %pad_add_fusion.1.refs_0_.here, bf16[384,768]{1,0:T(8,128)(2,1)} %get-tuple-element.221.p_0, bf16[384,768]{1,0:T(8,128)(2,1)} %copy-done.33, bf16[384,768]{1,0:T(8,128)(2,1)} %collective-permute-done.58.p_2, bf16[384,768]{1,0:T(8,128)(2,1)} %copy-done.34), custom_call_target="tpu_custom_call" | custom-call | flops 3000000000 | bytes 8388608 | tf_op jit(solution)/shard_map/spread/pallas_call | solution.py:671
  277.9 4.1 %spread.2 = f32[1536,768]{1,0:T(8,128)} custom-call(s32[3]{0:T(128)} %pad_add_fusion.1.refs_0_.here, bf16[384,768]{1,0:T(8,128)(2,1)} %fusion.1.p_0, bf16[384,768]{1,0:T(8,128)(2,1)} %copy-done.35, bf16[384,768]{1,0:T(8,128)(2,1)} %copy-done.32, bf16[384,768]{1,0:T(8,128)(2,1)} %copy-done.36), custom_call_target="tpu_custom_call" | custom-call | flops 3000000000 | bytes 8388608 | tf_op jit(solution)/shard_map/spread/pallas_call | solution.py:671
  283.4 2.5 finish.1
  (254 shorter events, 35.4 us)
Async XLA Ops:
  2.6 13.4 %collective-permute-start.3 = (bf16[1,96,576]{2,1,0:T(8,128)(2,1)S(1)}, bf16[1,96,576]{2,1,0:T(8,128)(2,1)S(1)}, u32[]{:S(2)}, u32[]{:S(2)}) collective-permute-start(bf16[1,96,576]{2,1,0:T(8,128)(2,1)S(1)} %constant_dynamic-slice_fusion.1), channel_id=1, source_target_pairs={{0,24},{8,0},{16,8},{24,16},{1,25},{9,1},{17,9},{25,17},{2,26},{10... | collective-permute-start | bytes 331784 | tf_op jit(solution)/shard_map/ppermute | solution.py:41
  3.1 12.8 %collective-permute-start.2 = (bf16[1,96,576]{2,1,0:T(8,128)(2,1)S(1)}, bf16[1,96,576]{2,1,0:T(8,128)(2,1)S(1)}, u32[]{:S(2)}, u32[]{:S(2)}) collective-permute-start(bf16[1,96,576]{2,1,0:T(8,128)(2,1)S(1)} %constant_dynamic-slice_fusion.1), channel_id=1, source_target_pairs={{0,16},{8,24},{16,0},{24,8},{1,17},{9,25},{17,1},{25,9},{2,18},{10... | collective-permute-start | bytes 331784 | tf_op jit(solution)/shard_map/ppermute | solution.py:41
  5.7 10.2 %collective-permute-start.1 = (bf16[1,96,576]{2,1,0:T(8,128)(2,1)S(1)}, bf16[1,96,576]{2,1,0:T(8,128)(2,1)S(1)}, u32[]{:S(2)}, u32[]{:S(2)}) collective-permute-start(bf16[1,96,576]{2,1,0:T(8,128)(2,1)S(1)} %constant_dynamic-slice_fusion.1), channel_id=1, source_target_pairs={{0,8},{8,16},{16,24},{24,0},{1,9},{9,17},{17,25},{25,1},{2,10},{10... | collective-permute-start | bytes 331784 | tf_op jit(solution)/shard_map/ppermute | solution.py:41
  10.0 11.1 %collective-permute-start = (bf16[272,768]{1,0:T(8,128)(2,1)S(1)}, bf16[272,768]{1,0:T(8,128)(2,1)S(1)}, u32[]{:S(2)}, u32[]{:S(2)}) collective-permute-start(bf16[272,768]{1,0:T(8,128)(2,1)S(1)} %fusion.5), channel_id=1, source_target_pairs={{0,4},{4,0},{1,5},{5,1},{2,6},{6,2},{3,7},{7,3},{8,12},{12,8},{9,1... | collective-permute-start | bytes 1253384 | tf_op jit(solution)/shard_map/ppermute | solution.py:36
  11.9 16.7 %collective-permute-start.7 = (bf16[200,1728]{1,0:T(8,128)(2,1)S(1)}, bf16[200,1728]{1,0:T(8,128)(2,1)S(1)}, u32[]{:S(2)}, u32[]{:S(2)}) collective-permute-start(bf16[200,1728]{1,0:T(8,128)(2,1)S(1)} %pad_maximum_fusion.2.refs_8_), channel_id=1, source_target_pairs={{0,2},{1,3},{2,0},{3,1},{4,6},{5,7},{6,4},{7,5},{8,10},{9,11},{10,... | collective-permute-start | bytes 2073608 | tf_op jit(solution)/shard_map/ppermute | solution.py:36
  16.0 35.0 %collective-permute-start.5 = (bf16[96,1728]{1,0:T(8,128)(2,1)}, bf16[96,1728]{1,0:T(8,128)(2,1)}, u32[]{:S(2)}, u32[]{:S(2)}) collective-permute-start(bf16[96,1728]{1,0:T(8,128)(2,1)} %fusion.7), channel_id=1, source_target_pairs={{0,24},{8,0},{16,8},{24,16},{1,25},{9,1},{17,9},{25,17},{2,26},{10... | collective-permute-start | bytes 995336 | tf_op jit(solution)/shard_map/ppermute | solution.py:41
  17.4 36.6 %collective-permute-start.4 = (bf16[96,1728]{1,0:T(8,128)(2,1)}, bf16[96,1728]{1,0:T(8,128)(2,1)}, u32[]{:S(2)}, u32[]{:S(2)}) collective-permute-start(bf16[96,1728]{1,0:T(8,128)(2,1)} %fusion.7), channel_id=1, source_target_pairs={{0,8},{8,16},{16,24},{24,0},{1,9},{9,17},{17,25},{25,1},{2,10},{10... | collective-permute-start | bytes 995336 | tf_op jit(solution)/shard_map/ppermute | solution.py:41
  18.6 12.3 %collective-permute-start.10 = (bf16[3,96,576]{2,1,0:T(8,128)(2,1)S(1)}, bf16[3,96,576]{2,1,0:T(8,128)(2,1)S(1)}, u32[]{:S(2)}, u32[]{:S(2)}) collective-permute-start(bf16[3,96,576]{2,1,0:T(8,128)(2,1)S(1)} %constant_dynamic-update-slice_fusion.refs_9_), channel_id=1, source_target_pairs={{0,4},{4,0},{1,5},{5,1},{2,6},{6,2},{3,7},{7,3},{8,12},{12,8},{9,1... | collective-permute-start | bytes 995336 | tf_op jit(solution)/shard_map/ppermute | solution.py:36
  21.1 2.2 collective-permute-start.6
  28.6 25.4 %collective-permute-start.9 = (bf16[96,1728]{1,0:T(8,128)(2,1)S(1)}, bf16[96,1728]{1,0:T(8,128)(2,1)}, u32[]{:S(2)}, u32[]{:S(2)}) collective-permute-start(bf16[96,1728]{1,0:T(8,128)(2,1)S(1)} %constant_dynamic-slice_fusion), channel_id=1, source_target_pairs={{0,24},{8,0},{16,8},{24,16},{1,25},{9,1},{17,9},{25,17},{2,26},{10... | collective-permute-start | bytes 995336 | tf_op jit(solution)/shard_map/ppermute | solution.py:41
  28.7 25.4 %collective-permute-start.8 = (bf16[96,1728]{1,0:T(8,128)(2,1)S(1)}, bf16[96,1728]{1,0:T(8,128)(2,1)}, u32[]{:S(2)}, u32[]{:S(2)}) collective-permute-start(bf16[96,1728]{1,0:T(8,128)(2,1)S(1)} %constant_dynamic-slice_fusion), channel_id=1, source_target_pairs={{0,8},{8,16},{16,24},{24,0},{1,9},{9,17},{17,25},{25,1},{2,10},{10... | collective-permute-start | bytes 995336 | tf_op jit(solution)/shard_map/ppermute | solution.py:41
  30.9 27.8 %collective-permute-start.14 = (bf16[400,1728]{1,0:T(8,128)(2,1)S(1)}, bf16[400,1728]{1,0:T(8,128)(2,1)}, u32[]{:S(2)}, u32[]{:S(2)}) collective-permute-start(bf16[400,1728]{1,0:T(8,128)(2,1)S(1)} %pad_maximum_fusion), channel_id=1, source_target_pairs={{0,1},{1,0},{2,3},{3,2},{4,5},{5,4},{6,7},{7,6},{8,9},{9,8},{10,11... | collective-permute-start | bytes 4147208 | tf_op jit(solution)/shard_map/ppermute | solution.py:36
  50.9 24.1 %collective-permute-start.18 = (bf16[96,1728]{1,0:T(8,128)(2,1)}, bf16[96,1728]{1,0:T(8,128)(2,1)}, u32[]{:S(2)}, u32[]{:S(2)}) collective-permute-start(bf16[96,1728]{1,0:T(8,128)(2,1)} %fusion.7), channel_id=1, source_target_pairs={{0,16},{8,24},{16,0},{24,8},{1,17},{9,25},{17,1},{25,9},{2,18},{10... | collective-permute-start | bytes 995336 | tf_op jit(solution)/shard_map/ppermute | solution.py:41
  54.0 39.6 %collective-permute-start.28 = (bf16[96,1728]{1,0:T(8,128)(2,1)S(1)}, bf16[96,1728]{1,0:T(8,128)(2,1)S(1)}, u32[]{:S(2)}, u32[]{:S(2)}) collective-permute-start(bf16[96,1728]{1,0:T(8,128)(2,1)S(1)} %constant_dynamic-slice_fusion), channel_id=1, source_target_pairs={{0,16},{8,24},{16,0},{24,8},{1,17},{9,25},{17,1},{25,9},{2,18},{10... | collective-permute-start | bytes 995336 | tf_op jit(solution)/shard_map/ppermute | solution.py:41
  56.1 17.4 %collective-permute-start.13 = (bf16[192,1728]{1,0:T(8,128)(2,1)S(1)}, bf16[192,1728]{1,0:T(8,128)(2,1)S(1)}, u32[]{:S(2)}, u32[]{:S(2)}) collective-permute-start(bf16[192,1728]{1,0:T(8,128)(2,1)S(1)} %constant_dynamic-update-slice_fusion.3.refs_11_), channel_id=1, source_target_pairs={{0,4},{4,0},{1,5},{5,1},{2,6},{6,2},{3,7},{7,3},{8,12},{12,8},{9,1... | collective-permute-start | bytes 1990664 | tf_op jit(solution)/shard_map/ppermute | solution.py:36
  58.6 16.4 %collective-permute-start.12 = (bf16[192,1728]{1,0:T(8,128)(2,1)S(1)}, bf16[192,1728]{1,0:T(8,128)(2,1)}, u32[]{:S(2)}, u32[]{:S(2)}) collective-permute-start(bf16[192,1728]{1,0:T(8,128)(2,1)S(1)} %constant_dynamic-update-slice_fusion.3.refs_11_), channel_id=1, source_target_pairs={{0,2},{1,3},{2,0},{3,1},{4,6},{5,7},{6,4},{7,5},{8,10},{9,11},{10,... | collective-permute-start | bytes 1990664 | tf_op jit(solution)/shard_map/ppermute | solution.py:36
  58.6 16.4 %collective-permute-start.11 = (bf16[192,1728]{1,0:T(8,128)(2,1)S(1)}, bf16[192,1728]{1,0:T(8,128)(2,1)S(1)}, u32[]{:S(2)}, u32[]{:S(2)}) collective-permute-start(bf16[192,1728]{1,0:T(8,128)(2,1)S(1)} %constant_dynamic-update-slice_fusion.3.refs_11_), channel_id=1, source_target_pairs={{0,1},{1,0},{2,3},{3,2},{4,5},{5,4},{6,7},{7,6},{8,9},{9,8},{10,11... | collective-permute-start | bytes 1990664 | tf_op jit(solution)/shard_map/ppermute | solution.py:36
  58.7 38.8 %copy-start.21 = (bf16[768]{0:T(1024)(128)(2,1)S(1)}, bf16[768]{0:T(1024)(128)(2,1)}, u32[]{:S(2)}) copy-start(bf16[768]{0:T(1024)(128)(2,1)} %param.33) | copy-start | bytes 4612
  58.7 38.8 %copy-start.22 = (bf16[768]{0:T(1024)(128)(2,1)S(1)}, bf16[768]{0:T(1024)(128)(2,1)}, u32[]{:S(2)}) copy-start(bf16[768]{0:T(1024)(128)(2,1)} %param.34) | copy-start | bytes 4612
  75.0 19.2 %collective-permute-start.26 = (bf16[96,1728]{1,0:T(8,128)(2,1)}, bf16[96,1728]{1,0:T(8,128)(2,1)S(1)}, u32[]{:S(2)}, u32[]{:S(2)}) collective-permute-start(bf16[96,1728]{1,0:T(8,128)(2,1)} %collective-permute-done.18.refs_21_), channel_id=1, source_target_pairs={{0,4},{4,0},{1,5},{5,1},{2,6},{6,2},{3,7},{7,3},{8,12},{12,8},{9,1... | collective-permute-start | bytes 995336 | tf_op jit(solution)/shard_map/ppermute | solution.py:36
  75.5 19.3 %collective-permute-start.24 = (bf16[96,1728]{1,0:T(8,128)(2,1)}, bf16[96,1728]{1,0:T(8,128)(2,1)}, u32[]{:S(2)}, u32[]{:S(2)}) collective-permute-start(bf16[96,1728]{1,0:T(8,128)(2,1)} %collective-permute-done.18.refs_21_), channel_id=1, source_target_pairs={{0,2},{1,3},{2,0},{3,1},{4,6},{5,7},{6,4},{7,5},{8,10},{9,11},{10,... | collective-permute-start | bytes 995336 | tf_op jit(solution)/shard_map/ppermute | solution.py:36
  76.5 1.7 collective-permute-start.15
  76.5 14.3 %collective-permute-start.16 = (bf16[384,192]{1,0:T(8,128)(2,1)S(1)}, bf16[384,192]{1,0:T(8,128)(2,1)S(1)}, u32[]{:S(2)}, u32[]{:S(2)}) collective-permute-start(bf16[384,192]{1,0:T(8,128)(2,1)S(1)} %copy-done.49), channel_id=1, source_target_pairs={{0,2},{1,3},{2,0},{3,1},{4,6},{5,7},{6,4},{7,5},{8,10},{9,11},{10,... | collective-permute-start | bytes 442376 | tf_op jit(solution)/shard_map/ppermute | solution.py:36
  78.2 14.1 %collective-permute-start.17 = (bf16[384,192]{1,0:T(8,128)(2,1)S(1)}, bf16[384,192]{1,0:T(8,128)(2,1)}, u32[]{:S(2)}, u32[]{:S(2)}) collective-permute-start(bf16[384,192]{1,0:T(8,128)(2,1)S(1)} %copy-done.48), channel_id=1, source_target_pairs={{0,3},{1,2},{2,1},{3,0},{4,7},{5,6},{6,5},{7,4},{8,11},{9,10},{10,... | collective-permute-start | bytes 442376 | tf_op jit(solution)/shard_map/ppermute | solution.py:36
  92.3 2.7 collective-permute-start.19
  93.5 2.0 collective-permute-start.20
  93.5 2.5 collective-permute-start.23
  94.3 5.3 %collective-permute-start.21 = (bf16[192,1728]{1,0:T(8,128)(2,1)}, bf16[192,1728]{1,0:T(8,128)(2,1)S(1)}, u32[]{:S(2)}, u32[]{:S(2)}) collective-permute-start(bf16[192,1728]{1,0:T(8,128)(2,1)} %collective-permute-done.12.refs_17_), channel_id=1, source_target_pairs={{0,1},{1,0},{2,3},{3,2},{4,5},{5,4},{6,7},{7,6},{8,9},{9,8},{10,11... | collective-permute-start | bytes 1990664 | tf_op jit(solution)/shard_map/ppermute | solution.py:36
  94.8 4.8 %collective-permute-start.22 = (bf16[192,1728]{1,0:T(8,128)(2,1)S(1)}, bf16[192,1728]{1,0:T(8,128)(2,1)S(1)}, u32[]{:S(2)}, u32[]{:S(2)}) collective-permute-start(bf16[192,1728]{1,0:T(8,128)(2,1)S(1)} %collective-permute-done.13.refs_19_), channel_id=1, source_target_pairs={{0,1},{1,0},{2,3},{3,2},{4,5},{5,4},{6,7},{7,6},{8,9},{9,8},{10,11... | collective-permute-start | bytes 1990664 | tf_op jit(solution)/shard_map/ppermute | solution.py:36
  95.0 3.6 %collective-permute-start.29 = (bf16[96,1728]{1,0:T(8,128)(2,1)}, bf16[96,1728]{1,0:T(8,128)(2,1)}, u32[]{:S(2)}, u32[]{:S(2)}) collective-permute-start(bf16[96,1728]{1,0:T(8,128)(2,1)} %copy-done.40), channel_id=1, source_target_pairs={{0,1},{1,0},{2,3},{3,2},{4,5},{5,4},{6,7},{7,6},{8,9},{9,8},{10,11... | collective-permute-start | bytes 995336 | tf_op jit(solution)/shard_map/ppermute | solution.py:36
  95.5 3.6 %collective-permute-start.27 = (bf16[96,1728]{1,0:T(8,128)(2,1)S(1)}, bf16[96,1728]{1,0:T(8,128)(2,1)}, u32[]{:S(2)}, u32[]{:S(2)}) collective-permute-start(bf16[96,1728]{1,0:T(8,128)(2,1)S(1)} %collective-permute-done.26.refs_25_), channel_id=1, source_target_pairs={{0,1},{1,0},{2,3},{3,2},{4,5},{5,4},{6,7},{7,6},{8,9},{9,8},{10,11... | collective-permute-start | bytes 995336 | tf_op jit(solution)/shard_map/ppermute | solution.py:36
  97.0 2.6 collective-permute-start.25
  125.0 5.4 %collective-permute-start.31 = (bf16[2,384,1792]{2,1,0:T(8,128)(2,1)}, bf16[2,384,1792]{2,1,0:T(8,128)(2,1)S(1)}, u32[]{:S(2)}, u32[]{:S(2)}) collective-permute-start(bf16[2,384,1792]{2,1,0:T(8,128)(2,1)} %get-tuple-element.160), channel_id=1, source_target_pairs={{0,1},{1,0},{2,3},{3,2},{4,5},{5,4},{6,7},{7,6},{8,9},{9,8},{10,11... | collective-permute-start | bytes 8257544 | tf_op jit(solution)/shard_map/ppermute | solution.py:36
  125.4 7.6 %collective-permute-start.30 = (bf16[3,768,384]{2,1,0:T(8,128)(2,1)}, bf16[3,768,384]{2,1,0:T(8,128)(2,1)}, u32[]{:S(2)}, u32[]{:S(2)}) collective-permute-start(bf16[3,768,384]{2,1,0:T(8,128)(2,1)} %get-tuple-element.158.refs_1_), channel_id=1, source_target_pairs={{0,1},{1,0},{2,3},{3,2},{4,5},{5,4},{6,7},{7,6},{8,9},{9,8},{10,11... | collective-permute-start | bytes 5308424 | tf_op jit(solution)/shard_map/ppermute | solution.py:36
  126.3 19.5 %collective-permute-start.33 = (bf16[384,192]{1,0:T(8,128)(2,1)}, bf16[384,192]{1,0:T(8,128)(2,1)S(1)}, u32[]{:S(2)}, u32[]{:S(2)}) collective-permute-start(bf16[384,192]{1,0:T(8,128)(2,1)} %get-tuple-element.166), channel_id=1, source_target_pairs={{0,1},{1,0},{2,3},{3,2},{4,5},{5,4},{6,7},{7,6},{8,9},{9,8},{10,11... | collective-permute-start | bytes 442376 | tf_op jit(solution)/shard_map/ppermute | solution.py:36
  126.7 19.1 %collective-permute-start.34 = (bf16[384,192]{1,0:T(8,128)(2,1)}, bf16[384,192]{1,0:T(8,128)(2,1)S(1)}, u32[]{:S(2)}, u32[]{:S(2)}) collective-permute-start(bf16[384,192]{1,0:T(8,128)(2,1)} %get-tuple-element.167), channel_id=1, source_target_pairs={{0,2},{1,3},{2,0},{3,1},{4,6},{5,7},{6,4},{7,5},{8,10},{9,11},{10,... | collective-permute-start | bytes 442376 | tf_op jit(solution)/shard_map/ppermute | solution.py:36
  127.4 18.4 %collective-permute-start.35 = (bf16[384,192]{1,0:T(8,128)(2,1)}, bf16[384,192]{1,0:T(8,128)(2,1)S(1)}, u32[]{:S(2)}, u32[]{:S(2)}) collective-permute-start(bf16[384,192]{1,0:T(8,128)(2,1)} %get-tuple-element.168), channel_id=1, source_target_pairs={{0,3},{1,2},{2,1},{3,0},{4,7},{5,6},{6,5},{7,4},{8,11},{9,10},{10,... | collective-permute-start | bytes 442376 | tf_op jit(solution)/shard_map/ppermute | solution.py:36
  130.3 15.5 %collective-permute-start.32 = (f32[8,768]{1,0:T(8,128)S(1)}, f32[8,768]{1,0:T(8,128)S(1)}, u32[]{:S(2)}, u32[]{:S(2)}) collective-permute-start(f32[8,768]{1,0:T(8,128)S(1)} %pad_maximum_fusion.4), channel_id=1, source_target_pairs={{0,1},{1,0},{2,3},{3,2},{4,5},{5,4},{6,7},{7,6},{8,9},{9,8},{10,11... | collective-permute-start | bytes 73736 | tf_op jit(solution)/shard_map/ppermute | solution.py:36
  145.9 27.2 %collective-permute-start.38 = (f32[8,768]{1,0:T(8,128)S(1)}, f32[8,768]{1,0:T(8,128)S(1)}, u32[]{:S(2)}, u32[]{:S(2)}) collective-permute-start(f32[8,768]{1,0:T(8,128)S(1)} %pad_maximum_fusion.5), channel_id=1, source_target_pairs={{0,2},{1,3},{2,0},{3,1},{4,6},{5,7},{6,4},{7,5},{8,10},{9,11},{10,... | collective-permute-start | bytes 73736 | tf_op jit(solution)/shard_map/ppermute | solution.py:36
  146.7 32.6 %collective-permute-start.36 = (bf16[4,96,1728]{2,1,0:T(8,128)(2,1)}, bf16[4,96,1728]{2,1,0:T(8,128)(2,1)S(1)}, u32[]{:S(2)}, u32[]{:S(2)}) collective-permute-start(bf16[4,96,1728]{2,1,0:T(8,128)(2,1)} %get-tuple-element.186), channel_id=1, source_target_pairs={{0,2},{1,3},{2,0},{3,1},{4,6},{5,7},{6,4},{7,5},{8,10},{9,11},{10,... | collective-permute-start | bytes 3981320 | tf_op jit(solution)/shard_map/ppermute | solution.py:36
  148.0 32.1 %collective-permute-start.37 = (bf16[2,2,96,1728]{3,2,1,0:T(8,128)(2,1)}, bf16[2,2,96,1728]{3,2,1,0:T(8,128)(2,1)S(1)}, u32[]{:S(2)}, u32[]{:S(2)}) collective-permute-start(bf16[2,2,96,1728]{3,2,1,0:T(8,128)(2,1)} %get-tuple-element.187), channel_id=1, source_target_pairs={{0,4},{4,0},{1,5},{5,1},{2,6},{6,2},{3,7},{7,3},{8,12},{12,8},{9,1... | collective-permute-start | bytes 3981320 | tf_op jit(solution)/shard_map/ppermute | solution.py:36
  180.2 12.7 %collective-permute-start.39 = (bf16[512,384]{1,0:T(8,128)(2,1)}, bf16[512,384]{1,0:T(8,128)(2,1)S(1)}, u32[]{:S(2)}, u32[]{:S(2)}) collective-permute-start(bf16[512,384]{1,0:T(8,128)(2,1)} %get-tuple-element.193), channel_id=1, source_target_pairs={{0,4},{4,0},{1,5},{5,1},{2,6},{6,2},{3,7},{7,3},{8,12},{12,8},{9,1... | collective-permute-start | bytes 1179656 | tf_op jit(solution)/shard_map/ppermute | solution.py:36
  180.6 12.3 %collective-permute-start.40 = (f32[8,768]{1,0:T(8,128)S(1)}, f32[8,768]{1,0:T(8,128)S(1)}, u32[]{:S(2)}, u32[]{:S(2)}) collective-permute-start(f32[8,768]{1,0:T(8,128)S(1)} %add.60), channel_id=1, source_target_pairs={{0,4},{4,0},{1,5},{5,1},{2,6},{6,2},{3,7},{7,3},{8,12},{12,8},{9,1... | collective-permute-start | bytes 73736 | tf_op jit(solution)/shard_map/ppermute | solution.py:36
  186.5 19.1 %collective-permute-start.42 = (bf16[2,96,1728]{2,1,0:T(8,128)(2,1)}, bf16[2,96,1728]{2,1,0:T(8,128)(2,1)S(1)}, u32[]{:S(2)}, u32[]{:S(2)}) collective-permute-start(bf16[2,96,1728]{2,1,0:T(8,128)(2,1)} %get-tuple-element.196), channel_id=1, source_target_pairs={{0,4},{4,0},{1,5},{5,1},{2,6},{6,2},{3,7},{7,3},{8,12},{12,8},{9,1... | collective-permute-start | bytes 1990664 | tf_op jit(solution)/shard_map/ppermute | solution.py:36
  187.0 18.7 %collective-permute-start.43 = (bf16[2,96,1728]{2,1,0:T(8,128)(2,1)}, bf16[2,96,1728]{2,1,0:T(8,128)(2,1)S(1)}, u32[]{:S(2)}, u32[]{:S(2)}) collective-permute-start(bf16[2,96,1728]{2,1,0:T(8,128)(2,1)} %get-tuple-element.197), channel_id=1, source_target_pairs={{0,2},{1,3},{2,0},{3,1},{4,6},{5,7},{6,4},{7,5},{8,10},{9,11},{10,... | collective-permute-start | bytes 1990664 | tf_op jit(solution)/shard_map/ppermute | solution.py:36
  192.9 12.2 %collective-permute-start.48 = (f32[8,768]{1,0:T(8,128)S(1)}, f32[8,768]{1,0:T(8,128)S(1)}, u32[]{:S(2)}, u32[]{:S(2)}) collective-permute-start(f32[8,768]{1,0:T(8,128)S(1)} %add.61), channel_id=1, source_target_pairs={{0,8},{8,0},{16,24},{24,16},{1,9},{9,1},{17,25},{25,17},{2,10},{10... | collective-permute-start | bytes 73736 | tf_op jit(solution)/shard_map/ppermute | solution.py:36
  205.7 3.1 %collective-permute-start.49 = (bf16[2,384,768]{2,1,0:T(8,128)(2,1)}, bf16[2,384,768]{2,1,0:T(8,128)(2,1)S(1)}, u32[]{:S(2)}, u32[]{:S(2)}) collective-permute-start(bf16[2,384,768]{2,1,0:T(8,128)(2,1)} %get-tuple-element.213), channel_id=1, source_target_pairs={{0,1},{1,0},{2,3},{3,2},{4,5},{5,4},{6,7},{7,6},{8,9},{9,8},{10,11... | collective-permute-start | bytes 3538952 | tf_op jit(solution)/shard_map/ppermute | solution.py:36
  205.8 13.9 %collective-permute-start.41 = (bf16[4,96,640]{2,1,0:T(8,128)(2,1)}, bf16[4,96,640]{2,1,0:T(8,128)(2,1)S(1)}, u32[]{:S(2)}, u32[]{:S(2)}) collective-permute-start(bf16[4,96,640]{2,1,0:T(8,128)(2,1)} %get-tuple-element.201), channel_id=1, source_target_pairs={{0,4},{4,0},{1,5},{5,1},{2,6},{6,2},{3,7},{7,3},{8,12},{12,8},{9,1... | collective-permute-start | bytes 1474568 | tf_op jit(solution)/shard_map/ppermute | solution.py:36
  210.7 37.9 %collective-permute-start.50 = (bf16[384,768]{1,0:T(8,128)(2,1)}, bf16[384,768]{1,0:T(8,128)(2,1)}, u32[]{:S(2)}, u32[]{:S(2)}) collective-permute-start(bf16[384,768]{1,0:T(8,128)(2,1)} %fusion.3), channel_id=1, source_target_pairs={{0,2},{1,3},{2,0},{3,1},{4,6},{5,7},{6,4},{7,5},{8,10},{9,11},{10,... | collective-permute-start | bytes 1769480 | tf_op jit(solution)/shard_map/ppermute | solution.py:36
  214.4 11.8 %collective-permute-start.51 = (bf16[96,1728]{1,0:T(8,128)(2,1)}, bf16[96,1728]{1,0:T(8,128)(2,1)}, u32[]{:S(2)}, u32[]{:S(2)}) collective-permute-start(bf16[96,1728]{1,0:T(8,128)(2,1)} %get-tuple-element.214), channel_id=1, source_target_pairs={{0,8},{8,16},{16,24},{24,0},{1,9},{9,17},{17,25},{25,1},{2,10},{10... | collective-permute-start | bytes 995336 | tf_op jit(solution)/shard_map/ppermute | solution.py:41
  215.4 29.8 %collective-permute-start.52 = (bf16[96,1728]{1,0:T(8,128)(2,1)}, bf16[96,1728]{1,0:T(8,128)(2,1)}, u32[]{:S(2)}, u32[]{:S(2)}) collective-permute-start(bf16[96,1728]{1,0:T(8,128)(2,1)} %get-tuple-element.215), channel_id=1, source_target_pairs={{0,16},{8,24},{16,0},{24,8},{1,17},{9,25},{17,1},{25,9},{2,18},{10... | collective-permute-start | bytes 995336 | tf_op jit(solution)/shard_map/ppermute | solution.py:41
  219.3 29.4 %collective-permute-start.53 = (bf16[96,1728]{1,0:T(8,128)(2,1)}, bf16[96,1728]{1,0:T(8,128)(2,1)}, u32[]{:S(2)}, u32[]{:S(2)}) collective-permute-start(bf16[96,1728]{1,0:T(8,128)(2,1)} %get-tuple-element.216), channel_id=1, source_target_pairs={{0,24},{8,0},{16,8},{24,16},{1,25},{9,1},{17,9},{25,17},{2,26},{10... | collective-permute-start | bytes 995336 | tf_op jit(solution)/shard_map/ppermute | solution.py:41
  222.6 38.0 %collective-permute-start.58 = (bf16[384,768]{1,0:T(8,128)(2,1)}, bf16[384,768]{1,0:T(8,128)(2,1)}, u32[]{:S(2)}, u32[]{:S(2)}) collective-permute-start(bf16[384,768]{1,0:T(8,128)(2,1)} %get-tuple-element.221.p_0), channel_id=1, source_target_pairs={{0,2},{1,3},{2,0},{3,1},{4,6},{5,7},{6,4},{7,5},{8,10},{9,11},{10,... | collective-permute-start | bytes 1769480 | tf_op jit(solution)/shard_map/ppermute | solution.py:36
  250.9 14.6 %collective-permute-start.55 = (bf16[384,768]{1,0:T(8,128)(2,1)}, bf16[384,768]{1,0:T(8,128)(2,1)S(1)}, u32[]{:S(2)}, u32[]{:S(2)}) collective-permute-start(bf16[384,768]{1,0:T(8,128)(2,1)} %fusion.1.p_0), channel_id=1, source_target_pairs={{0,2},{1,3},{2,0},{3,1},{4,6},{5,7},{6,4},{7,5},{8,10},{9,11},{10,... | collective-permute-start | bytes 1769480 | tf_op jit(solution)/shard_map/ppermute | solution.py:36
  252.3 8.3 %collective-permute-start.44 = (bf16[96,640]{1,0:T(8,128)(2,1)S(1)}, bf16[96,640]{1,0:T(8,128)(2,1)S(1)}, u32[]{:S(2)}, u32[]{:S(2)}) collective-permute-start(bf16[96,640]{1,0:T(8,128)(2,1)S(1)} %copy-done.56), channel_id=1, source_target_pairs={{0,8},{8,16},{16,24},{24,0},{1,9},{9,17},{17,25},{25,1},{2,10},{10... | collective-permute-start | bytes 368648 | tf_op jit(solution)/shard_map/ppermute | solution.py:41
  252.3 5.0 %collective-permute-start.60 = (f32[8,768]{1,0:T(8,128)S(1)}, f32[8,768]{1,0:T(8,128)S(1)}, u32[]{:S(2)}, u32[]{:S(2)}) collective-permute-start(f32[8,768]{1,0:T(8,128)S(1)} %copy-done.11), channel_id=1, source_target_pairs={{0,16},{8,24},{16,0},{24,8},{1,17},{9,25},{17,1},{25,9},{2,18},{10... | collective-permute-start | bytes 73736 | tf_op jit(solution)/shard_map/ppermute | solution.py:36
  252.6 9.5 %collective-permute-start.45 = (bf16[96,640]{1,0:T(8,128)(2,1)S(1)}, bf16[96,640]{1,0:T(8,128)(2,1)}, u32[]{:S(2)}, u32[]{:S(2)}) collective-permute-start(bf16[96,640]{1,0:T(8,128)(2,1)S(1)} %copy-done.54), channel_id=1, source_target_pairs={{0,16},{8,24},{16,0},{24,8},{1,17},{9,25},{17,1},{25,9},{2,18},{10... | collective-permute-start | bytes 368648 | tf_op jit(solution)/shard_map/ppermute | solution.py:41
  257.3 7.0 %collective-permute-start.46 = (bf16[96,640]{1,0:T(8,128)(2,1)S(1)}, bf16[96,640]{1,0:T(8,128)(2,1)S(1)}, u32[]{:S(2)}, u32[]{:S(2)}) collective-permute-start(bf16[96,640]{1,0:T(8,128)(2,1)S(1)} %copy-done.53), channel_id=1, source_target_pairs={{0,24},{8,0},{16,8},{24,16},{1,25},{9,1},{17,9},{25,17},{2,26},{10... | collective-permute-start | bytes 368648 | tf_op jit(solution)/shard_map/ppermute | solution.py:41
  260.6 10.8 %collective-permute-start.57 = (bf16[384,768]{1,0:T(8,128)(2,1)}, bf16[384,768]{1,0:T(8,128)(2,1)S(1)}, u32[]{:S(2)}, u32[]{:S(2)}) collective-permute-start(bf16[384,768]{1,0:T(8,128)(2,1)} %get-tuple-element.221.p_0), channel_id=1, source_target_pairs={{0,1},{1,0},{2,3},{3,2},{4,5},{5,4},{6,7},{7,6},{8,9},{9,8},{10,11... | collective-permute-start | bytes 1769480 | tf_op jit(solution)/shard_map/ppermute | solution.py:36
  260.7 11.5 %collective-permute-start.59 = (bf16[384,768]{1,0:T(8,128)(2,1)}, bf16[384,768]{1,0:T(8,128)(2,1)S(1)}, u32[]{:S(2)}, u32[]{:S(2)}) collective-permute-start(bf16[384,768]{1,0:T(8,128)(2,1)} %collective-permute-done.58.p_2), channel_id=1, source_target_pairs={{0,1},{1,0},{2,3},{3,2},{4,5},{5,4},{6,7},{7,6},{8,9},{9,8},{10,11... | collective-permute-start | bytes 1769480 | tf_op jit(solution)/shard_map/ppermute | solution.py:36
  262.1 14.1 %collective-permute-start.54 = (bf16[384,768]{1,0:T(8,128)(2,1)}, bf16[384,768]{1,0:T(8,128)(2,1)S(1)}, u32[]{:S(2)}, u32[]{:S(2)}) collective-permute-start(bf16[384,768]{1,0:T(8,128)(2,1)} %fusion.1.p_0), channel_id=1, source_target_pairs={{0,1},{1,0},{2,3},{3,2},{4,5},{5,4},{6,7},{7,6},{8,9},{9,8},{10,11... | collective-permute-start | bytes 1769480 | tf_op jit(solution)/shard_map/ppermute | solution.py:36
  265.5 10.8 %collective-permute-start.56 = (bf16[384,768]{1,0:T(8,128)(2,1)S(1)}, bf16[384,768]{1,0:T(8,128)(2,1)S(1)}, u32[]{:S(2)}, u32[]{:S(2)}) collective-permute-start(bf16[384,768]{1,0:T(8,128)(2,1)S(1)} %collective-permute-done.55.p_2), channel_id=1, source_target_pairs={{0,1},{1,0},{2,3},{3,2},{4,5},{5,4},{6,7},{7,6},{8,9},{9,8},{10,11... | collective-permute-start | bytes 1769480 | tf_op jit(solution)/shard_map/ppermute | solution.py:36
  268.2 14.4 %collective-permute-start.61 = (bf16[96,1728]{1,0:T(8,128)(2,1)}, bf16[96,1728]{1,0:T(8,128)(2,1)S(1)}, u32[]{:S(2)}, u32[]{:S(2)}) collective-permute-start(bf16[96,1728]{1,0:T(8,128)(2,1)} %merge_three.3.own), channel_id=1, source_target_pairs={{0,4},{4,0},{1,5},{5,1},{2,6},{6,2},{3,7},{7,3},{8,12},{12,8},{9,1... | collective-permute-start | bytes 995336 | tf_op jit(solution)/shard_map/ppermute | solution.py:36
  271.5 10.5 %collective-permute-start.47 = (bf16[96,640]{1,0:T(8,128)(2,1)}, bf16[96,640]{1,0:T(8,128)(2,1)S(1)}, u32[]{:S(2)}, u32[]{:S(2)}) collective-permute-start(bf16[96,640]{1,0:T(8,128)(2,1)} %merge_three.2.d_own), channel_id=1, source_target_pairs={{0,4},{4,0},{1,5},{5,1},{2,6},{6,2},{3,7},{7,3},{8,12},{12,8},{9,1... | collective-permute-start | bytes 368648 | tf_op jit(solution)/shard_map/ppermute | solution.py:36
  (59 other events, 510.9 us)

commit v4 on v3

--- a/solution.py
+++ b/solution.py
@@ -1010,7 +1010,7 @@
         for r, value in ((0, near), (1, near_mate)):
             add(r, value, [spot(1, 0), spot(3, 0)])
         late = [corners[1], corners[3], near_x, near_y, last]
-        corners[1], corners[3], near_x, near_y, last = after(late, tuple(att[1:]))
+        corners[1], corners[3], near_x, near_y, last = after(late, (last_y, att[1]))
         add_both(2, corners[1], [spot(1, 1)])
         add_both(2, corners[3], [spot(3, 1)])
         add_both(2, near_x, [spot(1, 0), spot(3, 0)])
@@ -1018,7 +1018,7 @@
         add_both(0, last, [spot(2, 0)])
         add_both(2, last_x, [spot(2, 0)])
         add_both(0, last_y, [spot(2, 1)])
-        (corner,) = after([corners[2]], tuple(att[1:]))
+        (corner,) = after([corners[2]], (last_y, att[1], att[2]))
         add_both(2, corner, [spot(2, 1)])
     else:
         gathered = lax.all_gather(bundle_f, "fsdp", axis=0, tiled=True)
@@ -1109,11 +1109,11 @@
         d_totals = [outs[0]] + [shift(outs[s], "fsdp", s) for s in range(1, n_f)]
         (output,) = after([output], d_totals[0])
         output = everyone(output, swap(output, "tp", 2), low)
-        (far_got,) = after([far_got], (*totals, d_totals[0]))
+        total = merge_three(here, totals)
+        (far_got,) = after([far_got], (total, d_totals[0], pair))
         mine = (near_dx.astype(high) + far_got.astype(high) + g_one).astype(low)
         (far_mine,) = after([swap(mine, "tp", 2)], d_totals)
         grad_inputs = everyone(mine, far_mine, high)
-        total = merge_three(here, totals)
         got = swap(total, "ctx", 1)
         d_total = merge_three(here, d_totals)
         d_got = swap(d_total, "ctx", 1)

time: 292 us -> 284 us (0.973)
    ppermute x47, waiting for transfers between devices: 43.1 us -> 36.2 us  [swap(): return lax.ppermute(value, axis, [(i, i ^ bit) for i in range(count)])]
    ppermute x15, waiting for transfers between devices: 29.1 us -> 35.7 us  [shift(): lax.ppermute(value, axis, [(i, (i + step) % count) for i in range(count)])]
    ppermute x15, starting transfers between devices: 24.7 us -> 20.4 us  [shift(): lax.ppermute(value, axis, [(i, (i + step) % count) for i in range(count)])]
    unnamed x128 -> x130, local copies, waits for them, and re-layouts: 11 us -> 10.6 us
  transfers between devices with their start and end apart: 62 -> 62, of which waited for: 27 -> 26; matrix products, arithmetic and copies ran while one was open for 6% -> 6% of each run, Pallas kernels for 35% -> 35%
where the time goes in v4:
time: 284 us; the launch traced here: 282 us
  Pallas kernels  125 us (44%)
  waiting for transfers between devices  71.9 us (25%)
  starting transfers between devices  54.3 us (19%)
  local copies, waits for them, and re-layouts  17.7 us (6%)
  other arithmetic  11 us (4%)
    ppermute x47, waiting for transfers between devices, swap(): return lax.ppermute(value, axis, [(i, i ^ bit) for i in range(count)])  36.2 us
    ppermute x15, waiting for transfers between devices, shift(): lax.ppermute(value, axis, [(i, (i + step) % count) for i in range(count)])  35.7 us
    ppermute x47, starting transfers between devices, swap(): return lax.ppermute(value, axis, [(i, i ^ bit) for i in range(count)])  33.9 us
    pallas_call x1, Pallas kernels, attend_back(): pl.pallas_call(lambda *refs: attend_back_kernel(*refs, block=block, width...  23.7 us
    pallas_call x1, Pallas kernels, feed(): pl.pallas_call(lambda *refs: feed_kernel(*refs, plan=plan, count=len(piec...  23.7 us
    ppermute x15, starting transfers between devices, shift(): lax.ppermute(value, axis, [(i, (i + step) % count) for i in range(count)])  20.4 us
    pallas_call x1, Pallas kernels, attend_far(): pl.pallas_call(lambda *refs: attend_far_kernel(*refs, block=block, width=...  18.2 us
    pallas_call x1, Pallas kernels, attend_near(): pl.pallas_call(lambda *refs: attend_near_kernel(*refs, block=block, width...  13.6 us
  transfers between devices with their start and end apart: 62, of which 26 were waited for; matrix products, arithmetic and copies ran while one was open for 6% of the time, Pallas kernels for 35%

profile of v4, /device:TPU:10, one launch (start us, length us, event | category | flops | bytes accessed | tf_op | source)
XLA Modules:
  0.0 281.5 jit_solution(6191496455708511939)
XLA Ops:
  0.7 1.2 pad_maximum_fusion.3
  3.1 2.6 collective-permute-start.2
  5.7 2.5 collective-permute-start.1
  8.9 1.1 constant_dynamic-slice_fusion.2
  10.0 1.6 collective-permute-start
  14.7 1.2 collective-permute-done.1
  16.0 1.4 collective-permute-start.5
  17.4 1.2 collective-permute-start.4
  18.6 1.5 collective-permute-start.10
  21.2 1.2 or_convert_fusion
  24.4 4.2 %collective-permute-done.7.refs_9_ = bf16[200,1728]{1,0:T(8,128)(2,1)S(1)} collective-permute-done((bf16[200,1728]{1,0:T(8,128)(2,1)S(1)}, bf16[200,1728]{1,0:T(8,128)(2,1)S(1)}, u32[]{:S(2)}, u32[]{:S(2)}) %collective-permute-start.7) | collective-permute-done | bytes 691232 | tf_op jit(solution)/shard_map/ppermute | solution.py:36
  28.7 2.0 collective-permute-start.8
  31.6 18.2 %attend_far.1 = (bf16[384,192]{1,0:T(8,128)(2,1)}, bf16[384,192]{1,0:T(8,128)(2,1)}, f32[2,384,192]{2,1,0:T(8,128)}, bf16[3,2,384,128]{3,2,1,0:T(8,128)(2,1)}, b...) custom-call(s32[3]{0:T(128)} %pad_add_fusion.1.refs_0_.here, ...), custom_call_target="tpu_custom_call" | custom-call | flops 20000000000 | bytes 8388608 | tf_op jit(solution)/shard_map/attend_far/pallas_call | solution.py:227
  49.9 4.1 %collective-permute-start.18 = (bf16[96,1728]{1,0:T(8,128)(2,1)}, bf16[96,1728]{1,0:T(8,128)(2,1)S(1)}, u32[]{:S(2)}, u32[]{:S(2)}) collective-permute-start(bf16[96,1728]{1,0:T(8,128)(2,1)} %fusion.7), channel_id=1, source_target_pairs={{0,16},{8,24},{16,0},{24,8},{1,17},{9,25},{17,1},{25,9},{2,18},{10... | collective-permute-start | bytes 995336 | tf_op jit(solution)/shard_map/ppermute | solution.py:41
  54.0 1.0 constant_dynamic-update-slice_fusion.4
  55.0 1.0 constant_dynamic-update-slice_fusion.3.refs_11_
  56.0 2.7 collective-permute-start.13
  58.8 13.6 %attend_near.1 = (bf16[384,192]{1,0:T(8,128)(2,1)}, bf16[384,192]{1,0:T(8,128)(2,1)}, f32[2,384,192]{2,1,0:T(8,128)}, bf16[3,2,384,128]{3,2,1,0:T(8,128)(2,1)}) custom-call(s32[3]{0:T(128)} %pad_add_fusion.1.refs_0_.here, s32[1536]{0:T(1024)} %copy-done.14, s32[2048]{0:T(1024)} %copy-done.13, bf16[3,2,384,128]{3,2,1,0:T(8,128)(2,1)} %get-tuple-element.135.refs_3_, ...), custom_call_target="tpu_custom_call" | custom-call | flops 12000000000 | bytes 8388608 | tf_op jit(solution)/shard_map/attend_near/pallas_call | solution.py:255
  72.4 1.4 collective-permute-done.13.refs_19_
  73.8 1.6 collective-permute-done.12.refs_17_
  76.7 1.4 collective-permute-start.16
  78.4 1.1 collective-permute-start.17
  79.5 4.2 %collective-permute-done.19.refs_25_ = bf16[96,1728]{1,0:T(8,128)(2,1)S(1)} collective-permute-done((bf16[96,1728]{1,0:T(8,128)(2,1)S(1)}, bf16[96,1728]{1,0:T(8,128)(2,1)S(1)}, u32[]{:S(2)}, u32[]{:S(2)}) %collective-permute-start.19) | collective-permute-done | bytes 331808 | tf_op jit(solution)/shard_map/ppermute | solution.py:36
  83.8 2.9 %collective-permute-done.25.refs_23_ = bf16[96,1728]{1,0:T(8,128)(2,1)S(1)} collective-permute-done((bf16[96,1728]{1,0:T(8,128)(2,1)S(1)}, bf16[96,1728]{1,0:T(8,128)(2,1)S(1)}, u32[]{:S(2)}, u32[]{:S(2)}) %collective-permute-start.25) | collective-permute-done | bytes 331808 | tf_op jit(solution)/shard_map/ppermute | solution.py:36
  86.7 3.5 %collective-permute-done.28.refs_27_ = bf16[96,1728]{1,0:T(8,128)(2,1)S(1)} collective-permute-done((bf16[96,1728]{1,0:T(8,128)(2,1)S(1)}, bf16[96,1728]{1,0:T(8,128)(2,1)S(1)}, u32[]{:S(2)}, u32[]{:S(2)}) %collective-permute-start.28) | collective-permute-done | bytes 331808 | tf_op jit(solution)/shard_map/ppermute | solution.py:41
  97.5 23.7 %feed.1 = (bf16[384,768]{1,0:T(8,128)(2,1)}, f32[384,768]{1,0:T(8,128)}, f32[12,1,768]{2,1,0:T(1,128)}, bf16[384,192]{1,0:T(8,128)(2,1)}, bf16[384,192]{1,0:T(8,...) custom-call(s32[3]{0:T(128)} %pad_add_fusion.1.refs_0_.here, ...), custom_call_target="tpu_custom_call" | custom-call | flops 25999998976 | bytes 25165824 | tf_op jit(solution)/shard_map/feed/pallas_call | solution.py:433
  122.9 1.6 collective-permute-start.34
  125.2 1.3 collective-permute-done.31.refs_4_
  126.9 2.3 collective-permute-done.30.refs_2_
  129.2 12.8 %unit_grads.1 = (bf16[4,96,1728]{2,1,0:T(8,128)(2,1)}, bf16[4,96,1728]{2,1,0:T(8,128)(2,1)}, bf16[2,2,96,1728]{3,2,1,0:T(8,128)(2,1)}, bf16[2,2,96,1728]{3,2,1,0:T(8,128)(2,1)}) custom-call(s32[3]{0:T(128)} %pad_add_fusion.1.refs_0_.here, bf16[3,768,384]{2,1,0:T(8,128)(2,1)} %get-tuple-element.158.refs_1_, ...), custom_call_target="tpu_custom_call" | custom-call | flops 12000000000 | bytes 14680064 | tf_op jit(solution)/shard_map/unit_grads/pallas_call | solution.py:520
  142.1 1.7 collective-permute-start.38
  144.2 1.4 collective-permute-start.37
  145.6 23.7 %attend_back.1 = (bf16[1536,576]{1,0:T(8,128)(2,1)}, bf16[512,384]{1,0:T(8,128)(2,1)}) custom-call(s32[3]{0:T(128)} %pad_add_fusion.1.refs_0_.here, s32[1536]{0:T(1024)} %copy-done.14, s32[2048]{0:T(1024)} %copy-done.13, bf16[384,192]{1,0:T(8,128)(2,1)} %get-tuple-element.175.refs_3_, bf16[384,192]{1,0:T(8,128)(2,1)} %copy-done.51, ...), custom_call_target="tpu_custom_call" | custom-call | flops 24000000000 | bytes 8388608 | tf_op jit(solution)/shard_map/attend_back/pallas_call | solution.py:820
  169.4 6.9 %collective-permute-done.36.ga = bf16[4,96,1728]{2,1,0:T(8,128)(2,1)S(1)} collective-permute-done((bf16[4,96,1728]{2,1,0:T(8,128)(2,1)}, bf16[4,96,1728]{2,1,0:T(8,128)(2,1)S(1)}, u32[]{:S(2)}, u32[]{:S(2)}) %collective-permute-start.36) | collective-permute-done | bytes 1327136 | tf_op jit(solution)/shard_map/ppermute | solution.py:36
  176.3 1.4 collective-permute-start.39
  178.4 4.4 %merge_one.1 = (bf16[2,96,1728]{2,1,0:T(8,128)(2,1)}, bf16[2,96,1728]{2,1,0:T(8,128)(2,1)}, bf16[2,96,1728]{2,1,0:T(8,128)(2,1)}, bf16[2,96,1728]{2,1,0:T(8,128)(2,1)}) custom-call(s32[3]{0:T(128)} %pad_add_fusion.1.refs_0_.here, bf16[4,96,1728]{2,1,0:T(8,128)(2,1)} %get-tuple-element.194.ak, bf16[4,96,1728]{2,1,0:T(8,128)(2,1)} %copy-done.24, ...), custom_call_target="tpu_custom_call" | custom-call | flops 3000000000 | bytes 8388608 | tf_op jit(solution)/shard_map/merge_one/pallas_call | solution.py:561
  182.8 1.4 collective-permute-start.42
  184.8 4.3 %collective-permute-done.40 = f32[8,768]{1,0:T(8,128)S(1)} collective-permute-done((f32[8,768]{1,0:T(8,128)S(1)}, f32[8,768]{1,0:T(8,128)S(1)}, u32[]{:S(2)}, u32[]{:S(2)}) %collective-permute-start.40) | collective-permute-done | bytes 24608 | tf_op jit(solution)/shard_map/ppermute | solution.py:36
  189.1 1.8 collective-permute-start.48
  190.9 9.5 %project_back.1 = (bf16[2,384,768]{2,1,0:T(8,128)(2,1)}, bf16[2,384,768]{2,1,0:T(8,128)(2,1)}, bf16[4,96,640]{2,1,0:T(8,128)(2,1)}, bf16[4,96,640]{2,1,0:T(8,128)(2,1)}) custom-call(s32[3]{0:T(128)} %pad_add_fusion.1.refs_0_.here, bf16[1536,576]{1,0:T(8,128)(2,1)} %get-tuple-element.184.refs_1_, bf16[512,384]{1,0:T(8,128)(2,1)} %copy-done.36, ...), custom_call_target="tpu_custom_call" | custom-call | flops 8999999488 | bytes 8388608 | tf_op jit(solution)/shard_map/project_back/pallas_call | solution.py:729
  200.4 1.7 collective-permute-done.42.refs_2_
  203.0 1.1 collective-permute-start.41
  204.2 2.2 collective-permute-start.54
  206.4 3.1 %merge_two.2 = (bf16[96,1728]{1,0:T(8,128)(2,1)}, bf16[96,1728]{1,0:T(8,128)(2,1)}, bf16[96,1728]{1,0:T(8,128)(2,1)}, bf16[96,1728]{1,0:T(8,128)(2,1)}) custom-call(s32[3]{0:T(128)} %pad_add_fusion.1.refs_0_.here, bf16[2,96,1728]{2,1,0:T(8,128)(2,1)} %get-tuple-element.202.refs_1_, bf16[2,96,1728]{2,1,0:T(8,128)(2,1)} %copy-done.29, ...), custom_call_target="tpu_custom_call" | custom-call | flops 3000000000 | bytes 8388608 | tf_op jit(solution)/shard_map/merge_two/pallas_call | solution.py:583
  209.7 1.0 collective-permute-start.52
  210.7 1.5 collective-permute-start.53
  214.4 2.6 collective-permute-done.41.refs_2_
  217.0 2.0 merge_two.3
  219.0 1.4 collective-permute-start.59
  220.7 18.9 %collective-permute-done.52.got_2 = bf16[96,1728]{1,0:T(8,128)(2,1)} collective-permute-done((bf16[96,1728]{1,0:T(8,128)(2,1)}, bf16[96,1728]{1,0:T(8,128)(2,1)}, u32[]{:S(2)}, u32[]{:S(2)}) %collective-permute-start.52) | collective-permute-done | bytes 331808 | tf_op jit(solution)/shard_map/ppermute | solution.py:41
  239.6 1.6 collective-permute-done.53.got_3
  241.2 2.5 merge_three.3.own
  243.8 2.2 fusion.1.p_0
  245.9 1.5 collective-permute-start.56
  247.9 1.8 collective-permute-start.45
  249.7 4.4 %collective-permute-done.44.got_1 = bf16[96,640]{1,0:T(8,128)(2,1)S(1)} collective-permute-done((bf16[96,640]{1,0:T(8,128)(2,1)S(1)}, bf16[96,640]{1,0:T(8,128)(2,1)S(1)}, u32[]{:S(2)}, u32[]{:S(2)}) %collective-permute-start.44) | collective-permute-done | bytes 122912 | tf_op jit(solution)/shard_map/ppermute | solution.py:41
  254.1 1.2 collective-permute-start.46
  255.4 2.2 collective-permute-done.45.got_2
  257.6 3.5 %collective-permute-done.46.got_3 = bf16[96,640]{1,0:T(8,128)(2,1)S(1)} collective-permute-done((bf16[96,640]{1,0:T(8,128)(2,1)S(1)}, bf16[96,640]{1,0:T(8,128)(2,1)S(1)}, u32[]{:S(2)}, u32[]{:S(2)}) %collective-permute-start.46) | collective-permute-done | bytes 122912 | tf_op jit(solution)/shard_map/ppermute | solution.py:41
  262.7 1.9 merge_three.2.d_own
  264.6 1.3 collective-permute-start.47
  266.6 3.2 %spread.3 = bf16[1536,768]{1,0:T(8,128)(2,1)} custom-call(s32[3]{0:T(128)} %pad_add_fusion.1.refs_0_.here, bf16[384,768]{1,0:T(8,128)(2,1)} %get-tuple-element.221.p_0, bf16[384,768]{1,0:T(8,128)(2,1)} %copy-done.32, bf16[384,768]{1,0:T(8,128)(2,1)} %collective-permute-done.59.p_2, bf16[384,768]{1,0:T(8,128)(2,1)} %copy-done.33), custom_call_target="tpu_custom_call" | custom-call | flops 3000000000 | bytes 8388608 | tf_op jit(solution)/shard_map/spread/pallas_call | solution.py:671
  271.4 4.1 %spread.2 = f32[1536,768]{1,0:T(8,128)} custom-call(s32[3]{0:T(128)} %pad_add_fusion.1.refs_0_.here, bf16[384,768]{1,0:T(8,128)(2,1)} %fusion.1.p_0, bf16[384,768]{1,0:T(8,128)(2,1)} %copy-done.34, bf16[384,768]{1,0:T(8,128)(2,1)} %copy-done.31, bf16[384,768]{1,0:T(8,128)(2,1)} %copy-done.35), custom_call_target="tpu_custom_call" | custom-call | flops 3000000000 | bytes 8388608 | tf_op jit(solution)/shard_map/spread/pallas_call | solution.py:671
  277.0 2.5 finish.1
  (256 shorter events, 34.3 us)
Async XLA Ops:
  2.6 13.4 %collective-permute-start.3 = (bf16[1,96,576]{2,1,0:T(8,128)(2,1)S(1)}, bf16[1,96,576]{2,1,0:T(8,128)(2,1)S(1)}, u32[]{:S(2)}, u32[]{:S(2)}) collective-permute-start(bf16[1,96,576]{2,1,0:T(8,128)(2,1)S(1)} %constant_dynamic-slice_fusion.1), channel_id=1, source_target_pairs={{0,24},{8,0},{16,8},{24,16},{1,25},{9,1},{17,9},{25,17},{2,26},{10... | collective-permute-start | bytes 331784 | tf_op jit(solution)/shard_map/ppermute | solution.py:41
  3.1 12.8 %collective-permute-start.2 = (bf16[1,96,576]{2,1,0:T(8,128)(2,1)S(1)}, bf16[1,96,576]{2,1,0:T(8,128)(2,1)S(1)}, u32[]{:S(2)}, u32[]{:S(2)}) collective-permute-start(bf16[1,96,576]{2,1,0:T(8,128)(2,1)S(1)} %constant_dynamic-slice_fusion.1), channel_id=1, source_target_pairs={{0,16},{8,24},{16,0},{24,8},{1,17},{9,25},{17,1},{25,9},{2,18},{10... | collective-permute-start | bytes 331784 | tf_op jit(solution)/shard_map/ppermute | solution.py:41
  5.7 10.2 %collective-permute-start.1 = (bf16[1,96,576]{2,1,0:T(8,128)(2,1)S(1)}, bf16[1,96,576]{2,1,0:T(8,128)(2,1)S(1)}, u32[]{:S(2)}, u32[]{:S(2)}) collective-permute-start(bf16[1,96,576]{2,1,0:T(8,128)(2,1)S(1)} %constant_dynamic-slice_fusion.1), channel_id=1, source_target_pairs={{0,8},{8,16},{16,24},{24,0},{1,9},{9,17},{17,25},{25,1},{2,10},{10... | collective-permute-start | bytes 331784 | tf_op jit(solution)/shard_map/ppermute | solution.py:41
  10.0 11.1 %collective-permute-start = (bf16[272,768]{1,0:T(8,128)(2,1)S(1)}, bf16[272,768]{1,0:T(8,128)(2,1)S(1)}, u32[]{:S(2)}, u32[]{:S(2)}) collective-permute-start(bf16[272,768]{1,0:T(8,128)(2,1)S(1)} %fusion.5), channel_id=1, source_target_pairs={{0,4},{4,0},{1,5},{5,1},{2,6},{6,2},{3,7},{7,3},{8,12},{12,8},{9,1... | collective-permute-start | bytes 1253384 | tf_op jit(solution)/shard_map/ppermute | solution.py:36
  11.9 16.7 %collective-permute-start.7 = (bf16[200,1728]{1,0:T(8,128)(2,1)S(1)}, bf16[200,1728]{1,0:T(8,128)(2,1)S(1)}, u32[]{:S(2)}, u32[]{:S(2)}) collective-permute-start(bf16[200,1728]{1,0:T(8,128)(2,1)S(1)} %pad_maximum_fusion.2.refs_8_), channel_id=1, source_target_pairs={{0,2},{1,3},{2,0},{3,1},{4,6},{5,7},{6,4},{7,5},{8,10},{9,11},{10,... | collective-permute-start | bytes 2073608 | tf_op jit(solution)/shard_map/ppermute | solution.py:36
  16.0 33.9 %collective-permute-start.5 = (bf16[96,1728]{1,0:T(8,128)(2,1)}, bf16[96,1728]{1,0:T(8,128)(2,1)}, u32[]{:S(2)}, u32[]{:S(2)}) collective-permute-start(bf16[96,1728]{1,0:T(8,128)(2,1)} %fusion.7), channel_id=1, source_target_pairs={{0,24},{8,0},{16,8},{24,16},{1,25},{9,1},{17,9},{25,17},{2,26},{10... | collective-permute-start | bytes 995336 | tf_op jit(solution)/shard_map/ppermute | solution.py:41
  17.4 36.6 %collective-permute-start.4 = (bf16[96,1728]{1,0:T(8,128)(2,1)}, bf16[96,1728]{1,0:T(8,128)(2,1)}, u32[]{:S(2)}, u32[]{:S(2)}) collective-permute-start(bf16[96,1728]{1,0:T(8,128)(2,1)} %fusion.7), channel_id=1, source_target_pairs={{0,8},{8,16},{16,24},{24,0},{1,9},{9,17},{17,25},{25,1},{2,10},{10... | collective-permute-start | bytes 995336 | tf_op jit(solution)/shard_map/ppermute | solution.py:41
  18.6 12.3 %collective-permute-start.10 = (bf16[3,96,576]{2,1,0:T(8,128)(2,1)S(1)}, bf16[3,96,576]{2,1,0:T(8,128)(2,1)S(1)}, u32[]{:S(2)}, u32[]{:S(2)}) collective-permute-start(bf16[3,96,576]{2,1,0:T(8,128)(2,1)S(1)} %constant_dynamic-update-slice_fusion.refs_9_), channel_id=1, source_target_pairs={{0,4},{4,0},{1,5},{5,1},{2,6},{6,2},{3,7},{7,3},{8,12},{12,8},{9,1... | collective-permute-start | bytes 995336 | tf_op jit(solution)/shard_map/ppermute | solution.py:36
  21.1 2.2 collective-permute-start.6
  28.6 25.3 %collective-permute-start.9 = (bf16[96,1728]{1,0:T(8,128)(2,1)S(1)}, bf16[96,1728]{1,0:T(8,128)(2,1)}, u32[]{:S(2)}, u32[]{:S(2)}) collective-permute-start(bf16[96,1728]{1,0:T(8,128)(2,1)S(1)} %constant_dynamic-slice_fusion), channel_id=1, source_target_pairs={{0,24},{8,0},{16,8},{24,16},{1,25},{9,1},{17,9},{25,17},{2,26},{10... | collective-permute-start | bytes 995336 | tf_op jit(solution)/shard_map/ppermute | solution.py:41
  28.7 25.3 %collective-permute-start.8 = (bf16[96,1728]{1,0:T(8,128)(2,1)S(1)}, bf16[96,1728]{1,0:T(8,128)(2,1)}, u32[]{:S(2)}, u32[]{:S(2)}) collective-permute-start(bf16[96,1728]{1,0:T(8,128)(2,1)S(1)} %constant_dynamic-slice_fusion), channel_id=1, source_target_pairs={{0,8},{8,16},{16,24},{24,0},{1,9},{9,17},{17,25},{25,1},{2,10},{10... | collective-permute-start | bytes 995336 | tf_op jit(solution)/shard_map/ppermute | solution.py:41
  30.9 27.8 %collective-permute-start.14 = (bf16[400,1728]{1,0:T(8,128)(2,1)S(1)}, bf16[400,1728]{1,0:T(8,128)(2,1)}, u32[]{:S(2)}, u32[]{:S(2)}) collective-permute-start(bf16[400,1728]{1,0:T(8,128)(2,1)S(1)} %pad_maximum_fusion), channel_id=1, source_target_pairs={{0,1},{1,0},{2,3},{3,2},{4,5},{5,4},{6,7},{7,6},{8,9},{9,8},{10,11... | collective-permute-start | bytes 4147208 | tf_op jit(solution)/shard_map/ppermute | solution.py:36
  49.9 25.5 %collective-permute-start.18 = (bf16[96,1728]{1,0:T(8,128)(2,1)}, bf16[96,1728]{1,0:T(8,128)(2,1)S(1)}, u32[]{:S(2)}, u32[]{:S(2)}) collective-permute-start(bf16[96,1728]{1,0:T(8,128)(2,1)} %fusion.7), channel_id=1, source_target_pairs={{0,16},{8,24},{16,0},{24,8},{1,17},{9,25},{17,1},{25,9},{2,18},{10... | collective-permute-start | bytes 995336 | tf_op jit(solution)/shard_map/ppermute | solution.py:41
  56.0 17.8 %collective-permute-start.13 = (bf16[192,1728]{1,0:T(8,128)(2,1)S(1)}, bf16[192,1728]{1,0:T(8,128)(2,1)S(1)}, u32[]{:S(2)}, u32[]{:S(2)}) collective-permute-start(bf16[192,1728]{1,0:T(8,128)(2,1)S(1)} %constant_dynamic-update-slice_fusion.3.refs_11_), channel_id=1, source_target_pairs={{0,4},{4,0},{1,5},{5,1},{2,6},{6,2},{3,7},{7,3},{8,12},{12,8},{9,1... | collective-permute-start | bytes 1990664 | tf_op jit(solution)/shard_map/ppermute | solution.py:36
  58.7 16.7 %collective-permute-start.12 = (bf16[192,1728]{1,0:T(8,128)(2,1)S(1)}, bf16[192,1728]{1,0:T(8,128)(2,1)}, u32[]{:S(2)}, u32[]{:S(2)}) collective-permute-start(bf16[192,1728]{1,0:T(8,128)(2,1)S(1)} %constant_dynamic-update-slice_fusion.3.refs_11_), channel_id=1, source_target_pairs={{0,2},{1,3},{2,0},{3,1},{4,6},{5,7},{6,4},{7,5},{8,10},{9,11},{10,... | collective-permute-start | bytes 1990664 | tf_op jit(solution)/shard_map/ppermute | solution.py:36
  58.7 16.7 %collective-permute-start.11 = (bf16[192,1728]{1,0:T(8,128)(2,1)S(1)}, bf16[192,1728]{1,0:T(8,128)(2,1)}, u32[]{:S(2)}, u32[]{:S(2)}) collective-permute-start(bf16[192,1728]{1,0:T(8,128)(2,1)S(1)} %constant_dynamic-update-slice_fusion.3.refs_11_), channel_id=1, source_target_pairs={{0,1},{1,0},{2,3},{3,2},{4,5},{5,4},{6,7},{7,6},{8,9},{9,8},{10,11... | collective-permute-start | bytes 1990664 | tf_op jit(solution)/shard_map/ppermute | solution.py:36
  58.7 35.7 %copy-start.21 = (bf16[768]{0:T(1024)(128)(2,1)S(1)}, bf16[768]{0:T(1024)(128)(2,1)}, u32[]{:S(2)}) copy-start(bf16[768]{0:T(1024)(128)(2,1)} %param.33) | copy-start | bytes 4612
  58.8 35.7 %copy-start.22 = (bf16[768]{0:T(1024)(128)(2,1)S(1)}, bf16[768]{0:T(1024)(128)(2,1)}, u32[]{:S(2)}) copy-start(bf16[768]{0:T(1024)(128)(2,1)} %param.34) | copy-start | bytes 4612
  75.4 8.4 %collective-permute-start.19 = (bf16[96,1728]{1,0:T(8,128)(2,1)S(1)}, bf16[96,1728]{1,0:T(8,128)(2,1)S(1)}, u32[]{:S(2)}, u32[]{:S(2)}) collective-permute-start(bf16[96,1728]{1,0:T(8,128)(2,1)S(1)} %collective-permute-done.18.refs_21_), channel_id=1, source_target_pairs={{0,4},{4,0},{1,5},{5,1},{2,6},{6,2},{3,7},{7,3},{8,12},{12,8},{9,1... | collective-permute-start | bytes 995336 | tf_op jit(solution)/shard_map/ppermute | solution.py:36
  75.8 10.9 %collective-permute-start.25 = (bf16[96,1728]{1,0:T(8,128)(2,1)S(1)}, bf16[96,1728]{1,0:T(8,128)(2,1)S(1)}, u32[]{:S(2)}, u32[]{:S(2)}) collective-permute-start(bf16[96,1728]{1,0:T(8,128)(2,1)S(1)} %collective-permute-done.18.refs_21_), channel_id=1, source_target_pairs={{0,2},{1,3},{2,0},{3,1},{4,6},{5,7},{6,4},{7,5},{8,10},{9,11},{10,... | collective-permute-start | bytes 995336 | tf_op jit(solution)/shard_map/ppermute | solution.py:36
  76.4 13.8 %collective-permute-start.28 = (bf16[96,1728]{1,0:T(8,128)(2,1)S(1)}, bf16[96,1728]{1,0:T(8,128)(2,1)S(1)}, u32[]{:S(2)}, u32[]{:S(2)}) collective-permute-start(bf16[96,1728]{1,0:T(8,128)(2,1)S(1)} %constant_dynamic-slice_fusion), channel_id=1, source_target_pairs={{0,16},{8,24},{16,0},{24,8},{1,17},{9,25},{17,1},{25,9},{2,18},{10... | collective-permute-start | bytes 995336 | tf_op jit(solution)/shard_map/ppermute | solution.py:41
  76.7 1.7 collective-permute-start.15
  76.7 13.7 %collective-permute-start.16 = (bf16[384,192]{1,0:T(8,128)(2,1)S(1)}, bf16[384,192]{1,0:T(8,128)(2,1)S(1)}, u32[]{:S(2)}, u32[]{:S(2)}) collective-permute-start(bf16[384,192]{1,0:T(8,128)(2,1)S(1)} %copy-done.48), channel_id=1, source_target_pairs={{0,2},{1,3},{2,0},{3,1},{4,6},{5,7},{6,4},{7,5},{8,10},{9,11},{10,... | collective-permute-start | bytes 442376 | tf_op jit(solution)/shard_map/ppermute | solution.py:36
  78.4 13.3 %collective-permute-start.17 = (bf16[384,192]{1,0:T(8,128)(2,1)S(1)}, bf16[384,192]{1,0:T(8,128)(2,1)S(1)}, u32[]{:S(2)}, u32[]{:S(2)}) collective-permute-start(bf16[384,192]{1,0:T(8,128)(2,1)S(1)} %copy-done.46), channel_id=1, source_target_pairs={{0,3},{1,2},{2,1},{3,0},{4,7},{5,6},{6,5},{7,4},{8,11},{9,10},{10,... | collective-permute-start | bytes 442376 | tf_op jit(solution)/shard_map/ppermute | solution.py:36
  83.8 8.7 %collective-permute-start.20 = (bf16[96,1728]{1,0:T(8,128)(2,1)}, bf16[96,1728]{1,0:T(8,128)(2,1)S(1)}, u32[]{:S(2)}, u32[]{:S(2)}) collective-permute-start(bf16[96,1728]{1,0:T(8,128)(2,1)} %collective-permute-done.8.refs_13_), channel_id=1, source_target_pairs={{0,1},{1,0},{2,3},{3,2},{4,5},{5,4},{6,7},{7,6},{8,9},{9,8},{10,11... | collective-permute-start | bytes 995336 | tf_op jit(solution)/shard_map/ppermute | solution.py:36
  86.7 5.7 %collective-permute-start.26 = (bf16[96,1728]{1,0:T(8,128)(2,1)S(1)}, bf16[96,1728]{1,0:T(8,128)(2,1)S(1)}, u32[]{:S(2)}, u32[]{:S(2)}) collective-permute-start(bf16[96,1728]{1,0:T(8,128)(2,1)S(1)} %collective-permute-done.25.refs_23_), channel_id=1, source_target_pairs={{0,1},{1,0},{2,3},{3,2},{4,5},{5,4},{6,7},{7,6},{8,9},{9,8},{10,11... | collective-permute-start | bytes 995336 | tf_op jit(solution)/shard_map/ppermute | solution.py:36
  90.2 2.7 collective-permute-start.21
  90.4 5.3 %collective-permute-start.22 = (bf16[192,1728]{1,0:T(8,128)(2,1)}, bf16[192,1728]{1,0:T(8,128)(2,1)S(1)}, u32[]{:S(2)}, u32[]{:S(2)}) collective-permute-start(bf16[192,1728]{1,0:T(8,128)(2,1)} %collective-permute-done.12.refs_17_), channel_id=1, source_target_pairs={{0,1},{1,0},{2,3},{3,2},{4,5},{5,4},{6,7},{7,6},{8,9},{9,8},{10,11... | collective-permute-start | bytes 1990664 | tf_op jit(solution)/shard_map/ppermute | solution.py:36
  91.7 4.1 %collective-permute-start.23 = (bf16[192,1728]{1,0:T(8,128)(2,1)S(1)}, bf16[192,1728]{1,0:T(8,128)(2,1)S(1)}, u32[]{:S(2)}, u32[]{:S(2)}) collective-permute-start(bf16[192,1728]{1,0:T(8,128)(2,1)S(1)} %collective-permute-done.13.refs_19_), channel_id=1, source_target_pairs={{0,1},{1,0},{2,3},{3,2},{4,5},{5,4},{6,7},{7,6},{8,9},{9,8},{10,11... | collective-permute-start | bytes 1990664 | tf_op jit(solution)/shard_map/ppermute | solution.py:36
  92.4 2.7 collective-permute-start.24
  92.5 2.8 collective-permute-start.29
  94.0 1.8 collective-permute-start.27
  121.1 5.4 %collective-permute-start.31 = (bf16[2,384,1792]{2,1,0:T(8,128)(2,1)}, bf16[2,384,1792]{2,1,0:T(8,128)(2,1)S(1)}, u32[]{:S(2)}, u32[]{:S(2)}) collective-permute-start(bf16[2,384,1792]{2,1,0:T(8,128)(2,1)} %get-tuple-element.160), channel_id=1, source_target_pairs={{0,1},{1,0},{2,3},{3,2},{4,5},{5,4},{6,7},{7,6},{8,9},{9,8},{10,11... | collective-permute-start | bytes 8257544 | tf_op jit(solution)/shard_map/ppermute | solution.py:36
  121.6 7.6 %collective-permute-start.30 = (bf16[3,768,384]{2,1,0:T(8,128)(2,1)}, bf16[3,768,384]{2,1,0:T(8,128)(2,1)}, u32[]{:S(2)}, u32[]{:S(2)}) collective-permute-start(bf16[3,768,384]{2,1,0:T(8,128)(2,1)} %get-tuple-element.158.refs_1_), channel_id=1, source_target_pairs={{0,1},{1,0},{2,3},{3,2},{4,5},{5,4},{6,7},{7,6},{8,9},{9,8},{10,11... | collective-permute-start | bytes 5308424 | tf_op jit(solution)/shard_map/ppermute | solution.py:36
  122.5 19.6 %collective-permute-start.33 = (bf16[384,192]{1,0:T(8,128)(2,1)}, bf16[384,192]{1,0:T(8,128)(2,1)S(1)}, u32[]{:S(2)}, u32[]{:S(2)}) collective-permute-start(bf16[384,192]{1,0:T(8,128)(2,1)} %get-tuple-element.166), channel_id=1, source_target_pairs={{0,1},{1,0},{2,3},{3,2},{4,5},{5,4},{6,7},{7,6},{8,9},{9,8},{10,11... | collective-permute-start | bytes 442376 | tf_op jit(solution)/shard_map/ppermute | solution.py:36
  122.9 19.1 %collective-permute-start.34 = (bf16[384,192]{1,0:T(8,128)(2,1)}, bf16[384,192]{1,0:T(8,128)(2,1)S(1)}, u32[]{:S(2)}, u32[]{:S(2)}) collective-permute-start(bf16[384,192]{1,0:T(8,128)(2,1)} %get-tuple-element.167), channel_id=1, source_target_pairs={{0,2},{1,3},{2,0},{3,1},{4,6},{5,7},{6,4},{7,5},{8,10},{9,11},{10,... | collective-permute-start | bytes 442376 | tf_op jit(solution)/shard_map/ppermute | solution.py:36
  124.5 17.5 %collective-permute-start.35 = (bf16[384,192]{1,0:T(8,128)(2,1)}, bf16[384,192]{1,0:T(8,128)(2,1)S(1)}, u32[]{:S(2)}, u32[]{:S(2)}) collective-permute-start(bf16[384,192]{1,0:T(8,128)(2,1)} %get-tuple-element.168), channel_id=1, source_target_pairs={{0,3},{1,2},{2,1},{3,0},{4,7},{5,6},{6,5},{7,4},{8,11},{9,10},{10,... | collective-permute-start | bytes 442376 | tf_op jit(solution)/shard_map/ppermute | solution.py:36
  126.5 15.6 %collective-permute-start.32 = (f32[8,768]{1,0:T(8,128)S(1)}, f32[8,768]{1,0:T(8,128)S(1)}, u32[]{:S(2)}, u32[]{:S(2)}) collective-permute-start(f32[8,768]{1,0:T(8,128)S(1)} %pad_maximum_fusion.4), channel_id=1, source_target_pairs={{0,1},{1,0},{2,3},{3,2},{4,5},{5,4},{6,7},{7,6},{8,9},{9,8},{10,11... | collective-permute-start | bytes 73736 | tf_op jit(solution)/shard_map/ppermute | solution.py:36
  142.1 27.2 %collective-permute-start.38 = (f32[8,768]{1,0:T(8,128)S(1)}, f32[8,768]{1,0:T(8,128)S(1)}, u32[]{:S(2)}, u32[]{:S(2)}) collective-permute-start(f32[8,768]{1,0:T(8,128)S(1)} %pad_maximum_fusion.5), channel_id=1, source_target_pairs={{0,2},{1,3},{2,0},{3,1},{4,6},{5,7},{6,4},{7,5},{8,10},{9,11},{10,... | collective-permute-start | bytes 73736 | tf_op jit(solution)/shard_map/ppermute | solution.py:36
  143.8 32.4 %collective-permute-start.36 = (bf16[4,96,1728]{2,1,0:T(8,128)(2,1)}, bf16[4,96,1728]{2,1,0:T(8,128)(2,1)S(1)}, u32[]{:S(2)}, u32[]{:S(2)}) collective-permute-start(bf16[4,96,1728]{2,1,0:T(8,128)(2,1)} %get-tuple-element.186), channel_id=1, source_target_pairs={{0,2},{1,3},{2,0},{3,1},{4,6},{5,7},{6,4},{7,5},{8,10},{9,11},{10,... | collective-permute-start | bytes 3981320 | tf_op jit(solution)/shard_map/ppermute | solution.py:36
  144.2 32.1 %collective-permute-start.37 = (bf16[2,2,96,1728]{3,2,1,0:T(8,128)(2,1)}, bf16[2,2,96,1728]{3,2,1,0:T(8,128)(2,1)S(1)}, u32[]{:S(2)}, u32[]{:S(2)}) collective-permute-start(bf16[2,2,96,1728]{3,2,1,0:T(8,128)(2,1)} %get-tuple-element.187), channel_id=1, source_target_pairs={{0,4},{4,0},{1,5},{5,1},{2,6},{6,2},{3,7},{7,3},{8,12},{12,8},{9,1... | collective-permute-start | bytes 3981320 | tf_op jit(solution)/shard_map/ppermute | solution.py:36
  176.3 12.7 %collective-permute-start.39 = (bf16[512,384]{1,0:T(8,128)(2,1)}, bf16[512,384]{1,0:T(8,128)(2,1)S(1)}, u32[]{:S(2)}, u32[]{:S(2)}) collective-permute-start(bf16[512,384]{1,0:T(8,128)(2,1)} %get-tuple-element.193), channel_id=1, source_target_pairs={{0,4},{4,0},{1,5},{5,1},{2,6},{6,2},{3,7},{7,3},{8,12},{12,8},{9,1... | collective-permute-start | bytes 1179656 | tf_op jit(solution)/shard_map/ppermute | solution.py:36
  177.7 11.3 %collective-permute-start.40 = (f32[8,768]{1,0:T(8,128)S(1)}, f32[8,768]{1,0:T(8,128)S(1)}, u32[]{:S(2)}, u32[]{:S(2)}) collective-permute-start(f32[8,768]{1,0:T(8,128)S(1)} %add.60), channel_id=1, source_target_pairs={{0,4},{4,0},{1,5},{5,1},{2,6},{6,2},{3,7},{7,3},{8,12},{12,8},{9,1... | collective-permute-start | bytes 73736 | tf_op jit(solution)/shard_map/ppermute | solution.py:36
  182.8 19.3 %collective-permute-start.42 = (bf16[2,96,1728]{2,1,0:T(8,128)(2,1)}, bf16[2,96,1728]{2,1,0:T(8,128)(2,1)S(1)}, u32[]{:S(2)}, u32[]{:S(2)}) collective-permute-start(bf16[2,96,1728]{2,1,0:T(8,128)(2,1)} %get-tuple-element.196), channel_id=1, source_target_pairs={{0,4},{4,0},{1,5},{5,1},{2,6},{6,2},{3,7},{7,3},{8,12},{12,8},{9,1... | collective-permute-start | bytes 1990664 | tf_op jit(solution)/shard_map/ppermute | solution.py:36
  184.2 17.9 %collective-permute-start.43 = (bf16[2,96,1728]{2,1,0:T(8,128)(2,1)}, bf16[2,96,1728]{2,1,0:T(8,128)(2,1)S(1)}, u32[]{:S(2)}, u32[]{:S(2)}) collective-permute-start(bf16[2,96,1728]{2,1,0:T(8,128)(2,1)} %get-tuple-element.197), channel_id=1, source_target_pairs={{0,2},{1,3},{2,0},{3,1},{4,6},{5,7},{6,4},{7,5},{8,10},{9,11},{10,... | collective-permute-start | bytes 1990664 | tf_op jit(solution)/shard_map/ppermute | solution.py:36
  189.1 11.3 %collective-permute-start.48 = (f32[8,768]{1,0:T(8,128)S(1)}, f32[8,768]{1,0:T(8,128)S(1)}, u32[]{:S(2)}, u32[]{:S(2)}) collective-permute-start(f32[8,768]{1,0:T(8,128)S(1)} %add.61), channel_id=1, source_target_pairs={{0,8},{8,0},{16,24},{24,16},{1,9},{9,1},{17,25},{25,17},{2,10},{10... | collective-permute-start | bytes 73736 | tf_op jit(solution)/shard_map/ppermute | solution.py:36
  203.0 7.7 %collective-permute-start.49 = (bf16[2,384,768]{2,1,0:T(8,128)(2,1)}, bf16[2,384,768]{2,1,0:T(8,128)(2,1)S(1)}, u32[]{:S(2)}, u32[]{:S(2)}) collective-permute-start(bf16[2,384,768]{2,1,0:T(8,128)(2,1)} %get-tuple-element.213), channel_id=1, source_target_pairs={{0,1},{1,0},{2,3},{3,2},{4,5},{5,4},{6,7},{7,6},{8,9},{9,8},{10,11... | collective-permute-start | bytes 3538952 | tf_op jit(solution)/shard_map/ppermute | solution.py:36
  203.0 13.9 %collective-permute-start.41 = (bf16[4,96,640]{2,1,0:T(8,128)(2,1)}, bf16[4,96,640]{2,1,0:T(8,128)(2,1)}, u32[]{:S(2)}, u32[]{:S(2)}) collective-permute-start(bf16[4,96,640]{2,1,0:T(8,128)(2,1)} %get-tuple-element.201), channel_id=1, source_target_pairs={{0,4},{4,0},{1,5},{5,1},{2,6},{6,2},{3,7},{7,3},{8,12},{12,8},{9,1... | collective-permute-start | bytes 1474568 | tf_op jit(solution)/shard_map/ppermute | solution.py:36
  204.2 8.9 %collective-permute-start.54 = (f32[8,768]{1,0:T(8,128)S(1)}, f32[8,768]{1,0:T(8,128)S(1)}, u32[]{:S(2)}, u32[]{:S(2)}) collective-permute-start(f32[8,768]{1,0:T(8,128)S(1)} %add.62), channel_id=1, source_target_pairs={{0,16},{8,24},{16,0},{24,8},{1,17},{9,25},{17,1},{25,9},{2,18},{10... | collective-permute-start | bytes 73736 | tf_op jit(solution)/shard_map/ppermute | solution.py:36
  209.5 11.2 %collective-permute-start.51 = (bf16[96,1728]{1,0:T(8,128)(2,1)}, bf16[96,1728]{1,0:T(8,128)(2,1)}, u32[]{:S(2)}, u32[]{:S(2)}) collective-permute-start(bf16[96,1728]{1,0:T(8,128)(2,1)} %get-tuple-element.214), channel_id=1, source_target_pairs={{0,8},{8,16},{16,24},{24,0},{1,9},{9,17},{17,25},{25,1},{2,10},{10... | collective-permute-start | bytes 995336 | tf_op jit(solution)/shard_map/ppermute | solution.py:41
  209.7 29.9 %collective-permute-start.52 = (bf16[96,1728]{1,0:T(8,128)(2,1)}, bf16[96,1728]{1,0:T(8,128)(2,1)}, u32[]{:S(2)}, u32[]{:S(2)}) collective-permute-start(bf16[96,1728]{1,0:T(8,128)(2,1)} %get-tuple-element.215), channel_id=1, source_target_pairs={{0,16},{8,24},{16,0},{24,8},{1,17},{9,25},{17,1},{25,9},{2,18},{10... | collective-permute-start | bytes 995336 | tf_op jit(solution)/shard_map/ppermute | solution.py:41
  210.7 30.5 %collective-permute-start.53 = (bf16[96,1728]{1,0:T(8,128)(2,1)}, bf16[96,1728]{1,0:T(8,128)(2,1)}, u32[]{:S(2)}, u32[]{:S(2)}) collective-permute-start(bf16[96,1728]{1,0:T(8,128)(2,1)} %get-tuple-element.216), channel_id=1, source_target_pairs={{0,24},{8,0},{16,8},{24,16},{1,25},{9,1},{17,9},{25,17},{2,26},{10... | collective-permute-start | bytes 995336 | tf_op jit(solution)/shard_map/ppermute | solution.py:41
  213.1 30.6 %collective-permute-start.50 = (bf16[384,768]{1,0:T(8,128)(2,1)}, bf16[384,768]{1,0:T(8,128)(2,1)}, u32[]{:S(2)}, u32[]{:S(2)}) collective-permute-start(bf16[384,768]{1,0:T(8,128)(2,1)} %fusion.3), channel_id=1, source_target_pairs={{0,2},{1,3},{2,0},{3,1},{4,6},{5,7},{6,4},{7,5},{8,10},{9,11},{10,... | collective-permute-start | bytes 1769480 | tf_op jit(solution)/shard_map/ppermute | solution.py:36
  219.0 28.4 %collective-permute-start.59 = (bf16[384,768]{1,0:T(8,128)(2,1)}, bf16[384,768]{1,0:T(8,128)(2,1)}, u32[]{:S(2)}, u32[]{:S(2)}) collective-permute-start(bf16[384,768]{1,0:T(8,128)(2,1)} %get-tuple-element.221.p_0), channel_id=1, source_target_pairs={{0,2},{1,3},{2,0},{3,1},{4,6},{5,7},{6,4},{7,5},{8,10},{9,11},{10,... | collective-permute-start | bytes 1769480 | tf_op jit(solution)/shard_map/ppermute | solution.py:36
  245.9 15.8 %collective-permute-start.56 = (bf16[384,768]{1,0:T(8,128)(2,1)}, bf16[384,768]{1,0:T(8,128)(2,1)S(1)}, u32[]{:S(2)}, u32[]{:S(2)}) collective-permute-start(bf16[384,768]{1,0:T(8,128)(2,1)} %fusion.1.p_0), channel_id=1, source_target_pairs={{0,2},{1,3},{2,0},{3,1},{4,6},{5,7},{6,4},{7,5},{8,10},{9,11},{10,... | collective-permute-start | bytes 1769480 | tf_op jit(solution)/shard_map/ppermute | solution.py:36
  247.4 17.1 %collective-permute-start.58 = (bf16[384,768]{1,0:T(8,128)(2,1)}, bf16[384,768]{1,0:T(8,128)(2,1)S(1)}, u32[]{:S(2)}, u32[]{:S(2)}) collective-permute-start(bf16[384,768]{1,0:T(8,128)(2,1)} %get-tuple-element.221.p_0), channel_id=1, source_target_pairs={{0,1},{1,0},{2,3},{3,2},{4,5},{5,4},{6,7},{7,6},{8,9},{9,8},{10,11... | collective-permute-start | bytes 1769480 | tf_op jit(solution)/shard_map/ppermute | solution.py:36
  247.4 18.4 %collective-permute-start.60 = (bf16[384,768]{1,0:T(8,128)(2,1)}, bf16[384,768]{1,0:T(8,128)(2,1)S(1)}, u32[]{:S(2)}, u32[]{:S(2)}) collective-permute-start(bf16[384,768]{1,0:T(8,128)(2,1)} %collective-permute-done.59.p_2), channel_id=1, source_target_pairs={{0,1},{1,0},{2,3},{3,2},{4,5},{5,4},{6,7},{7,6},{8,9},{9,8},{10,11... | collective-permute-start | bytes 1769480 | tf_op jit(solution)/shard_map/ppermute | solution.py:36
  247.9 6.2 %collective-permute-start.44 = (bf16[96,640]{1,0:T(8,128)(2,1)S(1)}, bf16[96,640]{1,0:T(8,128)(2,1)S(1)}, u32[]{:S(2)}, u32[]{:S(2)}) collective-permute-start(bf16[96,640]{1,0:T(8,128)(2,1)S(1)} %copy-done.56), channel_id=1, source_target_pairs={{0,8},{8,16},{16,24},{24,0},{1,9},{9,17},{17,25},{25,1},{2,10},{10... | collective-permute-start | bytes 368648 | tf_op jit(solution)/shard_map/ppermute | solution.py:41
  247.9 9.7 %collective-permute-start.45 = (bf16[96,640]{1,0:T(8,128)(2,1)S(1)}, bf16[96,640]{1,0:T(8,128)(2,1)}, u32[]{:S(2)}, u32[]{:S(2)}) collective-permute-start(bf16[96,640]{1,0:T(8,128)(2,1)S(1)} %copy-done.55), channel_id=1, source_target_pairs={{0,16},{8,24},{16,0},{24,8},{1,17},{9,25},{17,1},{25,9},{2,18},{10... | collective-permute-start | bytes 368648 | tf_op jit(solution)/shard_map/ppermute | solution.py:41
  254.1 7.0 %collective-permute-start.46 = (bf16[96,640]{1,0:T(8,128)(2,1)S(1)}, bf16[96,640]{1,0:T(8,128)(2,1)S(1)}, u32[]{:S(2)}, u32[]{:S(2)}) collective-permute-start(bf16[96,640]{1,0:T(8,128)(2,1)S(1)} %copy-done.54), channel_id=1, source_target_pairs={{0,24},{8,0},{16,8},{24,16},{1,25},{9,1},{17,9},{25,17},{2,26},{10... | collective-permute-start | bytes 368648 | tf_op jit(solution)/shard_map/ppermute | solution.py:41
  257.6 12.2 %collective-permute-start.55 = (bf16[384,768]{1,0:T(8,128)(2,1)}, bf16[384,768]{1,0:T(8,128)(2,1)S(1)}, u32[]{:S(2)}, u32[]{:S(2)}) collective-permute-start(bf16[384,768]{1,0:T(8,128)(2,1)} %fusion.1.p_0), channel_id=1, source_target_pairs={{0,1},{1,0},{2,3},{3,2},{4,5},{5,4},{6,7},{7,6},{8,9},{9,8},{10,11... | collective-permute-start | bytes 1769480 | tf_op jit(solution)/shard_map/ppermute | solution.py:36
  261.8 8.1 %collective-permute-start.57 = (bf16[384,768]{1,0:T(8,128)(2,1)S(1)}, bf16[384,768]{1,0:T(8,128)(2,1)S(1)}, u32[]{:S(2)}, u32[]{:S(2)}) collective-permute-start(bf16[384,768]{1,0:T(8,128)(2,1)S(1)} %collective-permute-done.56.p_2), channel_id=1, source_target_pairs={{0,1},{1,0},{2,3},{3,2},{4,5},{5,4},{6,7},{7,6},{8,9},{9,8},{10,11... | collective-permute-start | bytes 1769480 | tf_op jit(solution)/shard_map/ppermute | solution.py:36
  261.8 14.4 %collective-permute-start.61 = (bf16[96,1728]{1,0:T(8,128)(2,1)}, bf16[96,1728]{1,0:T(8,128)(2,1)S(1)}, u32[]{:S(2)}, u32[]{:S(2)}) collective-permute-start(bf16[96,1728]{1,0:T(8,128)(2,1)} %merge_three.3.own), channel_id=1, source_target_pairs={{0,4},{4,0},{1,5},{5,1},{2,6},{6,2},{3,7},{7,3},{8,12},{12,8},{9,1... | collective-permute-start | bytes 995336 | tf_op jit(solution)/shard_map/ppermute | solution.py:36
  264.6 11.0 %collective-permute-start.47 = (bf16[96,640]{1,0:T(8,128)(2,1)}, bf16[96,640]{1,0:T(8,128)(2,1)S(1)}, u32[]{:S(2)}, u32[]{:S(2)}) collective-permute-start(bf16[96,640]{1,0:T(8,128)(2,1)} %merge_three.2.d_own), channel_id=1, source_target_pairs={{0,4},{4,0},{1,5},{5,1},{2,6},{6,2},{3,7},{7,3},{8,12},{12,8},{9,1... | collective-permute-start | bytes 368648 | tf_op jit(solution)/shard_map/ppermute | solution.py:36
  (60 other events, 477.5 us)

commit v5 on v4

--- a/solution.py
+++ b/solution.py
@@ -1115,9 +1115,10 @@
         (far_mine,) = after([swap(mine, "tp", 2)], d_totals)
         grad_inputs = everyone(mine, far_mine, high)
         got = swap(total, "ctx", 1)
+        d_totals[1], output = lax.optimization_barrier((d_totals[1], output))
         d_total = merge_three(here, d_totals)
         d_got = swap(d_total, "ctx", 1)
-        d_got, grad_inputs, output, pair = lax.optimization_barrier((d_got, grad_inputs, output, pair))
+        d_got, grad_inputs, pair = lax.optimization_barrier((d_got, grad_inputs, pair))
         s_inner, s_outer, s_out, s_query, s_key, s_value, s_bias = finish(
             here, total, got, d_total, d_got, hidden, local
         )

time: 284 us -> 284 us (level)
    unnamed x130 -> x132, local copies, waits for them, and re-layouts: 10.6 us -> 11.2 us
  transfers between devices with their start and end apart: 62 -> 62, of which waited for: 26 -> 25; matrix products, arithmetic and copies ran while one was open for 6% -> 6% of each run, Pallas kernels for 35% -> 35%
where the time goes in v5:
time: 284 us; the launch traced here: 282 us
  Pallas kernels  125 us (44%)
  waiting for transfers between devices  73.2 us (26%)
  starting transfers between devices  52.9 us (19%)
  local copies, waits for them, and re-layouts  18.3 us (6%)
  other arithmetic  11 us (4%)
    ppermute x15, waiting for transfers between devices, shift(): lax.ppermute(value, axis, [(i, (i + step) % count) for i in range(count)])  37.2 us
    ppermute x47, waiting for transfers between devices, swap(): return lax.ppermute(value, axis, [(i, i ^ bit) for i in range(count)])  36 us
    ppermute x47, starting transfers between devices, swap(): return lax.ppermute(value, axis, [(i, i ^ bit) for i in range(count)])  32.8 us
    pallas_call x1, Pallas kernels, attend_back(): pl.pallas_call(lambda *refs: attend_back_kernel(*refs, block=block, width...  23.7 us
    pallas_call x1, Pallas kernels, feed(): pl.pallas_call(lambda *refs: feed_kernel(*refs, plan=plan, count=len(piec...  23.7 us
    ppermute x15, starting transfers between devices, shift(): lax.ppermute(value, axis, [(i, (i + step) % count) for i in range(count)])  20.1 us
    pallas_call x1, Pallas kernels, attend_far(): pl.pallas_call(lambda *refs: attend_far_kernel(*refs, block=block, width=...  18.3 us
    pallas_call x1, Pallas kernels, attend_near(): pl.pallas_call(lambda *refs: attend_near_kernel(*refs, block=block, width...  13.6 us
  transfers between devices with their start and end apart: 62, of which 25 were waited for; matrix products, arithmetic and copies ran while one was open for 6% of the time, Pallas kernels for 35%

profile of v5, /device:TPU:10, one launch (start us, length us, event | category | flops | bytes accessed | tf_op | source)
XLA Modules:
  0.0 282.1 jit_solution(8815226440163371039)
XLA Ops:
  0.7 1.2 pad_maximum_fusion.3
  3.1 2.6 collective-permute-start.2
  5.7 2.5 collective-permute-start.1
  8.9 1.1 constant_dynamic-slice_fusion.2
  10.0 1.6 collective-permute-start
  14.7 1.2 collective-permute-done.1
  16.0 1.4 collective-permute-start.5
  17.4 1.2 collective-permute-start.4
  18.6 1.5 collective-permute-start.10
  21.2 1.2 or_convert_fusion
  24.4 4.2 %collective-permute-done.7.refs_9_ = bf16[200,1728]{1,0:T(8,128)(2,1)S(1)} collective-permute-done((bf16[200,1728]{1,0:T(8,128)(2,1)S(1)}, bf16[200,1728]{1,0:T(8,128)(2,1)S(1)}, u32[]{:S(2)}, u32[]{:S(2)}) %collective-permute-start.7) | collective-permute-done | bytes 691232 | tf_op jit(solution)/shard_map/ppermute | solution.py:36
  28.7 2.0 collective-permute-start.8
  31.6 18.3 %attend_far.1 = (bf16[384,192]{1,0:T(8,128)(2,1)}, bf16[384,192]{1,0:T(8,128)(2,1)}, f32[2,384,192]{2,1,0:T(8,128)}, bf16[3,2,384,128]{3,2,1,0:T(8,128)(2,1)}, b...) custom-call(s32[3]{0:T(128)} %pad_add_fusion.1.refs_0_.here, ...), custom_call_target="tpu_custom_call" | custom-call | flops 20000000000 | bytes 8388608 | tf_op jit(solution)/shard_map/attend_far/pallas_call | solution.py:227
  49.9 4.1 %collective-permute-start.18 = (bf16[96,1728]{1,0:T(8,128)(2,1)}, bf16[96,1728]{1,0:T(8,128)(2,1)S(1)}, u32[]{:S(2)}, u32[]{:S(2)}) collective-permute-start(bf16[96,1728]{1,0:T(8,128)(2,1)} %fusion.7), channel_id=1, source_target_pairs={{0,16},{8,24},{16,0},{24,8},{1,17},{9,25},{17,1},{25,9},{2,18},{10... | collective-permute-start | bytes 995336 | tf_op jit(solution)/shard_map/ppermute | solution.py:41
  54.0 1.0 constant_dynamic-update-slice_fusion.4
  55.0 1.0 constant_dynamic-update-slice_fusion.3.refs_11_
  56.6 1.1 collective-permute-start.12
  57.8 13.6 %attend_near.1 = (bf16[384,192]{1,0:T(8,128)(2,1)}, bf16[384,192]{1,0:T(8,128)(2,1)}, f32[2,384,192]{2,1,0:T(8,128)}, bf16[3,2,384,128]{3,2,1,0:T(8,128)(2,1)}) custom-call(s32[3]{0:T(128)} %pad_add_fusion.1.refs_0_.here, s32[1536]{0:T(1024)} %copy-done.14, s32[2048]{0:T(1024)} %copy-done.13, bf16[3,2,384,128]{3,2,1,0:T(8,128)(2,1)} %get-tuple-element.136.refs_3_, ...), custom_call_target="tpu_custom_call" | custom-call | flops 12000000000 | bytes 8388608 | tf_op jit(solution)/shard_map/attend_near/pallas_call | solution.py:255
  71.4 1.5 collective-permute-done.13.refs_19_
  73.3 1.6 collective-permute-start.19
  74.9 1.6 collective-permute-start.25
  77.2 1.2 collective-permute-done.15.refs_4_
  78.7 3.2 %collective-permute-done.19.refs_25_ = bf16[96,1728]{1,0:T(8,128)(2,1)S(1)} collective-permute-done((bf16[96,1728]{1,0:T(8,128)(2,1)S(1)}, bf16[96,1728]{1,0:T(8,128)(2,1)S(1)}, u32[]{:S(2)}, u32[]{:S(2)}) %collective-permute-start.19) | collective-permute-done | bytes 331808 | tf_op jit(solution)/shard_map/ppermute | solution.py:36
  81.9 3.9 %collective-permute-done.25.refs_23_ = bf16[96,1728]{1,0:T(8,128)(2,1)S(1)} collective-permute-done((bf16[96,1728]{1,0:T(8,128)(2,1)S(1)}, bf16[96,1728]{1,0:T(8,128)(2,1)S(1)}, u32[]{:S(2)}, u32[]{:S(2)}) %collective-permute-start.25) | collective-permute-done | bytes 331808 | tf_op jit(solution)/shard_map/ppermute | solution.py:36
  85.8 3.9 %collective-permute-done.28.refs_27_ = bf16[96,1728]{1,0:T(8,128)(2,1)S(1)} collective-permute-done((bf16[96,1728]{1,0:T(8,128)(2,1)S(1)}, bf16[96,1728]{1,0:T(8,128)(2,1)S(1)}, u32[]{:S(2)}, u32[]{:S(2)}) %collective-permute-start.28) | collective-permute-done | bytes 331808 | tf_op jit(solution)/shard_map/ppermute | solution.py:41
  96.9 23.7 %feed.1 = (bf16[384,768]{1,0:T(8,128)(2,1)}, f32[384,768]{1,0:T(8,128)}, f32[12,1,768]{2,1,0:T(1,128)}, bf16[384,192]{1,0:T(8,128)(2,1)}, bf16[384,192]{1,0:T(8,...) custom-call(s32[3]{0:T(128)} %pad_add_fusion.1.refs_0_.here, ...), custom_call_target="tpu_custom_call" | custom-call | flops 25999998976 | bytes 25165824 | tf_op jit(solution)/shard_map/feed/pallas_call | solution.py:433
  122.1 1.3 collective-permute-start.34
  124.5 1.4 collective-permute-done.31.refs_4_
  126.1 2.5 collective-permute-done.30.refs_2_
  128.6 12.8 %unit_grads.1 = (bf16[4,96,1728]{2,1,0:T(8,128)(2,1)}, bf16[4,96,1728]{2,1,0:T(8,128)(2,1)}, bf16[2,2,96,1728]{3,2,1,0:T(8,128)(2,1)}, bf16[2,2,96,1728]{3,2,1,0:T(8,128)(2,1)}) custom-call(s32[3]{0:T(128)} %pad_add_fusion.1.refs_0_.here, bf16[3,768,384]{2,1,0:T(8,128)(2,1)} %get-tuple-element.159.refs_1_, ...), custom_call_target="tpu_custom_call" | custom-call | flops 12000000000 | bytes 14680064 | tf_op jit(solution)/shard_map/unit_grads/pallas_call | solution.py:520
  141.5 1.1 collective-permute-start.38
  142.6 1.0 collective-permute-start.36
  144.0 23.7 %attend_back.1 = (bf16[1536,576]{1,0:T(8,128)(2,1)}, bf16[512,384]{1,0:T(8,128)(2,1)}) custom-call(s32[3]{0:T(128)} %pad_add_fusion.1.refs_0_.here, s32[1536]{0:T(1024)} %copy-done.14, s32[2048]{0:T(1024)} %copy-done.13, bf16[384,192]{1,0:T(8,128)(2,1)} %get-tuple-element.176.refs_3_, bf16[384,192]{1,0:T(8,128)(2,1)} %copy-done.52, ...), custom_call_target="tpu_custom_call" | custom-call | flops 24000000000 | bytes 8388608 | tf_op jit(solution)/shard_map/attend_back/pallas_call | solution.py:820
  167.7 7.3 %collective-permute-done.36.ga = bf16[4,96,1728]{2,1,0:T(8,128)(2,1)S(1)} collective-permute-done((bf16[4,96,1728]{2,1,0:T(8,128)(2,1)}, bf16[4,96,1728]{2,1,0:T(8,128)(2,1)S(1)}, u32[]{:S(2)}, u32[]{:S(2)}) %collective-permute-start.36) | collective-permute-done | bytes 1327136 | tf_op jit(solution)/shard_map/ppermute | solution.py:36
  175.9 1.6 collective-permute-start.40
  177.5 4.4 %merge_one.1 = (bf16[2,96,1728]{2,1,0:T(8,128)(2,1)}, bf16[2,96,1728]{2,1,0:T(8,128)(2,1)}, bf16[2,96,1728]{2,1,0:T(8,128)(2,1)}, bf16[2,96,1728]{2,1,0:T(8,128)(2,1)}) custom-call(s32[3]{0:T(128)} %pad_add_fusion.1.refs_0_.here, bf16[4,96,1728]{2,1,0:T(8,128)(2,1)} %get-tuple-element.195.ak, bf16[4,96,1728]{2,1,0:T(8,128)(2,1)} %copy-done.24, ...), custom_call_target="tpu_custom_call" | custom-call | flops 3000000000 | bytes 8388608 | tf_op jit(solution)/shard_map/merge_one/pallas_call | solution.py:561
  182.3 1.5 collective-permute-start.43
  183.9 4.4 %collective-permute-done.40 = f32[8,768]{1,0:T(8,128)S(1)} collective-permute-done((f32[8,768]{1,0:T(8,128)S(1)}, f32[8,768]{1,0:T(8,128)S(1)}, u32[]{:S(2)}, u32[]{:S(2)}) %collective-permute-start.40) | collective-permute-done | bytes 24608 | tf_op jit(solution)/shard_map/ppermute | solution.py:36
  188.2 1.7 collective-permute-start.51
  189.9 9.5 %project_back.1 = (bf16[2,384,768]{2,1,0:T(8,128)(2,1)}, bf16[2,384,768]{2,1,0:T(8,128)(2,1)}, bf16[4,96,640]{2,1,0:T(8,128)(2,1)}, bf16[4,96,640]{2,1,0:T(8,128)(2,1)}) custom-call(s32[3]{0:T(128)} %pad_add_fusion.1.refs_0_.here, bf16[1536,576]{1,0:T(8,128)(2,1)} %get-tuple-element.185.refs_1_, bf16[512,384]{1,0:T(8,128)(2,1)} %copy-done.37, ...), custom_call_target="tpu_custom_call" | custom-call | flops 8999999488 | bytes 8388608 | tf_op jit(solution)/shard_map/project_back/pallas_call | solution.py:729
  199.4 1.4 collective-permute-done.42.refs_2_
  202.4 3.0 %collective-permute-start.57 = (f32[8,768]{1,0:T(8,128)S(1)}, f32[8,768]{1,0:T(8,128)S(1)}, u32[]{:S(2)}, u32[]{:S(2)}) collective-permute-start(f32[8,768]{1,0:T(8,128)S(1)} %add.62), channel_id=1, source_target_pairs={{0,16},{8,24},{16,0},{24,8},{1,17},{9,25},{17,1},{25,9},{2,18},{10... | collective-permute-start | bytes 73736 | tf_op jit(solution)/shard_map/ppermute | solution.py:36
  205.4 3.1 %merge_two.2 = (bf16[96,1728]{1,0:T(8,128)(2,1)}, bf16[96,1728]{1,0:T(8,128)(2,1)}, bf16[96,1728]{1,0:T(8,128)(2,1)}, bf16[96,1728]{1,0:T(8,128)(2,1)}) custom-call(s32[3]{0:T(128)} %pad_add_fusion.1.refs_0_.here, bf16[2,96,1728]{2,1,0:T(8,128)(2,1)} %get-tuple-element.203.refs_1_, bf16[2,96,1728]{2,1,0:T(8,128)(2,1)} %copy-done.29, ...), custom_call_target="tpu_custom_call" | custom-call | flops 3000000000 | bytes 8388608 | tf_op jit(solution)/shard_map/merge_two/pallas_call | solution.py:583
  208.5 1.0 collective-permute-start.54
  211.9 1.4 collective-permute-start.53
  213.9 1.9 collective-permute-done.41.refs_2_
  215.8 2.0 merge_two.3
  217.8 1.4 collective-permute-start.46
  219.2 13.7 %collective-permute-done.54.got_1 = bf16[96,1728]{1,0:T(8,128)(2,1)} collective-permute-done((bf16[96,1728]{1,0:T(8,128)(2,1)}, bf16[96,1728]{1,0:T(8,128)(2,1)}, u32[]{:S(2)}, u32[]{:S(2)}) %collective-permute-start.54) | collective-permute-done | bytes 331808 | tf_op jit(solution)/shard_map/ppermute | solution.py:41
  232.9 6.5 %collective-permute-done.55.got_2 = bf16[96,1728]{1,0:T(8,128)(2,1)} collective-permute-done((bf16[96,1728]{1,0:T(8,128)(2,1)}, bf16[96,1728]{1,0:T(8,128)(2,1)}, u32[]{:S(2)}, u32[]{:S(2)}) %collective-permute-start.55) | collective-permute-done | bytes 331808 | tf_op jit(solution)/shard_map/ppermute | solution.py:41
  239.4 1.7 collective-permute-done.56.got_3
  241.1 2.5 merge_three.3.own
  243.6 2.2 fusion.1.p_0
  245.8 1.4 collective-permute-start.59
  247.7 1.8 collective-permute-start.48
  249.5 4.4 %collective-permute-done.44.got_1 = bf16[96,640]{1,0:T(8,128)(2,1)S(1)} collective-permute-done((bf16[96,640]{1,0:T(8,128)(2,1)S(1)}, bf16[96,640]{1,0:T(8,128)(2,1)S(1)}, u32[]{:S(2)}, u32[]{:S(2)}) %collective-permute-start.44) | collective-permute-done | bytes 122912 | tf_op jit(solution)/shard_map/ppermute | solution.py:41
  253.9 1.2 collective-permute-start.49
  255.2 2.2 collective-permute-done.48.got_2
  257.4 3.5 %collective-permute-done.49.got_3 = bf16[96,640]{1,0:T(8,128)(2,1)S(1)} collective-permute-done((bf16[96,640]{1,0:T(8,128)(2,1)S(1)}, bf16[96,640]{1,0:T(8,128)(2,1)S(1)}, u32[]{:S(2)}, u32[]{:S(2)}) %collective-permute-start.49) | collective-permute-done | bytes 122912 | tf_op jit(solution)/shard_map/ppermute | solution.py:41
  263.9 3.2 %spread.2 = bf16[1536,768]{1,0:T(8,128)(2,1)} custom-call(s32[3]{0:T(128)} %pad_add_fusion.1.refs_0_.here, bf16[384,768]{1,0:T(8,128)(2,1)} %get-tuple-element.210.p_0, bf16[384,768]{1,0:T(8,128)(2,1)} %copy-done.33, bf16[384,768]{1,0:T(8,128)(2,1)} %collective-permute-done.46.p_2, bf16[384,768]{1,0:T(8,128)(2,1)} %copy-done.34), custom_call_target="tpu_custom_call" | custom-call | flops 3000000000 | bytes 8388608 | tf_op jit(solution)/shard_map/spread/pallas_call | solution.py:671
  267.1 1.9 merge_three.2.d_own
  269.0 1.4 collective-permute-start.50
  272.0 4.1 %spread.3 = f32[1536,768]{1,0:T(8,128)} custom-call(s32[3]{0:T(128)} %pad_add_fusion.1.refs_0_.here, bf16[384,768]{1,0:T(8,128)(2,1)} %fusion.1.p_0, bf16[384,768]{1,0:T(8,128)(2,1)} %copy-done.35, bf16[384,768]{1,0:T(8,128)(2,1)} %copy-done.32, bf16[384,768]{1,0:T(8,128)(2,1)} %copy-done.36), custom_call_target="tpu_custom_call" | custom-call | flops 3000000000 | bytes 8388608 | tf_op jit(solution)/shard_map/spread/pallas_call | solution.py:671
  277.5 2.5 finish.1
  (258 shorter events, 35.7 us)
Async XLA Ops:
  2.6 13.4 %collective-permute-start.3 = (bf16[1,96,576]{2,1,0:T(8,128)(2,1)S(1)}, bf16[1,96,576]{2,1,0:T(8,128)(2,1)S(1)}, u32[]{:S(2)}, u32[]{:S(2)}) collective-permute-start(bf16[1,96,576]{2,1,0:T(8,128)(2,1)S(1)} %constant_dynamic-slice_fusion.1), channel_id=1, source_target_pairs={{0,24},{8,0},{16,8},{24,16},{1,25},{9,1},{17,9},{25,17},{2,26},{10... | collective-permute-start | bytes 331784 | tf_op jit(solution)/shard_map/ppermute | solution.py:41
  3.1 12.8 %collective-permute-start.2 = (bf16[1,96,576]{2,1,0:T(8,128)(2,1)S(1)}, bf16[1,96,576]{2,1,0:T(8,128)(2,1)S(1)}, u32[]{:S(2)}, u32[]{:S(2)}) collective-permute-start(bf16[1,96,576]{2,1,0:T(8,128)(2,1)S(1)} %constant_dynamic-slice_fusion.1), channel_id=1, source_target_pairs={{0,16},{8,24},{16,0},{24,8},{1,17},{9,25},{17,1},{25,9},{2,18},{10... | collective-permute-start | bytes 331784 | tf_op jit(solution)/shard_map/ppermute | solution.py:41
  5.7 10.2 %collective-permute-start.1 = (bf16[1,96,576]{2,1,0:T(8,128)(2,1)S(1)}, bf16[1,96,576]{2,1,0:T(8,128)(2,1)S(1)}, u32[]{:S(2)}, u32[]{:S(2)}) collective-permute-start(bf16[1,96,576]{2,1,0:T(8,128)(2,1)S(1)} %constant_dynamic-slice_fusion.1), channel_id=1, source_target_pairs={{0,8},{8,16},{16,24},{24,0},{1,9},{9,17},{17,25},{25,1},{2,10},{10... | collective-permute-start | bytes 331784 | tf_op jit(solution)/shard_map/ppermute | solution.py:41
  10.0 11.1 %collective-permute-start = (bf16[272,768]{1,0:T(8,128)(2,1)S(1)}, bf16[272,768]{1,0:T(8,128)(2,1)S(1)}, u32[]{:S(2)}, u32[]{:S(2)}) collective-permute-start(bf16[272,768]{1,0:T(8,128)(2,1)S(1)} %fusion.5), channel_id=1, source_target_pairs={{0,4},{4,0},{1,5},{5,1},{2,6},{6,2},{3,7},{7,3},{8,12},{12,8},{9,1... | collective-permute-start | bytes 1253384 | tf_op jit(solution)/shard_map/ppermute | solution.py:36
  11.9 16.7 %collective-permute-start.7 = (bf16[200,1728]{1,0:T(8,128)(2,1)S(1)}, bf16[200,1728]{1,0:T(8,128)(2,1)S(1)}, u32[]{:S(2)}, u32[]{:S(2)}) collective-permute-start(bf16[200,1728]{1,0:T(8,128)(2,1)S(1)} %pad_maximum_fusion.2.refs_8_), channel_id=1, source_target_pairs={{0,2},{1,3},{2,0},{3,1},{4,6},{5,7},{6,4},{7,5},{8,10},{9,11},{10,... | collective-permute-start | bytes 2073608 | tf_op jit(solution)/shard_map/ppermute | solution.py:36
  16.0 33.9 %collective-permute-start.5 = (bf16[96,1728]{1,0:T(8,128)(2,1)}, bf16[96,1728]{1,0:T(8,128)(2,1)}, u32[]{:S(2)}, u32[]{:S(2)}) collective-permute-start(bf16[96,1728]{1,0:T(8,128)(2,1)} %fusion.7), channel_id=1, source_target_pairs={{0,24},{8,0},{16,8},{24,16},{1,25},{9,1},{17,9},{25,17},{2,26},{10... | collective-permute-start | bytes 995336 | tf_op jit(solution)/shard_map/ppermute | solution.py:41
  17.4 36.6 %collective-permute-start.4 = (bf16[96,1728]{1,0:T(8,128)(2,1)}, bf16[96,1728]{1,0:T(8,128)(2,1)}, u32[]{:S(2)}, u32[]{:S(2)}) collective-permute-start(bf16[96,1728]{1,0:T(8,128)(2,1)} %fusion.7), channel_id=1, source_target_pairs={{0,8},{8,16},{16,24},{24,0},{1,9},{9,17},{17,25},{25,1},{2,10},{10... | collective-permute-start | bytes 995336 | tf_op jit(solution)/shard_map/ppermute | solution.py:41
  18.6 12.3 %collective-permute-start.10 = (bf16[3,96,576]{2,1,0:T(8,128)(2,1)S(1)}, bf16[3,96,576]{2,1,0:T(8,128)(2,1)S(1)}, u32[]{:S(2)}, u32[]{:S(2)}) collective-permute-start(bf16[3,96,576]{2,1,0:T(8,128)(2,1)S(1)} %constant_dynamic-update-slice_fusion.refs_9_), channel_id=1, source_target_pairs={{0,4},{4,0},{1,5},{5,1},{2,6},{6,2},{3,7},{7,3},{8,12},{12,8},{9,1... | collective-permute-start | bytes 995336 | tf_op jit(solution)/shard_map/ppermute | solution.py:36
  21.1 2.2 collective-permute-start.6
  28.6 25.4 %collective-permute-start.9 = (bf16[96,1728]{1,0:T(8,128)(2,1)S(1)}, bf16[96,1728]{1,0:T(8,128)(2,1)}, u32[]{:S(2)}, u32[]{:S(2)}) collective-permute-start(bf16[96,1728]{1,0:T(8,128)(2,1)S(1)} %constant_dynamic-slice_fusion), channel_id=1, source_target_pairs={{0,24},{8,0},{16,8},{24,16},{1,25},{9,1},{17,9},{25,17},{2,26},{10... | collective-permute-start | bytes 995336 | tf_op jit(solution)/shard_map/ppermute | solution.py:41
  28.7 25.3 %collective-permute-start.8 = (bf16[96,1728]{1,0:T(8,128)(2,1)S(1)}, bf16[96,1728]{1,0:T(8,128)(2,1)}, u32[]{:S(2)}, u32[]{:S(2)}) collective-permute-start(bf16[96,1728]{1,0:T(8,128)(2,1)S(1)} %constant_dynamic-slice_fusion), channel_id=1, source_target_pairs={{0,8},{8,16},{16,24},{24,0},{1,9},{9,17},{17,25},{25,1},{2,10},{10... | collective-permute-start | bytes 995336 | tf_op jit(solution)/shard_map/ppermute | solution.py:41
  30.9 26.8 %collective-permute-start.14 = (bf16[400,1728]{1,0:T(8,128)(2,1)S(1)}, bf16[400,1728]{1,0:T(8,128)(2,1)}, u32[]{:S(2)}, u32[]{:S(2)}) collective-permute-start(bf16[400,1728]{1,0:T(8,128)(2,1)S(1)} %pad_maximum_fusion), channel_id=1, source_target_pairs={{0,1},{1,0},{2,3},{3,2},{4,5},{5,4},{6,7},{7,6},{8,9},{9,8},{10,11... | collective-permute-start | bytes 4147208 | tf_op jit(solution)/shard_map/ppermute | solution.py:36
  49.9 23.4 %collective-permute-start.18 = (bf16[96,1728]{1,0:T(8,128)(2,1)}, bf16[96,1728]{1,0:T(8,128)(2,1)S(1)}, u32[]{:S(2)}, u32[]{:S(2)}) collective-permute-start(bf16[96,1728]{1,0:T(8,128)(2,1)} %fusion.7), channel_id=1, source_target_pairs={{0,16},{8,24},{16,0},{24,8},{1,17},{9,25},{17,1},{25,9},{2,18},{10... | collective-permute-start | bytes 995336 | tf_op jit(solution)/shard_map/ppermute | solution.py:41
  56.0 16.9 %collective-permute-start.13 = (bf16[192,1728]{1,0:T(8,128)(2,1)S(1)}, bf16[192,1728]{1,0:T(8,128)(2,1)S(1)}, u32[]{:S(2)}, u32[]{:S(2)}) collective-permute-start(bf16[192,1728]{1,0:T(8,128)(2,1)S(1)} %constant_dynamic-update-slice_fusion.3.refs_11_), channel_id=1, source_target_pairs={{0,4},{4,0},{1,5},{5,1},{2,6},{6,2},{3,7},{7,3},{8,12},{12,8},{9,1... | collective-permute-start | bytes 1990664 | tf_op jit(solution)/shard_map/ppermute | solution.py:36
  56.6 16.7 %collective-permute-start.12 = (bf16[192,1728]{1,0:T(8,128)(2,1)S(1)}, bf16[192,1728]{1,0:T(8,128)(2,1)}, u32[]{:S(2)}, u32[]{:S(2)}) collective-permute-start(bf16[192,1728]{1,0:T(8,128)(2,1)S(1)} %constant_dynamic-update-slice_fusion.3.refs_11_), channel_id=1, source_target_pairs={{0,2},{1,3},{2,0},{3,1},{4,6},{5,7},{6,4},{7,5},{8,10},{9,11},{10,... | collective-permute-start | bytes 1990664 | tf_op jit(solution)/shard_map/ppermute | solution.py:36
  57.7 15.6 %collective-permute-start.11 = (bf16[192,1728]{1,0:T(8,128)(2,1)S(1)}, bf16[192,1728]{1,0:T(8,128)(2,1)}, u32[]{:S(2)}, u32[]{:S(2)}) collective-permute-start(bf16[192,1728]{1,0:T(8,128)(2,1)S(1)} %constant_dynamic-update-slice_fusion.3.refs_11_), channel_id=1, source_target_pairs={{0,1},{1,0},{2,3},{3,2},{4,5},{5,4},{6,7},{7,6},{8,9},{9,8},{10,11... | collective-permute-start | bytes 1990664 | tf_op jit(solution)/shard_map/ppermute | solution.py:36
  57.8 35.5 %copy-start.21 = (bf16[768]{0:T(1024)(128)(2,1)S(1)}, bf16[768]{0:T(1024)(128)(2,1)}, u32[]{:S(2)}) copy-start(bf16[768]{0:T(1024)(128)(2,1)} %param.33) | copy-start | bytes 4612
  57.8 35.5 %copy-start.22 = (bf16[768]{0:T(1024)(128)(2,1)S(1)}, bf16[768]{0:T(1024)(128)(2,1)}, u32[]{:S(2)}) copy-start(bf16[768]{0:T(1024)(128)(2,1)} %param.34) | copy-start | bytes 4612
  73.3 8.7 %collective-permute-start.19 = (bf16[96,1728]{1,0:T(8,128)(2,1)S(1)}, bf16[96,1728]{1,0:T(8,128)(2,1)S(1)}, u32[]{:S(2)}, u32[]{:S(2)}) collective-permute-start(bf16[96,1728]{1,0:T(8,128)(2,1)S(1)} %collective-permute-done.18.refs_21_), channel_id=1, source_target_pairs={{0,4},{4,0},{1,5},{5,1},{2,6},{6,2},{3,7},{7,3},{8,12},{12,8},{9,1... | collective-permute-start | bytes 995336 | tf_op jit(solution)/shard_map/ppermute | solution.py:36
  74.9 10.9 %collective-permute-start.25 = (bf16[96,1728]{1,0:T(8,128)(2,1)S(1)}, bf16[96,1728]{1,0:T(8,128)(2,1)S(1)}, u32[]{:S(2)}, u32[]{:S(2)}) collective-permute-start(bf16[96,1728]{1,0:T(8,128)(2,1)S(1)} %collective-permute-done.18.refs_21_), channel_id=1, source_target_pairs={{0,2},{1,3},{2,0},{3,1},{4,6},{5,7},{6,4},{7,5},{8,10},{9,11},{10,... | collective-permute-start | bytes 995336 | tf_op jit(solution)/shard_map/ppermute | solution.py:36
  76.4 13.3 %collective-permute-start.28 = (bf16[96,1728]{1,0:T(8,128)(2,1)S(1)}, bf16[96,1728]{1,0:T(8,128)(2,1)S(1)}, u32[]{:S(2)}, u32[]{:S(2)}) collective-permute-start(bf16[96,1728]{1,0:T(8,128)(2,1)S(1)} %constant_dynamic-slice_fusion), channel_id=1, source_target_pairs={{0,16},{8,24},{16,0},{24,8},{1,17},{9,25},{17,1},{25,9},{2,18},{10... | collective-permute-start | bytes 995336 | tf_op jit(solution)/shard_map/ppermute | solution.py:41
  76.7 1.7 collective-permute-start.15
  76.8 13.0 %collective-permute-start.16 = (bf16[384,192]{1,0:T(8,128)(2,1)S(1)}, bf16[384,192]{1,0:T(8,128)(2,1)S(1)}, u32[]{:S(2)}, u32[]{:S(2)}) collective-permute-start(bf16[384,192]{1,0:T(8,128)(2,1)S(1)} %copy-done.49), channel_id=1, source_target_pairs={{0,2},{1,3},{2,0},{3,1},{4,6},{5,7},{6,4},{7,5},{8,10},{9,11},{10,... | collective-permute-start | bytes 442376 | tf_op jit(solution)/shard_map/ppermute | solution.py:36
  78.4 12.1 %collective-permute-start.17 = (bf16[384,192]{1,0:T(8,128)(2,1)S(1)}, bf16[384,192]{1,0:T(8,128)(2,1)S(1)}, u32[]{:S(2)}, u32[]{:S(2)}) collective-permute-start(bf16[384,192]{1,0:T(8,128)(2,1)S(1)} %copy-done.47), channel_id=1, source_target_pairs={{0,3},{1,2},{2,1},{3,0},{4,7},{5,6},{6,5},{7,4},{8,11},{9,10},{10,... | collective-permute-start | bytes 442376 | tf_op jit(solution)/shard_map/ppermute | solution.py:36
  81.9 9.4 %collective-permute-start.20 = (bf16[96,1728]{1,0:T(8,128)(2,1)}, bf16[96,1728]{1,0:T(8,128)(2,1)S(1)}, u32[]{:S(2)}, u32[]{:S(2)}) collective-permute-start(bf16[96,1728]{1,0:T(8,128)(2,1)} %collective-permute-done.8.refs_13_), channel_id=1, source_target_pairs={{0,1},{1,0},{2,3},{3,2},{4,5},{5,4},{6,7},{7,6},{8,9},{9,8},{10,11... | collective-permute-start | bytes 995336 | tf_op jit(solution)/shard_map/ppermute | solution.py:36
  85.8 5.4 %collective-permute-start.26 = (bf16[96,1728]{1,0:T(8,128)(2,1)S(1)}, bf16[96,1728]{1,0:T(8,128)(2,1)S(1)}, u32[]{:S(2)}, u32[]{:S(2)}) collective-permute-start(bf16[96,1728]{1,0:T(8,128)(2,1)S(1)} %collective-permute-done.25.refs_23_), channel_id=1, source_target_pairs={{0,1},{1,0},{2,3},{3,2},{4,5},{5,4},{6,7},{7,6},{8,9},{9,8},{10,11... | collective-permute-start | bytes 995336 | tf_op jit(solution)/shard_map/ppermute | solution.py:36
  89.7 2.0 collective-permute-start.21
  89.7 5.4 %collective-permute-start.22 = (bf16[192,1728]{1,0:T(8,128)(2,1)}, bf16[192,1728]{1,0:T(8,128)(2,1)S(1)}, u32[]{:S(2)}, u32[]{:S(2)}) collective-permute-start(bf16[192,1728]{1,0:T(8,128)(2,1)} %collective-permute-done.12.refs_17_), channel_id=1, source_target_pairs={{0,1},{1,0},{2,3},{3,2},{4,5},{5,4},{6,7},{7,6},{8,9},{9,8},{10,11... | collective-permute-start | bytes 1990664 | tf_op jit(solution)/shard_map/ppermute | solution.py:36
  90.5 4.7 %collective-permute-start.23 = (bf16[192,1728]{1,0:T(8,128)(2,1)S(1)}, bf16[192,1728]{1,0:T(8,128)(2,1)S(1)}, u32[]{:S(2)}, u32[]{:S(2)}) collective-permute-start(bf16[192,1728]{1,0:T(8,128)(2,1)S(1)} %collective-permute-done.13.refs_19_), channel_id=1, source_target_pairs={{0,1},{1,0},{2,3},{3,2},{4,5},{5,4},{6,7},{7,6},{8,9},{9,8},{10,11... | collective-permute-start | bytes 1990664 | tf_op jit(solution)/shard_map/ppermute | solution.py:36
  91.2 3.0 %collective-permute-start.24 = (bf16[96,1728]{1,0:T(8,128)(2,1)}, bf16[96,1728]{1,0:T(8,128)(2,1)}, u32[]{:S(2)}, u32[]{:S(2)}) collective-permute-start(bf16[96,1728]{1,0:T(8,128)(2,1)} %copy-done.39), channel_id=1, source_target_pairs={{0,1},{1,0},{2,3},{3,2},{4,5},{5,4},{6,7},{7,6},{8,9},{9,8},{10,11... | collective-permute-start | bytes 995336 | tf_op jit(solution)/shard_map/ppermute | solution.py:36
  91.3 3.4 %collective-permute-start.29 = (bf16[96,1728]{1,0:T(8,128)(2,1)S(1)}, bf16[96,1728]{1,0:T(8,128)(2,1)}, u32[]{:S(2)}, u32[]{:S(2)}) collective-permute-start(bf16[96,1728]{1,0:T(8,128)(2,1)S(1)} %collective-permute-done.28.refs_27_), channel_id=1, source_target_pairs={{0,1},{1,0},{2,3},{3,2},{4,5},{5,4},{6,7},{7,6},{8,9},{9,8},{10,11... | collective-permute-start | bytes 995336 | tf_op jit(solution)/shard_map/ppermute | solution.py:36
  92.8 2.4 collective-permute-start.27
  120.5 5.4 %collective-permute-start.31 = (bf16[2,384,1792]{2,1,0:T(8,128)(2,1)}, bf16[2,384,1792]{2,1,0:T(8,128)(2,1)S(1)}, u32[]{:S(2)}, u32[]{:S(2)}) collective-permute-start(bf16[2,384,1792]{2,1,0:T(8,128)(2,1)} %get-tuple-element.161), channel_id=1, source_target_pairs={{0,1},{1,0},{2,3},{3,2},{4,5},{5,4},{6,7},{7,6},{8,9},{9,8},{10,11... | collective-permute-start | bytes 8257544 | tf_op jit(solution)/shard_map/ppermute | solution.py:36
  120.7 7.8 %collective-permute-start.30 = (bf16[3,768,384]{2,1,0:T(8,128)(2,1)}, bf16[3,768,384]{2,1,0:T(8,128)(2,1)}, u32[]{:S(2)}, u32[]{:S(2)}) collective-permute-start(bf16[3,768,384]{2,1,0:T(8,128)(2,1)} %get-tuple-element.159.refs_1_), channel_id=1, source_target_pairs={{0,1},{1,0},{2,3},{3,2},{4,5},{5,4},{6,7},{7,6},{8,9},{9,8},{10,11... | collective-permute-start | bytes 5308424 | tf_op jit(solution)/shard_map/ppermute | solution.py:36
  121.9 19.5 %collective-permute-start.33 = (bf16[384,192]{1,0:T(8,128)(2,1)}, bf16[384,192]{1,0:T(8,128)(2,1)S(1)}, u32[]{:S(2)}, u32[]{:S(2)}) collective-permute-start(bf16[384,192]{1,0:T(8,128)(2,1)} %get-tuple-element.167), channel_id=1, source_target_pairs={{0,1},{1,0},{2,3},{3,2},{4,5},{5,4},{6,7},{7,6},{8,9},{9,8},{10,11... | collective-permute-start | bytes 442376 | tf_op jit(solution)/shard_map/ppermute | solution.py:36
  122.1 19.4 %collective-permute-start.34 = (bf16[384,192]{1,0:T(8,128)(2,1)}, bf16[384,192]{1,0:T(8,128)(2,1)S(1)}, u32[]{:S(2)}, u32[]{:S(2)}) collective-permute-start(bf16[384,192]{1,0:T(8,128)(2,1)} %get-tuple-element.168), channel_id=1, source_target_pairs={{0,2},{1,3},{2,0},{3,1},{4,6},{5,7},{6,4},{7,5},{8,10},{9,11},{10,... | collective-permute-start | bytes 442376 | tf_op jit(solution)/shard_map/ppermute | solution.py:36
  123.3 18.1 %collective-permute-start.35 = (bf16[384,192]{1,0:T(8,128)(2,1)}, bf16[384,192]{1,0:T(8,128)(2,1)S(1)}, u32[]{:S(2)}, u32[]{:S(2)}) collective-permute-start(bf16[384,192]{1,0:T(8,128)(2,1)} %get-tuple-element.169), channel_id=1, source_target_pairs={{0,3},{1,2},{2,1},{3,0},{4,7},{5,6},{6,5},{7,4},{8,11},{9,10},{10,... | collective-permute-start | bytes 442376 | tf_op jit(solution)/shard_map/ppermute | solution.py:36
  125.9 15.5 %collective-permute-start.32 = (f32[8,768]{1,0:T(8,128)S(1)}, f32[8,768]{1,0:T(8,128)S(1)}, u32[]{:S(2)}, u32[]{:S(2)}) collective-permute-start(f32[8,768]{1,0:T(8,128)S(1)} %pad_maximum_fusion.4), channel_id=1, source_target_pairs={{0,1},{1,0},{2,3},{3,2},{4,5},{5,4},{6,7},{7,6},{8,9},{9,8},{10,11... | collective-permute-start | bytes 73736 | tf_op jit(solution)/shard_map/ppermute | solution.py:36
  141.5 26.2 %collective-permute-start.38 = (f32[8,768]{1,0:T(8,128)S(1)}, f32[8,768]{1,0:T(8,128)S(1)}, u32[]{:S(2)}, u32[]{:S(2)}) collective-permute-start(f32[8,768]{1,0:T(8,128)S(1)} %pad_maximum_fusion.5), channel_id=1, source_target_pairs={{0,2},{1,3},{2,0},{3,1},{4,6},{5,7},{6,4},{7,5},{8,10},{9,11},{10,... | collective-permute-start | bytes 73736 | tf_op jit(solution)/shard_map/ppermute | solution.py:36
  142.6 32.4 %collective-permute-start.36 = (bf16[4,96,1728]{2,1,0:T(8,128)(2,1)}, bf16[4,96,1728]{2,1,0:T(8,128)(2,1)S(1)}, u32[]{:S(2)}, u32[]{:S(2)}) collective-permute-start(bf16[4,96,1728]{2,1,0:T(8,128)(2,1)} %get-tuple-element.187), channel_id=1, source_target_pairs={{0,2},{1,3},{2,0},{3,1},{4,6},{5,7},{6,4},{7,5},{8,10},{9,11},{10,... | collective-permute-start | bytes 3981320 | tf_op jit(solution)/shard_map/ppermute | solution.py:36
  143.6 31.9 %collective-permute-start.37 = (bf16[2,2,96,1728]{3,2,1,0:T(8,128)(2,1)}, bf16[2,2,96,1728]{3,2,1,0:T(8,128)(2,1)S(1)}, u32[]{:S(2)}, u32[]{:S(2)}) collective-permute-start(bf16[2,2,96,1728]{3,2,1,0:T(8,128)(2,1)} %get-tuple-element.188), channel_id=1, source_target_pairs={{0,4},{4,0},{1,5},{5,1},{2,6},{6,2},{3,7},{7,3},{8,12},{12,8},{9,1... | collective-permute-start | bytes 3981320 | tf_op jit(solution)/shard_map/ppermute | solution.py:36
  175.5 12.7 %collective-permute-start.39 = (bf16[512,384]{1,0:T(8,128)(2,1)}, bf16[512,384]{1,0:T(8,128)(2,1)S(1)}, u32[]{:S(2)}, u32[]{:S(2)}) collective-permute-start(bf16[512,384]{1,0:T(8,128)(2,1)} %get-tuple-element.194), channel_id=1, source_target_pairs={{0,4},{4,0},{1,5},{5,1},{2,6},{6,2},{3,7},{7,3},{8,12},{12,8},{9,1... | collective-permute-start | bytes 1179656 | tf_op jit(solution)/shard_map/ppermute | solution.py:36
  175.9 12.3 %collective-permute-start.40 = (f32[8,768]{1,0:T(8,128)S(1)}, f32[8,768]{1,0:T(8,128)S(1)}, u32[]{:S(2)}, u32[]{:S(2)}) collective-permute-start(f32[8,768]{1,0:T(8,128)S(1)} %add.60), channel_id=1, source_target_pairs={{0,4},{4,0},{1,5},{5,1},{2,6},{6,2},{3,7},{7,3},{8,12},{12,8},{9,1... | collective-permute-start | bytes 73736 | tf_op jit(solution)/shard_map/ppermute | solution.py:36
  182.0 18.9 %collective-permute-start.42 = (bf16[2,96,1728]{2,1,0:T(8,128)(2,1)}, bf16[2,96,1728]{2,1,0:T(8,128)(2,1)S(1)}, u32[]{:S(2)}, u32[]{:S(2)}) collective-permute-start(bf16[2,96,1728]{2,1,0:T(8,128)(2,1)} %get-tuple-element.197), channel_id=1, source_target_pairs={{0,4},{4,0},{1,5},{5,1},{2,6},{6,2},{3,7},{7,3},{8,12},{12,8},{9,1... | collective-permute-start | bytes 1990664 | tf_op jit(solution)/shard_map/ppermute | solution.py:36
  182.3 18.5 %collective-permute-start.43 = (bf16[2,96,1728]{2,1,0:T(8,128)(2,1)}, bf16[2,96,1728]{2,1,0:T(8,128)(2,1)S(1)}, u32[]{:S(2)}, u32[]{:S(2)}) collective-permute-start(bf16[2,96,1728]{2,1,0:T(8,128)(2,1)} %get-tuple-element.198), channel_id=1, source_target_pairs={{0,2},{1,3},{2,0},{3,1},{4,6},{5,7},{6,4},{7,5},{8,10},{9,11},{10,... | collective-permute-start | bytes 1990664 | tf_op jit(solution)/shard_map/ppermute | solution.py:36
  188.2 11.2 %collective-permute-start.51 = (f32[8,768]{1,0:T(8,128)S(1)}, f32[8,768]{1,0:T(8,128)S(1)}, u32[]{:S(2)}, u32[]{:S(2)}) collective-permute-start(f32[8,768]{1,0:T(8,128)S(1)} %add.61), channel_id=1, source_target_pairs={{0,8},{8,0},{16,24},{24,16},{1,9},{9,1},{17,25},{25,17},{2,10},{10... | collective-permute-start | bytes 73736 | tf_op jit(solution)/shard_map/ppermute | solution.py:36
  201.8 8.6 %collective-permute-start.52 = (bf16[2,384,768]{2,1,0:T(8,128)(2,1)}, bf16[2,384,768]{2,1,0:T(8,128)(2,1)S(1)}, u32[]{:S(2)}, u32[]{:S(2)}) collective-permute-start(bf16[2,384,768]{2,1,0:T(8,128)(2,1)} %get-tuple-element.218), channel_id=1, source_target_pairs={{0,1},{1,0},{2,3},{3,2},{4,5},{5,4},{6,7},{7,6},{8,9},{9,8},{10,11... | collective-permute-start | bytes 3538952 | tf_op jit(solution)/shard_map/ppermute | solution.py:36
  201.8 13.9 %collective-permute-start.41 = (bf16[4,96,640]{2,1,0:T(8,128)(2,1)}, bf16[4,96,640]{2,1,0:T(8,128)(2,1)}, u32[]{:S(2)}, u32[]{:S(2)}) collective-permute-start(bf16[4,96,640]{2,1,0:T(8,128)(2,1)} %get-tuple-element.202), channel_id=1, source_target_pairs={{0,4},{4,0},{1,5},{5,1},{2,6},{6,2},{3,7},{7,3},{8,12},{12,8},{9,1... | collective-permute-start | bytes 1474568 | tf_op jit(solution)/shard_map/ppermute | solution.py:36
  202.4 9.5 %collective-permute-start.57 = (f32[8,768]{1,0:T(8,128)S(1)}, f32[8,768]{1,0:T(8,128)S(1)}, u32[]{:S(2)}, u32[]{:S(2)}) collective-permute-start(f32[8,768]{1,0:T(8,128)S(1)} %add.62), channel_id=1, source_target_pairs={{0,16},{8,24},{16,0},{24,8},{1,17},{9,25},{17,1},{25,9},{2,18},{10... | collective-permute-start | bytes 73736 | tf_op jit(solution)/shard_map/ppermute | solution.py:36
  208.5 24.4 %collective-permute-start.54 = (bf16[96,1728]{1,0:T(8,128)(2,1)}, bf16[96,1728]{1,0:T(8,128)(2,1)}, u32[]{:S(2)}, u32[]{:S(2)}) collective-permute-start(bf16[96,1728]{1,0:T(8,128)(2,1)} %get-tuple-element.219), channel_id=1, source_target_pairs={{0,8},{8,16},{16,24},{24,0},{1,9},{9,17},{17,25},{25,1},{2,10},{10... | collective-permute-start | bytes 995336 | tf_op jit(solution)/shard_map/ppermute | solution.py:41
  209.5 29.9 %collective-permute-start.55 = (bf16[96,1728]{1,0:T(8,128)(2,1)}, bf16[96,1728]{1,0:T(8,128)(2,1)}, u32[]{:S(2)}, u32[]{:S(2)}) collective-permute-start(bf16[96,1728]{1,0:T(8,128)(2,1)} %get-tuple-element.220), channel_id=1, source_target_pairs={{0,16},{8,24},{16,0},{24,8},{1,17},{9,25},{17,1},{25,9},{2,18},{10... | collective-permute-start | bytes 995336 | tf_op jit(solution)/shard_map/ppermute | solution.py:41
  210.4 30.6 %collective-permute-start.56 = (bf16[96,1728]{1,0:T(8,128)(2,1)}, bf16[96,1728]{1,0:T(8,128)(2,1)}, u32[]{:S(2)}, u32[]{:S(2)}) collective-permute-start(bf16[96,1728]{1,0:T(8,128)(2,1)} %get-tuple-element.221), channel_id=1, source_target_pairs={{0,24},{8,0},{16,8},{24,16},{1,25},{9,1},{17,9},{25,17},{2,26},{10... | collective-permute-start | bytes 995336 | tf_op jit(solution)/shard_map/ppermute | solution.py:41
  211.9 31.7 %collective-permute-start.53 = (bf16[384,768]{1,0:T(8,128)(2,1)}, bf16[384,768]{1,0:T(8,128)(2,1)}, u32[]{:S(2)}, u32[]{:S(2)}) collective-permute-start(bf16[384,768]{1,0:T(8,128)(2,1)} %fusion.3), channel_id=1, source_target_pairs={{0,2},{1,3},{2,0},{3,1},{4,6},{5,7},{6,4},{7,5},{8,10},{9,11},{10,... | collective-permute-start | bytes 1769480 | tf_op jit(solution)/shard_map/ppermute | solution.py:36
  217.8 29.4 %collective-permute-start.46 = (bf16[384,768]{1,0:T(8,128)(2,1)}, bf16[384,768]{1,0:T(8,128)(2,1)}, u32[]{:S(2)}, u32[]{:S(2)}) collective-permute-start(bf16[384,768]{1,0:T(8,128)(2,1)} %get-tuple-element.210.p_0), channel_id=1, source_target_pairs={{0,2},{1,3},{2,0},{3,1},{4,6},{5,7},{6,4},{7,5},{8,10},{9,11},{10,... | collective-permute-start | bytes 1769480 | tf_op jit(solution)/shard_map/ppermute | solution.py:36
  245.8 15.8 %collective-permute-start.59 = (bf16[384,768]{1,0:T(8,128)(2,1)}, bf16[384,768]{1,0:T(8,128)(2,1)S(1)}, u32[]{:S(2)}, u32[]{:S(2)}) collective-permute-start(bf16[384,768]{1,0:T(8,128)(2,1)} %fusion.1.p_0), channel_id=1, source_target_pairs={{0,2},{1,3},{2,0},{3,1},{4,6},{5,7},{6,4},{7,5},{8,10},{9,11},{10,... | collective-permute-start | bytes 1769480 | tf_op jit(solution)/shard_map/ppermute | solution.py:36
  247.2 15.1 %collective-permute-start.45 = (bf16[384,768]{1,0:T(8,128)(2,1)S(1)}, bf16[384,768]{1,0:T(8,128)(2,1)S(1)}, u32[]{:S(2)}, u32[]{:S(2)}) collective-permute-start(bf16[384,768]{1,0:T(8,128)(2,1)S(1)} %copy-done.31), channel_id=1, source_target_pairs={{0,1},{1,0},{2,3},{3,2},{4,5},{5,4},{6,7},{7,6},{8,9},{9,8},{10,11... | collective-permute-start | bytes 1769480 | tf_op jit(solution)/shard_map/ppermute | solution.py:36
  247.2 15.1 %collective-permute-start.47 = (bf16[384,768]{1,0:T(8,128)(2,1)}, bf16[384,768]{1,0:T(8,128)(2,1)S(1)}, u32[]{:S(2)}, u32[]{:S(2)}) collective-permute-start(bf16[384,768]{1,0:T(8,128)(2,1)} %collective-permute-done.46.p_2), channel_id=1, source_target_pairs={{0,1},{1,0},{2,3},{3,2},{4,5},{5,4},{6,7},{7,6},{8,9},{9,8},{10,11... | collective-permute-start | bytes 1769480 | tf_op jit(solution)/shard_map/ppermute | solution.py:36
  247.7 6.2 %collective-permute-start.44 = (bf16[96,640]{1,0:T(8,128)(2,1)S(1)}, bf16[96,640]{1,0:T(8,128)(2,1)S(1)}, u32[]{:S(2)}, u32[]{:S(2)}) collective-permute-start(bf16[96,640]{1,0:T(8,128)(2,1)S(1)} %copy-done.57), channel_id=1, source_target_pairs={{0,8},{8,16},{16,24},{24,0},{1,9},{9,17},{17,25},{25,1},{2,10},{10... | collective-permute-start | bytes 368648 | tf_op jit(solution)/shard_map/ppermute | solution.py:41
  247.7 9.7 %collective-permute-start.48 = (bf16[96,640]{1,0:T(8,128)(2,1)S(1)}, bf16[96,640]{1,0:T(8,128)(2,1)}, u32[]{:S(2)}, u32[]{:S(2)}) collective-permute-start(bf16[96,640]{1,0:T(8,128)(2,1)S(1)} %copy-done.56), channel_id=1, source_target_pairs={{0,16},{8,24},{16,0},{24,8},{1,17},{9,25},{17,1},{25,9},{2,18},{10... | collective-permute-start | bytes 368648 | tf_op jit(solution)/shard_map/ppermute | solution.py:41
  253.9 7.0 %collective-permute-start.49 = (bf16[96,640]{1,0:T(8,128)(2,1)S(1)}, bf16[96,640]{1,0:T(8,128)(2,1)S(1)}, u32[]{:S(2)}, u32[]{:S(2)}) collective-permute-start(bf16[96,640]{1,0:T(8,128)(2,1)S(1)} %copy-done.55), channel_id=1, source_target_pairs={{0,24},{8,0},{16,8},{24,16},{1,25},{9,1},{17,9},{25,17},{2,26},{10... | collective-permute-start | bytes 368648 | tf_op jit(solution)/shard_map/ppermute | solution.py:41
  257.4 13.0 %collective-permute-start.58 = (bf16[384,768]{1,0:T(8,128)(2,1)}, bf16[384,768]{1,0:T(8,128)(2,1)S(1)}, u32[]{:S(2)}, u32[]{:S(2)}) collective-permute-start(bf16[384,768]{1,0:T(8,128)(2,1)} %fusion.1.p_0), channel_id=1, source_target_pairs={{0,1},{1,0},{2,3},{3,2},{4,5},{5,4},{6,7},{7,6},{8,9},{9,8},{10,11... | collective-permute-start | bytes 1769480 | tf_op jit(solution)/shard_map/ppermute | solution.py:36
  261.6 8.8 %collective-permute-start.60 = (bf16[384,768]{1,0:T(8,128)(2,1)S(1)}, bf16[384,768]{1,0:T(8,128)(2,1)S(1)}, u32[]{:S(2)}, u32[]{:S(2)}) collective-permute-start(bf16[384,768]{1,0:T(8,128)(2,1)S(1)} %collective-permute-done.59.p_2), channel_id=1, source_target_pairs={{0,1},{1,0},{2,3},{3,2},{4,5},{5,4},{6,7},{7,6},{8,9},{9,8},{10,11... | collective-permute-start | bytes 1769480 | tf_op jit(solution)/shard_map/ppermute | solution.py:36
  261.6 15.2 %collective-permute-start.61 = (bf16[96,1728]{1,0:T(8,128)(2,1)}, bf16[96,1728]{1,0:T(8,128)(2,1)S(1)}, u32[]{:S(2)}, u32[]{:S(2)}) collective-permute-start(bf16[96,1728]{1,0:T(8,128)(2,1)} %merge_three.3.own), channel_id=1, source_target_pairs={{0,4},{4,0},{1,5},{5,1},{2,6},{6,2},{3,7},{7,3},{8,12},{12,8},{9,1... | collective-permute-start | bytes 995336 | tf_op jit(solution)/shard_map/ppermute | solution.py:36
  269.0 7.1 %collective-permute-start.50 = (bf16[96,640]{1,0:T(8,128)(2,1)}, bf16[96,640]{1,0:T(8,128)(2,1)S(1)}, u32[]{:S(2)}, u32[]{:S(2)}) collective-permute-start(bf16[96,640]{1,0:T(8,128)(2,1)} %merge_three.2.d_own), channel_id=1, source_target_pairs={{0,4},{4,0},{1,5},{5,1},{2,6},{6,2},{3,7},{7,3},{8,12},{12,8},{9,1... | collective-permute-start | bytes 368648 | tf_op jit(solution)/shard_map/ppermute | solution.py:36
  (61 other events, 490.5 us)
